TPU v7x, 32 devices: a whole 2x2x4 slice. The times are simulated.
32 devices in a mesh: dp: 8 (over z, x), tensor: 4 (over y, core).
Axes of the slice: x: 2, y: 2, z: 4, core: 2. Of those that a mesh axis runs over, the one named last changes fastest.
Arguments:
- image_tokens: bfloat16 [16, 1024, 1536], P('dp', 'tensor'), may hold values from -6 to 6
- text_tokens: bfloat16 [16, 154, 1536], P('dp'), may hold values from -6 to 6
- condition: bfloat16 [16, 1536], P('dp'), may hold values from -6 to 6
- group_size: int32 [8], P('dp'), may hold values from 1 to 2, as said below
- image_modulation: bfloat16 [1536, 6, 1536], P('dp', None, 'tensor'), may hold values from -0.15625 to 0.15625
- image_attention_in: bfloat16 [1536, 3, 1536], P('dp', None, 'tensor'), may hold values from -0.15625 to 0.15625
- image_attention_out: bfloat16 [1536, 1536], P('tensor', 'dp'), may hold values from -1.25 to 1.25
- image_hidden_in: bfloat16 [1536, 6144], P('dp', 'tensor'), may hold values from -0.15625 to 0.15625
- image_hidden_out: bfloat16 [6144, 1536], P('tensor', 'dp'), may hold values from -0.078125 to 0.078125
- text_modulation: bfloat16 [1536, 6, 1536], P('dp', None, 'tensor'), may hold values from -0.15625 to 0.15625
- text_attention_in: bfloat16 [1536, 3, 1536], P('dp', None, 'tensor'), may hold values from -0.15625 to 0.15625
- text_attention_out: bfloat16 [1536, 1536], P('tensor', 'dp'), may hold values from -1.25 to 1.25
- text_hidden_in: bfloat16 [1536, 6144], P('dp', 'tensor'), may hold values from -0.15625 to 0.15625
- text_hidden_out: bfloat16 [6144, 1536], P('tensor', 'dp'), may hold values from -0.078125 to 0.078125
- image_cotangent: bfloat16 [16, 1024, 1536], P('dp', 'tensor'), may hold values from -6 to 6
- text_cotangent: bfloat16 [16, 154, 1536], P('dp'), may hold values from -6 to 6
Outputs:
- image_output: bfloat16 [16, 1024, 1536], P('dp', 'tensor')
- text_output: bfloat16 [16, 154, 1536], P('dp')
- image_gradient: float32 [16, 1024, 1536], P('dp', 'tensor')
- text_gradient: float32 [16, 154, 1536], P('dp')
- condition_gradient: float32 [16, 1536], P('dp')
- image_modulation_gradient: float32 [1536, 6, 1536], P('dp', None, 'tensor')
- image_attention_in_gradient: float32 [1536, 3, 1536], P('dp', None, 'tensor')
- image_attention_out_gradient: float32 [1536, 1536], P('tensor', 'dp')
- image_hidden_in_gradient: float32 [1536, 6144], P('dp', 'tensor')
- image_hidden_out_gradient: float32 [6144, 1536], P('tensor', 'dp')
- text_modulation_gradient: float32 [1536, 6, 1536], P('dp', None, 'tensor')
- text_attention_in_gradient: float32 [1536, 3, 1536], P('dp', None, 'tensor')
- text_attention_out_gradient: float32 [1536, 1536], P('tensor', 'dp')
- text_hidden_in_gradient: float32 [1536, 6144], P('dp', 'tensor')
- text_hidden_out_gradient: float32 [6144, 1536], P('tensor', 'dp')
Inputs may be any that keep to these rules, and one draw needn't show every extreme that they name: `group_size`: each entry is the number of live sequences of that group; the entries sum to 13.
All inputs are finite; a program needn't handle non-finite values.
Results may differ from a plain program's by a relative error of at most 0.018.
The roundings to bfloat16 on the way count: a program that leaves them out, or rounds other values in their place, can miss the bound.
Values may be sent and summed in bfloat16 or wider, within the bound.
No kernel may reach another device: no remote copies, remote signals or barrier semaphores. Data moves between devices by JAX's collectives and lax.ppermute only.
A program may use at most 248 MiB of HBM per device.

v0:
```python
import jax
import jax.numpy as jnp
from jax import lax
from jax.sharding import PartitionSpec as P

HEAD = 64


def norm_rows(values):
    center = values - jnp.mean(values, axis=-1, keepdims=True)
    inverse = lax.rsqrt(jnp.mean(center * center, axis=-1, keepdims=True) + 1e-06)
    return (center * inverse, inverse)


def norm_back(upstream, normed, inverse):
    first = jnp.mean(upstream, axis=-1, keepdims=True)
    second = jnp.mean(upstream * normed, axis=-1, keepdims=True)
    return inverse * (upstream - first - normed * second)


def gelu_tanh(values):
    return jax.nn.gelu(values, approximate=True)


def spread(vector):
    return vector[:, None, :]


def image_rows(values):
    return lax.all_gather(values, "tensor", axis=1, tiled=True)


def image_partial(values):
    return lax.psum_scatter(values, "tensor", scatter_dimension=1, tiled=True)


def text_partial(values):
    return lax.psum(values, "tensor")


def keep_rows(values):
    return values


def split_heads(joint):
    length = joint.shape[0]
    width = joint.shape[2]
    heads = width // HEAD
    queries = joint[:, 0].reshape(length, heads, HEAD)
    key_rows = joint[:, 1].reshape(length, heads, HEAD)
    value_rows = joint[:, 2].reshape(length, heads, HEAD)
    scores = jnp.einsum(
        "qhe,khe->hqk", queries, key_rows, preferred_element_type=jnp.float32
    ) * HEAD ** (-0.5)
    return (queries, key_rows, value_rows, scores)


def attend(joint):
    length = joint.shape[0]
    width = joint.shape[2]
    queries, key_rows, value_rows, scores = split_heads(joint)
    highest = jnp.max(scores, axis=-1, keepdims=True)
    layer_weights = jnp.exp(scores - highest)
    totals = jnp.sum(layer_weights, axis=-1, keepdims=True)
    weights_low = (layer_weights / totals).astype(jnp.bfloat16)
    mixed = jnp.einsum("hqk,khe->qhe", weights_low, value_rows, preferred_element_type=jnp.float32)
    return (mixed.reshape(length, width).astype(jnp.bfloat16), highest + jnp.log(totals))


def attend_back(item):
    joint, upstream, logsum = item
    length = joint.shape[0]
    width = joint.shape[2]
    heads = width // HEAD
    queries, key_rows, value_rows, scores = split_heads(joint)
    layer_weights = jnp.exp(scores - logsum)
    upstream_heads = upstream.reshape(length, heads, HEAD)
    along = jnp.einsum(
        "qhe,khe->hqk", upstream_heads, value_rows, preferred_element_type=jnp.float32
    )
    value_grad = jnp.einsum(
        "hqk,qhe->khe",
        layer_weights.astype(jnp.bfloat16),
        upstream_heads,
        preferred_element_type=jnp.float32,
    )
    score_grad = (
        layer_weights * (along - jnp.sum(layer_weights * along, axis=-1, keepdims=True))
    ).astype(jnp.bfloat16)
    query_grad = jnp.einsum(
        "hqk,khe->qhe", score_grad, key_rows, preferred_element_type=jnp.float32
    ) * HEAD ** (-0.5)
    key_grad = jnp.einsum(
        "hqk,qhe->khe", score_grad, queries, preferred_element_type=jnp.float32
    ) * HEAD ** (-0.5)
    stacked = jnp.stack([query_grad, key_grad, value_grad], axis=1)
    return stacked.reshape(length, 3, width).astype(jnp.bfloat16)


def on_device(
    image_tokens,
    text_tokens,
    condition,
    group_size,
    image_modulation,
    image_attention_in,
    image_attention_out,
    image_hidden_in,
    image_hidden_out,
    text_modulation,
    text_attention_in,
    text_attention_out,
    text_hidden_in,
    text_hidden_out,
    image_cotangent,
    text_cotangent,
):
    layer_weights = (
        lax.all_gather(image_modulation, "dp", axis=0, tiled=True),
        lax.all_gather(image_attention_in, "dp", axis=0, tiled=True),
        lax.all_gather(image_attention_out, "dp", axis=1, tiled=True),
        lax.all_gather(image_hidden_in, "dp", axis=0, tiled=True),
        lax.all_gather(image_hidden_out, "dp", axis=1, tiled=True),
        lax.all_gather(text_modulation, "dp", axis=0, tiled=True),
        lax.all_gather(text_attention_in, "dp", axis=0, tiled=True),
        lax.all_gather(text_attention_out, "dp", axis=1, tiled=True),
        lax.all_gather(text_hidden_in, "dp", axis=0, tiled=True),
        lax.all_gather(text_hidden_out, "dp", axis=1, tiled=True),
    )
    tensor_rank = lax.axis_index("tensor")
    slots = image_tokens.shape[0]
    text_length = text_tokens.shape[1]
    alive = (jnp.arange(slots) < group_size[0]).astype(jnp.float32)[:, None, None]
    cond_full = condition.astype(jnp.float32)
    activated_low = jax.nn.silu(cond_full).astype(jnp.bfloat16)
    mod_parts = jnp.stack(
        [
            jnp.einsum(
                "sd,dkc->skc", activated_low, layer_weights[0], preferred_element_type=jnp.float32
            ),
            jnp.einsum(
                "sd,dkc->skc", activated_low, layer_weights[5], preferred_element_type=jnp.float32
            ),
        ]
    )
    modulations = lax.all_gather(mod_parts, "tensor", axis=3, tiled=True)
    inputs = (image_tokens.astype(jnp.float32), text_tokens.astype(jnp.float32))
    collectors = (image_rows, keep_rows)
    reducers = (image_partial, text_partial)
    first_saved = []
    packs = []
    for stream in range(2):
        mods = modulations[stream]
        normed, inverse = norm_rows(inputs[stream])
        first_in = normed * (1.0 + spread(mods[:, 1])) + spread(mods[:, 0])
        gathered_first = collectors[stream](first_in.astype(jnp.bfloat16))
        packs.append(
            jnp.einsum(
                "reu,upn->repn",
                gathered_first,
                layer_weights[5 * stream + 1],
                preferred_element_type=jnp.float32,
            ).astype(jnp.bfloat16)
        )
        first_saved.append((normed, inverse, gathered_first))
    joint = jnp.concatenate([packs[1], packs[0]], axis=1)
    attended, logsum = lax.map(attend, joint)
    attended_parts = (attended[:, text_length:], attended[:, :text_length])
    second_saved = []
    outputs = []
    for stream in range(2):
        mods = modulations[stream]
        base_offset = 5 * stream
        branch = reducers[stream](
            jnp.einsum(
                "yhj,jx->yhx",
                attended_parts[stream],
                layer_weights[base_offset + 2],
                preferred_element_type=jnp.float32,
            )
        )
        middle = inputs[stream] + spread(mods[:, 2]) * branch
        normed_two, inverse_two = norm_rows(middle)
        second_in = normed_two * (1.0 + spread(mods[:, 4])) + spread(mods[:, 3])
        gathered_second = collectors[stream](second_in.astype(jnp.bfloat16))
        hidden = jnp.einsum(
            "uan,nc->uac",
            gathered_second,
            layer_weights[base_offset + 3],
            preferred_element_type=jnp.float32,
        )
        active_rows = gelu_tanh(hidden).astype(jnp.bfloat16)
        branch_two = reducers[stream](
            jnp.einsum(
                "eaz,zh->eah",
                active_rows,
                layer_weights[base_offset + 4],
                preferred_element_type=jnp.float32,
            )
        )
        result = middle + spread(mods[:, 5]) * branch_two
        outputs.append((result * alive).astype(jnp.bfloat16))
        second_saved.append(
            (branch, normed_two, inverse_two, gathered_second, hidden, active_rows, branch_two)
        )
    backward_weights = (
        lax.all_gather(image_modulation, "dp", axis=0, tiled=True),
        lax.all_gather(image_attention_in, "dp", axis=0, tiled=True),
        lax.all_gather(image_attention_out, "dp", axis=1, tiled=True),
        lax.all_gather(image_hidden_in, "dp", axis=0, tiled=True),
        lax.all_gather(image_hidden_out, "dp", axis=1, tiled=True),
        lax.all_gather(text_modulation, "dp", axis=0, tiled=True),
        lax.all_gather(text_attention_in, "dp", axis=0, tiled=True),
        lax.all_gather(text_attention_out, "dp", axis=1, tiled=True),
        lax.all_gather(text_hidden_in, "dp", axis=0, tiled=True),
        lax.all_gather(text_hidden_out, "dp", axis=1, tiled=True),
    )
    cotangents = (
        image_cotangent.astype(jnp.float32) * alive,
        text_cotangent.astype(jnp.float32) * alive,
    )
    middle_grads = []
    stat_parts = []
    upstream_parts = []
    up_grads = []
    down_grads = []
    out_grads = []
    for stream in range(2):
        mods = modulations[stream]
        base_offset = 5 * stream
        branch, normed_two, inverse_two, gathered_second, hidden, active_rows, branch_two = (
            second_saved[stream]
        )
        outgoing = cotangents[stream]
        gate_two_grad = jnp.sum(outgoing * branch_two, axis=1)
        down_projection_grad = collectors[stream](
            (outgoing * spread(mods[:, 5])).astype(jnp.bfloat16)
        )
        active_grad = jnp.einsum(
            "wxe,qe->wxq",
            down_projection_grad,
            backward_weights[base_offset + 4],
            preferred_element_type=jnp.float32,
        )
        down_grads.append(
            jnp.einsum(
                "qeu,qeh->uh", active_rows, down_projection_grad, preferred_element_type=jnp.float32
            )
        )
        gelu_value, gelu_pull = jax.vjp(gelu_tanh, hidden)
        hidden_state_grad = gelu_pull(active_grad)[0].astype(jnp.bfloat16)
        up_grads.append(
            jnp.einsum(
                "hne,hnx->ex",
                gathered_second,
                hidden_state_grad,
                preferred_element_type=jnp.float32,
            )
        )
        second_grad = reducers[stream](
            jnp.einsum(
                "xhu,wu->xhw",
                hidden_state_grad,
                backward_weights[base_offset + 3],
                preferred_element_type=jnp.float32,
            )
        )
        shift_two_grad = jnp.sum(second_grad, axis=1)
        scale_two_grad = jnp.sum(second_grad * normed_two, axis=1)
        middle_grad = outgoing + norm_back(
            second_grad * (1.0 + spread(mods[:, 4])), normed_two, inverse_two
        )
        gate_one_grad = jnp.sum(middle_grad * branch, axis=1)
        branch_grad = collectors[stream]((middle_grad * spread(mods[:, 2])).astype(jnp.bfloat16))
        out_grads.append(
            jnp.einsum(
                "nxu,nxi->ui",
                attended_parts[stream],
                branch_grad,
                preferred_element_type=jnp.float32,
            )
        )
        upstream_parts.append(
            jnp.einsum(
                "pbz,oz->pbo",
                branch_grad,
                backward_weights[base_offset + 2],
                preferred_element_type=jnp.float32,
            ).astype(jnp.bfloat16)
        )
        middle_grads.append(middle_grad)
        stat_parts.append((gate_one_grad, shift_two_grad, scale_two_grad, gate_two_grad))
    upstream = jnp.concatenate([upstream_parts[1], upstream_parts[0]], axis=1)
    joint_grad = lax.map(attend_back, (joint, upstream, logsum))
    packed_grads = (joint_grad[:, text_length:], joint_grad[:, :text_length])
    in_grads = []
    input_grads = []
    mod_grads = []
    for stream in range(2):
        mods = modulations[stream]
        normed, inverse, gathered_first = first_saved[stream]
        gate_one_grad, shift_two_grad, scale_two_grad, gate_two_grad = stat_parts[stream]
        packed_gradient = packed_grads[stream]
        in_grads.append(
            jnp.einsum(
                "exq,exfy->qfy", gathered_first, packed_gradient, preferred_element_type=jnp.float32
            )
        )
        first_grad = reducers[stream](
            jnp.einsum(
                "qmjo,fjo->qmf",
                packed_gradient,
                backward_weights[5 * stream + 1],
                preferred_element_type=jnp.float32,
            )
        )
        shift_one_grad = jnp.sum(first_grad, axis=1)
        scale_one_grad = jnp.sum(first_grad * normed, axis=1)
        input_grads.append(
            middle_grads[stream]
            + norm_back(first_grad * (1.0 + spread(mods[:, 1])), normed, inverse)
        )
        mod_grads.append(
            jnp.stack(
                [
                    shift_one_grad,
                    scale_one_grad,
                    gate_one_grad,
                    shift_two_grad,
                    scale_two_grad,
                    gate_two_grad,
                ],
                axis=1,
            )
        )
    image_share = lax.psum_scatter(mod_grads[0], "tensor", scatter_dimension=2, tiled=True)
    share_width = image_share.shape[2]
    text_share = lax.dynamic_slice_in_dim(mod_grads[1], tensor_rank * share_width, share_width, 2)
    image_share_low = image_share.astype(jnp.bfloat16)
    text_share_low = text_share.astype(jnp.bfloat16)
    activated_part = jnp.einsum(
        "skc,dkc->sd", image_share_low, backward_weights[0], preferred_element_type=jnp.float32
    )
    activated_part = activated_part + jnp.einsum(
        "skc,dkc->sd", text_share_low, backward_weights[5], preferred_element_type=jnp.float32
    )
    activated_grad = lax.psum(activated_part, "tensor")
    silu_value, silu_pull = jax.vjp(jax.nn.silu, cond_full)
    condition_gradient = silu_pull(activated_grad)[0]
    image_ada_grad = jnp.einsum(
        "sd,skc->dkc", activated_low, image_share_low, preferred_element_type=jnp.float32
    )
    text_ada_grad = jnp.einsum(
        "sd,skc->dkc", activated_low, text_share_low, preferred_element_type=jnp.float32
    )
    modulation_sums = (
        lax.psum_scatter(
            image_ada_grad.astype(jnp.bfloat16), "dp", scatter_dimension=0, tiled=True
        ).astype(jnp.float32),
        lax.psum_scatter(
            text_ada_grad.astype(jnp.bfloat16), "dp", scatter_dimension=0, tiled=True
        ).astype(jnp.float32),
    )
    rest = (
        lax.psum_scatter(
            in_grads[0].astype(jnp.bfloat16), "dp", scatter_dimension=0, tiled=True
        ).astype(jnp.float32),
        lax.psum_scatter(
            out_grads[0].astype(jnp.bfloat16), "dp", scatter_dimension=1, tiled=True
        ).astype(jnp.float32),
        lax.psum_scatter(
            up_grads[0].astype(jnp.bfloat16), "dp", scatter_dimension=0, tiled=True
        ).astype(jnp.float32),
        lax.psum_scatter(
            down_grads[0].astype(jnp.bfloat16), "dp", scatter_dimension=1, tiled=True
        ).astype(jnp.float32),
        lax.psum_scatter(
            in_grads[1].astype(jnp.bfloat16), "dp", scatter_dimension=0, tiled=True
        ).astype(jnp.float32),
        lax.psum_scatter(
            out_grads[1].astype(jnp.bfloat16), "dp", scatter_dimension=1, tiled=True
        ).astype(jnp.float32),
        lax.psum_scatter(
            up_grads[1].astype(jnp.bfloat16), "dp", scatter_dimension=0, tiled=True
        ).astype(jnp.float32),
        lax.psum_scatter(
            down_grads[1].astype(jnp.bfloat16), "dp", scatter_dimension=1, tiled=True
        ).astype(jnp.float32),
    )
    summed = (
        modulation_sums[0],
        rest[0],
        rest[1],
        rest[2],
        rest[3],
        modulation_sums[1],
        rest[4],
        rest[5],
        rest[6],
        rest[7],
    )
    return (
        outputs[0],
        outputs[1],
        input_grads[0],
        input_grads[1],
        condition_gradient,
        summed[0],
        summed[1],
        summed[2],
        summed[3],
        summed[4],
        summed[5],
        summed[6],
        summed[7],
        summed[8],
        summed[9],
    )


def solution(mesh):
    placed = (
        P("dp", "tensor", None),
        P("dp", None, None),
        P("dp", None),
        P("dp"),
        P("dp", None, "tensor"),
        P("dp", None, "tensor"),
        P("tensor", "dp"),
        P("dp", "tensor"),
        P("tensor", "dp"),
        P("dp", None, "tensor"),
        P("dp", None, "tensor"),
        P("tensor", "dp"),
        P("dp", "tensor"),
        P("tensor", "dp"),
        P("dp", "tensor", None),
        P("dp", None, None),
    )
    return jax.shard_map(
        on_device,
        mesh=mesh,
        in_specs=placed,
        out_specs=(
            P("dp", "tensor", None),
            P("dp", None, None),
            P("dp", "tensor", None),
            P("dp", None, None),
            P("dp", None),
            P("dp", None, "tensor"),
            P("dp", None, "tensor"),
            P("tensor", "dp"),
            P("dp", "tensor"),
            P("tensor", "dp"),
            P("dp", None, "tensor"),
            P("dp", None, "tensor"),
            P("tensor", "dp"),
            P("dp", "tensor"),
            P("tensor", "dp"),
        ),
        check_vma=False,
    )
```

profile of v0, /device:TPU:0, one launch (start us, length us, event | category | flops | bytes accessed | tf_op | source)
XLA Modules:
  0.0 2900.4 jit_solution(14672864139969126312)
XLA Ops:
  10.9 110.8 %all-gather.17.cloned.1.call-done = bf16[1536,6,384]{2,0,1:T(8,128)(2,1)} async-done(((bf16[192,6,384]{2,0,1:T(8,128)(2,1)}), bf16[1536,6,384]{2,0,1:T(8,128)(2,1)}) %all-gather.17.cloned.1.call-update) | async-done | bytes 7077904 | tf_op jit(solution)/shard_map/all_gather | solution.py:124
  125.8 105.2 %all-gather.15.cloned.1.call-done = bf16[1536,6,384]{2,0,1:T(8,128)(2,1)} async-done(((bf16[192,6,384]{2,0,1:T(8,128)(2,1)}), bf16[1536,6,384]{2,0,1:T(8,128)(2,1)}) %all-gather.15.cloned.1.call-update) | async-done | bytes 7077904 | tf_op jit(solution)/shard_map/all_gather | solution.py:119
  245.6 51.0 %all-gather.19.cloned.1.call-done = bf16[1536,3,384]{2,0,1:T(8,128)(2,1)} async-done(((bf16[192,3,384]{2,0,1:T(8,128)(2,1)}), bf16[1536,3,384]{2,0,1:T(8,128)(2,1)}) %all-gather.19.cloned.1.call-update) | async-done | bytes 3538960 | tf_op jit(solution)/shard_map/all_gather | solution.py:125
  300.2 62.1 %all-gather.23.cloned.1.call-done = bf16[1536,3,384]{2,0,1:T(8,128)(2,1)} async-done(((bf16[192,3,384]{2,0,1:T(8,128)(2,1)}), bf16[1536,3,384]{2,0,1:T(8,128)(2,1)}) %all-gather.23.cloned.1.call-update) | async-done | bytes 3538960 | tf_op jit(solution)/shard_map/all_gather | solution.py:120
  362.3 46.9 %all-gather.21.cloned.1.call-done = bf16[2,1024,1536]{2,1,0:T(8,128)(2,1)} async-done(((bf16[2,256,1536]{2,1,0:T(8,128)(2,1)}), bf16[2,1024,1536]{2,1,0:T(8,128)(2,1)}) %all-gather.21.cloned.1.call-update) | async-done | bytes 6291472 | tf_op jit(solution)/shard_map/all_gather | solution.py:30
  433.1 95.1 %while.22 = (s32[]{:T(128)}, bf16[2,1178,384]{2,1,0:T(8,128)(2,1)}, f32[2,6,1178,1]{2,1,3,0:T(8,128)S(1)}, bf16[2,1178,3,384]{1,3,2,0:T(8,128)(2,1)}, s32[]{:T(128)}) while((s32[]{:T(128)}, bf16[2,1178,384]{2,1,0:T(8,128)(2,1)}, f32[2,6,1178,1]{2,1,3,0:T(8,128)S(1)}, bf16[2,1178,3,384]{1,3,2,0:T(8,128)(2,1)}, s32[]{:T(128)}) %tuple.90), condition=%wide.region_7.8_spmd, body=%wide.region_4.7_spmd.sunk | while | flops 2190210560 | bytes 118276256 | solution.py:167
  539.6 97.7 %reduce-scatter.18.cloned.1.call-done = f32[2,256,1536]{2,1,0:T(8,128)} async-done(((f32[2,1024,1536]{2,1,0:T(8,128)}), f32[2,256,1536]{2,1,0:T(8,128)}) %reduce-scatter.18.cloned.1.call-update) | async-done | bytes 3145744 | tf_op jit(solution)/shard_map/reduce_scatter | solution.py:34
  647.1 33.4 %all-gather.33.cloned.1.call-done = bf16[384,1536]{0,1:T(8,128)(2,1)} async-done(((bf16[384,192]{0,1:T(8,128)(2,1)}), bf16[384,1536]{0,1:T(8,128)(2,1)}) %all-gather.33.cloned.1.call-update) | async-done | bytes 1179664 | tf_op jit(solution)/shard_map/all_gather | solution.py:126
  685.1 76.3 %all-gather.29.cloned.1.call-done = bf16[1536,1536]{1,0:T(8,128)(2,1)} async-done(((bf16[192,1536]{1,0:T(8,128)(2,1)}), bf16[1536,1536]{1,0:T(8,128)(2,1)}) %all-gather.29.cloned.1.call-update) | async-done | bytes 4718608 | tf_op jit(solution)/shard_map/all_gather | solution.py:122
  761.4 46.5 %all-gather.27.cloned.1.call-done = bf16[2,1024,1536]{2,1,0:T(8,128)(2,1)} async-done(((bf16[2,256,1536]{2,1,0:T(8,128)(2,1)}), bf16[2,1024,1536]{2,1,0:T(8,128)(2,1)}) %all-gather.27.cloned.1.call-update) | async-done | bytes 6291472 | tf_op jit(solution)/shard_map/all_gather | solution.py:30
  824.0 66.1 %all-gather.31.cloned.1.call-done = bf16[1536,1536]{0,1:T(8,128)(2,1)} async-done(((bf16[1536,192]{0,1:T(8,128)(2,1)}), bf16[1536,1536]{0,1:T(8,128)(2,1)}) %all-gather.31.cloned.1.call-update) | async-done | bytes 4718608 | tf_op jit(solution)/shard_map/all_gather | solution.py:123
  890.0 46.6 %all-gather.39.cloned.1.call-done = bf16[2,1024,1536]{2,1,0:T(8,128)(2,1)} async-done(((bf16[2,256,1536]{2,1,0:T(8,128)(2,1)}), bf16[2,1024,1536]{2,1,0:T(8,128)(2,1)}) %all-gather.39.cloned.1.call-update) | async-done | bytes 6291472 | tf_op jit(solution)/shard_map/all_gather | solution.py:30
  999.3 71.6 %all-gather.35.cloned.1.call-done = bf16[1536,1536]{1,0:T(8,128)(2,1)} async-done(((bf16[192,1536]{1,0:T(8,128)(2,1)}), bf16[1536,1536]{1,0:T(8,128)(2,1)}) %all-gather.35.cloned.1.call-update) | async-done | bytes 4718608 | tf_op jit(solution)/shard_map/all_gather | solution.py:127
  1076.9 74.0 %all-gather.37.cloned.1.call-done = bf16[1536,1536]{0,1:T(8,128)(2,1)} async-done(((bf16[1536,192]{0,1:T(8,128)(2,1)}), bf16[1536,1536]{0,1:T(8,128)(2,1)}) %all-gather.37.cloned.1.call-update) | async-done | bytes 4718608 | tf_op jit(solution)/shard_map/all_gather | solution.py:128
  1161.0 89.6 %reduce-scatter.22.cloned.1.call-done = f32[2,256,1536]{2,1,0:T(8,128)} async-done(((f32[2,1024,1536]{2,1,0:T(8,128)}), f32[2,256,1536]{2,1,0:T(8,128)}) %reduce-scatter.22.cloned.1.call-update) | async-done | bytes 3145744 | tf_op jit(solution)/shard_map/reduce_scatter | solution.py:34
  1254.3 97.8 %reduce-scatter.20.cloned.1.call-done = f32[2,256,1536]{2,1,0:T(8,128)} async-done(((f32[2,1024,1536]{2,1,0:T(8,128)}), f32[2,256,1536]{2,1,0:T(8,128)}) %reduce-scatter.20.cloned.1.call-update) | async-done | bytes 3145744 | tf_op jit(solution)/shard_map/reduce_scatter | solution.py:34
  1362.2 41.5 %all-reduce.7.cloned.1.call-done = f32[2,154,1536]{2,1,0:T(8,128)} async-done(((f32[2,154,1536]{2,1,0:T(8,128)}), f32[2,154,1536]{2,1,0:T(8,128)}) %all-reduce.7.cloned.1.call-update) | async-done | bytes 1892368 | tf_op jit(solution)/shard_map/psum | solution.py:38
  1410.6 41.7 %all-gather.41.cloned.1.call-done = bf16[2,1024,1536]{2,1,0:T(8,128)(2,1)} async-done(((bf16[2,256,1536]{2,1,0:T(8,128)(2,1)}), bf16[2,1024,1536]{2,1,0:T(8,128)(2,1)}) %all-gather.41.cloned.1.call-update) | async-done | bytes 6291472 | tf_op jit(solution)/shard_map/all_gather | solution.py:30
  1460.2 246.3 %while.23 = (s32[]{:T(128)}, bf16[2,1178,3,384]{3,1,2,0:T(8,128)(2,1)}, bf16[2,1178,3,384]{1,3,2,0:T(8,128)(2,1)}, f32[2,6,1178,1]{2,1,3,0:T(8,128)S(1)}, bf16[2,1178,384]{2,1,0:T(8,128)(2,1)}, /*index=5*/s32[]{:T(128)}) while((s32[]{:T(128)}, bf16[2,1178,3,384]{3,1,2,0:T(8,128)(2,1)}, bf16[2,1178,3,384]{1,3,2,0:T(8,128)(2,1)}, ...), condition=%wide.region_24.25_spmd, body=%wide.region_22.24_spmd.sunk | while | flops 5400284160 | bytes 289759168 | solution.py:294
  1506.6 29.7 %multiply_convert_fusion.18 = bf16[6,1178,1178]{1,2,0:T(8,128)(2,1)} fusion(f32[6,1178,1178]{1,2,0:T(8,128)} %get-tuple-element.268, f32[6,1178,1178]{1,2,0:T(8,128)} %fusion.207, f32[6,1178]{1,0:T(8,128)S(1)} %get-tuple-element.269), kind=kLoop, calls=%fused_computation.11.clone.1 | loop fusion | flops 24978312 | bytes 83289312 | tf_op jit(solution)/shard_map/while/body/eval_jaxpr/convert_element_type | solution.py:89
  1629.5 29.7 %multiply_convert_fusion.18 = bf16[6,1178,1178]{1,2,0:T(8,128)(2,1)} fusion(f32[6,1178,1178]{1,2,0:T(8,128)} %get-tuple-element.268, f32[6,1178,1178]{1,2,0:T(8,128)} %fusion.207, f32[6,1178]{1,0:T(8,128)S(1)} %get-tuple-element.269), kind=kLoop, calls=%fused_computation.11.clone.1 | loop fusion | flops 24978312 | bytes 83289312 | tf_op jit(solution)/shard_map/while/body/eval_jaxpr/convert_element_type | solution.py:89
  1730.8 88.9 %reduce-scatter.24.cloned.1.call-done = f32[2,256,1536]{2,1,0:T(8,128)} async-done(((f32[2,1024,1536]{2,1,0:T(8,128)}), f32[2,256,1536]{2,1,0:T(8,128)}) %reduce-scatter.24.cloned.1.call-update) | async-done | bytes 3145744 | tf_op jit(solution)/shard_map/reduce_scatter | solution.py:34
  1936.8 61.7 %reduce-scatter.40.cloned.1.call-done = bf16[384,192]{0,1:T(8,128)(2,1)} async-done(((bf16[384,1536]{0,1:T(8,128)(2,1)}), bf16[384,192]{0,1:T(8,128)(2,1)}) %reduce-scatter.40.cloned.1.call-update) | async-done | bytes 147472 | tf_op jit(solution)/shard_map/reduce_scatter | solution.py:380
  2000.2 96.6 %reduce-scatter.44.cloned.1.call-done = bf16[1536,192]{0,1:T(8,128)(2,1)} async-done(((bf16[1536,1536]{0,1:T(8,128)(2,1)}), bf16[1536,192]{0,1:T(8,128)(2,1)}) %reduce-scatter.44.cloned.1.call-update) | async-done | bytes 589840 | tf_op jit(solution)/shard_map/reduce_scatter | solution.py:386
  2099.0 96.9 %reduce-scatter.42.cloned.1.call-done = bf16[192,1536]{1,0:T(8,128)(2,1)} async-done(((bf16[1536,1536]{1,0:T(8,128)(2,1)}), bf16[192,1536]{1,0:T(8,128)(2,1)}) %reduce-scatter.42.cloned.1.call-update) | async-done | bytes 589840 | tf_op jit(solution)/shard_map/reduce_scatter | solution.py:383
  2198.1 96.8 %reduce-scatter.34.cloned.1.call-done = bf16[1536,192]{0,1:T(8,128)(2,1)} async-done(((bf16[1536,1536]{0,1:T(8,128)(2,1)}), bf16[1536,192]{0,1:T(8,128)(2,1)}) %reduce-scatter.34.cloned.1.call-update) | async-done | bytes 589840 | tf_op jit(solution)/shard_map/reduce_scatter | solution.py:374
  2297.1 96.8 %reduce-scatter.32.cloned.1.call-done = bf16[192,1536]{1,0:T(8,128)(2,1)} async-done(((bf16[1536,1536]{1,0:T(8,128)(2,1)}), bf16[192,1536]{1,0:T(8,128)(2,1)}) %reduce-scatter.32.cloned.1.call-update) | async-done | bytes 589840 | tf_op jit(solution)/shard_map/reduce_scatter | solution.py:371
  2403.0 59.0 %reduce-scatter.30.cloned.1.call-done = bf16[384,192]{0,1:T(8,128)(2,1)} async-done(((bf16[384,1536]{0,1:T(8,128)(2,1)}), bf16[384,192]{0,1:T(8,128)(2,1)}) %reduce-scatter.30.cloned.1.call-update) | async-done | bytes 147472 | tf_op jit(solution)/shard_map/reduce_scatter | solution.py:368
  2463.6 80.6 %reduce-scatter.28.cloned.1.call-done = bf16[192,3,384]{2,0,1:T(8,128)(2,1)} async-done(((bf16[1536,3,384]{2,0,1:T(8,128)(2,1)}), bf16[192,3,384]{2,0,1:T(8,128)(2,1)}) %reduce-scatter.28.cloned.1.call-update) | async-done | bytes 442384 | tf_op jit(solution)/shard_map/reduce_scatter | solution.py:365
  2546.1 80.5 %reduce-scatter.38.cloned.1.call-done = bf16[192,3,384]{2,0,1:T(8,128)(2,1)} async-done(((bf16[1536,3,384]{2,0,1:T(8,128)(2,1)}), bf16[192,3,384]{2,0,1:T(8,128)(2,1)}) %reduce-scatter.38.cloned.1.call-update) | async-done | bytes 442384 | tf_op jit(solution)/shard_map/reduce_scatter | solution.py:377
  2628.6 130.8 %reduce-scatter.36.cloned.1.call-done = bf16[192,6,384]{2,0,1:T(8,128)(2,1)} async-done(((bf16[1536,6,384]{2,0,1:T(8,128)(2,1)}), bf16[192,6,384]{2,0,1:T(8,128)(2,1)}) %reduce-scatter.36.cloned.1.call-update) | async-done | bytes 884752 | tf_op jit(solution)/shard_map/reduce_scatter | solution.py:360
  2789.5 101.6 %reduce-scatter.26.cloned.1.call-done = bf16[192,6,384]{2,0,1:T(8,128)(2,1)} async-done(((bf16[1536,6,384]{2,0,1:T(8,128)(2,1)}), bf16[192,6,384]{2,0,1:T(8,128)(2,1)}) %reduce-scatter.26.cloned.1.call-update) | async-done | bytes 884752 | tf_op jit(solution)/shard_map/reduce_scatter | solution.py:357
  (371 shorter events, 675.5 us)
Async XLA Ops:
  7.2 114.6 %all-gather.17.cloned.1.call-start = ((), (), s32[]{:S(2)}) async-start(), calls=%async_computation.16 | async-start | bytes 7962624 | tf_op jit(solution)/shard_map/all_gather | solution.py:124
  7.9 223.0 %all-gather.15.cloned.1.call-start = ((), (), s32[]{:S(2)}) async-start(), calls=%async_computation.15 | async-start | bytes 7962624 | tf_op jit(solution)/shard_map/all_gather | solution.py:119
  8.7 287.9 %all-gather.19.cloned.1.call-start = ((), (), s32[]{:S(2)}) async-start(), calls=%async_computation.17 | async-start | bytes 3981312 | tf_op jit(solution)/shard_map/all_gather | solution.py:125
  9.4 352.9 %all-gather.23.cloned.1.call-start = ((), (), s32[]{:S(2)}) async-start(), calls=%async_computation.19 | async-start | bytes 3981312 | tf_op jit(solution)/shard_map/all_gather | solution.py:120
  10.0 399.2 %all-gather.21.cloned.1.call-start = ((), (), s32[]{:S(2)}) async-start(), calls=%async_computation.18 | async-start | bytes 7864320 | tf_op jit(solution)/shard_map/all_gather | solution.py:30
  243.7 284.6 %all-gather.25.cloned.1.call-start = ((), (), s32[]{:S(2)}) async-start(), calls=%async_computation.20 | async-start | bytes 1327104 | tf_op jit(solution)/shard_map/all_gather | solution.py:121
  244.3 393.0 %reduce-scatter.18.cloned.1.call-start = ((), (), s32[]{:S(2)}) async-start(), calls=%async_computation.21 | async-start | bytes 15728640 | tf_op jit(solution)/shard_map/reduce_scatter | solution.py:34
  538.0 142.5 %all-gather.33.cloned.1.call-start = ((), (), s32[]{:S(2)}) async-start(), calls=%async_computation.26 | async-start | bytes 1327104 | tf_op jit(solution)/shard_map/all_gather | solution.py:126
  538.8 222.6 %all-gather.29.cloned.1.call-start = ((), (), s32[]{:S(2)}) async-start(), calls=%async_computation.23 | async-start | bytes 5308416 | tf_op jit(solution)/shard_map/all_gather | solution.py:122
  539.5 268.4 %all-gather.27.cloned.1.call-start = ((), (), s32[]{:S(2)}) async-start(), calls=%async_computation.22 | async-start | bytes 7864320 | tf_op jit(solution)/shard_map/all_gather | solution.py:30
  642.6 247.4 %all-gather.31.cloned.1.call-start = ((), (), s32[]{:S(2)}) async-start(), calls=%async_computation.24 | async-start | bytes 5308416 | tf_op jit(solution)/shard_map/all_gather | solution.py:123
  643.4 293.2 %all-gather.39.cloned.1.call-start = ((), (), s32[]{:S(2)}) async-start(), calls=%async_computation.30 | async-start | bytes 7864320 | tf_op jit(solution)/shard_map/all_gather | solution.py:30
  647.1 348.0 %all-reduce.5.cloned.1.call-start = ((), (), s32[]{:S(2)}) async-start(), calls=%async_computation.27 | async-start | bytes 3932160 | tf_op jit(solution)/shard_map/psum | solution.py:38
  683.9 386.9 %all-gather.35.cloned.1.call-start = ((), (), s32[]{:S(2)}) async-start(), calls=%async_computation.28 | async-start | bytes 5308416 | tf_op jit(solution)/shard_map/all_gather | solution.py:127
  684.5 466.4 %all-gather.37.cloned.1.call-start = ((), (), s32[]{:S(2)}) async-start(), calls=%async_computation.29 | async-start | bytes 5308416 | tf_op jit(solution)/shard_map/all_gather | solution.py:128
  685.1 565.5 %reduce-scatter.22.cloned.1.call-start = ((), (), s32[]{:S(2)}) async-start(), calls=%async_computation.31 | async-start | bytes 15728640 | tf_op jit(solution)/shard_map/reduce_scatter | solution.py:34
  977.0 375.2 %reduce-scatter.20.cloned.1.call-start = ((), (), s32[]{:S(2)}) async-start(), calls=%async_computation.25 | async-start | bytes 15728640 | tf_op jit(solution)/shard_map/reduce_scatter | solution.py:34
  994.8 408.9 %all-reduce.7.cloned.1.call-start = ((), (), s32[]{:S(2)}) async-start(), calls=%async_computation.32 | async-start | bytes 3932160 | tf_op jit(solution)/shard_map/psum | solution.py:38
  1160.9 291.4 %all-gather.41.cloned.1.call-start = ((), (), s32[]{:S(2)}) async-start(), calls=%async_computation.33 | async-start | bytes 7864320 | tf_op jit(solution)/shard_map/all_gather | solution.py:30
  1362.2 457.6 %reduce-scatter.24.cloned.1.call-start = ((), (), s32[]{:S(2)}) async-start(), calls=%async_computation.34 | async-start | bytes 15728640 | tf_op jit(solution)/shard_map/reduce_scatter | solution.py:34
  1720.5 190.3 %all-reduce.9.cloned.1.call-start = ((), (), s32[]{:S(2)}) async-start(), calls=%async_computation.46 | async-start | bytes 7864320 | tf_op jit(solution)/shard_map/psum | solution.py:38
  1730.7 199.4 %reduce-scatter.46.cloned.1.call-start = ((), (), s32[]{:S(2)}) async-start(), calls=%async_computation.45 | async-start | bytes 983040
  1832.8 165.8 %reduce-scatter.40.cloned.1.call-start = ((), (), s32[]{:S(2)}) async-start(), calls=%async_computation.42 | async-start | bytes 1327104 | tf_op jit(solution)/shard_map/reduce_scatter | solution.py:380
  1835.8 261.0 %reduce-scatter.44.cloned.1.call-start = ((), (), s32[]{:S(2)}) async-start(), calls=%async_computation.44 | async-start | bytes 5308416 | tf_op jit(solution)/shard_map/reduce_scatter | solution.py:386
  1842.3 353.6 %reduce-scatter.42.cloned.1.call-start = ((), (), s32[]{:S(2)}) async-start(), calls=%async_computation.43 | async-start | bytes 5308416 | tf_op jit(solution)/shard_map/reduce_scatter | solution.py:383
  1849.0 445.9 %reduce-scatter.34.cloned.1.call-start = ((), (), s32[]{:S(2)}) async-start(), calls=%async_computation.39 | async-start | bytes 5308416 | tf_op jit(solution)/shard_map/reduce_scatter | solution.py:374
  1866.3 527.5 %reduce-scatter.32.cloned.1.call-start = ((), (), s32[]{:S(2)}) async-start(), calls=%async_computation.38 | async-start | bytes 5308416 | tf_op jit(solution)/shard_map/reduce_scatter | solution.py:371
  1883.0 578.9 %reduce-scatter.30.cloned.1.call-start = ((), (), s32[]{:S(2)}) async-start(), calls=%async_computation.37 | async-start | bytes 1327104 | tf_op jit(solution)/shard_map/reduce_scatter | solution.py:368
  1890.9 653.3 %reduce-scatter.28.cloned.1.call-start = ((), (), s32[]{:S(2)}) async-start(), calls=%async_computation.36 | async-start | bytes 3981312 | tf_op jit(solution)/shard_map/reduce_scatter | solution.py:365
  1904.4 722.2 %reduce-scatter.38.cloned.1.call-start = ((), (), s32[]{:S(2)}) async-start(), calls=%async_computation.41 | async-start | bytes 3981312 | tf_op jit(solution)/shard_map/reduce_scatter | solution.py:377
  1910.8 848.6 %reduce-scatter.36.cloned.1.call-start = ((), (), s32[]{:S(2)}) async-start(), calls=%async_computation.40 | async-start | bytes 7962624 | tf_op jit(solution)/shard_map/reduce_scatter | solution.py:360
  1920.6 970.5 %reduce-scatter.26.cloned.1.call-start = ((), (), s32[]{:S(2)}) async-start(), calls=%async_computation.35 | async-start | bytes 7962624 | tf_op jit(solution)/shard_map/reduce_scatter | solution.py:357
  (77 other events, 6240.1 us)
Sparse Core Ops, SparseCore 0:
  10.2 111.4 all-gather.16
  123.9 106.9 all-gather.14
  233.2 63.3 all-gather.18
  298.6 63.6 all-gather.22
  364.3 44.8 all-gather.20
  411.2 41.0 all-gather.24
  538.2 99.0 reduce-scatter.17
  639.4 41.0 all-gather.32
  682.7 78.6 all-gather.28
  763.4 44.5 all-gather.26
  810.1 79.8 all-gather.30
  892.0 44.5 all-gather.38
  939.5 49.2 all-reduce.4
  990.9 79.9 all-gather.34
  1072.9 78.0 all-gather.36
  1153.4 97.1 reduce-scatter.21
  1253.1 99.0 reduce-scatter.19
  1354.4 49.2 all-reduce.6
  1405.9 46.4 all-gather.40
  1720.7 99.0 reduce-scatter.23
  1822.1 81.4 all-reduce.8
  1906.7 23.3 reduce-scatter.45
  1934.5 64.0 reduce-scatter.39
  2002.5 94.2 reduce-scatter.43
  2100.9 94.9 reduce-scatter.41
  2199.8 94.9 reduce-scatter.33
  2298.8 94.9 reduce-scatter.31
  2398.2 63.7 reduce-scatter.29
  2466.0 78.0 reduce-scatter.27
  2548.1 78.4 reduce-scatter.37
  2630.7 128.5 reduce-scatter.35
  2763.0 128.0 reduce-scatter.25
where the time goes:
time: 2910 us; the launch traced here: 2900 us
  waiting for transfers between devices  2160 us (74%)
  matrix products  466 us (16%)
  other arithmetic  167 us (6%)
  local copies, waits for them, and re-layouts  67.4 us (2%)
    reduce_scatter x4, waiting for transfers between devices, image_partial(): return lax.psum_scatter(values, 'tensor', scatter_dimension=1, tiled=True)  374 us
    all_gather x4, waiting for transfers between devices, image_rows(): return lax.all_gather(values, 'tensor', axis=1, tiled=True)  182 us
    reduce_scatter x1, waiting for transfers between devices, on_device(): lax.psum_scatter(text_ada_grad.astype(jnp.bfloat16), 'dp', scatter_dimens...  131 us
    all_gather x1, waiting for transfers between devices, on_device(): lax.all_gather(text_modulation, 'dp', axis=0, tiled=True)  111 us
    all_gather x1, waiting for transfers between devices, on_device(): lax.all_gather(image_modulation, 'dp', axis=0, tiled=True)  105 us
    reduce_scatter x1, waiting for transfers between devices, on_device(): lax.psum_scatter(image_ada_grad.astype(jnp.bfloat16), 'dp', scatter_dimen...  102 us
    reduce_scatter x1, waiting for transfers between devices, on_device(): lax.psum_scatter(up_grads[1].astype(jnp.bfloat16), 'dp', scatter_dimensio...  96.9 us
    reduce_scatter x1, waiting for transfers between devices, on_device(): lax.psum_scatter(down_grads[0].astype(jnp.bfloat16), 'dp', scatter_dimens...  96.8 us
  transfers between devices with their start and end apart: 32, of which 29 were waited for; matrix products, arithmetic and copies ran while one was open for 14% of the time, Pallas kernels for 0%

commit v1 on v0

v1 whole, which is shorter than its diff:
```python
import functools

import jax
import jax.numpy as jnp
from jax import lax
from jax.experimental import pallas as pl
from jax.experimental.pallas import tpu as pltpu
from jax.sharding import PartitionSpec as P

HEAD = 64
LANES = 128
F32 = jnp.float32
BF16 = jnp.bfloat16


def norm_rows(values):
    center = values - jnp.mean(values, axis=-1, keepdims=True)
    inverse = lax.rsqrt(jnp.mean(center * center, axis=-1, keepdims=True) + 1e-06)
    return (center * inverse, inverse)


def norm_back(upstream, normed, inverse):
    first = jnp.mean(upstream, axis=-1, keepdims=True)
    second = jnp.mean(upstream * normed, axis=-1, keepdims=True)
    return inverse * (upstream - first - normed * second)


def gelu_tanh(values):
    return jax.nn.gelu(values, approximate=True)


def spread(vector):
    return vector[:, None, :]


def dot(left, right, left_dim, right_dim):
    return lax.dot_general(
        left, right, (((left_dim,), (right_dim,)), ((), ())), preferred_element_type=F32
    )


def swap(value, bit, size, axis="tensor"):
    return lax.ppermute(value, axis, [(i, i ^ bit) for i in range(size)])


def bits_of(size):
    bits = []
    bit = 1
    while bit < size:
        bits.append(bit)
        bit *= 2
    return bits


def gather_pieces(value, size, axis="tensor"):
    have = {0: value}
    for bit in reversed(bits_of(size)):
        have.update({k ^ bit: swap(v, bit, size, axis) for k, v in list(have.items())})
    return [have[k] for k in range(size)]


def exchange(blocks, size, axis):
    return [blocks[0]] + [swap(blocks[k], k, size, axis) for k in range(1, size)]


def sum_all(value, size, axis):
    for bit in bits_of(size):
        value = value + swap(value, bit, size, axis)
    return value


def scatter_sum(make_piece, size):
    have = {k: make_piece(k) for k in reversed(range(size))}
    for bit in bits_of(size):
        kept = {}
        for k in sorted(have, reverse=True):
            if not k & bit:
                other = swap(have[k ^ bit].astype(BF16), bit, size)
                kept[k] = have[k].astype(F32) + other.astype(F32)
        have = kept
    return have[0]


def ring_of(count):
    return list(range(0, count, 2)) + list(range(1, count, 2))[::-1]


def ring_member(place, count):
    place = lax.rem(place + count, count)
    return jnp.where(place < (count + 1) // 2, 2 * place, 2 * (count - 1 - place) + 1)


def ring_place(member, count):
    return jnp.where(member % 2 == 0, member // 2, count - 1 - member // 2)


def ring_step(value, way, count):
    ring = ring_of(count)
    hops = [(ring[i], ring[(i + way) % count]) for i in range(count)]
    return lax.ppermute(value, "dp", hops)


def ring_gather(block, count):
    share, wide = block.shape
    half = wide // 2 // LANES * LANES
    place = ring_place(lax.axis_index("dp"), count)
    whole = jnp.zeros((count * share, wide), block.dtype)

    def put(whole, value, offset, column):
        row = ring_member(place + offset, count) * share
        return lax.dynamic_update_slice(whole, value, (row, column))

    whole = put(whole, block, 0, 0)
    behind = ahead = block
    for hop in range(1, count // 2):
        behind = ring_step(behind, 1, count)
        ahead = ring_step(ahead, -1, count)
        whole = put(put(whole, behind, -hop, 0), ahead, hop, 0)
    behind = ring_step(behind[:, :half], 1, count)
    ahead = ring_step(ahead[:, half:], -1, count)
    return put(put(whole, behind, -(count // 2), 0), ahead, count // 2, half)


def ring_scatter(grad, count):
    wide = grad.shape[1]
    share = grad.shape[0] // count
    half = wide // 2 // LANES * LANES
    place = ring_place(lax.axis_index("dp"), count)

    def own(offset):
        row = ring_member(place + offset, count) * share
        return lax.dynamic_slice_in_dim(grad, row, share, 0).astype(F32)

    far = own(count // 2).astype(BF16)
    behind = ring_step(far[:, :half], 1, count)
    ahead = ring_step(far[:, half:], -1, count)
    behind, ahead = yield behind, ahead
    behind = jnp.pad(behind.astype(F32), ((0, 0), (0, wide - half)))
    ahead = jnp.pad(ahead.astype(F32), ((0, 0), (half, 0)))
    for hop in range(count // 2 - 1, 0, -1):
        behind = ring_step((own(hop) + behind).astype(BF16), 1, count)
        ahead = ring_step((own(-hop) + ahead).astype(BF16), -1, count)
        behind, ahead = yield behind, ahead
        behind, ahead = behind.astype(F32), ahead.astype(F32)
    yield own(0) + behind + ahead


def text_sum(value, size):
    for bit in bits_of(size):
        if bit == 1:
            value = value + swap(value, bit, size)
        else:
            value = lax.reduce_precision(value, 8, 7)
            value = value + swap(value.astype(BF16), bit, size).astype(F32)
    return value


def lane_mask(half, shape):
    lane = lax.broadcasted_iota(jnp.int32, shape, 1)
    return (lane >= HEAD) if half else (lane < HEAD)


def pick(value, half):
    return jnp.where(lane_mask(half, value.shape), value, jnp.zeros_like(value))


def load_rows(refs, store):
    start = 0
    for ref in refs:
        rows = ref.shape[1]
        store[start : start + rows, :] = ref[0]
        start += rows


def attend_kernel(count, *refs):
    queries, keys, values = refs[:count], refs[count : 2 * count], refs[2 * count : 3 * count]
    outs = refs[3 * count : 4 * count]
    sums = refs[4 * count : 5 * count]
    key_all, value_all = refs[5 * count :]
    load_rows(keys, key_all)
    load_rows(values, value_all)
    for index in range(count):
        query = queries[index][0] * jnp.asarray(HEAD**-0.5, BF16)
        halves = []
        for half in range(2):
            scores = dot(key_all[...], pick(query, half), 1, 1)
            highest = jnp.max(scores, axis=0, keepdims=True)
            weights = jnp.exp(scores - highest)
            total = jnp.sum(weights, axis=0, keepdims=True)
            weights = (weights * (1.0 / total)).astype(BF16)
            mixed = dot(value_all[...], weights, 0, 0)
            halves.append(mixed[half * HEAD : (half + 1) * HEAD])
            sums[index][0, 0, half : half + 1, :] = highest + jnp.log(total)
        outs[index][0] = jnp.concatenate(halves, axis=0).T.astype(BF16)


def attend_back_kernel(count, groups, *refs):
    queries, keys, values = refs[:count], refs[count : 2 * count], refs[2 * count : 3 * count]
    upstreams = refs[3 * count : 4 * count]
    sums = refs[4 * count : 5 * count]
    outs = refs[5 * count : 6 * count]
    key_all, value_all, key_grad, value_grad = refs[6 * count :]
    load_rows(keys, key_all)
    load_rows(values, value_all)
    pair = pl.program_id(1)
    scale = jnp.asarray(HEAD**-0.5, BF16)
    query_lanes = pl.ds(pl.multiple_of(pair * LANES, LANES), LANES)
    key_lanes = pl.ds(pl.multiple_of((groups + pair) * LANES, LANES), LANES)
    value_lanes = pl.ds(pl.multiple_of((2 * groups + pair) * LANES, LANES), LANES)
    for index in range(count):
        query = queries[index][0] * scale
        upstream = upstreams[index][0]
        halves = []
        for half in range(2):
            query_half = pick(query, half)
            upstream_half = pick(upstream, half)
            scores = dot(key_all[...], query_half, 1, 1)
            weights = jnp.exp(scores - sums[index][0, 0, half : half + 1, :])
            along = dot(value_all[...], upstream_half, 1, 1)
            value_part = dot(weights.astype(BF16), upstream_half, 1, 0)
            product = weights * along
            score_grad = (product - weights * jnp.sum(product, axis=0, keepdims=True)).astype(BF16)
            key_part = dot(score_grad, query_half, 1, 0)
            if index == 0 and half == 0:
                value_grad[...] = value_part
                key_grad[...] = key_part
            else:
                value_grad[...] += value_part
                key_grad[...] += key_part
            mixed = dot(key_all[...], score_grad, 0, 0)
            halves.append(mixed[half * HEAD : (half + 1) * HEAD])
        query_grad = jnp.concatenate(halves, axis=0).T * HEAD**-0.5
        outs[index][0, :, query_lanes] = query_grad.astype(BF16)
    start = 0
    for index in range(count):
        rows = outs[index].shape[1]
        outs[index][0, :, key_lanes] = key_grad[start : start + rows, :].astype(BF16)
        outs[index][0, :, value_lanes] = value_grad[start : start + rows, :].astype(BF16)
        start += rows


def lane_blocks(parts, offset):
    return [
        pl.BlockSpec((1, part.shape[1], LANES), lambda s, p, o=offset: (s, 0, o + p))
        for part in parts
    ]


def widen(part, copies):
    slots, rows, width = part.shape
    width = width // copies
    extra = -width % LANES
    if not extra:
        return part
    part = jnp.pad(part.reshape(slots, rows, copies, width), ((0, 0), (0, 0), (0, 0), (0, extra)))
    return part.reshape(slots, rows, copies * (width + extra))


def narrow(part, copies, width):
    slots, rows, wide = part.shape
    wide = wide // copies
    if wide == width:
        return part
    return part.reshape(slots, rows, copies, wide)[..., :width].reshape(slots, rows, -1)


def attention_cost(slots, rows, width, products):
    return pl.CostEstimate(
        flops=products * 8 * slots * rows * rows * width,
        transcendentals=slots * rows * rows * (width // HEAD),
        bytes_accessed=slots * rows * width * 2 * (4 + 3 * (products > 2)),
    )


def attend(parts):
    slots = parts[0].shape[0]
    width = parts[0].shape[2] // 3
    parts = [widen(part, 3) for part in parts]
    count = len(parts)
    wide = parts[0].shape[2] // 3
    groups = wide // LANES
    total = sum(part.shape[1] for part in parts)
    outs = pl.pallas_call(
        functools.partial(attend_kernel, count),
        grid=(slots, groups),
        in_specs=lane_blocks(parts, 0) + lane_blocks(parts, groups) + lane_blocks(parts, 2 * groups),
        out_specs=lane_blocks(parts, 0)
        + [
            pl.BlockSpec((1, 1, 2, part.shape[1]), lambda s, p: (s, p, 0, 0)) for part in parts
        ],
        out_shape=[jax.ShapeDtypeStruct((slots, part.shape[1], wide), BF16) for part in parts]
        + [jax.ShapeDtypeStruct((slots, groups, 2, part.shape[1]), F32) for part in parts],
        scratch_shapes=[pltpu.VMEM((total, LANES), BF16)] * 2,
        compiler_params=pltpu.CompilerParams(vmem_limit_bytes=48 * 1024 * 1024),
        cost_estimate=attention_cost(slots, total, wide, 2),
        name="attend",
    )(*parts, *parts, *parts)
    return [narrow(out, 1, width) for out in outs[:count]], outs[count:]


def attend_back(parts, upstreams, sums):
    slots = parts[0].shape[0]
    width = parts[0].shape[2] // 3
    parts = [widen(part, 3) for part in parts]
    upstreams = [widen(part, 1) for part in upstreams]
    count = len(parts)
    wide = parts[0].shape[2] // 3
    groups = wide // LANES
    total = sum(part.shape[1] for part in parts)
    outs = pl.pallas_call(
        functools.partial(attend_back_kernel, count, groups),
        grid=(slots, groups),
        in_specs=lane_blocks(parts, 0)
        + lane_blocks(parts, groups)
        + lane_blocks(parts, 2 * groups)
        + lane_blocks(upstreams, 0)
        + [
            pl.BlockSpec((1, 1, 2, part.shape[1]), lambda s, p: (s, p, 0, 0)) for part in parts
        ],
        out_specs=[
            pl.BlockSpec((1, part.shape[1], 3 * wide), lambda s, p: (s, 0, 0)) for part in parts
        ],
        out_shape=[jax.ShapeDtypeStruct((slots, part.shape[1], 3 * wide), BF16) for part in parts],
        scratch_shapes=[pltpu.VMEM((total, LANES), BF16)] * 2 + [pltpu.VMEM((total, LANES), F32)] * 2,
        compiler_params=pltpu.CompilerParams(vmem_limit_bytes=48 * 1024 * 1024),
        cost_estimate=attention_cost(slots, total, wide, 5),
        name="attend_back",
    )(*parts, *parts, *parts, *upstreams, *sums)
    return [narrow(out, 3, width) for out in outs]


def rows_kernel(count, *refs):
    lefts, rights, out = refs[:count], refs[count : 2 * count], refs[-1]
    total = None
    for left, right in zip(lefts, rights):
        for slot in range(left.shape[0]):
            part = dot(left[slot], right[slot], 0, 0)
            total = part if total is None else total + part
    out[...] = total.astype(BF16)


def weight_grad(pairs):
    joined = None
    rows = pairs[0][0][0].shape[-1]
    wide = sum(rights[0].shape[-1] for _, rights in pairs)
    start = 0
    for lefts, rights in pairs:
        part = rights[0].shape[-1]
        if part % LANES or start % part:
            return jnp.concatenate([plain_grad(*pair) for pair in pairs], axis=1)
        count = len(lefts)
        step = 256
        length = sum(left.shape[0] * left.shape[1] for left in lefts)
        ins = [
            pl.BlockSpec((left.shape[0], left.shape[1], step), lambda i: (0, 0, i))
            for left in lefts
        ] + [
            pl.BlockSpec(right.shape, lambda i: (0, 0, 0), pipeline_mode=pl.Buffered(1))
            for right in rights
        ]
        operands = (*lefts, *rights)
        if joined is not None:
            ins.append(pl.BlockSpec(memory_space=pl.ANY))
            operands += (joined,)
        joined = pl.pallas_call(
            functools.partial(rows_kernel, count),
            grid=(rows // step,),
            in_specs=ins,
            out_specs=pl.BlockSpec((step, part), lambda i, c=start // part: (i, c)),
            out_shape=jax.ShapeDtypeStruct((rows, wide), BF16),
            input_output_aliases={} if joined is None else {2 * count: 0},
            compiler_params=pltpu.CompilerParams(vmem_limit_bytes=48 * 1024 * 1024),
            cost_estimate=pl.CostEstimate(
                flops=2 * length * rows * part,
                transcendentals=0,
                bytes_accessed=2 * (length * (rows + part) + rows * part),
            ),
            name="weight_grad",
        )(*operands)
        start += part
    return joined


def plain_grad(lefts, rights):
    left = jnp.concatenate([v.reshape(-1, v.shape[-1]) for v in lefts], axis=0)
    right = jnp.concatenate([v.reshape(-1, v.shape[-1]) for v in rights], axis=0)
    return dot(left, right, 0, 0).astype(BF16)


def on_device(
    group_count,
    tensor_size,
    image_tokens,
    text_tokens,
    condition,
    group_size,
    image_modulation,
    image_attention_in,
    image_attention_out,
    image_hidden_in,
    image_hidden_out,
    text_modulation,
    text_attention_in,
    text_attention_out,
    text_hidden_in,
    text_hidden_out,
    image_cotangent,
    text_cotangent,
):
    size = tensor_size
    slots, image_length, model = image_tokens.shape
    text_length = text_tokens.shape[1]
    share, _, width = image_attention_in.shape
    units = image_hidden_in.shape[1]
    tensor_rank = lax.axis_index("tensor")
    group_rank = lax.axis_index("dp")

    def gathered(*blocks):
        joined = blocks[0] if len(blocks) == 1 else jnp.concatenate(blocks, axis=1)
        return lax.all_gather(joined, "dp", axis=0, tiled=True)

    packed_in = gathered(
        image_attention_in.reshape(share, 3 * width), text_attention_in.reshape(share, 3 * width)
    )
    packed_mid = gathered(image_attention_out.T, text_attention_out.T, image_hidden_in)
    image_down = gathered(image_hidden_out.T)
    weight_in = (packed_in[:, : 3 * width], packed_in[:, 3 * width :])
    weight_out = (packed_mid[:, :width], packed_mid[:, width : 2 * width])

    alive = (jnp.arange(slots) < group_size[0]).astype(F32)[:, None, None]
    cond_full = condition.astype(F32)
    group_order = group_rank ^ jnp.arange(group_count)
    activated_low = jax.nn.silu(cond_full).astype(BF16)
    activated_blocks = [
        lax.dynamic_slice_in_dim(activated_low, group_order[k] * share, share, 1)
        for k in range(group_count)
    ]
    activated_own = jnp.concatenate(exchange(activated_blocks, group_count, "dp"), axis=0)
    all_slots = activated_own.shape[0]
    mod_parts = jnp.concatenate(
        [
            dot(activated_own, image_modulation.reshape(share, 6 * width), 1, 0),
            dot(activated_own, text_modulation.reshape(share, 6 * width), 1, 0),
        ],
        axis=1,
    ).reshape(group_count, slots, 12 * width)
    mod_own = sum(exchange([mod_parts[k] for k in range(group_count)], group_count, "dp"))
    modulations = lax.all_gather(
        mod_own.reshape(slots, 2, 6, width), "tensor", axis=3, tiled=True
    )
    mods = (modulations[:, 0], modulations[:, 1])

    tokens = (image_tokens.astype(F32), text_tokens.astype(F32))
    outgoing = (image_cotangent.astype(F32) * alive, text_cotangent.astype(F32) * alive)

    def image_rows(values):
        return gather_pieces(values.astype(BF16), size)

    def text_rows(values):
        return [values.astype(BF16)]

    collect = (image_rows, text_rows)

    def flat(values):
        return values.reshape(-1, values.shape[-1])

    def apply(pieces, weight, weight_dim, low):
        return [
            dot(flat(piece), weight, 1, weight_dim)
            .astype(BF16 if low else F32)
            .reshape(slots, piece.shape[1], -1)
            for piece in pieces
        ]

    def reduced(stream, pieces, weight, weight_dim):
        if stream == 1:
            return text_sum(
                dot(flat(pieces[0]), weight, 1, weight_dim).reshape(slots, text_length, model), size
            )

        def make_piece(k):
            return dot(flat(pieces[k]), weight, 1, weight_dim).reshape(slots, image_length, model)

        return scatter_sum(make_piece, size)

    first_saved = []
    packed = []
    for stream in range(2):
        mod = mods[stream]
        normed, inverse = norm_rows(tokens[stream])
        first_in = normed * (1.0 + spread(mod[:, 1])) + spread(mod[:, 0])
        pieces = collect[stream](first_in)
        packed.append(apply(pieces, weight_in[stream], 0, True))
        first_saved.append((normed, inverse, pieces))
    parts = packed[0] + packed[1]
    down_pieces = [
        collect[stream](outgoing[stream] * spread(mods[stream][:, 5])) for stream in range(2)
    ]
    text_mlp_own = jnp.concatenate([text_hidden_in, text_hidden_out.T], axis=1)
    parts, down_pieces, text_mlp_own = lax.optimization_barrier((parts, down_pieces, text_mlp_own))
    packed_text = ring_gather(text_mlp_own, group_count)
    weight_up = (packed_mid[:, 2 * width :], packed_text[:, :units])
    weight_down = (image_down, packed_text[:, units:])
    attended, sums = attend(parts)
    attended_parts = (attended[:-1], attended[-1:])
    outputs = []
    second_saved = []
    for stream in range(2):
        mod = mods[stream]
        branch = reduced(stream, attended_parts[stream], weight_out[stream], 1)
        middle = tokens[stream] + spread(mod[:, 2]) * branch
        normed_two, inverse_two = norm_rows(middle)
        second_in = normed_two * (1.0 + spread(mod[:, 4])) + spread(mod[:, 3])
        pieces = collect[stream](second_in)
        hidden = apply(pieces, weight_up[stream], 0, False)
        active = [gelu_tanh(piece).astype(BF16) for piece in hidden]
        branch_two = reduced(stream, active, weight_down[stream], 1)
        result = middle + spread(mod[:, 5]) * branch_two
        outputs.append((result * alive).astype(BF16))
        second_saved.append((branch, normed_two, inverse_two, pieces, hidden, active, branch_two))

    def scattered(grad):
        return lax.psum_scatter(grad, "dp", scatter_dimension=0, tiled=True).astype(F32)

    mlp_grads = []
    middle_grads = []
    stats = []
    upstreams = []
    out_pairs = []
    for stream in range(2):
        mod = mods[stream]
        branch, normed_two, inverse_two, pieces, hidden, active, branch_two = second_saved[stream]
        gate_two_grad = jnp.sum(outgoing[stream] * branch_two, axis=1)
        active_grad = apply(down_pieces[stream], weight_down[stream], 0, False)
        hidden_grad = [
            jax.vjp(gelu_tanh, value)[1](grad)[0].astype(BF16)
            for value, grad in zip(hidden, active_grad)
        ]
        mlp_grads.append(weight_grad([(down_pieces[stream], active), (pieces, hidden_grad)]))
        second_grad = reduced(stream, hidden_grad, weight_up[stream], 1)
        shift_two_grad = jnp.sum(second_grad, axis=1)
        scale_two_grad = jnp.sum(second_grad * normed_two, axis=1)
        middle_grad = outgoing[stream] + norm_back(
            second_grad * (1.0 + spread(mod[:, 4])), normed_two, inverse_two
        )
        gate_one_grad = jnp.sum(middle_grad * branch, axis=1)
        branch_grad = collect[stream](middle_grad * spread(mod[:, 2]))
        out_pairs.append((branch_grad, attended_parts[stream]))
        upstreams.extend(apply(branch_grad, weight_out[stream], 0, True))
        middle_grads.append(middle_grad)
        stats.append((gate_one_grad, shift_two_grad, scale_two_grad, gate_two_grad))
    image_mlp = scattered(mlp_grads[0])
    text_grad, upstreams = lax.optimization_barrier((mlp_grads[1], upstreams))
    text_ring = ring_scatter(text_grad, group_count)
    text_hop = next(text_ring)
    packed_grads = attend_back(parts, upstreams, sums)
    packed_grads, text_hop = lax.optimization_barrier((packed_grads, text_hop))
    text_hop = text_ring.send(text_hop)
    late_grads, image_mlp = lax.optimization_barrier((packed_grads, image_mlp))
    packed_grads = (packed_grads[:-1], packed_grads[-1:])
    late_grads = (late_grads[:-1], late_grads[-1:])
    in_pairs = [(first_saved[stream][2], late_grads[stream]) for stream in range(2)]
    attention_grad = weight_grad(in_pairs + out_pairs)
    for _ in range(group_count // 2 - 3):
        attention_grad, text_hop = lax.optimization_barrier((attention_grad, text_hop))
        text_hop = text_ring.send(text_hop)
    attention_sum = scattered(attention_grad)
    input_grads = [None, None]
    mod_grads = [None, None]
    for stream in (1, 0):
        mod = mods[stream]
        normed, inverse, pieces = first_saved[stream]
        gate_one_grad, shift_two_grad, scale_two_grad, gate_two_grad = stats[stream]
        first_grad = reduced(stream, packed_grads[stream], weight_in[stream], 1)
        first_grad, text_hop = lax.optimization_barrier((first_grad, text_hop))
        text_hop = text_ring.send(text_hop)
        shift_one_grad = jnp.sum(first_grad, axis=1)
        scale_one_grad = jnp.sum(first_grad * normed, axis=1)
        input_grads[stream] = middle_grads[stream] + norm_back(
            first_grad * (1.0 + spread(mod[:, 1])), normed, inverse
        )
        mod_grads[stream] = jnp.stack(
            [
                shift_one_grad,
                scale_one_grad,
                gate_one_grad,
                shift_two_grad,
                scale_two_grad,
                gate_two_grad,
            ],
            axis=1,
        )
    text_mlp = text_hop

    image_share = sum(
        exchange(
            [
                lax.dynamic_slice_in_dim(mod_grads[0], (tensor_rank ^ k) * width, width, 2)
                for k in range(size)
            ],
            size,
            "tensor",
        )
    )
    text_share = lax.dynamic_slice_in_dim(mod_grads[1], tensor_rank * width, width, 2)
    share_low = jnp.stack([image_share, text_share], axis=1).astype(BF16)
    share_all = jnp.concatenate(gather_pieces(share_low, group_count, "dp"), axis=0)
    image_all = share_all[:, 0].reshape(all_slots, 6 * width)
    text_all = share_all[:, 1].reshape(all_slots, 6 * width)
    image_ada = dot(activated_own, image_all, 0, 0).reshape(share, 6, width)
    text_ada = dot(activated_own, text_all, 0, 0).reshape(share, 6, width)
    activated_part = dot(image_all, image_modulation.reshape(share, 6 * width), 1, 1) + dot(
        text_all, text_modulation.reshape(share, 6 * width), 1, 1
    )
    activated_part = sum_all(activated_part, size, "tensor").reshape(group_count, slots, share)
    activated_rows = jnp.stack(
        exchange([activated_part[k] for k in range(group_count)], group_count, "dp")
    )
    activated_grad = jnp.concatenate(
        [
            lax.dynamic_index_in_dim(activated_rows, group_order[k], 0, keepdims=False)
            for k in range(group_count)
        ],
        axis=1,
    )
    condition_gradient = jax.vjp(jax.nn.silu, cond_full)[1](activated_grad)[0]

    return (
        outputs[0],
        outputs[1],
        input_grads[0],
        input_grads[1],
        condition_gradient,
        image_ada,
        attention_sum[:, : 3 * width].reshape(share, 3, width),
        attention_sum[:, 6 * width : 7 * width].T,
        image_mlp[:, units:],
        image_mlp[:, :units].T,
        text_ada,
        attention_sum[:, 3 * width : 6 * width].reshape(share, 3, width),
        attention_sum[:, 7 * width :].T,
        text_mlp[:, units:],
        text_mlp[:, :units].T,
    )


def solution(mesh):
    image = P("dp", "tensor", None)
    text = P("dp", None, None)
    columns = P("dp", None, "tensor")
    rows = P("tensor", "dp")
    plain = P("dp", "tensor")
    weights = (columns, columns, rows, plain, rows)
    return jax.shard_map(
        functools.partial(on_device, mesh.shape["dp"], mesh.shape["tensor"]),
        mesh=mesh,
        in_specs=(image, text, P("dp", None), P("dp")) + weights + weights + (image, text),
        out_specs=(image, text, image, text, P("dp", None)) + weights + weights,
        check_vma=False,
    )
```

time: 2910 us -> 1030 us (0.35)
  waiting for transfers between devices: 2160 us -> 376 us
  matrix products: 466 us -> 180 us
  Pallas kernels: 0 us -> 182 us
  other arithmetic: 167 us -> 69.5 us
  starting transfers between devices: 1.69 us -> 90.4 us
    reduce_scatter x14 -> x2, waiting for transfers between devices: 1280 us -> 0.01 us  [scattered(): lax.psum_scatter(grad, 'dp', scatter_dimension=0, tiled=True).astype(F32)]
    all_gather x14 -> x3, waiting for transfers between devices: 832 us -> 49.2 us  [gathered(): return lax.all_gather(joined, 'dp', axis=0, tiled=True)]
    ppermute x0 -> x81, waiting for transfers between devices: none -> 327 us  [the longest x65 221 us: swap(): return lax.ppermute(value, axis, [(i, i ^ bit) for i in range(size)])]
    dot_general x44 -> x46, matrix products: 466 us -> 180 us  [dot(): lax.dot_general(left, right, (((left_dim,), (right_dim,)), ((), ())), pre...]
    pallas_call x0 -> x10, Pallas kernels: none -> 182 us  [the longest x8 68.8 us: weight_grad(): pl.pallas_call(functools.partial(rows_kernel, count), grid=(rows // step,...]
    ppermute x0 -> x81, starting transfers between devices: none -> 89.8 us  [the longest x65 63.7 us: swap(): return lax.ppermute(value, axis, [(i, i ^ bit) for i in range(size)])]
    convert_element_type x17 -> x19, other arithmetic: 88.4 us -> 27.2 us  [the longest x3 12.1 us: ring_scatter(): ahead = ring_step((own(-hop) + ahead).astype(BF16), -1, count)]
    psum x3 -> x0, waiting for transfers between devices: 41.5 us -> none  [text_partial(): return lax.psum(values, 'tensor')]
  transfers between devices with their start and end apart: 32 -> 86, of which waited for: 29 -> 28; matrix products, arithmetic and copies ran while one was open for 14% -> 29% of each run, Pallas kernels for 0% -> 15%
where the time goes in v1:
time: 1030 us; the launch traced here: 1020 us
  waiting for transfers between devices  376 us (37%)
  Pallas kernels  182 us (18%)
  matrix products  180 us (17%)
  starting transfers between devices  90.4 us (9%)
  local copies, waits for them, and re-layouts  77.5 us (8%)
  other arithmetic  69.5 us (7%)
  between operations  37.7 us (4%)
    ppermute x65, waiting for transfers between devices, swap(): return lax.ppermute(value, axis, [(i, i ^ bit) for i in range(size)])  221 us
    dot_general x46, matrix products, dot(): lax.dot_general(left, right, (((left_dim,), (right_dim,)), ((), ())), pre...  180 us
    ppermute x16, waiting for transfers between devices, ring_step(): return lax.ppermute(value, 'dp', hops)  106 us
    pallas_call x8, Pallas kernels, weight_grad(): pl.pallas_call(functools.partial(rows_kernel, count), grid=(rows // step,...  68.8 us
    ppermute x65, starting transfers between devices, swap(): return lax.ppermute(value, axis, [(i, i ^ bit) for i in range(size)])  63.7 us
    pallas_call x1, Pallas kernels, attend_back(): pl.pallas_call(functools.partial(attend_back_kernel, count, groups), grid...  58.1 us
    pallas_call x1, Pallas kernels, attend(): pl.pallas_call(functools.partial(attend_kernel, count), grid=(slots, grou...  55.2 us
    all_gather x3, waiting for transfers between devices, gathered(): return lax.all_gather(joined, 'dp', axis=0, tiled=True)  49.2 us
  transfers between devices with their start and end apart: 86, of which 28 were waited for; matrix products, arithmetic and copies ran while one was open for 29% of the time, Pallas kernels for 15%

profile of v1, /device:TPU:0, one launch (start us, length us, event | category | flops | bytes accessed | tf_op | source)
XLA Modules:
  0.0 1019.1 jit_solution(10323439901939101472)
XLA Ops:
  54.9 5.9 all_gather.12
  71.4 29.5 %collective-permute-done.15.refs_2_ = bf16[2,256,1536]{2,1,0:T(8,128)(2,1)} collective-permute-done((bf16[2,256,1536]{2,1,0:T(8,128)(2,1)}, bf16[2,256,1536]{2,1,0:T(8,128)(2,1)}, u32[]{:S(2)}, u32[]{:S(2)}) %collective-permute-start.15) | collective-permute-done | bytes 1572896 | tf_op jit(solution)/shard_map/ppermute | solution.py:43
  100.9 33.1 %collective-permute-done.18.refs_2_ = bf16[2,256,1536]{2,1,0:T(8,128)(2,1)} collective-permute-done((bf16[2,256,1536]{2,1,0:T(8,128)(2,1)S(1)}, bf16[2,256,1536]{2,1,0:T(8,128)(2,1)}, u32[]{:S(2)}, u32[]{:S(2)}) %collective-permute-start.18) | collective-permute-done | bytes 1572896 | tf_op jit(solution)/shard_map/ppermute | solution.py:43
  161.2 55.2 %attend.1 = (bf16[2,256,384]{2,1,0:T(8,128)(2,1)S(1)}, bf16[2,256,384]{2,1,0:T(8,128)(2,1)S(1)}, bf16[2,256,384]{2,1,0:T(8,128)(2,1)S(1)}, bf16[2,256,384]{2,1,0...) custom-call(bf16[2,256,1152]{2,1,0:T(8,128)(2,1)S(1)} %bitcast.317, ...), custom_call_target="tpu_custom_call" | custom-call | flops 17051860992 | bytes 7237632 | tf_op jit(solution)/shard_map/attend/pallas_call | solution.py:283
  220.2 33.5 %all-gather.6.cloned.1.call-done = bf16[1536,2304]{1,0:T(8,128)(2,1)} async-done(((bf16[192,2304]{1,0:T(8,128)(2,1)}), bf16[1536,2304]{1,0:T(8,128)(2,1)}) %all-gather.6.cloned.1.call-update) | async-done | bytes 7077904 | tf_op jit(solution)/shard_map/all_gather | solution.py:420
  285.5 29.9 %collective-permute-done.33 = bf16[192,3072]{1,0:T(8,128)(2,1)} collective-permute-done((bf16[192,3072]{1,0:T(8,128)(2,1)}, bf16[192,3072]{1,0:T(8,128)(2,1)}, u32[]{:S(2)}, u32[]{:S(2)}) %collective-permute-start.33) | collective-permute-done | bytes 1179680 | tf_op jit(solution)/shard_map/ppermute | solution.py:100
  315.4 8.9 collective-permute-start.35
  346.8 6.1 multiply_convert_fusion.5
  352.9 15.7 %all-gather.8.cloned.1.call-done = bf16[1536,1536]{1,0:T(8,128)(2,1)} async-done(((bf16[192,1536]{1,0:T(8,128)(2,1)}), bf16[1536,1536]{1,0:T(8,128)(2,1)}) %all-gather.8.cloned.1.call-update) | async-done | bytes 4718608 | tf_op jit(solution)/shard_map/all_gather | solution.py:420
  368.6 7.0 fusion.59.refs_4_
  379.9 6.6 fusion.202
  396.5 6.9 collective-permute-done.37
  407.6 5.9 multiply_convert_fusion.9
  419.2 6.7 fusion.73.refs_6_
  431.6 6.5 fusion.66.refs_5_
  442.6 15.3 %weight_grad.10.refs_8_ = bf16[1536,3072]{1,0:T(8,128)(2,1)} custom-call(bf16[2,256,1536]{2,1,0:T(8,128)(2,1)S(1)} %copy-done.4, bf16[2,256,1536]{2,1,0:T(8,128)(2,1)} %collective-permute-done.17.refs_1_, bf16[2,256,1536]{2,1,0:T(8,128)(2,1)} %collective-permute-done.18.refs_2_, bf16[2,256,1536]{2,1,0:T(8,128)(2,1)} %collective-permute-done.19.refs_3_, ...), custom_call_target="tpu_custom_call" | custom-call | flops 9663676416 | bytes 17301504 | tf_op jit(solution)/shard_map/weight_grad/pallas_call | solution.py:365
  457.9 6.5 fusion.80.refs_7_
  464.4 15.2 %weight_grad.11 = bf16[1536,3072]{1,0:T(8,128)(2,1)} custom-call(bf16[2,256,1536]{2,1,0:T(8,128)(2,1)} %add_convert_fusion.2.refs_0_, bf16[2,256,1536]{2,1,0:T(8,128)(2,1)} %collective-permute-done.23.refs_1_, bf16[2,256,1536]{2,1,0:T(8,128)(2,1)} %collective-permute-done.25.refs_2_, ...), custom_call_target="tpu_custom_call", output_to_operand_aliasing={{}: (8, {})} | custom-call | flops 9663676416 | bytes 17301504 | tf_op jit(solution)/shard_map/weight_grad/pallas_call | solution.py:365
  517.0 6.4 fusion.101
  547.4 25.0 %collective-permute-done.43 = bf16[2,256,1536]{2,1,0:T(8,128)(2,1)} collective-permute-done((bf16[2,256,1536]{2,1,0:T(8,128)(2,1)}, bf16[2,256,1536]{2,1,0:T(8,128)(2,1)}, u32[]{:S(2)}, u32[]{:S(2)}) %collective-permute-start.43) | collective-permute-done | bytes 1572896 | tf_op jit(solution)/shard_map/ppermute | solution.py:43
  576.0 50.2 %collective-permute-done.28 = bf16[2,256,1536]{2,1,0:T(8,128)(2,1)S(1)} collective-permute-done((bf16[2,256,1536]{2,1,0:T(8,128)(2,1)}, bf16[2,256,1536]{2,1,0:T(8,128)(2,1)S(1)}, u32[]{:S(2)}, u32[]{:S(2)}) %collective-permute-start.28) | collective-permute-done | bytes 1572896 | tf_op jit(solution)/shard_map/ppermute | solution.py:43
  627.5 6.2 multiply_reduce_fusion
  635.8 10.8 %collective-permute-done.48 = bf16[2,154,1536]{2,0,1:T(2,128)(2,1)} collective-permute-done((bf16[2,154,1536]{2,0,1:T(2,128)(2,1)}, bf16[2,154,1536]{2,0,1:T(2,128)(2,1)}, u32[]{:S(2)}, u32[]{:S(2)}) %collective-permute-start.48) | collective-permute-done | bytes 946208 | tf_op jit(solution)/shard_map/ppermute | solution.py:43
  655.2 24.6 %collective-permute-done.45.refs_2_ = bf16[2,256,1536]{2,1,0:T(8,128)(2,1)} collective-permute-done((bf16[2,256,1536]{2,1,0:T(8,128)(2,1)S(1)}, bf16[2,256,1536]{2,1,0:T(8,128)(2,1)}, u32[]{:S(2)}, u32[]{:S(2)}) %collective-permute-start.45) | collective-permute-done | bytes 1572896 | tf_op jit(solution)/shard_map/ppermute | solution.py:43
  699.7 58.1 %attend_back.1 = (bf16[2,256,1152]{2,1,0:T(8,128)(2,1)S(1)}, bf16[2,256,1152]{2,1,0:T(8,128)(2,1)S(1)}, bf16[2,256,1152]{2,1,0:T(8,128)(2,1)}, bf16[2,256,1152]{2,1,0:T(8,128)(2,1)}, bf16[2,154,1152]{2,1,0:T(8,128)(2,1)S(1)}) custom-call(bf16[2,256,1152]{2,1,0:T(8,128)(2,1)} %bitcast.320, bf16[2,256,1152]{2,1,0:T(8,128)(2,1)} %bitcast.326, ...), custom_call_target="tpu_custom_call" | custom-call | flops 42629652480 | bytes 12665856 | tf_op jit(solution)/shard_map/attend_back/pallas_call | solution.py:310
  769.0 11.6 %weight_grad.12.refs_2_ = bf16[1536,3072]{1,0:T(8,128)(2,1)} custom-call(bf16[2,256,1536]{2,1,0:T(8,128)(2,1)} %fusion.46.refs_0_, bf16[2,256,1536]{2,1,0:T(8,128)(2,1)} %collective-permute-done.14.refs_1_, bf16[2,256,1536]{2,1,0:T(8,128)(2,1)} %collective-permute-done.15.refs_2_, bf16[2,256,1536]{2,1,0:T(8,128)(2,1)} %collective-permute-done.16.refs_3_, ...), custom_call_target="tpu_custom_call" | custom-call | flops 7247757312 | bytes 14548992 | tf_op jit(solution)/shard_map/weight_grad/pallas_call | solution.py:365
  785.4 7.5 weight_grad.14.refs_2_
  846.5 21.5 %collective-permute-done.53 = bf16[2,256,1536]{2,1,0:T(8,128)(2,1)} collective-permute-done((bf16[2,256,1536]{2,1,0:T(8,128)(2,1)}, bf16[2,256,1536]{2,1,0:T(8,128)(2,1)}, u32[]{:S(2)}, u32[]{:S(2)}) %collective-permute-start.53) | collective-permute-done | bytes 1572896 | tf_op jit(solution)/shard_map/ppermute | solution.py:43
  868.0 6.8 fusion.39
  876.4 20.3 %collective-permute-done.58 = bf16[192,3072]{1,0:T(8,128)(2,1)S(1)} collective-permute-done((bf16[192,3072]{1,0:T(8,128)(2,1)S(1)}, bf16[192,3072]{1,0:T(8,128)(2,1)S(1)}, u32[]{:S(2)}, u32[]{:S(2)}) %collective-permute-start.58) | collective-permute-done | bytes 1179680 | tf_op jit(solution)/shard_map/ppermute | solution.py:100
  896.7 11.9 %collective-permute-done.59 = bf16[192,3072]{1,0:T(8,128)(2,1)S(1)} collective-permute-done((bf16[192,3072]{1,0:T(8,128)(2,1)S(1)}, bf16[192,3072]{1,0:T(8,128)(2,1)S(1)}, u32[]{:S(2)}, u32[]{:S(2)}) %collective-permute-start.59) | collective-permute-done | bytes 1179680 | tf_op jit(solution)/shard_map/ppermute | solution.py:100
  919.5 33.8 %collective-permute-done.60 = bf16[192,3072]{1,0:T(8,128)(2,1)S(1)} collective-permute-done((bf16[192,3072]{1,0:T(8,128)(2,1)}, bf16[192,3072]{1,0:T(8,128)(2,1)S(1)}, u32[]{:S(2)}, u32[]{:S(2)}) %collective-permute-start.60) | collective-permute-done | bytes 1179680 | tf_op jit(solution)/shard_map/ppermute | solution.py:100
  (689 shorter events, 392.3 us)
Async XLA Ops:
  7.2 126.9 %all-gather.4.cloned.1.call-start = ((), (), s32[]{:S(2)}) async-start(), calls=%async_computation.2 | async-start | bytes 7962624 | tf_op jit(solution)/shard_map/all_gather | solution.py:420
  10.5 243.2 %all-gather.6.cloned.1.call-start = ((), (), s32[]{:S(2)}) async-start(), calls=%async_computation.3 | async-start | bytes 7962624 | tf_op jit(solution)/shard_map/all_gather | solution.py:420
  11.5 357.0 %all-gather.8.cloned.1.call-start = ((), (), s32[]{:S(2)}) async-start(), calls=%async_computation.4 | async-start | bytes 5308416 | tf_op jit(solution)/shard_map/all_gather | solution.py:420
  26.5 738.0 %reduce-scatter.3.cloned.1.call-start = ((), (), s32[]{:S(2)}) async-start(), calls=%async_computation.5 | async-start | bytes 10616832 | tf_op jit(solution)/shard_map/reduce_scatter | solution.py:523
  65.4 68.7 %collective-permute-start.18 = (bf16[2,256,1536]{2,1,0:T(8,128)(2,1)S(1)}, bf16[2,256,1536]{2,1,0:T(8,128)(2,1)}, u32[]{:S(2)}, u32[]{:S(2)}) collective-permute-start(bf16[2,256,1536]{2,1,0:T(8,128)(2,1)S(1)} %multiply_convert_fusion.6.refs_0_), channel_id=1, source_target_pairs={{0,2},{1,3},{2,0},{3,1},{4,6},{5,7},{6,4},{7,5},{8,10},{9,11},{10,... | collective-permute-start | bytes 4718600 | tf_op jit(solution)/shard_map/ppermute | solution.py:43
  67.2 77.5 %collective-permute-start.14 = (bf16[2,256,1536]{2,1,0:T(8,128)(2,1)}, bf16[2,256,1536]{2,1,0:T(8,128)(2,1)}, u32[]{:S(2)}, u32[]{:S(2)}) collective-permute-start(bf16[2,256,1536]{2,1,0:T(8,128)(2,1)} %fusion.46.refs_0_), channel_id=1, source_target_pairs={{0,1},{1,0},{2,3},{3,2},{4,5},{5,4},{6,7},{7,6},{8,9},{9,8},{10,11... | collective-permute-start | bytes 4718600 | tf_op jit(solution)/shard_map/ppermute | solution.py:43
  67.2 91.8 %collective-permute-start.17 = (bf16[2,256,1536]{2,1,0:T(8,128)(2,1)S(1)}, bf16[2,256,1536]{2,1,0:T(8,128)(2,1)}, u32[]{:S(2)}, u32[]{:S(2)}) collective-permute-start(bf16[2,256,1536]{2,1,0:T(8,128)(2,1)S(1)} %multiply_convert_fusion.6.refs_0_), channel_id=1, source_target_pairs={{0,1},{1,0},{2,3},{3,2},{4,5},{5,4},{6,7},{7,6},{8,9},{9,8},{10,11... | collective-permute-start | bytes 4718600 | tf_op jit(solution)/shard_map/ppermute | solution.py:43
  100.9 53.0 %collective-permute-start.16 = (bf16[2,256,1536]{2,1,0:T(8,128)(2,1)}, bf16[2,256,1536]{2,1,0:T(8,128)(2,1)}, u32[]{:S(2)}, u32[]{:S(2)}) collective-permute-start(bf16[2,256,1536]{2,1,0:T(8,128)(2,1)} %collective-permute-done.15.refs_2_), channel_id=1, source_target_pairs={{0,1},{1,0},{2,3},{3,2},{4,5},{5,4},{6,7},{7,6},{8,9},{9,8},{10,11... | collective-permute-start | bytes 4718600 | tf_op jit(solution)/shard_map/ppermute | solution.py:43
  159.0 113.6 %collective-permute-start.31 = (bf16[192,3072]{1,0:T(8,128)(2,1)}, bf16[192,3072]{1,0:T(8,128)(2,1)}, u32[]{:S(2)}, u32[]{:S(2)}) collective-permute-start(bf16[192,3072]{1,0:T(8,128)(2,1)} %pad_maximum_fusion), channel_id=1, source_target_pairs={{0,8},{8,16},{16,24},{24,28},{28,20},{20,12},{12,4},{4,0},{1,9},{9... | collective-permute-start | bytes 3538952 | tf_op jit(solution)/shard_map/ppermute | solution.py:100
  159.9 112.7 %collective-permute-start.32 = (bf16[192,3072]{1,0:T(8,128)(2,1)}, bf16[192,3072]{1,0:T(8,128)(2,1)}, u32[]{:S(2)}, u32[]{:S(2)}) collective-permute-start(bf16[192,3072]{1,0:T(8,128)(2,1)} %pad_maximum_fusion), channel_id=1, source_target_pairs={{0,4},{8,0},{16,8},{24,16},{28,24},{20,28},{12,20},{4,12},{1,5},{9... | collective-permute-start | bytes 3538952 | tf_op jit(solution)/shard_map/ppermute | solution.py:100
  265.2 69.7 %collective-permute-start.20 = (bf16[2,256,1536]{2,1,0:T(8,128)(2,1)S(1)}, bf16[2,256,1536]{2,1,0:T(8,128)(2,1)S(1)}, u32[]{:S(2)}, u32[]{:S(2)}) collective-permute-start(bf16[2,256,1536]{2,1,0:T(8,128)(2,1)S(1)} %convolution_convert_fusion.7), channel_id=1, source_target_pairs={{0,1},{1,0},{2,3},{3,2},{4,5},{5,4},{6,7},{7,6},{8,9},{9,8},{10,11... | collective-permute-start | bytes 4718600 | tf_op jit(solution)/shard_map/ppermute | solution.py:43
  272.6 42.9 %collective-permute-start.33 = (bf16[192,3072]{1,0:T(8,128)(2,1)}, bf16[192,3072]{1,0:T(8,128)(2,1)}, u32[]{:S(2)}, u32[]{:S(2)}) collective-permute-start(bf16[192,3072]{1,0:T(8,128)(2,1)} %collective-permute-done.31), channel_id=1, source_target_pairs={{0,8},{8,16},{16,24},{24,28},{28,20},{20,12},{12,4},{4,0},{1,9},{9... | collective-permute-start | bytes 3538952 | tf_op jit(solution)/shard_map/ppermute | solution.py:100
  272.6 52.2 %collective-permute-start.34 = (bf16[192,3072]{1,0:T(8,128)(2,1)}, bf16[192,3072]{1,0:T(8,128)(2,1)}, u32[]{:S(2)}, u32[]{:S(2)}) collective-permute-start(bf16[192,3072]{1,0:T(8,128)(2,1)} %collective-permute-done.32), channel_id=1, source_target_pairs={{0,4},{8,0},{16,8},{24,16},{28,24},{20,28},{12,20},{4,12},{1,5},{9... | collective-permute-start | bytes 3538952 | tf_op jit(solution)/shard_map/ppermute | solution.py:100
  282.3 48.8 %collective-permute-start.30 = (bf16[2,154,1536]{2,0,1:T(2,128)(2,1)S(1)}, bf16[2,154,1536]{2,0,1:T(2,128)(2,1)S(1)}, u32[]{:S(2)}, u32[]{:S(2)}) collective-permute-start(bf16[2,154,1536]{2,0,1:T(2,128)(2,1)S(1)} %copy.67), channel_id=1, source_target_pairs={{0,2},{1,3},{2,0},{3,1},{4,6},{5,7},{6,4},{7,5},{8,10},{9,11},{10,... | collective-permute-start | bytes 2838536 | tf_op jit(solution)/shard_map/ppermute | solution.py:43
  284.9 53.9 %collective-permute-start.22 = (bf16[2,256,1536]{2,1,0:T(8,128)(2,1)S(1)}, bf16[2,256,1536]{2,1,0:T(8,128)(2,1)S(1)}, u32[]{:S(2)}, u32[]{:S(2)}) collective-permute-start(bf16[2,256,1536]{2,1,0:T(8,128)(2,1)S(1)} %add_convert_fusion.3), channel_id=1, source_target_pairs={{0,2},{1,3},{2,0},{3,1},{4,6},{5,7},{6,4},{7,5},{8,10},{9,11},{10,... | collective-permute-start | bytes 4718600 | tf_op jit(solution)/shard_map/ppermute | solution.py:43
  315.4 71.1 %collective-permute-start.35 = (bf16[192,3072]{1,0:T(8,128)(2,1)}, bf16[192,3072]{1,0:T(8,128)(2,1)}, u32[]{:S(2)}, u32[]{:S(2)}) collective-permute-start(bf16[192,3072]{1,0:T(8,128)(2,1)} %collective-permute-done.33), channel_id=1, source_target_pairs={{0,8},{8,16},{16,24},{24,28},{28,20},{20,12},{12,4},{4,0},{1,9},{9... | collective-permute-start | bytes 3538952 | tf_op jit(solution)/shard_map/ppermute | solution.py:100
  324.8 65.8 %collective-permute-start.36 = (bf16[192,3072]{1,0:T(8,128)(2,1)}, bf16[192,3072]{1,0:T(8,128)(2,1)}, u32[]{:S(2)}, u32[]{:S(2)}) collective-permute-start(bf16[192,3072]{1,0:T(8,128)(2,1)} %collective-permute-done.34), channel_id=1, source_target_pairs={{0,4},{8,0},{16,8},{24,16},{28,24},{20,28},{12,20},{4,12},{1,5},{9... | collective-permute-start | bytes 3538952 | tf_op jit(solution)/shard_map/ppermute | solution.py:100
  345.3 68.2 %collective-permute-start.25 = (bf16[2,256,1536]{2,1,0:T(8,128)(2,1)}, bf16[2,256,1536]{2,1,0:T(8,128)(2,1)}, u32[]{:S(2)}, u32[]{:S(2)}) collective-permute-start(bf16[2,256,1536]{2,1,0:T(8,128)(2,1)} %add_convert_fusion.2.refs_0_), channel_id=1, source_target_pairs={{0,2},{1,3},{2,0},{3,1},{4,6},{5,7},{6,4},{7,5},{8,10},{9,11},{10,... | collective-permute-start | bytes 4718600 | tf_op jit(solution)/shard_map/ppermute | solution.py:43
  346.8 79.2 %collective-permute-start.23 = (bf16[2,256,1536]{2,1,0:T(8,128)(2,1)}, bf16[2,256,1536]{2,1,0:T(8,128)(2,1)}, u32[]{:S(2)}, u32[]{:S(2)}) collective-permute-start(bf16[2,256,1536]{2,1,0:T(8,128)(2,1)} %add_convert_fusion.2.refs_0_), channel_id=1, source_target_pairs={{0,1},{1,0},{2,3},{3,2},{4,5},{5,4},{6,7},{7,6},{8,9},{9,8},{10,11... | collective-permute-start | bytes 4718600 | tf_op jit(solution)/shard_map/ppermute | solution.py:43
  479.6 528.3 %reduce-scatter.5.cloned.1.call-start = ((), (), s32[]{:S(2)}) async-start(), calls=%async_computation.6 | async-start | bytes 10616832 | tf_op jit(solution)/shard_map/reduce_scatter | solution.py:523
  487.5 47.3 %collective-permute-start.39 = (f32[2,154,1536]{2,0,1:T(2,128)}, f32[2,154,1536]{2,0,1:T(2,128)S(1)}, u32[]{:S(2)}, u32[]{:S(2)}) collective-permute-start(f32[2,154,1536]{2,0,1:T(2,128)} %copy.69), channel_id=1, source_target_pairs={{0,1},{1,0},{2,3},{3,2},{4,5},{5,4},{6,7},{7,6},{8,9},{9,8},{10,11... | collective-permute-start | bytes 5677064 | tf_op jit(solution)/shard_map/ppermute | solution.py:43
  500.5 41.9 %collective-permute-start.47 = (f32[2,154,1536]{2,0,1:T(2,128)}, f32[2,154,1536]{2,0,1:T(2,128)S(1)}, u32[]{:S(2)}, u32[]{:S(2)}) collective-permute-start(f32[2,154,1536]{2,0,1:T(2,128)} %copy.73), channel_id=1, source_target_pairs={{0,1},{1,0},{2,3},{3,2},{4,5},{5,4},{6,7},{7,6},{8,9},{9,8},{10,11... | collective-permute-start | bytes 5677064 | tf_op jit(solution)/shard_map/ppermute | solution.py:43
  523.3 52.7 %collective-permute-start.24 = (bf16[2,256,1536]{2,1,0:T(8,128)(2,1)}, bf16[2,256,1536]{2,1,0:T(8,128)(2,1)S(1)}, u32[]{:S(2)}, u32[]{:S(2)}) collective-permute-start(bf16[2,256,1536]{2,1,0:T(8,128)(2,1)} %fusion.101), channel_id=1, source_target_pairs={{0,1},{1,0},{2,3},{3,2},{4,5},{5,4},{6,7},{7,6},{8,9},{9,8},{10,11... | collective-permute-start | bytes 4718600 | tf_op jit(solution)/shard_map/ppermute | solution.py:43
  538.0 111.8 %collective-permute-start.40 = (bf16[2,154,1536]{2,0,1:T(2,128)(2,1)S(1)}, bf16[2,154,1536]{2,0,1:T(2,128)(2,1)}, u32[]{:S(2)}, u32[]{:S(2)}) collective-permute-start(bf16[2,154,1536]{2,0,1:T(2,128)(2,1)S(1)} %copy.71), channel_id=1, source_target_pairs={{0,2},{1,3},{2,0},{3,1},{4,6},{5,7},{6,4},{7,5},{8,10},{9,11},{10,... | collective-permute-start | bytes 2838536 | tf_op jit(solution)/shard_map/ppermute | solution.py:43
  542.4 83.8 %collective-permute-start.28 = (bf16[2,256,1536]{2,1,0:T(8,128)(2,1)}, bf16[2,256,1536]{2,1,0:T(8,128)(2,1)S(1)}, u32[]{:S(2)}, u32[]{:S(2)}) collective-permute-start(bf16[2,256,1536]{2,1,0:T(8,128)(2,1)} %add_convert_fusion.1), channel_id=1, source_target_pairs={{0,2},{1,3},{2,0},{3,1},{4,6},{5,7},{6,4},{7,5},{8,10},{9,11},{10,... | collective-permute-start | bytes 4718600 | tf_op jit(solution)/shard_map/ppermute | solution.py:43
  546.6 100.0 %collective-permute-start.48 = (bf16[2,154,1536]{2,0,1:T(2,128)(2,1)}, bf16[2,154,1536]{2,0,1:T(2,128)(2,1)}, u32[]{:S(2)}, u32[]{:S(2)}) collective-permute-start(bf16[2,154,1536]{2,0,1:T(2,128)(2,1)} %copy.75), channel_id=1, source_target_pairs={{0,2},{1,3},{2,0},{3,1},{4,6},{5,7},{6,4},{7,5},{8,10},{9,11},{10,... | collective-permute-start | bytes 2838536 | tf_op jit(solution)/shard_map/ppermute | solution.py:43
  634.1 45.7 %collective-permute-start.45 = (bf16[2,256,1536]{2,1,0:T(8,128)(2,1)S(1)}, bf16[2,256,1536]{2,1,0:T(8,128)(2,1)}, u32[]{:S(2)}, u32[]{:S(2)}) collective-permute-start(bf16[2,256,1536]{2,1,0:T(8,128)(2,1)S(1)} %multiply_convert_fusion.refs_0_), channel_id=1, source_target_pairs={{0,2},{1,3},{2,0},{3,1},{4,6},{5,7},{6,4},{7,5},{8,10},{9,11},{10,... | collective-permute-start | bytes 4718600 | tf_op jit(solution)/shard_map/ppermute | solution.py:43
  697.6 60.3 %collective-permute-start.49 = (bf16[192,1536]{1,0:T(8,128)(2,1)S(1)}, bf16[192,1536]{1,0:T(8,128)(2,1)S(1)}, u32[]{:S(2)}, u32[]{:S(2)}) collective-permute-start(bf16[192,1536]{1,0:T(8,128)(2,1)S(1)} %get-tuple-element.201), channel_id=1, source_target_pairs={{0,8},{8,16},{16,24},{24,28},{28,20},{20,12},{12,4},{4,0},{1,9},{9... | collective-permute-start | bytes 1769480 | tf_op jit(solution)/shard_map/ppermute | solution.py:100
  699.1 58.8 %collective-permute-start.50 = (bf16[192,1536]{1,0:T(8,128)(2,1)S(1)}, bf16[192,1536]{1,0:T(8,128)(2,1)S(1)}, u32[]{:S(2)}, u32[]{:S(2)}) collective-permute-start(bf16[192,1536]{1,0:T(8,128)(2,1)S(1)} %get-tuple-element.200), channel_id=1, source_target_pairs={{0,4},{8,0},{16,8},{24,16},{28,24},{20,28},{12,20},{4,12},{1,5},{9... | collective-permute-start | bytes 1769480 | tf_op jit(solution)/shard_map/ppermute | solution.py:100
  819.6 48.5 %collective-permute-start.53 = (bf16[2,256,1536]{2,1,0:T(8,128)(2,1)}, bf16[2,256,1536]{2,1,0:T(8,128)(2,1)}, u32[]{:S(2)}, u32[]{:S(2)}) collective-permute-start(bf16[2,256,1536]{2,1,0:T(8,128)(2,1)} %fusion.98), channel_id=1, source_target_pairs={{0,2},{1,3},{2,0},{3,1},{4,6},{5,7},{6,4},{7,5},{8,10},{9,11},{10,... | collective-permute-start | bytes 4718600 | tf_op jit(solution)/shard_map/ppermute | solution.py:43
  844.2 52.5 %collective-permute-start.58 = (bf16[192,3072]{1,0:T(8,128)(2,1)S(1)}, bf16[192,3072]{1,0:T(8,128)(2,1)S(1)}, u32[]{:S(2)}, u32[]{:S(2)}) collective-permute-start(bf16[192,3072]{1,0:T(8,128)(2,1)S(1)} %get-tuple-element.197), channel_id=1, source_target_pairs={{0,8},{8,16},{16,24},{24,28},{28,20},{20,12},{12,4},{4,0},{1,9},{9... | collective-permute-start | bytes 3538952 | tf_op jit(solution)/shard_map/ppermute | solution.py:100
  845.4 63.3 %collective-permute-start.59 = (bf16[192,3072]{1,0:T(8,128)(2,1)S(1)}, bf16[192,3072]{1,0:T(8,128)(2,1)S(1)}, u32[]{:S(2)}, u32[]{:S(2)}) collective-permute-start(bf16[192,3072]{1,0:T(8,128)(2,1)S(1)} %get-tuple-element.196), channel_id=1, source_target_pairs={{0,4},{8,0},{16,8},{24,16},{28,24},{20,28},{12,20},{4,12},{1,5},{9... | collective-permute-start | bytes 3538952 | tf_op jit(solution)/shard_map/ppermute | solution.py:100
  (217 other events, 3682.6 us)
Sparse Core Ops, SparseCore 0:
  10.8 117.8 all-gather.3
  131.5 122.1 all-gather.5
  255.9 112.6 all-gather.7
  479.7 165.4 reduce-scatter.2
  796.9 201.7 reduce-scatter.4

commit v2 on v1

--- a/solution.py
+++ b/solution.py
@@ -59,8 +59,17 @@
     return [have[k] for k in range(size)]
 
 
-def exchange(blocks, size, axis):
-    return [blocks[0]] + [swap(blocks[k], k, size, axis) for k in range(1, size)]
+def gather_stack(value, size, axis):
+    value = value[None]
+    for bit in bits_of(size):
+        value = jnp.concatenate([value, swap(value, bit, size, axis)], axis=0)
+    return value
+
+
+def scatter_stack(value, size, axis):
+    for bit in reversed(bits_of(size)):
+        value = value[:bit] + swap(value[bit:], bit, size, axis)
+    return value[0]
 
 
 def sum_all(value, size, axis):
@@ -69,8 +78,8 @@
     return value
 
 
-def scatter_sum(make_piece, size):
-    have = {k: make_piece(k) for k in reversed(range(size))}
+def scatter_sum(pieces, size):
+    have = dict(enumerate(pieces))
     for bit in bits_of(size):
         kept = {}
         for k in sorted(have, reverse=True):
@@ -79,6 +88,10 @@
                 kept[k] = have[k].astype(F32) + other.astype(F32)
         have = kept
     return have[0]
+
+
+def after(values, *others):
+    return lax.optimization_barrier((values, others))[0]
 
 
 def ring_of(count):
@@ -350,7 +363,6 @@
             return jnp.concatenate([plain_grad(*pair) for pair in pairs], axis=1)
         count = len(lefts)
         step = 256
-        length = sum(left.shape[0] * left.shape[1] for left in lefts)
         ins = [
             pl.BlockSpec((left.shape[0], left.shape[1], step), lambda i: (0, 0, i))
             for left in lefts
@@ -370,11 +382,7 @@
             out_shape=jax.ShapeDtypeStruct((rows, wide), BF16),
             input_output_aliases={} if joined is None else {2 * count: 0},
             compiler_params=pltpu.CompilerParams(vmem_limit_bytes=48 * 1024 * 1024),
-            cost_estimate=pl.CostEstimate(
-                flops=2 * length * rows * part,
-                transcendentals=0,
-                bytes_accessed=2 * (length * (rows + part) + rows * part),
-            ),
+            cost_estimate=pl.CostEstimate(flops=0, transcendentals=0, bytes_accessed=1024),
             name="weight_grad",
         )(*operands)
         start += part
@@ -419,23 +427,22 @@
         joined = blocks[0] if len(blocks) == 1 else jnp.concatenate(blocks, axis=1)
         return lax.all_gather(joined, "dp", axis=0, tiled=True)
 
-    packed_in = gathered(
-        image_attention_in.reshape(share, 3 * width), text_attention_in.reshape(share, 3 * width)
-    )
-    packed_mid = gathered(image_attention_out.T, text_attention_out.T, image_hidden_in)
+    image_in = gathered(image_attention_in.reshape(share, 3 * width))
+    image_up = gathered(image_hidden_in)
     image_down = gathered(image_hidden_out.T)
-    weight_in = (packed_in[:, : 3 * width], packed_in[:, 3 * width :])
-    weight_out = (packed_mid[:, :width], packed_mid[:, width : 2 * width])
+    text_in = ring_gather(text_attention_in.reshape(share, 3 * width), group_count)
+    both_out = ring_gather(
+        after(jnp.concatenate([image_attention_out.T, text_attention_out.T], axis=1), text_in),
+        group_count,
+    )
+    weight_in = (image_in, text_in)
+    weight_out = (both_out[:, :width], both_out[:, width:])
 
     alive = (jnp.arange(slots) < group_size[0]).astype(F32)[:, None, None]
     cond_full = condition.astype(F32)
-    group_order = group_rank ^ jnp.arange(group_count)
     activated_low = jax.nn.silu(cond_full).astype(BF16)
-    activated_blocks = [
-        lax.dynamic_slice_in_dim(activated_low, group_order[k] * share, share, 1)
-        for k in range(group_count)
-    ]
-    activated_own = jnp.concatenate(exchange(activated_blocks, group_count, "dp"), axis=0)
+    activated_all = gather_stack(activated_low, group_count, "dp").reshape(-1, model)
+    activated_own = lax.dynamic_slice_in_dim(activated_all, group_rank * share, share, 1)
     all_slots = activated_own.shape[0]
     mod_parts = jnp.concatenate(
         [
@@ -444,7 +451,7 @@
         ],
         axis=1,
     ).reshape(group_count, slots, 12 * width)
-    mod_own = sum(exchange([mod_parts[k] for k in range(group_count)], group_count, "dp"))
+    mod_own = scatter_stack(mod_parts, group_count, "dp")
     modulations = lax.all_gather(
         mod_own.reshape(slots, 2, 6, width), "tensor", axis=3, tiled=True
     )
@@ -453,127 +460,134 @@
     tokens = (image_tokens.astype(F32), text_tokens.astype(F32))
     outgoing = (image_cotangent.astype(F32) * alive, text_cotangent.astype(F32) * alive)
 
-    def image_rows(values):
-        return gather_pieces(values.astype(BF16), size)
-
-    def text_rows(values):
-        return [values.astype(BF16)]
-
-    collect = (image_rows, text_rows)
-
-    def flat(values):
-        return values.reshape(-1, values.shape[-1])
+    def collect(stream, values):
+        values = values.astype(BF16)
+        return [values] if stream else gather_pieces(values, size)
 
     def apply(pieces, weight, weight_dim, low):
         return [
-            dot(flat(piece), weight, 1, weight_dim)
-            .astype(BF16 if low else F32)
-            .reshape(slots, piece.shape[1], -1)
-            for piece in pieces
+            dot(piece, weight, 2, weight_dim).astype(BF16 if low else F32) for piece in pieces
         ]
 
-    def reduced(stream, pieces, weight, weight_dim):
-        if stream == 1:
-            return text_sum(
-                dot(flat(pieces[0]), weight, 1, weight_dim).reshape(slots, text_length, model), size
-            )
-
-        def make_piece(k):
-            return dot(flat(pieces[k]), weight, 1, weight_dim).reshape(slots, image_length, model)
-
-        return scatter_sum(make_piece, size)
+    def reduced(stream, pieces):
+        return text_sum(pieces[0], size) if stream else scatter_sum(pieces, size)
+
+    def scattered(grad):
+        return lax.psum_scatter(grad, "dp", scatter_dimension=0, tiled=True).astype(F32)
 
     first_saved = []
     packed = []
+    down_pieces = []
     for stream in range(2):
         mod = mods[stream]
         normed, inverse = norm_rows(tokens[stream])
         first_in = normed * (1.0 + spread(mod[:, 1])) + spread(mod[:, 0])
-        pieces = collect[stream](first_in)
+        pieces = collect(stream, first_in)
         packed.append(apply(pieces, weight_in[stream], 0, True))
         first_saved.append((normed, inverse, pieces))
+        down = (outgoing[stream] * spread(mod[:, 5])).astype(BF16)
+        down_pieces.append(collect(stream, after(down, pieces)))
     parts = packed[0] + packed[1]
-    down_pieces = [
-        collect[stream](outgoing[stream] * spread(mods[stream][:, 5])) for stream in range(2)
-    ]
-    text_mlp_own = jnp.concatenate([text_hidden_in, text_hidden_out.T], axis=1)
-    parts, down_pieces, text_mlp_own = lax.optimization_barrier((parts, down_pieces, text_mlp_own))
-    packed_text = ring_gather(text_mlp_own, group_count)
-    weight_up = (packed_mid[:, 2 * width :], packed_text[:, :units])
+    packed_text = ring_gather(
+        after(jnp.concatenate([text_hidden_in, text_hidden_out.T], axis=1), parts, both_out),
+        group_count,
+    )
+    weight_up = (image_up, packed_text[:, :units])
     weight_down = (image_down, packed_text[:, units:])
     attended, sums = attend(parts)
+    attended, down_pieces = lax.optimization_barrier((attended, down_pieces))
     attended_parts = (attended[:-1], attended[-1:])
-    outputs = []
-    second_saved = []
-    for stream in range(2):
+
+    middles = [None, None]
+    actives = [None, None]
+    mlp_grads = [None, None]
+    middle_grads = [None, None]
+    branch_grads = [None, None]
+    lows = [None, None]
+    stats = [None, None]
+    upstreams = [None, None]
+
+    def stream_branch(stream):
         mod = mods[stream]
-        branch = reduced(stream, attended_parts[stream], weight_out[stream], 1)
+        branch = reduced(stream, apply(attended_parts[stream], weight_out[stream], 1, False))
         middle = tokens[stream] + spread(mod[:, 2]) * branch
-        normed_two, inverse_two = norm_rows(middle)
-        second_in = normed_two * (1.0 + spread(mod[:, 4])) + spread(mod[:, 3])
-        pieces = collect[stream](second_in)
+        normed, inverse = norm_rows(middle)
+        second_in = normed * (1.0 + spread(mod[:, 4])) + spread(mod[:, 3])
+        middles[stream] = middle
+        return branch, normed, inverse, collect(stream, second_in)
+
+    def stream_back(stream, branch, normed, inverse, pieces):
+        mod = mods[stream]
         hidden = apply(pieces, weight_up[stream], 0, False)
-        active = [gelu_tanh(piece).astype(BF16) for piece in hidden]
-        branch_two = reduced(stream, active, weight_down[stream], 1)
-        result = middle + spread(mod[:, 5]) * branch_two
-        outputs.append((result * alive).astype(BF16))
-        second_saved.append((branch, normed_two, inverse_two, pieces, hidden, active, branch_two))
-
-    def scattered(grad):
-        return lax.psum_scatter(grad, "dp", scatter_dimension=0, tiled=True).astype(F32)
-
-    mlp_grads = []
-    middle_grads = []
-    stats = []
-    upstreams = []
-    out_pairs = []
-    for stream in range(2):
-        mod = mods[stream]
-        branch, normed_two, inverse_two, pieces, hidden, active, branch_two = second_saved[stream]
-        gate_two_grad = jnp.sum(outgoing[stream] * branch_two, axis=1)
+        active = [gelu_tanh(value).astype(BF16) for value in hidden]
         active_grad = apply(down_pieces[stream], weight_down[stream], 0, False)
         hidden_grad = [
             jax.vjp(gelu_tanh, value)[1](grad)[0].astype(BF16)
             for value, grad in zip(hidden, active_grad)
         ]
-        mlp_grads.append(weight_grad([(down_pieces[stream], active), (pieces, hidden_grad)]))
-        second_grad = reduced(stream, hidden_grad, weight_up[stream], 1)
+        products = apply(hidden_grad, weight_up[stream], 1, False)
+        late = after((down_pieces[stream], active, pieces, hidden_grad), products)
+        mlp_grads[stream] = weight_grad([late[:2], late[2:]])
+        second_grad = reduced(stream, products)
         shift_two_grad = jnp.sum(second_grad, axis=1)
-        scale_two_grad = jnp.sum(second_grad * normed_two, axis=1)
+        scale_two_grad = jnp.sum(second_grad * normed, axis=1)
         middle_grad = outgoing[stream] + norm_back(
-            second_grad * (1.0 + spread(mod[:, 4])), normed_two, inverse_two
+            second_grad * (1.0 + spread(mod[:, 4])), normed, inverse
         )
         gate_one_grad = jnp.sum(middle_grad * branch, axis=1)
-        branch_grad = collect[stream](middle_grad * spread(mod[:, 2]))
-        out_pairs.append((branch_grad, attended_parts[stream]))
-        upstreams.extend(apply(branch_grad, weight_out[stream], 0, True))
-        middle_grads.append(middle_grad)
-        stats.append((gate_one_grad, shift_two_grad, scale_two_grad, gate_two_grad))
+        low = (middle_grad * spread(mod[:, 2])).astype(BF16)
+        branch_grads[stream] = collect(stream, low)
+        upstreams[stream] = apply(branch_grads[stream], weight_out[stream], 0, True)
+        middle_grads[stream] = middle_grad
+        actives[stream] = after(active, low)
+        stats[stream] = (gate_one_grad, shift_two_grad, scale_two_grad)
+
+    image_state = stream_branch(0)
+    text_state = stream_branch(1)
+    stream_back(0, *image_state)
+    stream_back(1, *text_state)
     image_mlp = scattered(mlp_grads[0])
-    text_grad, upstreams = lax.optimization_barrier((mlp_grads[1], upstreams))
-    text_ring = ring_scatter(text_grad, group_count)
+    text_ring = ring_scatter(mlp_grads[1], group_count)
     text_hop = next(text_ring)
-    packed_grads = attend_back(parts, upstreams, sums)
+    upstreams, text_hop = lax.optimization_barrier((upstreams, text_hop))
+    text_hop = text_ring.send(text_hop)
+
+    packed_grads = attend_back(parts, upstreams[0] + upstreams[1], sums)
     packed_grads, text_hop = lax.optimization_barrier((packed_grads, text_hop))
     text_hop = text_ring.send(text_hop)
-    late_grads, image_mlp = lax.optimization_barrier((packed_grads, image_mlp))
-    packed_grads = (packed_grads[:-1], packed_grads[-1:])
-    late_grads = (late_grads[:-1], late_grads[-1:])
-    in_pairs = [(first_saved[stream][2], late_grads[stream]) for stream in range(2)]
-    attention_grad = weight_grad(in_pairs + out_pairs)
-    for _ in range(group_count // 2 - 3):
+    image_in_grad = weight_grad([(first_saved[0][2], packed_grads[:-1])])
+    image_in_sum = scattered(image_in_grad)
+    attention_grad = weight_grad(
+        [
+            (first_saved[1][2], packed_grads[-1:]),
+            (branch_grads[0], attended_parts[0]),
+            (branch_grads[1], attended_parts[1]),
+        ]
+    )
+    packed_grads = after(packed_grads, image_in_grad, attention_grad)
+    for _ in range(group_count // 2 - 2):
         attention_grad, text_hop = lax.optimization_barrier((attention_grad, text_hop))
         text_hop = text_ring.send(text_hop)
-    attention_sum = scattered(attention_grad)
+    text_mlp = text_hop
+    attention_ring = ring_scatter(attention_grad, group_count)
+    attention_hop = next(attention_ring)
+    packed_grads = (packed_grads[:-1], packed_grads[-1:])
+    outputs = [None, None]
     input_grads = [None, None]
     mod_grads = [None, None]
     for stream in (1, 0):
         mod = mods[stream]
-        normed, inverse, pieces = first_saved[stream]
-        gate_one_grad, shift_two_grad, scale_two_grad, gate_two_grad = stats[stream]
-        first_grad = reduced(stream, packed_grads[stream], weight_in[stream], 1)
-        first_grad, text_hop = lax.optimization_barrier((first_grad, text_hop))
-        text_hop = text_ring.send(text_hop)
+        normed, inverse, _ = first_saved[stream]
+        gate_one_grad, shift_two_grad, scale_two_grad = stats[stream]
+        branch_two = reduced(stream, apply(actives[stream], weight_down[stream], 1, False))
+        result = middles[stream] + spread(mod[:, 5]) * branch_two
+        outputs[stream] = (result * alive).astype(BF16)
+        gate_two_grad = jnp.sum(outgoing[stream] * branch_two, axis=1)
+        first_grad = reduced(stream, apply(packed_grads[stream], weight_in[stream], 1, False))
+        first_grad, attention_hop = lax.optimization_barrier((first_grad, attention_hop))
+        if stream == 0:
+            first_grad, image_mlp = lax.optimization_barrier((first_grad, image_mlp))
+        attention_hop = attention_ring.send(attention_hop)
         shift_one_grad = jnp.sum(first_grad, axis=1)
         scale_one_grad = jnp.sum(first_grad * normed, axis=1)
         input_grads[stream] = middle_grads[stream] + norm_back(
@@ -590,21 +604,20 @@
             ],
             axis=1,
         )
-    text_mlp = text_hop
-
-    image_share = sum(
-        exchange(
-            [
-                lax.dynamic_slice_in_dim(mod_grads[0], (tensor_rank ^ k) * width, width, 2)
-                for k in range(size)
-            ],
-            size,
-            "tensor",
-        )
-    )
+    for _ in range(group_count // 2 - 2):
+        attention_hop = attention_ring.send(attention_hop)
+    attention_sum = attention_hop
+
+    image_blocks = jnp.stack(
+        [
+            lax.dynamic_slice_in_dim(mod_grads[0], (tensor_rank ^ k) * width, width, 2)
+            for k in range(size)
+        ]
+    )
+    image_share = scatter_stack(image_blocks, size, "tensor")
     text_share = lax.dynamic_slice_in_dim(mod_grads[1], tensor_rank * width, width, 2)
     share_low = jnp.stack([image_share, text_share], axis=1).astype(BF16)
-    share_all = jnp.concatenate(gather_pieces(share_low, group_count, "dp"), axis=0)
+    share_all = gather_stack(share_low, group_count, "dp").reshape(all_slots, 2, 6, width)
     image_all = share_all[:, 0].reshape(all_slots, 6 * width)
     text_all = share_all[:, 1].reshape(all_slots, 6 * width)
     image_ada = dot(activated_own, image_all, 0, 0).reshape(share, 6, width)
@@ -613,9 +626,9 @@
         text_all, text_modulation.reshape(share, 6 * width), 1, 1
     )
     activated_part = sum_all(activated_part, size, "tensor").reshape(group_count, slots, share)
-    activated_rows = jnp.stack(
-        exchange([activated_part[k] for k in range(group_count)], group_count, "dp")
-    )
+    activated_rows = gather_stack(activated_part, group_count, "dp")
+    activated_rows = jnp.stack([activated_rows[k, k] for k in range(group_count)])
+    group_order = group_rank ^ jnp.arange(group_count)
     activated_grad = jnp.concatenate(
         [
             lax.dynamic_index_in_dim(activated_rows, group_order[k], 0, keepdims=False)
@@ -632,13 +645,13 @@
         input_grads[1],
         condition_gradient,
         image_ada,
-        attention_sum[:, : 3 * width].reshape(share, 3, width),
-        attention_sum[:, 6 * width : 7 * width].T,
+        image_in_sum.reshape(share, 3, width),
+        attention_sum[:, 3 * width : 4 * width].T,
         image_mlp[:, units:],
         image_mlp[:, :units].T,
         text_ada,
-        attention_sum[:, 3 * width : 6 * width].reshape(share, 3, width),
-        attention_sum[:, 7 * width :].T,
+        attention_sum[:, : 3 * width].reshape(share, 3, width),
+        attention_sum[:, 4 * width :].T,
         text_mlp[:, units:],
         text_mlp[:, :units].T,
     )

time: 1030 us -> 1000 us (0.971)
  matrix products: 180 us -> 146 us
  starting transfers between devices: 90.4 us -> 111 us
  other arithmetic: 69.5 us -> 79.9 us
    ppermute x16 -> x40, waiting for transfers between devices: 106 us -> 230 us  [ring_step(): return lax.ppermute(value, 'dp', hops)]
    ppermute x65 -> x48, waiting for transfers between devices: 221 us -> 136 us  [swap(): return lax.ppermute(value, axis, [(i, i ^ bit) for i in range(size)])]
    all_gather x3, waiting for transfers between devices: 49.2 us -> 0.02 us  [gathered(): return lax.all_gather(joined, 'dp', axis=0, tiled=True)]
    ppermute x16 -> x40, starting transfers between devices: 26.1 us -> 71.9 us  [ring_step(): return lax.ppermute(value, 'dp', hops)]
    dot_general x46, matrix products: 180 us -> 146 us  [dot(): lax.dot_general(left, right, (((left_dim,), (right_dim,)), ((), ())), pre...]
    ppermute x65 -> x48, starting transfers between devices: 63.7 us -> 38.5 us  [swap(): return lax.ppermute(value, axis, [(i, i ^ bit) for i in range(size)])]
  transfers between devices with their start and end apart: 86 -> 93, of which waited for: 28 -> 39; matrix products, arithmetic and copies ran while one was open for 29% -> 28% of each run, Pallas kernels for 15% -> 15%
where the time goes in v2:
time: 1000 us; the launch traced here: 995 us
  waiting for transfers between devices  367 us (37%)
  Pallas kernels  181 us (18%)
  matrix products  146 us (15%)
  starting transfers between devices  111 us (11%)
  other arithmetic  79.9 us (8%)
  local copies, waits for them, and re-layouts  71.2 us (7%)
  between operations  32.4 us (3%)
    ppermute x40, waiting for transfers between devices, ring_step(): return lax.ppermute(value, 'dp', hops)  230 us
    dot_general x46, matrix products, dot(): lax.dot_general(left, right, (((left_dim,), (right_dim,)), ((), ())), pre...  146 us
    ppermute x48, waiting for transfers between devices, swap(): return lax.ppermute(value, axis, [(i, i ^ bit) for i in range(size)])  136 us
    ppermute x40, starting transfers between devices, ring_step(): return lax.ppermute(value, 'dp', hops)  71.9 us
    pallas_call x8, Pallas kernels, weight_grad(): pl.pallas_call(functools.partial(rows_kernel, count), grid=(rows // step,...  68.3 us
    pallas_call x1, Pallas kernels, attend_back(): pl.pallas_call(functools.partial(attend_back_kernel, count, groups), grid...  58.1 us
    pallas_call x1, Pallas kernels, attend(): pl.pallas_call(functools.partial(attend_kernel, count), grid=(slots, grou...  54.8 us
    ppermute x48, starting transfers between devices, swap(): return lax.ppermute(value, axis, [(i, i ^ bit) for i in range(size)])  38.5 us
  transfers between devices with their start and end apart: 93, of which 39 were waited for; matrix products, arithmetic and copies ran while one was open for 28% of the time, Pallas kernels for 15%

profile of v2, /device:TPU:0, one launch (start us, length us, event | category | flops | bytes accessed | tf_op | source)
XLA Modules:
  0.0 994.7 jit_solution(2580848615440063162)
XLA Ops:
  47.4 9.0 collective-permute-done.3
  59.2 6.7 collective-permute-done.4
  85.5 29.3 %collective-permute-done.7.refs_2_ = bf16[2,256,1536]{2,1,0:T(8,128)(2,1)} collective-permute-done((bf16[2,256,1536]{2,1,0:T(8,128)(2,1)}, bf16[2,256,1536]{2,1,0:T(8,128)(2,1)}, u32[]{:S(2)}, u32[]{:S(2)}) %collective-permute-start.7) | collective-permute-done | bytes 1572896 | tf_op jit(solution)/shard_map/ppermute | solution.py:43
  122.1 14.9 %collective-permute-done.13 = bf16[192,1152]{1,0:T(8,128)(2,1)S(1)} collective-permute-done((bf16[192,1152]{1,0:T(8,128)(2,1)S(1)}, bf16[192,1152]{1,0:T(8,128)(2,1)S(1)}, u32[]{:S(2)}, u32[]{:S(2)}) %collective-permute-start.13) | collective-permute-done | bytes 442400 | tf_op jit(solution)/shard_map/ppermute | solution.py:113
  137.1 15.8 %collective-permute-start.15 = (bf16[192,512]{1,0:T(8,128)(2,1)S(1)}, bf16[192,512]{1,0:T(8,128)(2,1)S(1)}, u32[]{:S(2)}, u32[]{:S(2)}) collective-permute-start(bf16[192,512]{1,0:T(8,128)(2,1)S(1)} %slice.277), channel_id=1, source_target_pairs={{0,8},{8,16},{16,24},{24,28},{28,20},{20,12},{12,4},{4,0},{1,9},{9... | collective-permute-start | bytes 589832 | tf_op jit(solution)/shard_map/ppermute | solution.py:113
  158.6 15.2 %collective-permute-done.16 = bf16[192,640]{1,0:T(8,128)(2,1)S(1)} collective-permute-done((bf16[192,640]{1,0:T(8,128)(2,1)S(1)}, bf16[192,640]{1,0:T(8,128)(2,1)S(1)}, u32[]{:S(2)}, u32[]{:S(2)}) %collective-permute-start.16) | collective-permute-done | bytes 245792 | tf_op jit(solution)/shard_map/ppermute | solution.py:113
  206.0 5.8 collective-permute-done.18.refs_2_
  229.0 54.8 %attend.1 = (bf16[2,256,384]{2,1,0:T(8,128)(2,1)S(1)}, bf16[2,256,384]{2,1,0:T(8,128)(2,1)S(1)}, bf16[2,256,384]{2,1,0:T(8,128)(2,1)S(1)}, bf16[2,256,384]{2,1,0...) custom-call(bf16[2,256,1152]{2,1,0:T(8,128)(2,1)S(1)} %fusion.116.re, ...), custom_call_target="tpu_custom_call" | custom-call | flops 17051860992 | bytes 7237632 | tf_op jit(solution)/shard_map/attend/pallas_call | solution.py:296
  304.5 34.1 %collective-permute-done.44 = bf16[192,3072]{1,0:T(8,128)(2,1)S(1)} collective-permute-done((bf16[192,3072]{1,0:T(8,128)(2,1)}, bf16[192,3072]{1,0:T(8,128)(2,1)S(1)}, u32[]{:S(2)}, u32[]{:S(2)}) %collective-permute-start.44) | collective-permute-done | bytes 1179680 | tf_op jit(solution)/shard_map/ppermute | solution.py:113
  345.9 46.3 %collective-permute-done.46 = bf16[192,3072]{1,0:T(8,128)(2,1)S(1)} collective-permute-done((bf16[192,3072]{1,0:T(8,128)(2,1)S(1)}, bf16[192,3072]{1,0:T(8,128)(2,1)S(1)}, u32[]{:S(2)}, u32[]{:S(2)}) %collective-permute-start.46) | collective-permute-done | bytes 1179680 | tf_op jit(solution)/shard_map/ppermute | solution.py:113
  393.1 10.8 %collective-permute-start.48 = (bf16[192,1536]{1,0:T(8,128)(2,1)}, bf16[192,1536]{1,0:T(8,128)(2,1)}, u32[]{:S(2)}, u32[]{:S(2)}) collective-permute-start(bf16[192,1536]{1,0:T(8,128)(2,1)} %slice.290), channel_id=1, source_target_pairs={{0,8},{8,16},{16,24},{24,28},{28,20},{20,12},{12,4},{4,0},{1,9},{9... | collective-permute-start | bytes 1769480 | tf_op jit(solution)/shard_map/ppermute | solution.py:113
  416.8 7.0 multiply_convert_fusion.5
  423.8 7.0 fusion.86.refs_4_
  451.1 5.7 multiply_convert_fusion.4
  457.1 5.6 fusion.93.refs_5_
  466.9 5.6 multiply_convert_fusion.3
  478.6 6.1 fusion.107.refs_7_
  503.8 15.1 %weight_grad.14.refs_8_ = bf16[1536,3072]{1,0:T(8,128)(2,1)} custom-call(bf16[2,256,1536]{2,1,0:T(8,128)(2,1)S(1)} %multiply_convert_fusion.6.refs_0_, bf16[2,256,1536]{2,1,0:T(8,128)(2,1)} %collective-permute-done.17.refs_1_, bf16[2,256,1536]{2,1,0:T(8,128)(2,1)S(1)} %copy-done.8, bf16[2,256,1536]{2,1,0:T(8,128)(2,1)} %collective-permute-done.19.refs_3_, ...), custom_call_target="tpu_custom_call" | custom-call | bytes 1024 | tf_op jit(solution)/shard_map/weight_grad/pallas_call | solution.py:377
  518.9 15.1 %weight_grad.15 = bf16[1536,3072]{1,0:T(8,128)(2,1)} custom-call(bf16[2,256,1536]{2,1,0:T(8,128)(2,1)S(1)} %add_convert_fusion.2.refs_0_, bf16[2,256,1536]{2,1,0:T(8,128)(2,1)} %collective-permute-done.31.refs_1_, bf16[2,256,1536]{2,1,0:T(8,128)(2,1)} %collective-permute-done.32.refs_2_, ...), custom_call_target="tpu_custom_call", output_to_operand_aliasing={{}: (8, {})} | custom-call | bytes 1024 | tf_op jit(solution)/shard_map/weight_grad/pallas_call | solution.py:377
  587.9 17.5 %collective-permute-done.53 = bf16[2,154,1536]{2,0,1:T(2,128)(2,1)} collective-permute-done((bf16[2,154,1536]{2,0,1:T(2,128)(2,1)}, bf16[2,154,1536]{2,0,1:T(2,128)(2,1)}, u32[]{:S(2)}, u32[]{:S(2)}) %collective-permute-start.53) | collective-permute-done | bytes 946208 | tf_op jit(solution)/shard_map/ppermute | solution.py:43
  629.0 25.0 %collective-permute-done.55.refs_2_ = bf16[2,256,1536]{2,1,0:T(8,128)(2,1)S(1)} collective-permute-done((bf16[2,256,1536]{2,1,0:T(8,128)(2,1)S(1)}, bf16[2,256,1536]{2,1,0:T(8,128)(2,1)S(1)}, u32[]{:S(2)}, u32[]{:S(2)}) %collective-permute-start.55) | collective-permute-done | bytes 1572896 | tf_op jit(solution)/shard_map/ppermute | solution.py:43
  668.0 58.1 %attend_back.1 = (bf16[2,256,1152]{2,1,0:T(8,128)(2,1)S(1)}, bf16[2,256,1152]{2,1,0:T(8,128)(2,1)S(1)}, bf16[2,256,1152]{2,1,0:T(8,128)(2,1)}, bf16[2,256,1152]{2,1,0:T(8,128)(2,1)}, bf16[2,154,1152]{2,1,0:T(8,128)(2,1)S(1)}) custom-call(bf16[2,256,1152]{2,1,0:T(8,128)(2,1)} %copy-done.32, bf16[2,256,1152]{2,1,0:T(8,128)(2,1)} %copy-done.33, ...), custom_call_target="tpu_custom_call" | custom-call | flops 42629652480 | bytes 12665856 | tf_op jit(solution)/shard_map/attend_back/pallas_call | solution.py:323
  726.2 6.1 multiply_reduce_fusion
  737.2 7.3 weight_grad.12.refs_2_
  748.3 11.5 %weight_grad.10 = bf16[1536,1152]{1,0:T(8,128)(2,1)} custom-call(bf16[2,256,1536]{2,1,0:T(8,128)(2,1)} %fusion.73.refs_0_, bf16[2,256,1536]{2,1,0:T(8,128)(2,1)} %copy-done.85, bf16[2,256,1536]{2,1,0:T(8,128)(2,1)} %collective-permute-done.7.refs_2_, bf16[2,256,1536]{2,1,0:T(8,128)(2,1)} %copy-done.87, bf16[2,256,1152]{2,1,0:T(8,128)(2,1)S(1)} %get-tuple-element.152.refs_4_, ...), custom_call_target="tpu_custom_call" | custom-call | bytes 1024 | tf_op jit(solution)/shard_map/weight_grad/pallas_call | solution.py:377
  780.1 17.1 %collective-permute-done.64 = bf16[192,3072]{1,0:T(8,128)(2,1)} collective-permute-done((bf16[192,3072]{1,0:T(8,128)(2,1)}, bf16[192,3072]{1,0:T(8,128)(2,1)}, u32[]{:S(2)}, u32[]{:S(2)}) %collective-permute-start.64) | collective-permute-done | bytes 1179680 | tf_op jit(solution)/shard_map/ppermute | solution.py:113
  816.8 27.0 %collective-permute-done.66 = bf16[192,3072]{1,0:T(8,128)(2,1)S(1)} collective-permute-done((bf16[192,3072]{1,0:T(8,128)(2,1)S(1)}, bf16[192,3072]{1,0:T(8,128)(2,1)S(1)}, u32[]{:S(2)}, u32[]{:S(2)}) %collective-permute-start.66) | collective-permute-done | bytes 1179680 | tf_op jit(solution)/shard_map/ppermute | solution.py:113
  851.7 10.6 %collective-permute-done.69 = bf16[2,154,1536]{2,0,1:T(2,128)(2,1)S(1)} collective-permute-done((bf16[2,154,1536]{2,0,1:T(2,128)(2,1)S(1)}, bf16[2,154,1536]{2,0,1:T(2,128)(2,1)S(1)}, u32[]{:S(2)}, u32[]{:S(2)}) %collective-permute-start.69) | collective-permute-done | bytes 946208 | tf_op jit(solution)/shard_map/ppermute | solution.py:43
  873.1 16.5 %collective-permute-done.72 = bf16[192,1920]{1,0:T(8,128)(2,1)S(1)} collective-permute-done((bf16[192,1920]{1,0:T(8,128)(2,1)S(1)}, bf16[192,1920]{1,0:T(8,128)(2,1)S(1)}, u32[]{:S(2)}, u32[]{:S(2)}) %collective-permute-start.72) | collective-permute-done | bytes 737312 | tf_op jit(solution)/shard_map/ppermute | solution.py:113
  892.6 13.0 %collective-permute-done.84 = bf16[192,1920]{1,0:T(8,128)(2,1)S(1)} collective-permute-done((bf16[192,1920]{1,0:T(8,128)(2,1)S(1)}, bf16[192,1920]{1,0:T(8,128)(2,1)S(1)}, u32[]{:S(2)}, u32[]{:S(2)}) %collective-permute-start.84) | collective-permute-done | bytes 737312 | tf_op jit(solution)/shard_map/ppermute | solution.py:113
  909.8 12.8 %collective-permute-done.86 = bf16[192,1920]{1,0:T(8,128)(2,1)S(1)} collective-permute-done((bf16[192,1920]{1,0:T(8,128)(2,1)S(1)}, bf16[192,1920]{1,0:T(8,128)(2,1)S(1)}, u32[]{:S(2)}, u32[]{:S(2)}) %collective-permute-start.86) | collective-permute-done | bytes 737312 | tf_op jit(solution)/shard_map/ppermute | solution.py:113
  928.4 7.4 collective-permute-done.87
  (688 shorter events, 422.4 us)
Async XLA Ops:
  7.2 204.6 %all-gather.4.cloned.1.call-start = ((), (), s32[]{:S(2)}) async-start(), calls=%async_computation.2 | async-start | bytes 3981312 | tf_op jit(solution)/shard_map/all_gather | solution.py:428
  9.2 407.6 %all-gather.6.cloned.1.call-start = ((), (), s32[]{:S(2)}) async-start(), calls=%async_computation.3 | async-start | bytes 5308416 | tf_op jit(solution)/shard_map/all_gather | solution.py:428
  11.1 72.4 %collective-permute-start.9 = (bf16[192,1152]{1,0:T(8,128)(2,1)}, bf16[192,1152]{1,0:T(8,128)(2,1)}, u32[]{:S(2)}, u32[]{:S(2)}) collective-permute-start(bf16[192,1152]{1,0:T(8,128)(2,1)} %bitcast.94), channel_id=1, source_target_pairs={{0,8},{8,16},{16,24},{24,28},{28,20},{20,12},{12,4},{4,0},{1,9},{9... | collective-permute-start | bytes 1327112 | tf_op jit(solution)/shard_map/ppermute | solution.py:113
  14.1 69.6 %collective-permute-start.10 = (bf16[192,1152]{1,0:T(8,128)(2,1)}, bf16[192,1152]{1,0:T(8,128)(2,1)}, u32[]{:S(2)}, u32[]{:S(2)}) collective-permute-start(bf16[192,1152]{1,0:T(8,128)(2,1)} %bitcast.94), channel_id=1, source_target_pairs={{0,4},{8,0},{16,8},{24,16},{28,24},{20,28},{12,20},{4,12},{1,5},{9... | collective-permute-start | bytes 1327112 | tf_op jit(solution)/shard_map/ppermute | solution.py:113
  16.8 407.0 %all-gather.8.cloned.1.call-start = ((), (), s32[]{:S(2)}) async-start(), calls=%async_computation.4 | async-start | bytes 5308416 | tf_op jit(solution)/shard_map/all_gather | solution.py:428
  79.5 97.0 %collective-permute-start.6 = (bf16[2,256,1536]{2,1,0:T(8,128)(2,1)}, bf16[2,256,1536]{2,1,0:T(8,128)(2,1)S(1)}, u32[]{:S(2)}, u32[]{:S(2)}) collective-permute-start(bf16[2,256,1536]{2,1,0:T(8,128)(2,1)} %fusion.73.refs_0_), channel_id=1, source_target_pairs={{0,1},{1,0},{2,3},{3,2},{4,5},{5,4},{6,7},{7,6},{8,9},{9,8},{10,11... | collective-permute-start | bytes 4718600 | tf_op jit(solution)/shard_map/ppermute | solution.py:43
  114.8 61.6 %collective-permute-start.8 = (bf16[2,256,1536]{2,1,0:T(8,128)(2,1)}, bf16[2,256,1536]{2,1,0:T(8,128)(2,1)S(1)}, u32[]{:S(2)}, u32[]{:S(2)}) collective-permute-start(bf16[2,256,1536]{2,1,0:T(8,128)(2,1)} %collective-permute-done.7.refs_2_), channel_id=1, source_target_pairs={{0,1},{1,0},{2,3},{3,2},{4,5},{5,4},{6,7},{7,6},{8,9},{9,8},{10,11... | collective-permute-start | bytes 4718600 | tf_op jit(solution)/shard_map/ppermute | solution.py:43
  205.9 77.9 %collective-permute-start.17 = (bf16[2,256,1536]{2,1,0:T(8,128)(2,1)S(1)}, bf16[2,256,1536]{2,1,0:T(8,128)(2,1)}, u32[]{:S(2)}, u32[]{:S(2)}) collective-permute-start(bf16[2,256,1536]{2,1,0:T(8,128)(2,1)S(1)} %multiply_convert_fusion.6.refs_0_), channel_id=1, source_target_pairs={{0,1},{1,0},{2,3},{3,2},{4,5},{5,4},{6,7},{7,6},{8,9},{9,8},{10,11... | collective-permute-start | bytes 4718600 | tf_op jit(solution)/shard_map/ppermute | solution.py:43
  211.8 72.0 %collective-permute-start.19 = (bf16[2,256,1536]{2,1,0:T(8,128)(2,1)S(1)}, bf16[2,256,1536]{2,1,0:T(8,128)(2,1)}, u32[]{:S(2)}, u32[]{:S(2)}) collective-permute-start(bf16[2,256,1536]{2,1,0:T(8,128)(2,1)S(1)} %collective-permute-done.18.refs_2_), channel_id=1, source_target_pairs={{0,1},{1,0},{2,3},{3,2},{4,5},{5,4},{6,7},{7,6},{8,9},{9,8},{10,11... | collective-permute-start | bytes 4718600 | tf_op jit(solution)/shard_map/ppermute | solution.py:43
  226.7 66.7 %collective-permute-start.42 = (bf16[192,3072]{1,0:T(8,128)(2,1)}, bf16[192,3072]{1,0:T(8,128)(2,1)}, u32[]{:S(2)}, u32[]{:S(2)}) collective-permute-start(bf16[192,3072]{1,0:T(8,128)(2,1)} %pad_maximum_fusion), channel_id=1, source_target_pairs={{0,8},{8,16},{16,24},{24,28},{28,20},{20,12},{12,4},{4,0},{1,9},{9... | collective-permute-start | bytes 3538952 | tf_op jit(solution)/shard_map/ppermute | solution.py:113
  227.0 66.7 %collective-permute-start.43 = (bf16[192,3072]{1,0:T(8,128)(2,1)}, bf16[192,3072]{1,0:T(8,128)(2,1)}, u32[]{:S(2)}, u32[]{:S(2)}) collective-permute-start(bf16[192,3072]{1,0:T(8,128)(2,1)} %pad_maximum_fusion), channel_id=1, source_target_pairs={{0,4},{8,0},{16,8},{24,16},{28,24},{20,28},{12,20},{4,12},{1,5},{9... | collective-permute-start | bytes 3538952 | tf_op jit(solution)/shard_map/ppermute | solution.py:113
  287.4 648.7 %reduce-scatter.3.cloned.1.call-start = ((), (), s32[]{:S(2)}) async-start(), calls=%async_computation.5 | async-start | bytes 10616832 | tf_op jit(solution)/shard_map/reduce_scatter | solution.py:476
  293.3 115.5 %collective-permute-start.28 = (bf16[2,256,1536]{2,1,0:T(8,128)(2,1)S(1)}, bf16[2,256,1536]{2,1,0:T(8,128)(2,1)S(1)}, u32[]{:S(2)}, u32[]{:S(2)}) collective-permute-start(bf16[2,256,1536]{2,1,0:T(8,128)(2,1)S(1)} %convolution_convert_fusion.1), channel_id=1, source_target_pairs={{0,1},{1,0},{2,3},{3,2},{4,5},{5,4},{6,7},{7,6},{8,9},{9,8},{10,11... | collective-permute-start | bytes 4718600 | tf_op jit(solution)/shard_map/ppermute | solution.py:43
  293.4 45.2 %collective-permute-start.44 = (bf16[192,3072]{1,0:T(8,128)(2,1)}, bf16[192,3072]{1,0:T(8,128)(2,1)S(1)}, u32[]{:S(2)}, u32[]{:S(2)}) collective-permute-start(bf16[192,3072]{1,0:T(8,128)(2,1)} %collective-permute-done.42), channel_id=1, source_target_pairs={{0,8},{8,16},{16,24},{24,28},{28,20},{20,12},{12,4},{4,0},{1,9},{9... | collective-permute-start | bytes 3538952 | tf_op jit(solution)/shard_map/ppermute | solution.py:113
  293.7 47.2 %collective-permute-start.45 = (bf16[192,3072]{1,0:T(8,128)(2,1)}, bf16[192,3072]{1,0:T(8,128)(2,1)S(1)}, u32[]{:S(2)}, u32[]{:S(2)}) collective-permute-start(bf16[192,3072]{1,0:T(8,128)(2,1)} %collective-permute-done.43), channel_id=1, source_target_pairs={{0,4},{8,0},{16,8},{24,16},{28,24},{20,28},{12,20},{4,12},{1,5},{9... | collective-permute-start | bytes 3538952 | tf_op jit(solution)/shard_map/ppermute | solution.py:113
  304.1 104.7 %collective-permute-start.30 = (bf16[2,256,1536]{2,1,0:T(8,128)(2,1)S(1)}, bf16[2,256,1536]{2,1,0:T(8,128)(2,1)S(1)}, u32[]{:S(2)}, u32[]{:S(2)}) collective-permute-start(bf16[2,256,1536]{2,1,0:T(8,128)(2,1)S(1)} %fusion.137), channel_id=1, source_target_pairs={{0,2},{1,3},{2,0},{3,1},{4,6},{5,7},{6,4},{7,5},{8,10},{9,11},{10,... | collective-permute-start | bytes 4718600 | tf_op jit(solution)/shard_map/ppermute | solution.py:43
  338.5 53.7 %collective-permute-start.46 = (bf16[192,3072]{1,0:T(8,128)(2,1)S(1)}, bf16[192,3072]{1,0:T(8,128)(2,1)S(1)}, u32[]{:S(2)}, u32[]{:S(2)}) collective-permute-start(bf16[192,3072]{1,0:T(8,128)(2,1)S(1)} %collective-permute-done.44), channel_id=1, source_target_pairs={{0,8},{8,16},{16,24},{24,28},{28,20},{20,12},{12,4},{4,0},{1,9},{9... | collective-permute-start | bytes 3538952 | tf_op jit(solution)/shard_map/ppermute | solution.py:113
  340.9 64.5 %collective-permute-start.47 = (bf16[192,3072]{1,0:T(8,128)(2,1)S(1)}, bf16[192,3072]{1,0:T(8,128)(2,1)S(1)}, u32[]{:S(2)}, u32[]{:S(2)}) collective-permute-start(bf16[192,3072]{1,0:T(8,128)(2,1)S(1)} %collective-permute-done.45), channel_id=1, source_target_pairs={{0,4},{8,0},{16,8},{24,16},{28,24},{20,28},{12,20},{4,12},{1,5},{9... | collective-permute-start | bytes 3538952 | tf_op jit(solution)/shard_map/ppermute | solution.py:113
  534.1 411.6 %reduce-scatter.5.cloned.1.call-start = ((), (), s32[]{:S(2)}) async-start(), calls=%async_computation.6 | async-start | bytes 3981312 | tf_op jit(solution)/shard_map/reduce_scatter | solution.py:476
  548.0 61.8 %collective-permute-start.34 = (bf16[2,256,1536]{2,1,0:T(8,128)(2,1)}, bf16[2,256,1536]{2,1,0:T(8,128)(2,1)}, u32[]{:S(2)}, u32[]{:S(2)}) collective-permute-start(bf16[2,256,1536]{2,1,0:T(8,128)(2,1)} %fusion.20), channel_id=1, source_target_pairs={{0,1},{1,0},{2,3},{3,2},{4,5},{5,4},{6,7},{7,6},{8,9},{9,8},{10,11... | collective-permute-start | bytes 4718600 | tf_op jit(solution)/shard_map/ppermute | solution.py:43
  548.4 61.3 %collective-permute-start.36 = (bf16[2,256,1536]{2,1,0:T(8,128)(2,1)}, bf16[2,256,1536]{2,1,0:T(8,128)(2,1)}, u32[]{:S(2)}, u32[]{:S(2)}) collective-permute-start(bf16[2,256,1536]{2,1,0:T(8,128)(2,1)} %add_convert_fusion.1), channel_id=1, source_target_pairs={{0,2},{1,3},{2,0},{3,1},{4,6},{5,7},{6,4},{7,5},{8,10},{9,11},{10,... | collective-permute-start | bytes 4718600 | tf_op jit(solution)/shard_map/ppermute | solution.py:43
  556.9 48.5 %collective-permute-start.53 = (bf16[2,154,1536]{2,0,1:T(2,128)(2,1)}, bf16[2,154,1536]{2,0,1:T(2,128)(2,1)}, u32[]{:S(2)}, u32[]{:S(2)}) collective-permute-start(bf16[2,154,1536]{2,0,1:T(2,128)(2,1)} %copy.83), channel_id=1, source_target_pairs={{0,2},{1,3},{2,0},{3,1},{4,6},{5,7},{6,4},{7,5},{8,10},{9,11},{10,... | collective-permute-start | bytes 2838536 | tf_op jit(solution)/shard_map/ppermute | solution.py:43
  585.1 77.7 %collective-permute-start.57 = (bf16[192,1536]{1,0:T(8,128)(2,1)S(1)}, bf16[192,1536]{1,0:T(8,128)(2,1)S(1)}, u32[]{:S(2)}, u32[]{:S(2)}) collective-permute-start(bf16[192,1536]{1,0:T(8,128)(2,1)S(1)} %get-tuple-element.284), channel_id=1, source_target_pairs={{0,8},{8,16},{16,24},{24,28},{28,20},{20,12},{12,4},{4,0},{1,9},{9... | collective-permute-start | bytes 1769480 | tf_op jit(solution)/shard_map/ppermute | solution.py:113
  585.2 77.6 %collective-permute-start.58 = (bf16[192,1536]{1,0:T(8,128)(2,1)S(1)}, bf16[192,1536]{1,0:T(8,128)(2,1)S(1)}, u32[]{:S(2)}, u32[]{:S(2)}) collective-permute-start(bf16[192,1536]{1,0:T(8,128)(2,1)S(1)} %get-tuple-element.283), channel_id=1, source_target_pairs={{0,4},{8,0},{16,8},{24,16},{28,24},{20,28},{12,20},{4,12},{1,5},{9... | collective-permute-start | bytes 1769480 | tf_op jit(solution)/shard_map/ppermute | solution.py:113
  617.1 43.2 %collective-permute-start.54 = (bf16[2,256,1536]{2,1,0:T(8,128)(2,1)S(1)}, bf16[2,256,1536]{2,1,0:T(8,128)(2,1)S(1)}, u32[]{:S(2)}, u32[]{:S(2)}) collective-permute-start(bf16[2,256,1536]{2,1,0:T(8,128)(2,1)S(1)} %multiply_convert_fusion.1.refs_0_), channel_id=1, source_target_pairs={{0,1},{1,0},{2,3},{3,2},{4,5},{5,4},{6,7},{7,6},{8,9},{9,8},{10,11... | collective-permute-start | bytes 4718600 | tf_op jit(solution)/shard_map/ppermute | solution.py:43
  656.0 70.2 %collective-permute-start.37 = (bf16[2,256,1536]{2,1,0:T(8,128)(2,1)}, bf16[2,256,1536]{2,1,0:T(8,128)(2,1)}, u32[]{:S(2)}, u32[]{:S(2)}) collective-permute-start(bf16[2,256,1536]{2,1,0:T(8,128)(2,1)} %fusion.138), channel_id=1, source_target_pairs={{0,1},{1,0},{2,3},{3,2},{4,5},{5,4},{6,7},{7,6},{8,9},{9,8},{10,11... | collective-permute-start | bytes 4718600 | tf_op jit(solution)/shard_map/ppermute | solution.py:43
  660.3 65.9 %collective-permute-start.39 = (bf16[2,256,1536]{2,1,0:T(8,128)(2,1)}, bf16[2,256,1536]{2,1,0:T(8,128)(2,1)}, u32[]{:S(2)}, u32[]{:S(2)}) collective-permute-start(bf16[2,256,1536]{2,1,0:T(8,128)(2,1)} %add_convert_fusion), channel_id=1, source_target_pairs={{0,2},{1,3},{2,0},{3,1},{4,6},{5,7},{6,4},{7,5},{8,10},{9,11},{10,... | collective-permute-start | bytes 4718600 | tf_op jit(solution)/shard_map/ppermute | solution.py:43
  665.9 66.3 %collective-permute-start.59 = (bf16[192,3072]{1,0:T(8,128)(2,1)}, bf16[192,3072]{1,0:T(8,128)(2,1)}, u32[]{:S(2)}, u32[]{:S(2)}) collective-permute-start(bf16[192,3072]{1,0:T(8,128)(2,1)} %get-tuple-element.282), channel_id=1, source_target_pairs={{0,8},{8,16},{16,24},{24,28},{28,20},{20,12},{12,4},{4,0},{1,9},{9... | collective-permute-start | bytes 3538952 | tf_op jit(solution)/shard_map/ppermute | solution.py:113
  665.9 66.3 %collective-permute-start.60 = (bf16[192,3072]{1,0:T(8,128)(2,1)S(1)}, bf16[192,3072]{1,0:T(8,128)(2,1)}, u32[]{:S(2)}, u32[]{:S(2)}) collective-permute-start(bf16[192,3072]{1,0:T(8,128)(2,1)S(1)} %get-tuple-element.281), channel_id=1, source_target_pairs={{0,4},{8,0},{16,8},{24,16},{28,24},{20,28},{12,20},{4,12},{1,5},{9... | collective-permute-start | bytes 3538952 | tf_op jit(solution)/shard_map/ppermute | solution.py:113
  780.1 87.6 %collective-permute-start.61 = (bf16[2,256,1536]{2,1,0:T(8,128)(2,1)}, bf16[2,256,1536]{2,1,0:T(8,128)(2,1)}, u32[]{:S(2)}, u32[]{:S(2)}) collective-permute-start(bf16[2,256,1536]{2,1,0:T(8,128)(2,1)} %fusion.128), channel_id=1, source_target_pairs={{0,1},{1,0},{2,3},{3,2},{4,5},{5,4},{6,7},{7,6},{8,9},{9,8},{10,11... | collective-permute-start | bytes 4718600 | tf_op jit(solution)/shard_map/ppermute | solution.py:43
  811.6 56.1 %collective-permute-start.63 = (bf16[2,256,1536]{2,1,0:T(8,128)(2,1)S(1)}, bf16[2,256,1536]{2,1,0:T(8,128)(2,1)S(1)}, u32[]{:S(2)}, u32[]{:S(2)}) collective-permute-start(bf16[2,256,1536]{2,1,0:T(8,128)(2,1)S(1)} %fusion.134), channel_id=1, source_target_pairs={{0,2},{1,3},{2,0},{3,1},{4,6},{5,7},{6,4},{7,5},{8,10},{9,11},{10,... | collective-permute-start | bytes 4718600 | tf_op jit(solution)/shard_map/ppermute | solution.py:43
  816.7 45.5 %collective-permute-start.69 = (bf16[2,154,1536]{2,0,1:T(2,128)(2,1)S(1)}, bf16[2,154,1536]{2,0,1:T(2,128)(2,1)S(1)}, u32[]{:S(2)}, u32[]{:S(2)}) collective-permute-start(bf16[2,154,1536]{2,0,1:T(2,128)(2,1)S(1)} %copy.87), channel_id=1, source_target_pairs={{0,2},{1,3},{2,0},{3,1},{4,6},{5,7},{6,4},{7,5},{8,10},{9,11},{10,... | collective-permute-start | bytes 2838536 | tf_op jit(solution)/shard_map/ppermute | solution.py:43
  (207 other events, 3101.0 us)
Sparse Core Ops, SparseCore 0:
  10.8 70.7 all-gather.3
  83.7 94.4 all-gather.5
  287.6 120.3 all-gather.7
  534.2 195.1 reduce-scatter.2
  780.3 107.8 reduce-scatter.4

commit v3 on v2

--- a/solution.py
+++ b/solution.py
@@ -128,10 +128,12 @@
     for hop in range(1, count // 2):
         behind = ring_step(behind, 1, count)
         ahead = ring_step(ahead, -1, count)
+        behind, ahead = yield behind, ahead
         whole = put(put(whole, behind, -hop, 0), ahead, hop, 0)
     behind = ring_step(behind[:, :half], 1, count)
     ahead = ring_step(ahead[:, half:], -1, count)
-    return put(put(whole, behind, -(count // 2), 0), ahead, count // 2, half)
+    behind, ahead = yield behind, ahead
+    yield put(put(whole, behind, -(count // 2), 0), ahead, count // 2, half)
 
 
 def ring_scatter(grad, count):
@@ -427,16 +429,15 @@
         joined = blocks[0] if len(blocks) == 1 else jnp.concatenate(blocks, axis=1)
         return lax.all_gather(joined, "dp", axis=0, tiled=True)
 
-    image_in = gathered(image_attention_in.reshape(share, 3 * width))
-    image_up = gathered(image_hidden_in)
-    image_down = gathered(image_hidden_out.T)
-    text_in = ring_gather(text_attention_in.reshape(share, 3 * width), group_count)
-    both_out = ring_gather(
-        after(jnp.concatenate([image_attention_out.T, text_attention_out.T], axis=1), text_in),
-        group_count,
-    )
-    weight_in = (image_in, text_in)
-    weight_out = (both_out[:, :width], both_out[:, width:])
+    packed_first = gathered(
+        image_attention_in.reshape(share, 3 * width),
+        text_attention_in.reshape(share, 3 * width),
+        image_attention_out.T,
+        text_attention_out.T,
+    )
+    packed_image = gathered(image_hidden_in, image_hidden_out.T)
+    weight_in = (packed_first[:, : 3 * width], packed_first[:, 3 * width : 6 * width])
+    weight_out = (packed_first[:, 6 * width : 7 * width], packed_first[:, 7 * width :])
 
     alive = (jnp.arange(slots) < group_size[0]).astype(F32)[:, None, None]
     cond_full = condition.astype(F32)
@@ -488,14 +489,13 @@
         down = (outgoing[stream] * spread(mod[:, 5])).astype(BF16)
         down_pieces.append(collect(stream, after(down, pieces)))
     parts = packed[0] + packed[1]
-    packed_text = ring_gather(
-        after(jnp.concatenate([text_hidden_in, text_hidden_out.T], axis=1), parts, both_out),
-        group_count,
-    )
-    weight_up = (image_up, packed_text[:, :units])
-    weight_down = (image_down, packed_text[:, units:])
+    text_ring = ring_gather(
+        after(jnp.concatenate([text_hidden_in, text_hidden_out.T], axis=1), parts), group_count
+    )
+    text_hop = next(text_ring)
     attended, sums = attend(parts)
-    attended, down_pieces = lax.optimization_barrier((attended, down_pieces))
+    attended, down_pieces, text_hop = lax.optimization_barrier((attended, down_pieces, text_hop))
+    text_hop = text_ring.send(text_hop)
     attended_parts = (attended[:-1], attended[-1:])
 
     middles = [None, None]
@@ -507,16 +507,18 @@
     stats = [None, None]
     upstreams = [None, None]
 
-    def stream_branch(stream):
+    def stream_branch(stream, hop):
         mod = mods[stream]
         branch = reduced(stream, apply(attended_parts[stream], weight_out[stream], 1, False))
+        branch, hop = lax.optimization_barrier((branch, hop))
+        hop = text_ring.send(hop)
         middle = tokens[stream] + spread(mod[:, 2]) * branch
         normed, inverse = norm_rows(middle)
         second_in = normed * (1.0 + spread(mod[:, 4])) + spread(mod[:, 3])
         middles[stream] = middle
-        return branch, normed, inverse, collect(stream, second_in)
-
-    def stream_back(stream, branch, normed, inverse, pieces):
+        return (branch, normed, inverse, collect(stream, second_in)), hop
+
+    def stream_back(stream, branch, normed, inverse, pieces, hop=None):
         mod = mods[stream]
         hidden = apply(pieces, weight_up[stream], 0, False)
         active = [gelu_tanh(value).astype(BF16) for value in hidden]
@@ -529,6 +531,9 @@
         late = after((down_pieces[stream], active, pieces, hidden_grad), products)
         mlp_grads[stream] = weight_grad([late[:2], late[2:]])
         second_grad = reduced(stream, products)
+        if hop is not None:
+            second_grad, hop = lax.optimization_barrier((second_grad, hop))
+            hop = text_ring.send(hop)
         shift_two_grad = jnp.sum(second_grad, axis=1)
         scale_two_grad = jnp.sum(second_grad * normed, axis=1)
         middle_grad = outgoing[stream] + norm_back(
@@ -541,36 +546,35 @@
         middle_grads[stream] = middle_grad
         actives[stream] = after(active, low)
         stats[stream] = (gate_one_grad, shift_two_grad, scale_two_grad)
-
-    image_state = stream_branch(0)
-    text_state = stream_branch(1)
-    stream_back(0, *image_state)
+        return hop
+
+    text_state, text_hop = stream_branch(1, text_hop)
+    image_state, text_hop = stream_branch(0, text_hop)
+    for _ in range(group_count // 2 - 4):
+        text_hop = text_ring.send(text_hop)
+    packed_text = text_ring.send(text_hop)
+    weight_up = (packed_image[:, :units], packed_text[:, :units])
+    weight_down = (packed_image[:, units:], packed_text[:, units:])
     stream_back(1, *text_state)
+    text_ring = ring_scatter(mlp_grads[1], group_count)
+    text_hop = stream_back(0, *image_state, hop=next(text_ring))
     image_mlp = scattered(mlp_grads[0])
-    text_ring = ring_scatter(mlp_grads[1], group_count)
-    text_hop = next(text_ring)
     upstreams, text_hop = lax.optimization_barrier((upstreams, text_hop))
     text_hop = text_ring.send(text_hop)
 
     packed_grads = attend_back(parts, upstreams[0] + upstreams[1], sums)
     packed_grads, text_hop = lax.optimization_barrier((packed_grads, text_hop))
     text_hop = text_ring.send(text_hop)
-    image_in_grad = weight_grad([(first_saved[0][2], packed_grads[:-1])])
-    image_in_sum = scattered(image_in_grad)
     attention_grad = weight_grad(
         [
+            (first_saved[0][2], packed_grads[:-1]),
             (first_saved[1][2], packed_grads[-1:]),
             (branch_grads[0], attended_parts[0]),
             (branch_grads[1], attended_parts[1]),
         ]
     )
-    packed_grads = after(packed_grads, image_in_grad, attention_grad)
-    for _ in range(group_count // 2 - 2):
-        attention_grad, text_hop = lax.optimization_barrier((attention_grad, text_hop))
-        text_hop = text_ring.send(text_hop)
-    text_mlp = text_hop
-    attention_ring = ring_scatter(attention_grad, group_count)
-    attention_hop = next(attention_ring)
+    attention_sum = scattered(attention_grad)
+    packed_grads = after(packed_grads, attention_grad)
     packed_grads = (packed_grads[:-1], packed_grads[-1:])
     outputs = [None, None]
     input_grads = [None, None]
@@ -584,10 +588,12 @@
         outputs[stream] = (result * alive).astype(BF16)
         gate_two_grad = jnp.sum(outgoing[stream] * branch_two, axis=1)
         first_grad = reduced(stream, apply(packed_grads[stream], weight_in[stream], 1, False))
-        first_grad, attention_hop = lax.optimization_barrier((first_grad, attention_hop))
         if stream == 0:
-            first_grad, image_mlp = lax.optimization_barrier((first_grad, image_mlp))
-        attention_hop = attention_ring.send(attention_hop)
+            first_grad, image_mlp, text_hop = lax.optimization_barrier(
+                (first_grad, image_mlp, text_hop)
+            )
+            for _ in range(group_count // 2 - 3):
+                text_hop = text_ring.send(text_hop)
         shift_one_grad = jnp.sum(first_grad, axis=1)
         scale_one_grad = jnp.sum(first_grad * normed, axis=1)
         input_grads[stream] = middle_grads[stream] + norm_back(
@@ -604,9 +610,7 @@
             ],
             axis=1,
         )
-    for _ in range(group_count // 2 - 2):
-        attention_hop = attention_ring.send(attention_hop)
-    attention_sum = attention_hop
+    text_mlp = text_hop
 
     image_blocks = jnp.stack(
         [
@@ -645,13 +649,13 @@
         input_grads[1],
         condition_gradient,
         image_ada,
-        image_in_sum.reshape(share, 3, width),
-        attention_sum[:, 3 * width : 4 * width].T,
+        attention_sum[:, : 3 * width].reshape(share, 3, width),
+        attention_sum[:, 6 * width : 7 * width].T,
         image_mlp[:, units:],
         image_mlp[:, :units].T,
         text_ada,
-        attention_sum[:, : 3 * width].reshape(share, 3, width),
-        attention_sum[:, 4 * width :].T,
+        attention_sum[:, 3 * width : 6 * width].reshape(share, 3, width),
+        attention_sum[:, 7 * width :].T,
         text_mlp[:, units:],
         text_mlp[:, :units].T,
     )

time: 1000 us -> 953 us (0.953)
  starting transfers between devices: 111 us -> 61.4 us
  matrix products: 146 us -> 163 us
  local copies, waits for them, and re-layouts: 71.2 us -> 59.1 us
    ppermute x40 -> x16, waiting for transfers between devices: 230 us -> 96.1 us  [ring_step(): return lax.ppermute(value, 'dp', hops)]
    ppermute x48, waiting for transfers between devices: 136 us -> 211 us  [swap(): return lax.ppermute(value, axis, [(i, i ^ bit) for i in range(size)])]
    reduce_scatter x2, waiting for transfers between devices: 0.02 us -> 54 us  [scattered(): lax.psum_scatter(grad, 'dp', scatter_dimension=0, tiled=True).astype(F32)]
    ppermute x40 -> x16, starting transfers between devices: 71.9 us -> 20.3 us  [ring_step(): return lax.ppermute(value, 'dp', hops)]
    dynamic_update_slice x27 -> x9, local copies, waits for them, and re-layouts: 20.2 us -> 3.25 us  [put(): return lax.dynamic_update_slice(whole, value, (row, column))]
    dot_general x46, matrix products: 146 us -> 163 us  [dot(): lax.dot_general(left, right, (((left_dim,), (right_dim,)), ((), ())), pre...]
    all_gather x3 -> x2, waiting for transfers between devices: 0.02 us -> 12.7 us  [gathered(): return lax.all_gather(joined, 'dp', axis=0, tiled=True)]
    unnamed x313 -> x371, local copies, waits for them, and re-layouts: 13.1 us -> 22.8 us
  transfers between devices with their start and end apart: 93 -> 68, of which waited for: 39 -> 29; matrix products, arithmetic and copies ran while one was open for 28% -> 28% of each run, Pallas kernels for 15% -> 16%
where the time goes in v3:
time: 953 us; the launch traced here: 947 us
  waiting for transfers between devices  374 us (39%)
  Pallas kernels  181 us (19%)
  matrix products  163 us (17%)
  other arithmetic  71 us (7%)
  starting transfers between devices  61.4 us (6%)
  local copies, waits for them, and re-layouts  59.1 us (6%)
  between operations  32.4 us (3%)
    ppermute x48, waiting for transfers between devices, swap(): return lax.ppermute(value, axis, [(i, i ^ bit) for i in range(size)])  211 us
    dot_general x46, matrix products, dot(): lax.dot_general(left, right, (((left_dim,), (right_dim,)), ((), ())), pre...  163 us
    ppermute x16, waiting for transfers between devices, ring_step(): return lax.ppermute(value, 'dp', hops)  96.1 us
    pallas_call x8, Pallas kernels, weight_grad(): pl.pallas_call(functools.partial(rows_kernel, count), grid=(rows // step,...  68.2 us
    pallas_call x1, Pallas kernels, attend_back(): pl.pallas_call(functools.partial(attend_back_kernel, count, groups), grid...  57.7 us
    pallas_call x1, Pallas kernels, attend(): pl.pallas_call(functools.partial(attend_kernel, count), grid=(slots, grou...  54.8 us
    reduce_scatter x2, waiting for transfers between devices, scattered(): lax.psum_scatter(grad, 'dp', scatter_dimension=0, tiled=True).astype(F32)  54 us
    ppermute x48, starting transfers between devices, swap(): return lax.ppermute(value, axis, [(i, i ^ bit) for i in range(size)])  40.4 us
  transfers between devices with their start and end apart: 68, of which 29 were waited for; matrix products, arithmetic and copies ran while one was open for 28% of the time, Pallas kernels for 16%

profile of v3, /device:TPU:0, one launch (start us, length us, event | category | flops | bytes accessed | tf_op | source)
XLA Modules:
  0.0 947.2 jit_solution(2042159315935691986)
XLA Ops:
  31.9 15.1 %collective-permute-done.3 = f32[4,2,4608]{2,1,0:T(2,128)} collective-permute-done((f32[4,2,4608]{2,1,0:T(2,128)}, f32[4,2,4608]{2,1,0:T(2,128)}, u32[]{:S(2)}, u32[]{:S(2)}) %collective-permute-start.3) | collective-permute-done | bytes 147488 | tf_op jit(solution)/shard_map/ppermute | solution.py:43
  49.7 6.8 collective-permute-done.4
  60.6 5.5 all_gather.9
  73.4 32.7 %collective-permute-done.7.refs_2_ = bf16[2,256,1536]{2,1,0:T(8,128)(2,1)} collective-permute-done((bf16[2,256,1536]{2,1,0:T(8,128)(2,1)}, bf16[2,256,1536]{2,1,0:T(8,128)(2,1)}, u32[]{:S(2)}, u32[]{:S(2)}) %collective-permute-start.7) | collective-permute-done | bytes 1572896 | tf_op jit(solution)/shard_map/ppermute | solution.py:43
  114.9 31.5 %collective-permute-done.10.refs_2_ = bf16[2,256,1536]{2,1,0:T(8,128)(2,1)S(1)} collective-permute-done((bf16[2,256,1536]{2,1,0:T(8,128)(2,1)S(1)}, bf16[2,256,1536]{2,1,0:T(8,128)(2,1)S(1)}, u32[]{:S(2)}, u32[]{:S(2)}) %collective-permute-start.10) | collective-permute-done | bytes 1572896 | tf_op jit(solution)/shard_map/ppermute | solution.py:43
  146.5 12.7 %all-gather.3.cloned.1.call-done = bf16[1536,3072]{1,0:T(8,128)(2,1)} async-done(((bf16[192,3072]{1,0:T(8,128)(2,1)}), bf16[1536,3072]{1,0:T(8,128)(2,1)}) %all-gather.3.cloned.1.call-update) | async-done | bytes 9437200 | tf_op jit(solution)/shard_map/all_gather | solution.py:430
  180.1 54.8 %attend.1 = (bf16[2,256,384]{2,1,0:T(8,128)(2,1)S(1)}, bf16[2,256,384]{2,1,0:T(8,128)(2,1)S(1)}, bf16[2,256,384]{2,1,0:T(8,128)(2,1)S(1)}, bf16[2,256,384]{2,1,0...) custom-call(bf16[2,256,1152]{2,1,0:T(8,128)(2,1)S(1)} %convolution_c, ...), custom_call_target="tpu_custom_call" | custom-call | flops 17051860992 | bytes 7237632 | tf_op jit(solution)/shard_map/attend/pallas_call | solution.py:298
  259.9 18.9 %collective-permute-done.18 = bf16[2,154,1536]{2,0,1:T(2,128)(2,1)S(1)} collective-permute-done((bf16[2,154,1536]{2,0,1:T(2,128)(2,1)S(1)}, bf16[2,154,1536]{2,0,1:T(2,128)(2,1)S(1)}, u32[]{:S(2)}, u32[]{:S(2)}) %collective-permute-start.18) | collective-permute-done | bytes 946208 | tf_op jit(solution)/shard_map/ppermute | solution.py:43
  280.9 17.3 %collective-permute-done.19 = bf16[192,3072]{1,0:T(8,128)(2,1)S(1)} collective-permute-done((bf16[192,3072]{1,0:T(8,128)(2,1)S(1)}, bf16[192,3072]{1,0:T(8,128)(2,1)S(1)}, u32[]{:S(2)}, u32[]{:S(2)}) %collective-permute-start.19) | collective-permute-done | bytes 1179680 | tf_op jit(solution)/shard_map/ppermute | solution.py:113
  298.2 29.2 %collective-permute-done.20 = bf16[192,3072]{1,0:T(8,128)(2,1)S(1)} collective-permute-done((bf16[192,3072]{1,0:T(8,128)(2,1)S(1)}, bf16[192,3072]{1,0:T(8,128)(2,1)S(1)}, u32[]{:S(2)}, u32[]{:S(2)}) %collective-permute-start.20) | collective-permute-done | bytes 1179680 | tf_op jit(solution)/shard_map/ppermute | solution.py:113
  336.3 34.0 %collective-permute-done.21 = bf16[192,3072]{1,0:T(8,128)(2,1)S(1)} collective-permute-done((bf16[192,3072]{1,0:T(8,128)(2,1)S(1)}, bf16[192,3072]{1,0:T(8,128)(2,1)S(1)}, u32[]{:S(2)}, u32[]{:S(2)}) %collective-permute-start.21) | collective-permute-done | bytes 1179680 | tf_op jit(solution)/shard_map/ppermute | solution.py:113
  378.8 6.7 multiply_convert_fusion.5
  409.1 5.9 multiply_convert_fusion.3
  415.0 5.9 multiply_convert_fusion.4
  420.9 5.9 fusion.32.refs_5_
  434.4 5.7 fusion.46.refs_7_
  459.3 15.1 %weight_grad.14.refs_8_ = bf16[1536,3072]{1,0:T(8,128)(2,1)} custom-call(bf16[2,256,1536]{2,1,0:T(8,128)(2,1)S(1)} %multiply_convert_fusion.6.refs_0_, bf16[2,256,1536]{2,1,0:T(8,128)(2,1)} %collective-permute-done.9.refs_1_, bf16[2,256,1536]{2,1,0:T(8,128)(2,1)S(1)} %copy-done.6, bf16[2,256,1536]{2,1,0:T(8,128)(2,1)} %collective-permute-done.11.refs_3_, ...), custom_call_target="tpu_custom_call" | custom-call | bytes 1024 | tf_op jit(solution)/shard_map/weight_grad/pallas_call | solution.py:379
  474.4 15.1 %weight_grad.15 = bf16[1536,3072]{1,0:T(8,128)(2,1)} custom-call(bf16[2,256,1536]{2,1,0:T(8,128)(2,1)S(1)} %add_convert_fusion.3.refs_0_, bf16[2,256,1536]{2,1,0:T(8,128)(2,1)} %collective-permute-done.23.refs_1_, bf16[2,256,1536]{2,1,0:T(8,128)(2,1)} %collective-permute-done.24.refs_2_, ...), custom_call_target="tpu_custom_call", output_to_operand_aliasing={{}: (8, {})} | custom-call | bytes 1024 | tf_op jit(solution)/shard_map/weight_grad/pallas_call | solution.py:379
  545.8 15.0 %collective-permute-done.39 = bf16[2,154,1536]{2,0,1:T(2,128)(2,1)} collective-permute-done((bf16[2,154,1536]{2,0,1:T(2,128)(2,1)}, bf16[2,154,1536]{2,0,1:T(2,128)(2,1)}, u32[]{:S(2)}, u32[]{:S(2)}) %collective-permute-start.39) | collective-permute-done | bytes 946208 | tf_op jit(solution)/shard_map/ppermute | solution.py:43
  567.8 15.4 %collective-permute-done.32 = bf16[192,1536]{1,0:T(8,128)(2,1)S(1)} collective-permute-done((bf16[192,1536]{1,0:T(8,128)(2,1)S(1)}, bf16[192,1536]{1,0:T(8,128)(2,1)S(1)}, u32[]{:S(2)}, u32[]{:S(2)}) %collective-permute-start.32) | collective-permute-done | bytes 589856 | tf_op jit(solution)/shard_map/ppermute | solution.py:113
  597.1 6.9 fusion.124
  604.0 6.1 convolution_convert_fusion.7
  610.0 13.6 %collective-permute-done.41.refs_2_ = bf16[2,256,1536]{2,1,0:T(8,128)(2,1)S(1)} collective-permute-done((bf16[2,256,1536]{2,1,0:T(8,128)(2,1)S(1)}, bf16[2,256,1536]{2,1,0:T(8,128)(2,1)S(1)}, u32[]{:S(2)}, u32[]{:S(2)}) %collective-permute-start.41) | collective-permute-done | bytes 1572896 | tf_op jit(solution)/shard_map/ppermute | solution.py:43
  629.0 6.3 add_convert_fusion.1
  646.3 57.7 %attend_back.1 = (bf16[2,256,1152]{2,1,0:T(8,128)(2,1)S(1)}, bf16[2,256,1152]{2,1,0:T(8,128)(2,1)S(1)}, bf16[2,256,1152]{2,1,0:T(8,128)(2,1)}, bf16[2,256,1152]{2,1,0:T(8,128)(2,1)}, bf16[2,154,1152]{2,1,0:T(8,128)(2,1)S(1)}) custom-call(bf16[2,256,1152]{2,1,0:T(8,128)(2,1)} %copy-done.27, bf16[2,256,1152]{2,1,0:T(8,128)(2,1)} %copy-done.29, ...), custom_call_target="tpu_custom_call" | custom-call | flops 42629652480 | bytes 12665856 | tf_op jit(solution)/shard_map/attend_back/pallas_call | solution.py:325
  707.8 11.6 %weight_grad.10.refs_2_ = bf16[1536,3072]{1,0:T(8,128)(2,1)} custom-call(bf16[2,256,1536]{2,1,0:T(8,128)(2,1)} %fusion.12.refs_0_, bf16[2,256,1536]{2,1,0:T(8,128)(2,1)} %copy-done.91, bf16[2,256,1536]{2,1,0:T(8,128)(2,1)} %collective-permute-done.7.refs_2_, bf16[2,256,1536]{2,1,0:T(8,128)(2,1)} %copy-done.93, ...), custom_call_target="tpu_custom_call" | custom-call | bytes 1024 | tf_op jit(solution)/shard_map/weight_grad/pallas_call | solution.py:379
  724.4 7.2 weight_grad.12.refs_2_
  774.5 17.1 %collective-permute-done.53 = bf16[2,154,1536]{2,0,1:T(2,128)(2,1)S(1)} collective-permute-done((bf16[2,154,1536]{2,0,1:T(2,128)(2,1)S(1)}, bf16[2,154,1536]{2,0,1:T(2,128)(2,1)S(1)}, u32[]{:S(2)}, u32[]{:S(2)}) %collective-permute-start.53) | collective-permute-done | bytes 946208 | tf_op jit(solution)/shard_map/ppermute | solution.py:43
  798.3 26.1 %collective-permute-done.49 = bf16[2,256,1536]{2,1,0:T(8,128)(2,1)S(1)} collective-permute-done((bf16[2,256,1536]{2,1,0:T(8,128)(2,1)S(1)}, bf16[2,256,1536]{2,1,0:T(8,128)(2,1)S(1)}, u32[]{:S(2)}, u32[]{:S(2)}) %collective-permute-start.49) | collective-permute-done | bytes 1572896 | tf_op jit(solution)/shard_map/ppermute | solution.py:43
  844.8 5.3 collective-permute-done.57
  851.9 7.4 collective-permute-done.58
  882.1 54.0 %reduce-scatter.5.cloned.1.call-done = bf16[192,3072]{1,0:T(8,128)(2,1)} async-done(((bf16[1536,3072]{1,0:T(8,128)(2,1)}), bf16[192,3072]{1,0:T(8,128)(2,1)}) %reduce-scatter.5.cloned.1.call-update) | async-done | bytes 1179664 | tf_op jit(solution)/shard_map/reduce_scatter | solution.py:477
  (668 shorter events, 346.1 us)
Async XLA Ops:
  7.2 152.1 %all-gather.3.cloned.1.call-start = ((), (), s32[]{:S(2)}) async-start(), calls=%async_computation.2 | async-start | bytes 10616832 | tf_op jit(solution)/shard_map/all_gather | solution.py:430
  11.7 367.1 %all-gather.5.cloned.1.call-start = ((), (), s32[]{:S(2)}) async-start(), calls=%async_computation.3 | async-start | bytes 10616832 | tf_op jit(solution)/shard_map/all_gather | solution.py:430
  69.1 37.0 %collective-permute-start.7 = (bf16[2,256,1536]{2,1,0:T(8,128)(2,1)}, bf16[2,256,1536]{2,1,0:T(8,128)(2,1)}, u32[]{:S(2)}, u32[]{:S(2)}) collective-permute-start(bf16[2,256,1536]{2,1,0:T(8,128)(2,1)} %fusion.12.refs_0_), channel_id=1, source_target_pairs={{0,2},{1,3},{2,0},{3,1},{4,6},{5,7},{6,4},{7,5},{8,10},{9,11},{10,... | collective-permute-start | bytes 4718600 | tf_op jit(solution)/shard_map/ppermute | solution.py:43
  72.0 754.9 %reduce-scatter.3.cloned.1.call-start = ((), (), s32[]{:S(2)}) async-start(), calls=%async_computation.4 | async-start | bytes 10616832 | tf_op jit(solution)/shard_map/reduce_scatter | solution.py:477
  109.7 36.7 %collective-permute-start.10 = (bf16[2,256,1536]{2,1,0:T(8,128)(2,1)S(1)}, bf16[2,256,1536]{2,1,0:T(8,128)(2,1)S(1)}, u32[]{:S(2)}, u32[]{:S(2)}) collective-permute-start(bf16[2,256,1536]{2,1,0:T(8,128)(2,1)S(1)} %multiply_convert_fusion.6.refs_0_), channel_id=1, source_target_pairs={{0,2},{1,3},{2,0},{3,1},{4,6},{5,7},{6,4},{7,5},{8,10},{9,11},{10,... | collective-permute-start | bytes 4718600 | tf_op jit(solution)/shard_map/ppermute | solution.py:43
  114.8 120.2 %collective-permute-start.9 = (bf16[2,256,1536]{2,1,0:T(8,128)(2,1)S(1)}, bf16[2,256,1536]{2,1,0:T(8,128)(2,1)}, u32[]{:S(2)}, u32[]{:S(2)}) collective-permute-start(bf16[2,256,1536]{2,1,0:T(8,128)(2,1)S(1)} %multiply_convert_fusion.6.refs_0_), channel_id=1, source_target_pairs={{0,1},{1,0},{2,3},{3,2},{4,5},{5,4},{6,7},{7,6},{8,9},{9,8},{10,11... | collective-permute-start | bytes 4718600 | tf_op jit(solution)/shard_map/ppermute | solution.py:43
  146.5 88.5 %collective-permute-start.11 = (bf16[2,256,1536]{2,1,0:T(8,128)(2,1)S(1)}, bf16[2,256,1536]{2,1,0:T(8,128)(2,1)}, u32[]{:S(2)}, u32[]{:S(2)}) collective-permute-start(bf16[2,256,1536]{2,1,0:T(8,128)(2,1)S(1)} %collective-permute-done.10.refs_2_), channel_id=1, source_target_pairs={{0,1},{1,0},{2,3},{3,2},{4,5},{5,4},{6,7},{7,6},{8,9},{9,8},{10,11... | collective-permute-start | bytes 4718600 | tf_op jit(solution)/shard_map/ppermute | solution.py:43
  177.9 57.4 %collective-permute-start.13 = (bf16[192,3072]{1,0:T(8,128)(2,1)S(1)}, bf16[192,3072]{1,0:T(8,128)(2,1)S(1)}, u32[]{:S(2)}, u32[]{:S(2)}) collective-permute-start(bf16[192,3072]{1,0:T(8,128)(2,1)S(1)} %copy-done.83), channel_id=1, source_target_pairs={{0,4},{8,0},{16,8},{24,16},{28,24},{20,28},{12,20},{4,12},{1,5},{9... | collective-permute-start | bytes 3538952 | tf_op jit(solution)/shard_map/ppermute | solution.py:113
  178.6 56.6 %collective-permute-start.12 = (bf16[192,3072]{1,0:T(8,128)(2,1)S(1)}, bf16[192,3072]{1,0:T(8,128)(2,1)S(1)}, u32[]{:S(2)}, u32[]{:S(2)}) collective-permute-start(bf16[192,3072]{1,0:T(8,128)(2,1)S(1)} %copy-done.83), channel_id=1, source_target_pairs={{0,8},{8,16},{16,24},{24,28},{28,20},{20,12},{12,4},{4,0},{1,9},{9... | collective-permute-start | bytes 3538952 | tf_op jit(solution)/shard_map/ppermute | solution.py:113
  244.3 53.9 %collective-permute-start.19 = (bf16[192,3072]{1,0:T(8,128)(2,1)S(1)}, bf16[192,3072]{1,0:T(8,128)(2,1)S(1)}, u32[]{:S(2)}, u32[]{:S(2)}) collective-permute-start(bf16[192,3072]{1,0:T(8,128)(2,1)S(1)} %copy-done.109), channel_id=1, source_target_pairs={{0,8},{8,16},{16,24},{24,28},{28,20},{20,12},{12,4},{4,0},{1,9},{9... | collective-permute-start | bytes 3538952 | tf_op jit(solution)/shard_map/ppermute | solution.py:113
  246.1 81.2 %collective-permute-start.20 = (bf16[192,3072]{1,0:T(8,128)(2,1)S(1)}, bf16[192,3072]{1,0:T(8,128)(2,1)S(1)}, u32[]{:S(2)}, u32[]{:S(2)}) collective-permute-start(bf16[192,3072]{1,0:T(8,128)(2,1)S(1)} %copy-done.107), channel_id=1, source_target_pairs={{0,4},{8,0},{16,8},{24,16},{28,24},{20,28},{12,20},{4,12},{1,5},{9... | collective-permute-start | bytes 3538952 | tf_op jit(solution)/shard_map/ppermute | solution.py:113
  251.5 81.5 %collective-permute-start.14 = (bf16[2,256,1536]{2,1,0:T(8,128)(2,1)S(1)}, bf16[2,256,1536]{2,1,0:T(8,128)(2,1)S(1)}, u32[]{:S(2)}, u32[]{:S(2)}) collective-permute-start(bf16[2,256,1536]{2,1,0:T(8,128)(2,1)S(1)} %convolution_convert_fusion.9), channel_id=1, source_target_pairs={{0,1},{1,0},{2,3},{3,2},{4,5},{5,4},{6,7},{7,6},{8,9},{9,8},{10,11... | collective-permute-start | bytes 4718600 | tf_op jit(solution)/shard_map/ppermute | solution.py:43
  259.2 73.8 %collective-permute-start.16 = (bf16[2,256,1536]{2,1,0:T(8,128)(2,1)S(1)}, bf16[2,256,1536]{2,1,0:T(8,128)(2,1)S(1)}, u32[]{:S(2)}, u32[]{:S(2)}) collective-permute-start(bf16[2,256,1536]{2,1,0:T(8,128)(2,1)S(1)} %fusion.47), channel_id=1, source_target_pairs={{0,2},{1,3},{2,0},{3,1},{4,6},{5,7},{6,4},{7,5},{8,10},{9,11},{10,... | collective-permute-start | bytes 4718600 | tf_op jit(solution)/shard_map/ppermute | solution.py:43
  327.4 43.0 %collective-permute-start.21 = (bf16[192,3072]{1,0:T(8,128)(2,1)S(1)}, bf16[192,3072]{1,0:T(8,128)(2,1)S(1)}, u32[]{:S(2)}, u32[]{:S(2)}) collective-permute-start(bf16[192,3072]{1,0:T(8,128)(2,1)S(1)} %collective-permute-done.19), channel_id=1, source_target_pairs={{0,8},{8,16},{16,24},{24,28},{28,20},{20,12},{12,4},{4,0},{1,9},{9... | collective-permute-start | bytes 3538952 | tf_op jit(solution)/shard_map/ppermute | solution.py:113
  327.4 43.0 %collective-permute-start.22 = (bf16[192,3072]{1,0:T(8,128)(2,1)S(1)}, bf16[192,3072]{1,0:T(8,128)(2,1)S(1)}, u32[]{:S(2)}, u32[]{:S(2)}) collective-permute-start(bf16[192,3072]{1,0:T(8,128)(2,1)S(1)} %collective-permute-done.20), channel_id=1, source_target_pairs={{0,4},{8,0},{16,8},{24,16},{28,24},{20,28},{12,20},{4,12},{1,5},{9... | collective-permute-start | bytes 3538952 | tf_op jit(solution)/shard_map/ppermute | solution.py:113
  374.2 40.7 %collective-permute-start.23 = (bf16[2,256,1536]{2,1,0:T(8,128)(2,1)S(1)}, bf16[2,256,1536]{2,1,0:T(8,128)(2,1)}, u32[]{:S(2)}, u32[]{:S(2)}) collective-permute-start(bf16[2,256,1536]{2,1,0:T(8,128)(2,1)S(1)} %add_convert_fusion.3.refs_0_), channel_id=1, source_target_pairs={{0,1},{1,0},{2,3},{3,2},{4,5},{5,4},{6,7},{7,6},{8,9},{9,8},{10,11... | collective-permute-start | bytes 4718600 | tf_op jit(solution)/shard_map/ppermute | solution.py:43
  489.6 446.5 %reduce-scatter.5.cloned.1.call-start = ((), (), s32[]{:S(2)}) async-start(), calls=%async_computation.5 | async-start | bytes 10616832 | tf_op jit(solution)/shard_map/reduce_scatter | solution.py:477
  503.4 61.7 %collective-permute-start.26 = (bf16[2,256,1536]{2,1,0:T(8,128)(2,1)}, bf16[2,256,1536]{2,1,0:T(8,128)(2,1)}, u32[]{:S(2)}, u32[]{:S(2)}) collective-permute-start(bf16[2,256,1536]{2,1,0:T(8,128)(2,1)} %fusion.117), channel_id=1, source_target_pairs={{0,1},{1,0},{2,3},{3,2},{4,5},{5,4},{6,7},{7,6},{8,9},{9,8},{10,11... | collective-permute-start | bytes 4718600 | tf_op jit(solution)/shard_map/ppermute | solution.py:43
  503.6 61.5 %collective-permute-start.28 = (bf16[2,256,1536]{2,1,0:T(8,128)(2,1)}, bf16[2,256,1536]{2,1,0:T(8,128)(2,1)}, u32[]{:S(2)}, u32[]{:S(2)}) collective-permute-start(bf16[2,256,1536]{2,1,0:T(8,128)(2,1)} %add_convert_fusion.2), channel_id=1, source_target_pairs={{0,2},{1,3},{2,0},{3,1},{4,6},{5,7},{6,4},{7,5},{8,10},{9,11},{10,... | collective-permute-start | bytes 4718600 | tf_op jit(solution)/shard_map/ppermute | solution.py:43
  510.8 50.0 %collective-permute-start.39 = (bf16[2,154,1536]{2,0,1:T(2,128)(2,1)}, bf16[2,154,1536]{2,0,1:T(2,128)(2,1)}, u32[]{:S(2)}, u32[]{:S(2)}) collective-permute-start(bf16[2,154,1536]{2,0,1:T(2,128)(2,1)} %copy.85), channel_id=1, source_target_pairs={{0,2},{1,3},{2,0},{3,1},{4,6},{5,7},{6,4},{7,5},{8,10},{9,11},{10,... | collective-permute-start | bytes 2838536 | tf_op jit(solution)/shard_map/ppermute | solution.py:43
  541.6 41.6 %collective-permute-start.32 = (bf16[192,1536]{1,0:T(8,128)(2,1)S(1)}, bf16[192,1536]{1,0:T(8,128)(2,1)S(1)}, u32[]{:S(2)}, u32[]{:S(2)}) collective-permute-start(bf16[192,1536]{1,0:T(8,128)(2,1)S(1)} %get-tuple-element.283), channel_id=1, source_target_pairs={{0,4},{8,0},{16,8},{24,16},{28,24},{20,28},{12,20},{4,12},{1,5},{9... | collective-permute-start | bytes 1769480 | tf_op jit(solution)/shard_map/ppermute | solution.py:113
  542.3 40.9 %collective-permute-start.31 = (bf16[192,1536]{1,0:T(8,128)(2,1)S(1)}, bf16[192,1536]{1,0:T(8,128)(2,1)S(1)}, u32[]{:S(2)}, u32[]{:S(2)}) collective-permute-start(bf16[192,1536]{1,0:T(8,128)(2,1)S(1)} %get-tuple-element.284), channel_id=1, source_target_pairs={{0,8},{8,16},{16,24},{24,28},{28,20},{20,12},{12,4},{4,0},{1,9},{9... | collective-permute-start | bytes 1769480 | tf_op jit(solution)/shard_map/ppermute | solution.py:113
  588.1 47.2 %collective-permute-start.40 = (bf16[2,256,1536]{2,1,0:T(8,128)(2,1)S(1)}, bf16[2,256,1536]{2,1,0:T(8,128)(2,1)S(1)}, u32[]{:S(2)}, u32[]{:S(2)}) collective-permute-start(bf16[2,256,1536]{2,1,0:T(8,128)(2,1)S(1)} %multiply_convert_fusion.1.refs_0_), channel_id=1, source_target_pairs={{0,1},{1,0},{2,3},{3,2},{4,5},{5,4},{6,7},{7,6},{8,9},{9,8},{10,11... | collective-permute-start | bytes 4718600 | tf_op jit(solution)/shard_map/ppermute | solution.py:43
  588.6 52.4 %collective-permute-start.44 = (bf16[192,3072]{1,0:T(8,128)(2,1)S(1)}, bf16[192,3072]{1,0:T(8,128)(2,1)S(1)}, u32[]{:S(2)}, u32[]{:S(2)}) collective-permute-start(bf16[192,3072]{1,0:T(8,128)(2,1)S(1)} %get-tuple-element.281), channel_id=1, source_target_pairs={{0,4},{8,0},{16,8},{24,16},{28,24},{20,28},{12,20},{4,12},{1,5},{9... | collective-permute-start | bytes 3538952 | tf_op jit(solution)/shard_map/ppermute | solution.py:113
  591.7 49.3 %collective-permute-start.43 = (bf16[192,3072]{1,0:T(8,128)(2,1)S(1)}, bf16[192,3072]{1,0:T(8,128)(2,1)S(1)}, u32[]{:S(2)}, u32[]{:S(2)}) collective-permute-start(bf16[192,3072]{1,0:T(8,128)(2,1)S(1)} %get-tuple-element.282), channel_id=1, source_target_pairs={{0,8},{8,16},{16,24},{24,28},{28,20},{20,12},{12,4},{4,0},{1,9},{9... | collective-permute-start | bytes 3538952 | tf_op jit(solution)/shard_map/ppermute | solution.py:113
  628.9 114.0 %collective-permute-start.33 = (bf16[2,256,1536]{2,1,0:T(8,128)(2,1)}, bf16[2,256,1536]{2,1,0:T(8,128)(2,1)}, u32[]{:S(2)}, u32[]{:S(2)}) collective-permute-start(bf16[2,256,1536]{2,1,0:T(8,128)(2,1)} %convolution_convert_fusion.7), channel_id=1, source_target_pairs={{0,1},{1,0},{2,3},{3,2},{4,5},{5,4},{6,7},{7,6},{8,9},{9,8},{10,11... | collective-permute-start | bytes 4718600 | tf_op jit(solution)/shard_map/ppermute | solution.py:43
  635.3 107.6 %collective-permute-start.35 = (bf16[2,256,1536]{2,1,0:T(8,128)(2,1)}, bf16[2,256,1536]{2,1,0:T(8,128)(2,1)}, u32[]{:S(2)}, u32[]{:S(2)}) collective-permute-start(bf16[2,256,1536]{2,1,0:T(8,128)(2,1)} %add_convert_fusion.1), channel_id=1, source_target_pairs={{0,2},{1,3},{2,0},{3,1},{4,6},{5,7},{6,4},{7,5},{8,10},{9,11},{10,... | collective-permute-start | bytes 4718600 | tf_op jit(solution)/shard_map/ppermute | solution.py:43
  642.9 61.2 %collective-permute-start.46 = (bf16[192,3072]{1,0:T(8,128)(2,1)}, bf16[192,3072]{1,0:T(8,128)(2,1)S(1)}, u32[]{:S(2)}, u32[]{:S(2)}) collective-permute-start(bf16[192,3072]{1,0:T(8,128)(2,1)} %get-tuple-element.279), channel_id=1, source_target_pairs={{0,4},{8,0},{16,8},{24,16},{28,24},{20,28},{12,20},{4,12},{1,5},{9... | collective-permute-start | bytes 3538952 | tf_op jit(solution)/shard_map/ppermute | solution.py:113
  645.9 58.2 %collective-permute-start.45 = (bf16[192,3072]{1,0:T(8,128)(2,1)S(1)}, bf16[192,3072]{1,0:T(8,128)(2,1)S(1)}, u32[]{:S(2)}, u32[]{:S(2)}) collective-permute-start(bf16[192,3072]{1,0:T(8,128)(2,1)S(1)} %get-tuple-element.280), channel_id=1, source_target_pairs={{0,8},{8,16},{16,24},{24,28},{28,20},{20,12},{12,4},{4,0},{1,9},{9... | collective-permute-start | bytes 3538952 | tf_op jit(solution)/shard_map/ppermute | solution.py:113
  751.4 77.3 %collective-permute-start.51 = (bf16[192,3072]{1,0:T(8,128)(2,1)}, bf16[192,3072]{1,0:T(8,128)(2,1)}, u32[]{:S(2)}, u32[]{:S(2)}) collective-permute-start(bf16[192,3072]{1,0:T(8,128)(2,1)} %get-tuple-element.277), channel_id=1, source_target_pairs={{0,4},{8,0},{16,8},{24,16},{28,24},{20,28},{12,20},{4,12},{1,5},{9... | collective-permute-start | bytes 3538952 | tf_op jit(solution)/shard_map/ppermute | solution.py:113
  753.4 75.3 %collective-permute-start.50 = (bf16[192,3072]{1,0:T(8,128)(2,1)}, bf16[192,3072]{1,0:T(8,128)(2,1)}, u32[]{:S(2)}, u32[]{:S(2)}) collective-permute-start(bf16[192,3072]{1,0:T(8,128)(2,1)} %get-tuple-element.278), channel_id=1, source_target_pairs={{0,8},{8,16},{16,24},{24,28},{28,20},{20,12},{12,4},{4,0},{1,9},{9... | collective-permute-start | bytes 3538952 | tf_op jit(solution)/shard_map/ppermute | solution.py:113
  774.2 50.2 %collective-permute-start.49 = (bf16[2,256,1536]{2,1,0:T(8,128)(2,1)S(1)}, bf16[2,256,1536]{2,1,0:T(8,128)(2,1)S(1)}, u32[]{:S(2)}, u32[]{:S(2)}) collective-permute-start(bf16[2,256,1536]{2,1,0:T(8,128)(2,1)S(1)} %add_convert_fusion), channel_id=1, source_target_pairs={{0,2},{1,3},{2,0},{3,1},{4,6},{5,7},{6,4},{7,5},{8,10},{9,11},{10,... | collective-permute-start | bytes 4718600 | tf_op jit(solution)/shard_map/ppermute | solution.py:43
  (211 other events, 2433.1 us)
Sparse Core Ops, SparseCore 0:
  11.9 147.3 all-gather.2
  162.0 200.7 all-gather.4
  489.8 211.0 reduce-scatter.2
  753.7 182.3 reduce-scatter.4

commit v4 on v3

--- a/solution.py
+++ b/solution.py
@@ -429,20 +429,20 @@
         joined = blocks[0] if len(blocks) == 1 else jnp.concatenate(blocks, axis=1)
         return lax.all_gather(joined, "dp", axis=0, tiled=True)
 
-    packed_first = gathered(
-        image_attention_in.reshape(share, 3 * width),
-        text_attention_in.reshape(share, 3 * width),
-        image_attention_out.T,
-        text_attention_out.T,
-    )
-    packed_image = gathered(image_hidden_in, image_hidden_out.T)
-    weight_in = (packed_first[:, : 3 * width], packed_first[:, 3 * width : 6 * width])
-    weight_out = (packed_first[:, 6 * width : 7 * width], packed_first[:, 7 * width :])
+    image_in = gathered(image_attention_in.reshape(share, 3 * width))
+    packed_mid = gathered(image_attention_out.T, text_attention_out.T, image_hidden_in)
+    image_down = gathered(image_hidden_out.T)
+    packed_text = gathered(text_hidden_in, text_hidden_out.T)
+    text_ring = ring_gather(text_attention_in.reshape(share, 3 * width), group_count)
+    text_hop = next(text_ring)
+    weight_out = (packed_mid[:, :width], packed_mid[:, width : 2 * width])
 
     alive = (jnp.arange(slots) < group_size[0]).astype(F32)[:, None, None]
     cond_full = condition.astype(F32)
     activated_low = jax.nn.silu(cond_full).astype(BF16)
     activated_all = gather_stack(activated_low, group_count, "dp").reshape(-1, model)
+    activated_all, text_hop = lax.optimization_barrier((activated_all, text_hop))
+    text_hop = text_ring.send(text_hop)
     activated_own = lax.dynamic_slice_in_dim(activated_all, group_rank * share, share, 1)
     all_slots = activated_own.shape[0]
     mod_parts = jnp.concatenate(
@@ -452,10 +452,17 @@
         ],
         axis=1,
     ).reshape(group_count, slots, 12 * width)
+    for _ in range(group_count // 2 - 3):
+        mod_parts, text_hop = lax.optimization_barrier((mod_parts, text_hop))
+        text_hop = text_ring.send(text_hop)
     mod_own = scatter_stack(mod_parts, group_count, "dp")
+    mod_own, text_hop = lax.optimization_barrier((mod_own, text_hop))
+    text_hop = text_ring.send(text_hop)
     modulations = lax.all_gather(
         mod_own.reshape(slots, 2, 6, width), "tensor", axis=3, tiled=True
     )
+    modulations, text_hop = lax.optimization_barrier((modulations, text_hop))
+    weight_in = (image_in, text_ring.send(text_hop))
     mods = (modulations[:, 0], modulations[:, 1])
 
     tokens = (image_tokens.astype(F32), text_tokens.astype(F32))
@@ -489,37 +496,28 @@
         down = (outgoing[stream] * spread(mod[:, 5])).astype(BF16)
         down_pieces.append(collect(stream, after(down, pieces)))
     parts = packed[0] + packed[1]
-    text_ring = ring_gather(
-        after(jnp.concatenate([text_hidden_in, text_hidden_out.T], axis=1), parts), group_count
-    )
-    text_hop = next(text_ring)
     attended, sums = attend(parts)
-    attended, down_pieces, text_hop = lax.optimization_barrier((attended, down_pieces, text_hop))
-    text_hop = text_ring.send(text_hop)
+    attended, down_pieces = lax.optimization_barrier((attended, down_pieces))
     attended_parts = (attended[:-1], attended[-1:])
 
     middles = [None, None]
     actives = [None, None]
-    mlp_grads = [None, None]
     middle_grads = [None, None]
     branch_grads = [None, None]
     lows = [None, None]
     stats = [None, None]
     upstreams = [None, None]
 
-    def stream_branch(stream, hop):
+    def stream_branch(stream):
         mod = mods[stream]
         branch = reduced(stream, apply(attended_parts[stream], weight_out[stream], 1, False))
-        branch, hop = lax.optimization_barrier((branch, hop))
-        hop = text_ring.send(hop)
         middle = tokens[stream] + spread(mod[:, 2]) * branch
         normed, inverse = norm_rows(middle)
         second_in = normed * (1.0 + spread(mod[:, 4])) + spread(mod[:, 3])
         middles[stream] = middle
-        return (branch, normed, inverse, collect(stream, second_in)), hop
-
-    def stream_back(stream, branch, normed, inverse, pieces, hop=None):
-        mod = mods[stream]
+        return branch, normed, inverse, collect(stream, second_in)
+
+    def stream_products(stream, pieces):
         hidden = apply(pieces, weight_up[stream], 0, False)
         active = [gelu_tanh(value).astype(BF16) for value in hidden]
         active_grad = apply(down_pieces[stream], weight_down[stream], 0, False)
@@ -529,11 +527,12 @@
         ]
         products = apply(hidden_grad, weight_up[stream], 1, False)
         late = after((down_pieces[stream], active, pieces, hidden_grad), products)
-        mlp_grads[stream] = weight_grad([late[:2], late[2:]])
+        actives[stream] = active
+        return products, late
+
+    def stream_back(stream, products, branch, normed, inverse, pieces):
+        mod = mods[stream]
         second_grad = reduced(stream, products)
-        if hop is not None:
-            second_grad, hop = lax.optimization_barrier((second_grad, hop))
-            hop = text_ring.send(hop)
         shift_two_grad = jnp.sum(second_grad, axis=1)
         scale_two_grad = jnp.sum(second_grad * normed, axis=1)
         middle_grad = outgoing[stream] + norm_back(
@@ -544,20 +543,23 @@
         branch_grads[stream] = collect(stream, low)
         upstreams[stream] = apply(branch_grads[stream], weight_out[stream], 0, True)
         middle_grads[stream] = middle_grad
-        actives[stream] = after(active, low)
         stats[stream] = (gate_one_grad, shift_two_grad, scale_two_grad)
-        return hop
-
-    text_state, text_hop = stream_branch(1, text_hop)
-    image_state, text_hop = stream_branch(0, text_hop)
-    for _ in range(group_count // 2 - 4):
-        text_hop = text_ring.send(text_hop)
-    packed_text = text_ring.send(text_hop)
-    weight_up = (packed_image[:, :units], packed_text[:, :units])
-    weight_down = (packed_image[:, units:], packed_text[:, units:])
-    stream_back(1, *text_state)
+        return low
+    image_state = stream_branch(0)
+    text_state = stream_branch(1)
+    weight_up = [packed_mid[:, 2 * width :], None]
+    weight_down = [image_down, None]
+    products, image_late = stream_products(0, image_state[-1])
+    image_low = stream_back(0, products, *image_state)
+    packed_text = after(packed_text, image_low)
+    weight_up[1] = packed_text[:, :units]
+    weight_down[1] = packed_text[:, units:]
+    products, text_late = stream_products(1, text_state[-1])
+    image_late = after(image_late, products)
+    stream_back(1, products, *text_state)
+    mlp_grads = [weight_grad([late[:2], late[2:]]) for late in (image_late, text_late)]
     text_ring = ring_scatter(mlp_grads[1], group_count)
-    text_hop = stream_back(0, *image_state, hop=next(text_ring))
+    text_hop = next(text_ring)
     image_mlp = scattered(mlp_grads[0])
     upstreams, text_hop = lax.optimization_barrier((upstreams, text_hop))
     text_hop = text_ring.send(text_hop)
@@ -575,6 +577,7 @@
     )
     attention_sum = scattered(attention_grad)
     packed_grads = after(packed_grads, attention_grad)
+    actives = after(actives, packed_grads)
     packed_grads = (packed_grads[:-1], packed_grads[-1:])
     outputs = [None, None]
     input_grads = [None, None]
@@ -588,12 +591,8 @@
         outputs[stream] = (result * alive).astype(BF16)
         gate_two_grad = jnp.sum(outgoing[stream] * branch_two, axis=1)
         first_grad = reduced(stream, apply(packed_grads[stream], weight_in[stream], 1, False))
-        if stream == 0:
-            first_grad, image_mlp, text_hop = lax.optimization_barrier(
-                (first_grad, image_mlp, text_hop)
-            )
-            for _ in range(group_count // 2 - 3):
-                text_hop = text_ring.send(text_hop)
+        first_grad, text_hop = lax.optimization_barrier((first_grad, text_hop))
+        text_hop = text_ring.send(text_hop)
         shift_one_grad = jnp.sum(first_grad, axis=1)
         scale_one_grad = jnp.sum(first_grad * normed, axis=1)
         input_grads[stream] = middle_grads[stream] + norm_back(
@@ -610,6 +609,8 @@
             ],
             axis=1,
         )
+    for _ in range(group_count // 2 - 4):
+        text_hop = text_ring.send(text_hop)
     text_mlp = text_hop
 
     image_blocks = jnp.stack(

time: 953 us -> 968 us (1.016)
  waiting for transfers between devices: 374 us -> 403 us
  other arithmetic: 71 us -> 58.7 us
    ppermute x48, waiting for transfers between devices: 211 us -> 323 us  [swap(): return lax.ppermute(value, axis, [(i, i ^ bit) for i in range(size)])]
    reduce_scatter x2, waiting for transfers between devices: 54 us -> 0.01 us  [scattered(): lax.psum_scatter(grad, 'dp', scatter_dimension=0, tiled=True).astype(F32)]
    ppermute x16, waiting for transfers between devices: 96.1 us -> 79.6 us  [ring_step(): return lax.ppermute(value, 'dp', hops)]
    all_gather x2 -> x4, waiting for transfers between devices: 12.7 us -> 0.05 us  [gathered(): return lax.all_gather(joined, 'dp', axis=0, tiled=True)]
    unnamed x371 -> x325, local copies, waits for them, and re-layouts: 22.8 us -> 13.8 us
  transfers between devices with their start and end apart: 68 -> 70, of which waited for: 29 -> 27; matrix products, arithmetic and copies ran while one was open for 28% -> 26% of each run, Pallas kernels for 16% -> 16%
where the time goes in v4:
time: 968 us; the launch traced here: 962 us
  waiting for transfers between devices  403 us (42%)
  Pallas kernels  183 us (19%)
  matrix products  161 us (17%)
  local copies, waits for them, and re-layouts  61.2 us (6%)
  other arithmetic  58.7 us (6%)
  starting transfers between devices  56.9 us (6%)
  between operations  32.9 us (3%)
    ppermute x48, waiting for transfers between devices, swap(): return lax.ppermute(value, axis, [(i, i ^ bit) for i in range(size)])  323 us
    dot_general x46, matrix products, dot(): lax.dot_general(left, right, (((left_dim,), (right_dim,)), ((), ())), pre...  161 us
    ppermute x16, waiting for transfers between devices, ring_step(): return lax.ppermute(value, 'dp', hops)  79.6 us
    pallas_call x8, Pallas kernels, weight_grad(): pl.pallas_call(functools.partial(rows_kernel, count), grid=(rows // step,...  69.2 us
    pallas_call x1, Pallas kernels, attend_back(): pl.pallas_call(functools.partial(attend_back_kernel, count, groups), grid...  58 us
    pallas_call x1, Pallas kernels, attend(): pl.pallas_call(functools.partial(attend_kernel, count), grid=(slots, grou...  55.4 us
    ppermute x48, starting transfers between devices, swap(): return lax.ppermute(value, axis, [(i, i ^ bit) for i in range(size)])  39 us
  transfers between devices with their start and end apart: 70, of which 27 were waited for; matrix products, arithmetic and copies ran while one was open for 26% of the time, Pallas kernels for 16%

profile of v4, /device:TPU:0, one launch (start us, length us, event | category | flops | bytes accessed | tf_op | source)
XLA Modules:
  0.0 962.1 jit_solution(3254773637825413649)
XLA Ops:
  23.0 8.5 collective-permute-done
  58.2 13.1 %collective-permute-done.7 = f32[4,2,4608]{2,1,0:T(2,128)S(1)} collective-permute-done((f32[4,2,4608]{2,1,0:T(2,128)}, f32[4,2,4608]{2,1,0:T(2,128)S(1)}, u32[]{:S(2)}, u32[]{:S(2)}) %collective-permute-start.7) | collective-permute-done | bytes 147488 | tf_op jit(solution)/shard_map/ppermute | solution.py:43
  74.3 8.0 collective-permute-done.8
  88.3 6.5 collective-permute-done.10
  101.4 5.6 all_gather.15
  115.6 28.9 %collective-permute-done.15.refs_2_ = bf16[2,256,1536]{2,1,0:T(8,128)(2,1)S(1)} collective-permute-done((bf16[2,256,1536]{2,1,0:T(8,128)(2,1)S(1)}, bf16[2,256,1536]{2,1,0:T(8,128)(2,1)S(1)}, u32[]{:S(2)}, u32[]{:S(2)}) %collective-permute-start.15) | collective-permute-done | bytes 1572896 | tf_op jit(solution)/shard_map/ppermute | solution.py:43
  167.3 23.1 %collective-permute-done.18.refs_2_ = bf16[2,256,1536]{2,1,0:T(8,128)(2,1)} collective-permute-done((bf16[2,256,1536]{2,1,0:T(8,128)(2,1)S(1)}, bf16[2,256,1536]{2,1,0:T(8,128)(2,1)}, u32[]{:S(2)}, u32[]{:S(2)}) %collective-permute-start.18) | collective-permute-done | bytes 1572896 | tf_op jit(solution)/shard_map/ppermute | solution.py:43
  190.4 55.4 %attend.1 = (bf16[2,256,384]{2,1,0:T(8,128)(2,1)S(1)}, bf16[2,256,384]{2,1,0:T(8,128)(2,1)S(1)}, bf16[2,256,384]{2,1,0:T(8,128)(2,1)S(1)}, bf16[2,256,384]{2,1,0...) custom-call(bf16[2,256,1152]{2,1,0:T(8,128)(2,1)S(1)} %fusion.99.ref, ...), custom_call_target="tpu_custom_call" | custom-call | flops 17051860992 | bytes 7237632 | tf_op jit(solution)/shard_map/attend/pallas_call | solution.py:298
  266.7 50.5 %collective-permute-done.27 = bf16[2,154,1536]{2,0,1:T(2,128)(2,1)} collective-permute-done((bf16[2,154,1536]{2,0,1:T(2,128)(2,1)}, bf16[2,154,1536]{2,0,1:T(2,128)(2,1)}, u32[]{:S(2)}, u32[]{:S(2)}) %collective-permute-start.27) | collective-permute-done | bytes 946208 | tf_op jit(solution)/shard_map/ppermute | solution.py:43
  320.5 6.0 fusion.202
  336.3 27.3 %collective-permute-done.24.refs_2_ = bf16[2,256,1536]{2,1,0:T(8,128)(2,1)S(1)} collective-permute-done((bf16[2,256,1536]{2,1,0:T(8,128)(2,1)S(1)}, bf16[2,256,1536]{2,1,0:T(8,128)(2,1)S(1)}, u32[]{:S(2)}, u32[]{:S(2)}) %collective-permute-start.24) | collective-permute-done | bytes 1572896 | tf_op jit(solution)/shard_map/ppermute | solution.py:43
  369.4 7.8 fusion.76.refs_5_
  377.3 5.6 fusion.195
  383.5 7.2 multiply_convert_fusion.2
  390.7 5.9 fusion.90.refs_7_
  403.7 5.5 fusion.83.refs_6_
  420.4 28.4 %collective-permute-done.30 = bf16[2,256,1536]{2,1,0:T(8,128)(2,1)S(1)} collective-permute-done((bf16[2,256,1536]{2,1,0:T(8,128)(2,1)S(1)}, bf16[2,256,1536]{2,1,0:T(8,128)(2,1)S(1)}, u32[]{:S(2)}, u32[]{:S(2)}) %collective-permute-start.30) | collective-permute-done | bytes 1572896 | tf_op jit(solution)/shard_map/ppermute | solution.py:43
  455.9 5.7 multiply_convert_fusion.9
  468.5 15.3 %weight_grad.14.refs_8_ = bf16[1536,3072]{1,0:T(8,128)(2,1)} custom-call(bf16[2,256,1536]{2,1,0:T(8,128)(2,1)S(1)} %multiply_convert_fusion.6.refs_0_, bf16[2,256,1536]{2,1,0:T(8,128)(2,1)} %collective-permute-done.17.refs_1_, bf16[2,256,1536]{2,1,0:T(8,128)(2,1)} %collective-permute-done.18.refs_2_, bf16[2,256,1536]{2,1,0:T(8,128)(2,1)} %collective-permute-done.19.refs_3_, ...), custom_call_target="tpu_custom_call" | custom-call | bytes 1024 | tf_op jit(solution)/shard_map/weight_grad/pallas_call | solution.py:379
  483.8 15.1 %weight_grad.15 = bf16[1536,3072]{1,0:T(8,128)(2,1)} custom-call(bf16[2,256,1536]{2,1,0:T(8,128)(2,1)S(1)} %copy-done.1, bf16[2,256,1536]{2,1,0:T(8,128)(2,1)S(1)} %copy-done.11, bf16[2,256,1536]{2,1,0:T(8,128)(2,1)S(1)} %copy-done.9, bf16[2,256,1536]{2,1,0:T(8,128)(2,1)} %collective-permute-done.25.refs_3_, ...), custom_call_target="tpu_custom_call", output_to_operand_aliasing={{}: (8, {})} | custom-call | bytes 1024 | tf_op jit(solution)/shard_map/weight_grad/pallas_call | solution.py:379
  546.6 13.9 %collective-permute-done.35 = bf16[2,154,1536]{2,0,1:T(2,128)(2,1)S(1)} collective-permute-done((bf16[2,154,1536]{2,0,1:T(2,128)(2,1)S(1)}, bf16[2,154,1536]{2,0,1:T(2,128)(2,1)S(1)}, u32[]{:S(2)}, u32[]{:S(2)}) %collective-permute-start.35) | collective-permute-done | bytes 946208 | tf_op jit(solution)/shard_map/ppermute | solution.py:43
  568.7 9.8 %collective-permute-done.37 = bf16[192,1536]{1,0:T(8,128)(2,1)S(1)} collective-permute-done((bf16[192,1536]{1,0:T(8,128)(2,1)S(1)}, bf16[192,1536]{1,0:T(8,128)(2,1)S(1)}, u32[]{:S(2)}, u32[]{:S(2)}) %collective-permute-start.37) | collective-permute-done | bytes 589856 | tf_op jit(solution)/shard_map/ppermute | solution.py:113
  582.7 58.0 %attend_back.1 = (bf16[2,256,1152]{2,1,0:T(8,128)(2,1)S(1)}, bf16[2,256,1152]{2,1,0:T(8,128)(2,1)S(1)}, bf16[2,256,1152]{2,1,0:T(8,128)(2,1)}, bf16[2,256,1152]{2,1,0:T(8,128)(2,1)}, bf16[2,154,1152]{2,1,0:T(8,128)(2,1)S(1)}) custom-call(bf16[2,256,1152]{2,1,0:T(8,128)(2,1)} %copy-done.33, bf16[2,256,1152]{2,1,0:T(8,128)(2,1)} %copy-done.35, ...), custom_call_target="tpu_custom_call" | custom-call | flops 42629652480 | bytes 12665856 | tf_op jit(solution)/shard_map/attend_back/pallas_call | solution.py:325
  647.6 12.1 %weight_grad.10.refs_2_ = bf16[1536,3072]{1,0:T(8,128)(2,1)} custom-call(bf16[2,256,1536]{2,1,0:T(8,128)(2,1)} %copy-done.77, bf16[2,256,1536]{2,1,0:T(8,128)(2,1)} %copy-done.82, bf16[2,256,1536]{2,1,0:T(8,128)(2,1)} %copy-done.80, bf16[2,256,1536]{2,1,0:T(8,128)(2,1)} %copy-done.84, bf16[2,256,1152]{2,1,0:T(8,128)(2,1)S(1)} %get-tuple-element.177.refs_4_, ...), custom_call_target="tpu_custom_call" | custom-call | bytes 1024 | tf_op jit(solution)/shard_map/weight_grad/pallas_call | solution.py:379
  664.6 7.5 weight_grad.12.refs_2_
  687.3 6.3 fusion.121
  711.8 6.3 add_convert_fusion.1
  728.1 15.1 %collective-permute-done.49 = bf16[2,154,1536]{2,0,1:T(2,128)(2,1)S(1)} collective-permute-done((bf16[2,154,1536]{2,0,1:T(2,128)(2,1)S(1)}, bf16[2,154,1536]{2,0,1:T(2,128)(2,1)S(1)}, u32[]{:S(2)}, u32[]{:S(2)}) %collective-permute-start.49) | collective-permute-done | bytes 946208 | tf_op jit(solution)/shard_map/ppermute | solution.py:43
  755.6 77.8 %collective-permute-done.44 = bf16[2,154,1536]{2,0,1:T(2,128)(2,1)S(1)} collective-permute-done((bf16[2,154,1536]{2,0,1:T(2,128)(2,1)S(1)}, bf16[2,154,1536]{2,0,1:T(2,128)(2,1)S(1)}, u32[]{:S(2)}, u32[]{:S(2)}) %collective-permute-start.44) | collective-permute-done | bytes 946208 | tf_op jit(solution)/shard_map/ppermute | solution.py:43
  842.0 56.3 %collective-permute-done.53 = bf16[192,3072]{1,0:T(8,128)(2,1)S(1)} collective-permute-done((bf16[192,3072]{1,0:T(8,128)(2,1)S(1)}, bf16[192,3072]{1,0:T(8,128)(2,1)S(1)}, u32[]{:S(2)}, u32[]{:S(2)}) %collective-permute-start.53) | collective-permute-done | bytes 1179680 | tf_op jit(solution)/shard_map/ppermute | solution.py:113
  905.4 5.7 collective-permute-start.56
  940.4 5.7 collective-permute-done.63
  (630 shorter events, 325.2 us)
Async XLA Ops:
  7.2 148.0 %all-gather.5.cloned.1.call-start = ((), (), s32[]{:S(2)}) async-start(), calls=%async_computation.2 | async-start | bytes 3981312 | tf_op jit(solution)/shard_map/all_gather | solution.py:430
  9.1 236.8 %all-gather.7.cloned.1.call-start = ((), (), s32[]{:S(2)}) async-start(), calls=%async_computation.3 | async-start | bytes 7962624 | tf_op jit(solution)/shard_map/all_gather | solution.py:430
  11.4 358.0 %all-gather.11.cloned.1.call-start = ((), (), s32[]{:S(2)}) async-start(), calls=%async_computation.5 | async-start | bytes 5308416 | tf_op jit(solution)/shard_map/all_gather | solution.py:430
  17.4 438.5 %all-gather.9.cloned.1.call-start = ((), (), s32[]{:S(2)}) async-start(), calls=%async_computation.4 | async-start | bytes 10616832 | tf_op jit(solution)/shard_map/all_gather | solution.py:430
  109.0 35.6 %collective-permute-start.15 = (bf16[2,256,1536]{2,1,0:T(8,128)(2,1)S(1)}, bf16[2,256,1536]{2,1,0:T(8,128)(2,1)S(1)}, u32[]{:S(2)}, u32[]{:S(2)}) collective-permute-start(bf16[2,256,1536]{2,1,0:T(8,128)(2,1)S(1)} %fusion.56.refs_0_), channel_id=1, source_target_pairs={{0,2},{1,3},{2,0},{3,1},{4,6},{5,7},{6,4},{7,5},{8,10},{9,11},{10,... | collective-permute-start | bytes 4718600 | tf_op jit(solution)/shard_map/ppermute | solution.py:43
  114.1 38.5 %collective-permute-start.14 = (bf16[2,256,1536]{2,1,0:T(8,128)(2,1)S(1)}, bf16[2,256,1536]{2,1,0:T(8,128)(2,1)S(1)}, u32[]{:S(2)}, u32[]{:S(2)}) collective-permute-start(bf16[2,256,1536]{2,1,0:T(8,128)(2,1)S(1)} %fusion.56.refs_0_), channel_id=1, source_target_pairs={{0,1},{1,0},{2,3},{3,2},{4,5},{5,4},{6,7},{7,6},{8,9},{9,8},{10,11... | collective-permute-start | bytes 4718600 | tf_op jit(solution)/shard_map/ppermute | solution.py:43
  153.7 36.7 %collective-permute-start.18 = (bf16[2,256,1536]{2,1,0:T(8,128)(2,1)S(1)}, bf16[2,256,1536]{2,1,0:T(8,128)(2,1)}, u32[]{:S(2)}, u32[]{:S(2)}) collective-permute-start(bf16[2,256,1536]{2,1,0:T(8,128)(2,1)S(1)} %multiply_convert_fusion.6.refs_0_), channel_id=1, source_target_pairs={{0,2},{1,3},{2,0},{3,1},{4,6},{5,7},{6,4},{7,5},{8,10},{9,11},{10,... | collective-permute-start | bytes 4718600 | tf_op jit(solution)/shard_map/ppermute | solution.py:43
  155.2 90.7 %collective-permute-start.17 = (bf16[2,256,1536]{2,1,0:T(8,128)(2,1)S(1)}, bf16[2,256,1536]{2,1,0:T(8,128)(2,1)}, u32[]{:S(2)}, u32[]{:S(2)}) collective-permute-start(bf16[2,256,1536]{2,1,0:T(8,128)(2,1)S(1)} %multiply_convert_fusion.6.refs_0_), channel_id=1, source_target_pairs={{0,1},{1,0},{2,3},{3,2},{4,5},{5,4},{6,7},{7,6},{8,9},{9,8},{10,11... | collective-permute-start | bytes 4718600 | tf_op jit(solution)/shard_map/ppermute | solution.py:43
  190.4 55.5 %collective-permute-start.19 = (bf16[2,256,1536]{2,1,0:T(8,128)(2,1)}, bf16[2,256,1536]{2,1,0:T(8,128)(2,1)}, u32[]{:S(2)}, u32[]{:S(2)}) collective-permute-start(bf16[2,256,1536]{2,1,0:T(8,128)(2,1)} %collective-permute-done.18.refs_2_), channel_id=1, source_target_pairs={{0,1},{1,0},{2,3},{3,2},{4,5},{5,4},{6,7},{7,6},{8,9},{9,8},{10,11... | collective-permute-start | bytes 4718600 | tf_op jit(solution)/shard_map/ppermute | solution.py:43
  256.4 64.1 %collective-permute-start.20 = (bf16[2,256,1536]{2,1,0:T(8,128)(2,1)}, bf16[2,256,1536]{2,1,0:T(8,128)(2,1)}, u32[]{:S(2)}, u32[]{:S(2)}) collective-permute-start(bf16[2,256,1536]{2,1,0:T(8,128)(2,1)} %convolution_convert_fusion.1), channel_id=1, source_target_pairs={{0,1},{1,0},{2,3},{3,2},{4,5},{5,4},{6,7},{7,6},{8,9},{9,8},{10,11... | collective-permute-start | bytes 4718600 | tf_op jit(solution)/shard_map/ppermute | solution.py:43
  260.3 60.2 %collective-permute-start.22 = (bf16[2,256,1536]{2,1,0:T(8,128)(2,1)}, bf16[2,256,1536]{2,1,0:T(8,128)(2,1)}, u32[]{:S(2)}, u32[]{:S(2)}) collective-permute-start(bf16[2,256,1536]{2,1,0:T(8,128)(2,1)} %fusion.117), channel_id=1, source_target_pairs={{0,2},{1,3},{2,0},{3,1},{4,6},{5,7},{6,4},{7,5},{8,10},{9,11},{10,... | collective-permute-start | bytes 4718600 | tf_op jit(solution)/shard_map/ppermute | solution.py:43
  265.0 52.2 %collective-permute-start.27 = (bf16[2,154,1536]{2,0,1:T(2,128)(2,1)}, bf16[2,154,1536]{2,0,1:T(2,128)(2,1)}, u32[]{:S(2)}, u32[]{:S(2)}) collective-permute-start(bf16[2,154,1536]{2,0,1:T(2,128)(2,1)} %copy.76), channel_id=1, source_target_pairs={{0,2},{1,3},{2,0},{3,1},{4,6},{5,7},{6,4},{7,5},{8,10},{9,11},{10,... | collective-permute-start | bytes 2838536 | tf_op jit(solution)/shard_map/ppermute | solution.py:43
  266.7 680.3 %reduce-scatter.5.cloned.1.call-start = ((), (), s32[]{:S(2)}) async-start(), calls=%async_computation.7 | async-start | bytes 10616832 | tf_op jit(solution)/shard_map/reduce_scatter | solution.py:484
  328.2 35.5 %collective-permute-start.24 = (bf16[2,256,1536]{2,1,0:T(8,128)(2,1)S(1)}, bf16[2,256,1536]{2,1,0:T(8,128)(2,1)S(1)}, u32[]{:S(2)}, u32[]{:S(2)}) collective-permute-start(bf16[2,256,1536]{2,1,0:T(8,128)(2,1)S(1)} %add_convert_fusion.3.refs_0_), channel_id=1, source_target_pairs={{0,2},{1,3},{2,0},{3,1},{4,6},{5,7},{6,4},{7,5},{8,10},{9,11},{10,... | collective-permute-start | bytes 4718600 | tf_op jit(solution)/shard_map/ppermute | solution.py:43
  382.9 37.4 %collective-permute-start.28 = (bf16[2,256,1536]{2,1,0:T(8,128)(2,1)S(1)}, bf16[2,256,1536]{2,1,0:T(8,128)(2,1)S(1)}, u32[]{:S(2)}, u32[]{:S(2)}) collective-permute-start(bf16[2,256,1536]{2,1,0:T(8,128)(2,1)S(1)} %fusion.195), channel_id=1, source_target_pairs={{0,1},{1,0},{2,3},{3,2},{4,5},{5,4},{6,7},{7,6},{8,9},{9,8},{10,11... | collective-permute-start | bytes 4718600 | tf_op jit(solution)/shard_map/ppermute | solution.py:43
  411.9 36.8 %collective-permute-start.30 = (bf16[2,256,1536]{2,1,0:T(8,128)(2,1)S(1)}, bf16[2,256,1536]{2,1,0:T(8,128)(2,1)S(1)}, u32[]{:S(2)}, u32[]{:S(2)}) collective-permute-start(bf16[2,256,1536]{2,1,0:T(8,128)(2,1)S(1)} %add_convert_fusion.2), channel_id=1, source_target_pairs={{0,2},{1,3},{2,0},{3,1},{4,6},{5,7},{6,4},{7,5},{8,10},{9,11},{10,... | collective-permute-start | bytes 4718600 | tf_op jit(solution)/shard_map/ppermute | solution.py:43
  499.0 451.7 %reduce-scatter.3.cloned.1.call-start = ((), (), s32[]{:S(2)}) async-start(), calls=%async_computation.6 | async-start | bytes 10616832 | tf_op jit(solution)/shard_map/reduce_scatter | solution.py:484
  503.4 38.0 %collective-permute-start.32 = (bf16[2,256,1536]{2,1,0:T(8,128)(2,1)S(1)}, bf16[2,256,1536]{2,1,0:T(8,128)(2,1)}, u32[]{:S(2)}, u32[]{:S(2)}) collective-permute-start(bf16[2,256,1536]{2,1,0:T(8,128)(2,1)S(1)} %multiply_convert_fusion.1.refs_0_), channel_id=1, source_target_pairs={{0,2},{1,3},{2,0},{3,1},{4,6},{5,7},{6,4},{7,5},{8,10},{9,11},{10,... | collective-permute-start | bytes 4718600 | tf_op jit(solution)/shard_map/ppermute | solution.py:43
  504.9 39.1 %collective-permute-start.31 = (bf16[2,256,1536]{2,1,0:T(8,128)(2,1)S(1)}, bf16[2,256,1536]{2,1,0:T(8,128)(2,1)}, u32[]{:S(2)}, u32[]{:S(2)}) collective-permute-start(bf16[2,256,1536]{2,1,0:T(8,128)(2,1)S(1)} %multiply_convert_fusion.1.refs_0_), channel_id=1, source_target_pairs={{0,1},{1,0},{2,3},{3,2},{4,5},{5,4},{6,7},{7,6},{8,9},{9,8},{10,11... | collective-permute-start | bytes 4718600 | tf_op jit(solution)/shard_map/ppermute | solution.py:43
  537.0 41.4 %collective-permute-start.37 = (bf16[192,1536]{1,0:T(8,128)(2,1)S(1)}, bf16[192,1536]{1,0:T(8,128)(2,1)S(1)}, u32[]{:S(2)}, u32[]{:S(2)}) collective-permute-start(bf16[192,1536]{1,0:T(8,128)(2,1)S(1)} %get-tuple-element.321), channel_id=1, source_target_pairs={{0,4},{8,0},{16,8},{24,16},{28,24},{20,28},{12,20},{4,12},{1,5},{9... | collective-permute-start | bytes 1769480 | tf_op jit(solution)/shard_map/ppermute | solution.py:113
  538.7 39.7 %collective-permute-start.36 = (bf16[192,1536]{1,0:T(8,128)(2,1)S(1)}, bf16[192,1536]{1,0:T(8,128)(2,1)S(1)}, u32[]{:S(2)}, u32[]{:S(2)}) collective-permute-start(bf16[192,1536]{1,0:T(8,128)(2,1)S(1)} %get-tuple-element.322), channel_id=1, source_target_pairs={{0,8},{8,16},{16,24},{24,28},{28,20},{20,12},{12,4},{4,0},{1,9},{9... | collective-permute-start | bytes 1769480 | tf_op jit(solution)/shard_map/ppermute | solution.py:113
  580.6 60.1 %collective-permute-start.39 = (bf16[192,3072]{1,0:T(8,128)(2,1)S(1)}, bf16[192,3072]{1,0:T(8,128)(2,1)S(1)}, u32[]{:S(2)}, u32[]{:S(2)}) collective-permute-start(bf16[192,3072]{1,0:T(8,128)(2,1)S(1)} %get-tuple-element.319), channel_id=1, source_target_pairs={{0,4},{8,0},{16,8},{24,16},{28,24},{20,28},{12,20},{4,12},{1,5},{9... | collective-permute-start | bytes 3538952 | tf_op jit(solution)/shard_map/ppermute | solution.py:113
  582.5 58.3 %collective-permute-start.38 = (bf16[192,3072]{1,0:T(8,128)(2,1)S(1)}, bf16[192,3072]{1,0:T(8,128)(2,1)S(1)}, u32[]{:S(2)}, u32[]{:S(2)}) collective-permute-start(bf16[192,3072]{1,0:T(8,128)(2,1)S(1)} %get-tuple-element.320), channel_id=1, source_target_pairs={{0,8},{8,16},{16,24},{24,28},{28,20},{20,12},{12,4},{4,0},{1,9},{9... | collective-permute-start | bytes 3538952 | tf_op jit(solution)/shard_map/ppermute | solution.py:113
  645.5 100.0 %collective-permute-start.51 = (bf16[192,3072]{1,0:T(8,128)(2,1)}, bf16[192,3072]{1,0:T(8,128)(2,1)}, u32[]{:S(2)}, u32[]{:S(2)}) collective-permute-start(bf16[192,3072]{1,0:T(8,128)(2,1)} %get-tuple-element.317), channel_id=1, source_target_pairs={{0,4},{8,0},{16,8},{24,16},{28,24},{20,28},{12,20},{4,12},{1,5},{9... | collective-permute-start | bytes 3538952 | tf_op jit(solution)/shard_map/ppermute | solution.py:113
  647.4 98.5 %collective-permute-start.50 = (bf16[192,3072]{1,0:T(8,128)(2,1)}, bf16[192,3072]{1,0:T(8,128)(2,1)}, u32[]{:S(2)}, u32[]{:S(2)}) collective-permute-start(bf16[192,3072]{1,0:T(8,128)(2,1)} %get-tuple-element.318), channel_id=1, source_target_pairs={{0,8},{8,16},{16,24},{24,28},{28,20},{20,12},{12,4},{4,0},{1,9},{9... | collective-permute-start | bytes 3538952 | tf_op jit(solution)/shard_map/ppermute | solution.py:113
  718.2 123.1 %collective-permute-start.45 = (bf16[2,256,1536]{2,1,0:T(8,128)(2,1)S(1)}, bf16[2,256,1536]{2,1,0:T(8,128)(2,1)S(1)}, u32[]{:S(2)}, u32[]{:S(2)}) collective-permute-start(bf16[2,256,1536]{2,1,0:T(8,128)(2,1)S(1)} %copy-done.137), channel_id=1, source_target_pairs={{0,1},{1,0},{2,3},{3,2},{4,5},{5,4},{6,7},{7,6},{8,9},{9,8},{10,11... | collective-permute-start | bytes 4718600 | tf_op jit(solution)/shard_map/ppermute | solution.py:43
  726.5 111.9 %collective-permute-start.40 = (bf16[2,256,1536]{2,1,0:T(8,128)(2,1)}, bf16[2,256,1536]{2,1,0:T(8,128)(2,1)S(1)}, u32[]{:S(2)}, u32[]{:S(2)}) collective-permute-start(bf16[2,256,1536]{2,1,0:T(8,128)(2,1)} %fusion.118), channel_id=1, source_target_pairs={{0,1},{1,0},{2,3},{3,2},{4,5},{5,4},{6,7},{7,6},{8,9},{9,8},{10,11... | collective-permute-start | bytes 4718600 | tf_op jit(solution)/shard_map/ppermute | solution.py:43
  743.2 98.1 %collective-permute-start.47 = (bf16[2,256,1536]{2,1,0:T(8,128)(2,1)}, bf16[2,256,1536]{2,1,0:T(8,128)(2,1)S(1)}, u32[]{:S(2)}, u32[]{:S(2)}) collective-permute-start(bf16[2,256,1536]{2,1,0:T(8,128)(2,1)} %add_convert_fusion), channel_id=1, source_target_pairs={{0,2},{1,3},{2,0},{3,1},{4,6},{5,7},{6,4},{7,5},{8,10},{9,11},{10,... | collective-permute-start | bytes 4718600 | tf_op jit(solution)/shard_map/ppermute | solution.py:43
  745.5 93.2 %collective-permute-start.42 = (bf16[2,256,1536]{2,1,0:T(8,128)(2,1)}, bf16[2,256,1536]{2,1,0:T(8,128)(2,1)S(1)}, u32[]{:S(2)}, u32[]{:S(2)}) collective-permute-start(bf16[2,256,1536]{2,1,0:T(8,128)(2,1)} %add_convert_fusion.1), channel_id=1, source_target_pairs={{0,2},{1,3},{2,0},{3,1},{4,6},{5,7},{6,4},{7,5},{8,10},{9,11},{10,... | collective-permute-start | bytes 4718600 | tf_op jit(solution)/shard_map/ppermute | solution.py:43
  745.9 87.5 %collective-permute-start.44 = (bf16[2,154,1536]{2,0,1:T(2,128)(2,1)S(1)}, bf16[2,154,1536]{2,0,1:T(2,128)(2,1)S(1)}, u32[]{:S(2)}, u32[]{:S(2)}) collective-permute-start(bf16[2,154,1536]{2,0,1:T(2,128)(2,1)S(1)} %copy.84), channel_id=1, source_target_pairs={{0,2},{1,3},{2,0},{3,1},{4,6},{5,7},{6,4},{7,5},{8,10},{9,11},{10,... | collective-permute-start | bytes 2838536 | tf_op jit(solution)/shard_map/ppermute | solution.py:43
  833.4 64.8 %collective-permute-start.53 = (bf16[192,3072]{1,0:T(8,128)(2,1)S(1)}, bf16[192,3072]{1,0:T(8,128)(2,1)S(1)}, u32[]{:S(2)}, u32[]{:S(2)}) collective-permute-start(bf16[192,3072]{1,0:T(8,128)(2,1)S(1)} %get-tuple-element.315), channel_id=1, source_target_pairs={{0,4},{8,0},{16,8},{24,16},{28,24},{20,28},{12,20},{4,12},{1,5},{9... | collective-permute-start | bytes 3538952 | tf_op jit(solution)/shard_map/ppermute | solution.py:113
  838.4 59.9 %collective-permute-start.52 = (bf16[192,3072]{1,0:T(8,128)(2,1)S(1)}, bf16[192,3072]{1,0:T(8,128)(2,1)S(1)}, u32[]{:S(2)}, u32[]{:S(2)}) collective-permute-start(bf16[192,3072]{1,0:T(8,128)(2,1)S(1)} %get-tuple-element.316), channel_id=1, source_target_pairs={{0,8},{8,16},{16,24},{24,28},{28,20},{20,12},{12,4},{4,0},{1,9},{9... | collective-permute-start | bytes 3538952 | tf_op jit(solution)/shard_map/ppermute | solution.py:113
  (190 other events, 3400.0 us)
Sparse Core Ops, SparseCore 0:
  10.8 78.3 all-gather.4
  91.9 110.4 all-gather.6
  204.6 78.0 all-gather.10
  285.3 136.1 all-gather.8
  499.1 212.2 reduce-scatter.4
  714.8 187.1 reduce-scatter.2

commit v5 on v3

--- a/solution.py
+++ b/solution.py
@@ -1,4 +1,5 @@
 import functools
+import math
 
 import jax
 import jax.numpy as jnp
@@ -52,9 +53,11 @@
     return bits
 
 
-def gather_pieces(value, size, axis="tensor"):
+def gather_pieces(value, size, axis="tensor", gate=None):
     have = {0: value}
     for bit in reversed(bits_of(size)):
+        if bit == 1 and gate is not None:
+            have = after(have, gate)
         have.update({k ^ bit: swap(v, bit, size, axis) for k, v in list(have.items())})
     return [have[k] for k in range(size)]
 
@@ -78,16 +81,21 @@
     return value
 
 
-def scatter_sum(pieces, size):
+def scatter_start(pieces, size):
     have = dict(enumerate(pieces))
-    for bit in bits_of(size):
+    for bit in bits_of(size)[:-1]:
         kept = {}
         for k in sorted(have, reverse=True):
             if not k & bit:
                 other = swap(have[k ^ bit].astype(BF16), bit, size)
                 kept[k] = have[k].astype(F32) + other.astype(F32)
         have = kept
-    return have[0]
+    kept, sent = (have[k] for k in sorted(have))
+    return kept, sent.astype(BF16)
+
+
+def scatter_end(kept, sent, size):
+    return kept.astype(F32) + swap(sent, size // 2, size).astype(F32)
 
 
 def after(values, *others):
@@ -160,14 +168,15 @@
     yield own(0) + behind + ahead
 
 
-def text_sum(value, size):
-    for bit in bits_of(size):
-        if bit == 1:
-            value = value + swap(value, bit, size)
-        else:
+def text_start(value, size):
+    for bit in bits_of(size)[:-1]:
+        if bit > 1:
             value = lax.reduce_precision(value, 8, 7)
             value = value + swap(value.astype(BF16), bit, size).astype(F32)
-    return value
+        else:
+            value = value + swap(value, bit, size)
+    value = lax.reduce_precision(value, 8, 7)
+    return value, value.astype(BF16)
 
 
 def lane_mask(half, shape):
@@ -209,20 +218,27 @@
         outs[index][0] = jnp.concatenate(halves, axis=0).T.astype(BF16)
 
 
-def attend_back_kernel(count, groups, *refs):
-    queries, keys, values = refs[:count], refs[count : 2 * count], refs[2 * count : 3 * count]
-    upstreams = refs[3 * count : 4 * count]
-    sums = refs[4 * count : 5 * count]
-    outs = refs[5 * count : 6 * count]
-    key_all, value_all, key_grad, value_grad = refs[6 * count :]
+def attend_back_kernel(count, asked, groups, last, *refs):
+    refs = list(refs)
+
+    def take(number):
+        return [refs.pop(0) for _ in range(number)]
+
+    keys, values = take(count), take(count)
+    queries, upstreams, sums = take(asked), take(asked), take(asked)
+    if last:
+        before = take(2)
+        query_grads = take(count - asked)
+        outs = take(count)
+    else:
+        outs = take(asked)
+        totals = take(2)
+    key_all, value_all, key_grad, value_grad = refs
     load_rows(keys, key_all)
     load_rows(values, value_all)
     pair = pl.program_id(1)
     scale = jnp.asarray(HEAD**-0.5, BF16)
-    query_lanes = pl.ds(pl.multiple_of(pair * LANES, LANES), LANES)
-    key_lanes = pl.ds(pl.multiple_of((groups + pair) * LANES, LANES), LANES)
-    value_lanes = pl.ds(pl.multiple_of((2 * groups + pair) * LANES, LANES), LANES)
-    for index in range(count):
+    for index in range(asked):
         query = queries[index][0] * scale
         upstream = upstreams[index][0]
         halves = []
@@ -236,7 +252,10 @@
             product = weights * along
             score_grad = (product - weights * jnp.sum(product, axis=0, keepdims=True)).astype(BF16)
             key_part = dot(score_grad, query_half, 1, 0)
-            if index == 0 and half == 0:
+            if index == 0 and half == 0 and last:
+                value_grad[...] = before[1][0, 0] + value_part
+                key_grad[...] = before[0][0, 0] + key_part
+            elif index == 0 and half == 0:
                 value_grad[...] = value_part
                 key_grad[...] = key_part
             else:
@@ -244,13 +263,25 @@
                 key_grad[...] += key_part
             mixed = dot(key_all[...], score_grad, 0, 0)
             halves.append(mixed[half * HEAD : (half + 1) * HEAD])
-        query_grad = jnp.concatenate(halves, axis=0).T * HEAD**-0.5
-        outs[index][0, :, query_lanes] = query_grad.astype(BF16)
+        query_grad = (jnp.concatenate(halves, axis=0).T * HEAD**-0.5).astype(BF16)
+        if last:
+            lanes = pl.ds(pl.multiple_of(pair * LANES, LANES), LANES)
+            outs[count - asked + index][0, :, lanes] = query_grad
+        else:
+            outs[index][0] = query_grad
+    if not last:
+        totals[0][0, 0] = key_grad[...]
+        totals[1][0, 0] = value_grad[...]
+        return
+    for index, query_grad in enumerate(query_grads):
+        lanes = pl.ds(pl.multiple_of(pair * LANES, LANES), LANES)
+        outs[index][0, :, lanes] = query_grad[0]
     start = 0
-    for index in range(count):
-        rows = outs[index].shape[1]
-        outs[index][0, :, key_lanes] = key_grad[start : start + rows, :].astype(BF16)
-        outs[index][0, :, value_lanes] = value_grad[start : start + rows, :].astype(BF16)
+    for out in outs:
+        rows = out.shape[1]
+        for number, grad in ((1, key_grad), (2, value_grad)):
+            lanes = pl.ds(pl.multiple_of((number * groups + pair) * LANES, LANES), LANES)
+            out[0, :, lanes] = grad[start : start + rows, :].astype(BF16)
         start += rows
 
 
@@ -313,35 +344,51 @@
     return [narrow(out, 1, width) for out in outs[:count]], outs[count:]
 
 
-def attend_back(parts, upstreams, sums):
+def attend_back(parts, asked, upstreams, sums, before=None):
     slots = parts[0].shape[0]
     width = parts[0].shape[2] // 3
     parts = [widen(part, 3) for part in parts]
     upstreams = [widen(part, 1) for part in upstreams]
+    last = before is not None
     count = len(parts)
+    queries = parts[-asked:] if last else parts[:asked]
     wide = parts[0].shape[2] // 3
     groups = wide // LANES
     total = sum(part.shape[1] for part in parts)
+    whole = pl.BlockSpec((1, 1, total, LANES), lambda s, p: (s, p, 0, 0))
+    ins = lane_blocks(parts, groups) + lane_blocks(parts, 2 * groups) + lane_blocks(queries, 0)
+    ins += lane_blocks(upstreams, 0)
+    ins += [pl.BlockSpec((1, 1, 2, part.shape[1]), lambda s, p: (s, p, 0, 0)) for part in queries]
+    operands = [*parts, *parts, *queries, *upstreams, *sums]
+    if last:
+        query_grads, totals = before
+        ins += [whole, whole] + lane_blocks(query_grads, 0)
+        operands += [*totals, *query_grads]
+        out_specs = [
+            pl.BlockSpec((1, part.shape[1], 3 * wide), lambda s, p: (s, 0, 0)) for part in parts
+        ]
+        out_shape = [
+            jax.ShapeDtypeStruct((slots, part.shape[1], 3 * wide), BF16) for part in parts
+        ]
+    else:
+        out_specs = lane_blocks(queries, 0) + [whole, whole]
+        out_shape = [
+            jax.ShapeDtypeStruct((slots, part.shape[1], wide), BF16) for part in queries
+        ] + [jax.ShapeDtypeStruct((slots, groups, total, LANES), F32)] * 2
     outs = pl.pallas_call(
-        functools.partial(attend_back_kernel, count, groups),
+        functools.partial(attend_back_kernel, count, asked, groups, last),
         grid=(slots, groups),
-        in_specs=lane_blocks(parts, 0)
-        + lane_blocks(parts, groups)
-        + lane_blocks(parts, 2 * groups)
-        + lane_blocks(upstreams, 0)
-        + [
-            pl.BlockSpec((1, 1, 2, part.shape[1]), lambda s, p: (s, p, 0, 0)) for part in parts
-        ],
-        out_specs=[
-            pl.BlockSpec((1, part.shape[1], 3 * wide), lambda s, p: (s, 0, 0)) for part in parts
-        ],
-        out_shape=[jax.ShapeDtypeStruct((slots, part.shape[1], 3 * wide), BF16) for part in parts],
+        in_specs=ins,
+        out_specs=out_specs,
+        out_shape=out_shape,
         scratch_shapes=[pltpu.VMEM((total, LANES), BF16)] * 2 + [pltpu.VMEM((total, LANES), F32)] * 2,
         compiler_params=pltpu.CompilerParams(vmem_limit_bytes=48 * 1024 * 1024),
-        cost_estimate=attention_cost(slots, total, wide, 5),
+        cost_estimate=attention_cost(slots, total, wide, 2 if last else 5),
         name="attend_back",
-    )(*parts, *parts, *parts, *upstreams, *sums)
-    return [narrow(out, 3, width) for out in outs]
+    )(*operands)
+    if last:
+        return [narrow(out, 3, width) for out in outs]
+    return outs[:asked], outs[asked:]
 
 
 def rows_kernel(count, *refs):
@@ -391,6 +438,133 @@
     return joined
 
 
+NO_COST = pl.CostEstimate(flops=0, transcendentals=0, bytes_accessed=1024)
+LIMIT = pltpu.CompilerParams(vmem_limit_bytes=48 * 1024 * 1024)
+
+
+def tile_of(wide, start, most):
+    return max(t for t in range(LANES, most + 1, LANES) if wide % t == 0 and start % t == 0)
+
+
+def fits(weight):
+    _, start, wide = weight
+    return wide % LANES == 0 and start % LANES == 0
+
+
+def cut(weight):
+    array, start, wide = weight
+    return array[:, start : start + wide]
+
+
+def product_kernel(count, weight_dim, *refs):
+    pieces, weight, outs, rows_all = refs[:count], refs[count], refs[count + 1 : -1], refs[-1]
+
+    @pl.when(pl.program_id(1) == 0)
+    def _():
+        load_rows(pieces, rows_all)
+
+    total = dot(rows_all[...], weight[...], 1, weight_dim)
+    start = 0
+    for out in outs:
+        rows = out.shape[1]
+        out[0] = total[start : start + rows].astype(out.dtype)
+        start += rows
+
+
+def products_of(pieces, weight, weight_dim, kinds):
+    array, start, wide = weight
+    if not fits(weight) or (weight_dim and start % wide):
+        return [
+            dot(piece, cut(weight), 2, weight_dim).astype(kind)
+            for piece, kind in zip(pieces, kinds)
+        ]
+    count = len(pieces)
+    slots, _, depth = pieces[0].shape
+    total = sum(piece.shape[1] for piece in pieces)
+    if weight_dim:
+        result = array.shape[0]
+        tile = tile_of(result, 0, 768)
+        block = pl.BlockSpec((tile, wide), lambda s, j: (j, start // wide))
+    else:
+        result = wide
+        tile = tile_of(wide, start, 768)
+        block = pl.BlockSpec((depth, tile), lambda s, j: (0, start // tile + j))
+    return pl.pallas_call(
+        functools.partial(product_kernel, count, weight_dim),
+        grid=(slots, result // tile),
+        in_specs=[
+            pl.BlockSpec((1, piece.shape[1], depth), lambda s, j: (s, 0, 0)) for piece in pieces
+        ]
+        + [block],
+        out_specs=[
+            pl.BlockSpec((1, piece.shape[1], tile), lambda s, j: (s, 0, j)) for piece in pieces
+        ],
+        out_shape=[
+            jax.ShapeDtypeStruct((slots, piece.shape[1], result), kind)
+            for piece, kind in zip(pieces, kinds)
+        ],
+        scratch_shapes=[pltpu.VMEM((total, depth), BF16)],
+        compiler_params=LIMIT,
+        cost_estimate=NO_COST,
+        name="products",
+    )(*pieces, array)
+
+
+def hidden_kernel(count, *refs):
+    pieces, downs, up, down = refs[:count], refs[count : 2 * count], refs[2 * count], refs[2 * count + 1]
+    actives, grads = refs[2 * count + 2 : 3 * count + 2], refs[3 * count + 2 :]
+    for piece, upstream, active, grad in zip(pieces, downs, actives, grads):
+        hidden = dot(piece[0], up[...], 1, 0)
+        active_grad = dot(upstream[0], down[...], 1, 0)
+        square = hidden * hidden
+        scale = (2 / math.pi) ** 0.5
+        bend = jnp.tanh(hidden * (scale + scale * 0.044715 * square))
+        half = 0.5 + 0.5 * bend
+        slope = half + hidden * (0.5 - 0.5 * bend * bend) * (scale + scale * 0.134145 * square)
+        active[0] = (hidden * half).astype(BF16)
+        grad[0] = (active_grad * slope).astype(BF16)
+
+
+def hidden_both(pieces, downs, up, down):
+    count = len(pieces)
+    if not (fits(up) and fits(down)):
+        hidden = [dot(piece, cut(up), 2, 0) for piece in pieces]
+        active_grad = [dot(piece, cut(down), 2, 0) for piece in downs]
+        return (
+            [gelu_tanh(value).astype(BF16) for value in hidden],
+            [
+                jax.vjp(gelu_tanh, value)[1](grad)[0].astype(BF16)
+                for value, grad in zip(hidden, active_grad)
+            ],
+        )
+    slots, _, depth = pieces[0].shape
+    wide = up[2]
+    tile = tile_of(wide, math.gcd(up[1], down[1]), 512)
+    rows = [pl.BlockSpec((1, piece.shape[1], depth), lambda s, j: (s, 0, 0)) for piece in pieces]
+    outs = pl.pallas_call(
+        functools.partial(hidden_kernel, count),
+        grid=(slots, wide // tile),
+        in_specs=rows
+        + rows
+        + [
+            pl.BlockSpec((depth, tile), lambda s, j, o=block[1] // tile: (0, o + j))
+            for block in (up, down)
+        ],
+        out_specs=[
+            pl.BlockSpec((1, piece.shape[1], tile), lambda s, j: (s, 0, j)) for piece in pieces
+        ]
+        * 2,
+        out_shape=[
+            jax.ShapeDtypeStruct((slots, piece.shape[1], wide), BF16) for piece in pieces
+        ]
+        * 2,
+        compiler_params=LIMIT,
+        cost_estimate=NO_COST,
+        name="hidden_both",
+    )(*pieces, *downs, up[0], down[0])
+    return outs[:count], outs[count:]
+
+
 def plain_grad(lefts, rights):
     left = jnp.concatenate([v.reshape(-1, v.shape[-1]) for v in lefts], axis=0)
     right = jnp.concatenate([v.reshape(-1, v.shape[-1]) for v in rights], axis=0)
@@ -429,20 +603,24 @@
         joined = blocks[0] if len(blocks) == 1 else jnp.concatenate(blocks, axis=1)
         return lax.all_gather(joined, "dp", axis=0, tiled=True)
 
-    packed_first = gathered(
-        image_attention_in.reshape(share, 3 * width),
-        text_attention_in.reshape(share, 3 * width),
-        image_attention_out.T,
-        text_attention_out.T,
-    )
-    packed_image = gathered(image_hidden_in, image_hidden_out.T)
-    weight_in = (packed_first[:, : 3 * width], packed_first[:, 3 * width : 6 * width])
-    weight_out = (packed_first[:, 6 * width : 7 * width], packed_first[:, 7 * width :])
+    packed_in = gathered(
+        image_attention_in.reshape(share, 3 * width), text_attention_in.reshape(share, 3 * width)
+    )
+    image_up = gathered(image_hidden_in)
+    image_down = gathered(image_hidden_out.T)
+    text_down = gathered(text_hidden_out.T)
+    out_ring = ring_gather(
+        jnp.concatenate([image_attention_out.T, text_attention_out.T], axis=1), group_count
+    )
+    out_hop = next(out_ring)
+    weight_in = ((packed_in, 0, 3 * width), (packed_in, 3 * width, 3 * width))
 
     alive = (jnp.arange(slots) < group_size[0]).astype(F32)[:, None, None]
     cond_full = condition.astype(F32)
     activated_low = jax.nn.silu(cond_full).astype(BF16)
     activated_all = gather_stack(activated_low, group_count, "dp").reshape(-1, model)
+    activated_all, out_hop = lax.optimization_barrier((activated_all, out_hop))
+    out_hop = out_ring.send(out_hop)
     activated_own = lax.dynamic_slice_in_dim(activated_all, group_rank * share, share, 1)
     all_slots = activated_own.shape[0]
     mod_parts = jnp.concatenate(
@@ -456,150 +634,182 @@
     modulations = lax.all_gather(
         mod_own.reshape(slots, 2, 6, width), "tensor", axis=3, tiled=True
     )
+    modulations, out_hop = lax.optimization_barrier((modulations, out_hop))
+    out_hop = out_ring.send(out_hop)
     mods = (modulations[:, 0], modulations[:, 1])
 
     tokens = (image_tokens.astype(F32), text_tokens.astype(F32))
     outgoing = (image_cotangent.astype(F32) * alive, text_cotangent.astype(F32) * alive)
 
-    def collect(stream, values):
-        values = values.astype(BF16)
-        return [values] if stream else gather_pieces(values, size)
-
-    def apply(pieces, weight, weight_dim, low):
-        return [
-            dot(piece, weight, 2, weight_dim).astype(BF16 if low else F32) for piece in pieces
-        ]
-
-    def reduced(stream, pieces):
-        return text_sum(pieces[0], size) if stream else scatter_sum(pieces, size)
+    half = size // 2
+    near_kinds = [F32] + [BF16] * (half - 1)
+
+    def gathered_rows(values, gate=None):
+        return gather_pieces(values, size, gate=gate)
 
     def scattered(grad):
         return lax.psum_scatter(grad, "dp", scatter_dimension=0, tiled=True).astype(F32)
 
-    first_saved = []
-    packed = []
-    down_pieces = []
-    for stream in range(2):
+    def row_products(pieces, weight, weight_dim):
+        far = products_of(pieces[half:], weight, weight_dim, near_kinds)
+        near = products_of(after(pieces[:half], far), weight, weight_dim, near_kinds)
+        return [*near, *far]
+
+    def image_sum(pieces, weight, weight_dim):
+        return scatter_end(*scatter_start(row_products(pieces, weight, weight_dim), size), size)
+
+    def text_sum(piece, weight, weight_dim):
+        (product,) = products_of([piece], weight, weight_dim, [F32])
+        return scatter_end(*text_start(product, size), size)
+
+    def modulated(values, mod, shift, scale):
+        normed, inverse = norm_rows(values)
+        rows = normed * (1.0 + spread(mod[:, scale])) + spread(mod[:, shift])
+        return normed, inverse, rows.astype(BF16)
+
+    def second_back(stream, second_grad, normed, inverse):
         mod = mods[stream]
-        normed, inverse = norm_rows(tokens[stream])
-        first_in = normed * (1.0 + spread(mod[:, 1])) + spread(mod[:, 0])
-        pieces = collect(stream, first_in)
-        packed.append(apply(pieces, weight_in[stream], 0, True))
-        first_saved.append((normed, inverse, pieces))
-        down = (outgoing[stream] * spread(mod[:, 5])).astype(BF16)
-        down_pieces.append(collect(stream, after(down, pieces)))
-    parts = packed[0] + packed[1]
-    text_ring = ring_gather(
-        after(jnp.concatenate([text_hidden_in, text_hidden_out.T], axis=1), parts), group_count
-    )
-    text_hop = next(text_ring)
-    attended, sums = attend(parts)
-    attended, down_pieces, text_hop = lax.optimization_barrier((attended, down_pieces, text_hop))
-    text_hop = text_ring.send(text_hop)
-    attended_parts = (attended[:-1], attended[-1:])
-
-    middles = [None, None]
-    actives = [None, None]
-    mlp_grads = [None, None]
-    middle_grads = [None, None]
-    branch_grads = [None, None]
-    lows = [None, None]
-    stats = [None, None]
-    upstreams = [None, None]
-
-    def stream_branch(stream, hop):
-        mod = mods[stream]
-        branch = reduced(stream, apply(attended_parts[stream], weight_out[stream], 1, False))
-        branch, hop = lax.optimization_barrier((branch, hop))
-        hop = text_ring.send(hop)
-        middle = tokens[stream] + spread(mod[:, 2]) * branch
-        normed, inverse = norm_rows(middle)
-        second_in = normed * (1.0 + spread(mod[:, 4])) + spread(mod[:, 3])
-        middles[stream] = middle
-        return (branch, normed, inverse, collect(stream, second_in)), hop
-
-    def stream_back(stream, branch, normed, inverse, pieces, hop=None):
-        mod = mods[stream]
-        hidden = apply(pieces, weight_up[stream], 0, False)
-        active = [gelu_tanh(value).astype(BF16) for value in hidden]
-        active_grad = apply(down_pieces[stream], weight_down[stream], 0, False)
-        hidden_grad = [
-            jax.vjp(gelu_tanh, value)[1](grad)[0].astype(BF16)
-            for value, grad in zip(hidden, active_grad)
-        ]
-        products = apply(hidden_grad, weight_up[stream], 1, False)
-        late = after((down_pieces[stream], active, pieces, hidden_grad), products)
-        mlp_grads[stream] = weight_grad([late[:2], late[2:]])
-        second_grad = reduced(stream, products)
-        if hop is not None:
-            second_grad, hop = lax.optimization_barrier((second_grad, hop))
-            hop = text_ring.send(hop)
         shift_two_grad = jnp.sum(second_grad, axis=1)
         scale_two_grad = jnp.sum(second_grad * normed, axis=1)
         middle_grad = outgoing[stream] + norm_back(
             second_grad * (1.0 + spread(mod[:, 4])), normed, inverse
         )
-        gate_one_grad = jnp.sum(middle_grad * branch, axis=1)
         low = (middle_grad * spread(mod[:, 2])).astype(BF16)
-        branch_grads[stream] = collect(stream, low)
-        upstreams[stream] = apply(branch_grads[stream], weight_out[stream], 0, True)
-        middle_grads[stream] = middle_grad
-        actives[stream] = after(active, low)
-        stats[stream] = (gate_one_grad, shift_two_grad, scale_two_grad)
-        return hop
-
-    text_state, text_hop = stream_branch(1, text_hop)
-    image_state, text_hop = stream_branch(0, text_hop)
+        return middle_grad, low, shift_two_grad, scale_two_grad
+
+    low_kinds = [BF16] * size
+
+    normed_one, inverse_one, image_first = modulated(tokens[0], mods[0], 0, 1)
+    text_normed_one, text_inverse_one, text_first = modulated(tokens[1], mods[1], 0, 1)
+    first_pieces = gathered_rows(image_first)
+    first_pieces, out_hop = lax.optimization_barrier((first_pieces, out_hop))
+    for _ in range(group_count // 2 - 3):
+        out_hop = out_ring.send(out_hop)
+    packed = products_of(first_pieces, weight_in[0], 0, low_kinds)
+    text_packed = products_of([text_first], weight_in[1], 0, [BF16])
+    parts = [*packed, *text_packed]
+    down_rows = [
+        (outgoing[stream] * spread(mods[stream][:, 5])).astype(BF16) for stream in range(2)
+    ]
+    up_ring = ring_gather(after(text_hidden_in, first_pieces), group_count)
+    up_hop = next(up_ring)
+    attended, sums = attend(parts)
+    down_pieces = gathered_rows(after(down_rows[0], first_pieces), attended)
+    attended, out_hop, up_hop = lax.optimization_barrier((attended, out_hop, up_hop))
+    both_out = out_ring.send(out_hop)
+    up_hop = up_ring.send(up_hop)
+    weight_out = ((both_out, 0, width), (both_out, width, width))
+    attended_parts = (attended[:-1], attended[-1:])
+
+    branch = image_sum(attended_parts[0], weight_out[0], 1)
+    branch, up_hop = lax.optimization_barrier((branch, up_hop))
+    up_hop = up_ring.send(up_hop)
+    text_branch = text_sum(attended_parts[1][0], weight_out[1], 1)
+    middle = tokens[0] + spread(mods[0][:, 2]) * branch
+    normed_two, inverse_two, image_second = modulated(middle, mods[0], 3, 4)
+    second_pieces = gathered_rows(image_second)
+    up_weight, down_weight = (image_up, 0, units), (image_down, 0, units)
+    near = hidden_both(second_pieces[:half], down_pieces[:half], up_weight, down_weight)
+    far_pieces, up_hop = after((second_pieces[half:], up_hop), near)
+    up_hop = up_ring.send(up_hop)
+    far = hidden_both(far_pieces, down_pieces[half:], up_weight, down_weight)
+    active = [*near[0], *far[0]]
+    hidden_grad = [*near[1], *far[1]]
+    kept, sent = scatter_start(row_products(hidden_grad, up_weight, 1), size)
+    image_mlp_grad = weight_grad(
+        after([(down_pieces, active), (second_pieces, hidden_grad)], sent)
+    )
+    second_grad, up_hop = after((scatter_end(kept, sent, size), up_hop), image_mlp_grad)
+    image_mlp = scattered(image_mlp_grad)
+    middle_grad, low, shift_two_grad, scale_two_grad = second_back(
+        0, second_grad, normed_two, inverse_two
+    )
+    gate_one_grad = jnp.sum(middle_grad * branch, axis=1)
+
+    for _ in range(group_count // 2 - 4):
+        up_hop = up_ring.send(up_hop)
+    text_up, text_down = after((up_ring.send(up_hop), text_down), low)
+    up_weight, text_down_weight = (text_up, 0, units), (text_down, 0, units)
+    text_middle = tokens[1] + spread(mods[1][:, 2]) * text_branch
+    text_normed_two, text_inverse_two, text_second = modulated(text_middle, mods[1], 3, 4)
+    text_active, text_hidden_grad = hidden_both(
+        [text_second], [down_rows[1]], up_weight, text_down_weight
+    )
+    (text_product,) = products_of(text_hidden_grad, up_weight, 1, [F32])
+    text_kept, text_sent = text_start(text_product, size)
+    text_mlp_grad = weight_grad(
+        after([([down_rows[1]], text_active), ([text_second], text_hidden_grad)], text_product)
+    )
+    text_ring = ring_scatter(text_mlp_grad, group_count)
+    text_hop = next(text_ring)
+
+    two_kept, two_sent = scatter_start(
+        row_products(after(active, low), down_weight, 1), size
+    )
+    branch_grads = gathered_rows(low)
+    branch_grads = after(branch_grads, two_sent)
+    upstreams = products_of(branch_grads, weight_out[0], 0, low_kinds)
+    upstreams = after(upstreams, text_sent, text_mlp_grad)
+    first_part = attend_back(parts, size, upstreams, sums[:-1])
+    text_second_grad = scatter_end(text_kept, text_sent, size)
+    branch_two = scatter_end(two_kept, two_sent, size)
+    first_part, text_second_grad, branch_two, text_hop = lax.optimization_barrier(
+        (first_part, text_second_grad, branch_two, text_hop)
+    )
+    text_hop = text_ring.send(text_hop)
+    text_middle_grad, text_low, text_shift_two_grad, text_scale_two_grad = second_back(
+        1, text_second_grad, text_normed_two, text_inverse_two
+    )
+    text_gate_one_grad = jnp.sum(text_middle_grad * text_branch, axis=1)
+    text_upstream = products_of([text_low], weight_out[1], 0, [BF16])
+    packed_grads = attend_back(parts, 1, text_upstream, sums[-1:], first_part)
+    attention_grad = weight_grad(
+        [
+            (first_pieces, packed_grads[:-1]),
+            ([text_first], packed_grads[-1:]),
+            (branch_grads, attended_parts[0]),
+            ([text_low], attended_parts[1]),
+        ]
+    )
+    attention_sum = scattered(attention_grad)
+    packed_grads, text_hop = after((packed_grads, text_hop), attention_grad)
+    text_hop = text_ring.send(text_hop)
+
+    def first_back(stream, first_grad, normed, inverse, middle_grad):
+        mod = mods[stream]
+        shift_one_grad = jnp.sum(first_grad, axis=1)
+        scale_one_grad = jnp.sum(first_grad * normed, axis=1)
+        input_grad = middle_grad + norm_back(
+            first_grad * (1.0 + spread(mod[:, 1])), normed, inverse
+        )
+        return input_grad, shift_one_grad, scale_one_grad
+
+    def finish(stream, middle, branch_two):
+        result = middle + spread(mods[stream][:, 5]) * branch_two
+        gate_two_grad = jnp.sum(outgoing[stream] * branch_two, axis=1)
+        return (result * alive).astype(BF16), gate_two_grad
+
+    first_grad = image_sum(packed_grads[:-1], weight_in[0], 1)
+    text_first_grad = text_sum(packed_grads[-1], weight_in[1], 1)
+    text_branch_two = text_sum(text_active[0], text_down_weight, 1)
+    text_first_grad, text_hop = lax.optimization_barrier((text_first_grad, text_hop))
+    text_hop = text_ring.send(text_hop)
     for _ in range(group_count // 2 - 4):
         text_hop = text_ring.send(text_hop)
-    packed_text = text_ring.send(text_hop)
-    weight_up = (packed_image[:, :units], packed_text[:, :units])
-    weight_down = (packed_image[:, units:], packed_text[:, units:])
-    stream_back(1, *text_state)
-    text_ring = ring_scatter(mlp_grads[1], group_count)
-    text_hop = stream_back(0, *image_state, hop=next(text_ring))
-    image_mlp = scattered(mlp_grads[0])
-    upstreams, text_hop = lax.optimization_barrier((upstreams, text_hop))
-    text_hop = text_ring.send(text_hop)
-
-    packed_grads = attend_back(parts, upstreams[0] + upstreams[1], sums)
-    packed_grads, text_hop = lax.optimization_barrier((packed_grads, text_hop))
-    text_hop = text_ring.send(text_hop)
-    attention_grad = weight_grad(
-        [
-            (first_saved[0][2], packed_grads[:-1]),
-            (first_saved[1][2], packed_grads[-1:]),
-            (branch_grads[0], attended_parts[0]),
-            (branch_grads[1], attended_parts[1]),
-        ]
-    )
-    attention_sum = scattered(attention_grad)
-    packed_grads = after(packed_grads, attention_grad)
-    packed_grads = (packed_grads[:-1], packed_grads[-1:])
+    first_grad, text_hop = lax.optimization_barrier((first_grad, text_hop))
+    text_mlp = text_ring.send(text_hop)
+    input_grads = [None, None]
+    input_grads[0], shift_one_grad, scale_one_grad = first_back(
+        0, first_grad, normed_one, inverse_one, middle_grad
+    )
+    input_grads[1], text_shift_one_grad, text_scale_one_grad = first_back(
+        1, text_first_grad, text_normed_one, text_inverse_one, text_middle_grad
+    )
     outputs = [None, None]
-    input_grads = [None, None]
-    mod_grads = [None, None]
-    for stream in (1, 0):
-        mod = mods[stream]
-        normed, inverse, _ = first_saved[stream]
-        gate_one_grad, shift_two_grad, scale_two_grad = stats[stream]
-        branch_two = reduced(stream, apply(actives[stream], weight_down[stream], 1, False))
-        result = middles[stream] + spread(mod[:, 5]) * branch_two
-        outputs[stream] = (result * alive).astype(BF16)
-        gate_two_grad = jnp.sum(outgoing[stream] * branch_two, axis=1)
-        first_grad = reduced(stream, apply(packed_grads[stream], weight_in[stream], 1, False))
-        if stream == 0:
-            first_grad, image_mlp, text_hop = lax.optimization_barrier(
-                (first_grad, image_mlp, text_hop)
-            )
-            for _ in range(group_count // 2 - 3):
-                text_hop = text_ring.send(text_hop)
-        shift_one_grad = jnp.sum(first_grad, axis=1)
-        scale_one_grad = jnp.sum(first_grad * normed, axis=1)
-        input_grads[stream] = middle_grads[stream] + norm_back(
-            first_grad * (1.0 + spread(mod[:, 1])), normed, inverse
-        )
-        mod_grads[stream] = jnp.stack(
+    outputs[0], gate_two_grad = finish(0, middle, branch_two)
+    outputs[1], text_gate_two_grad = finish(1, text_middle, text_branch_two)
+    mod_grads = (
+        jnp.stack(
             [
                 shift_one_grad,
                 scale_one_grad,
@@ -609,8 +819,19 @@
                 gate_two_grad,
             ],
             axis=1,
-        )
-    text_mlp = text_hop
+        ),
+        jnp.stack(
+            [
+                text_shift_one_grad,
+                text_scale_one_grad,
+                text_gate_one_grad,
+                text_shift_two_grad,
+                text_scale_two_grad,
+                text_gate_two_grad,
+            ],
+            axis=1,
+        ),
+    )
 
     image_blocks = jnp.stack(
         [

time: 953 us -> 972 us (1.020)
  Pallas kernels: 181 us -> 342 us
  matrix products: 163 us -> 7.97 us
  waiting for transfers between devices: 374 us -> 320 us
  local copies, waits for them, and re-layouts: 59.1 us -> 98.3 us
  other arithmetic: 71 us -> 91.4 us
    pallas_call x1 -> x21, Pallas kernels: 57.7 us -> 219 us  [the longest x16 111 us: products_of(): pl.pallas_call(functools.partial(product_kernel, count, weight_dim), grid...]
    dot_general x46 -> x6, matrix products: 163 us -> 7.97 us  [dot(): lax.dot_general(left, right, (((left_dim,), (right_dim,)), ((), ())), pre...]
    reduce_scatter x2, waiting for transfers between devices: 54 us -> 18.5 us  [scattered(): lax.psum_scatter(grad, 'dp', scatter_dimension=0, tiled=True).astype(F32)]
    ppermute x48, waiting for transfers between devices: 211 us -> 187 us  [swap(): return lax.ppermute(value, axis, [(i, i ^ bit) for i in range(size)])]
    ppermute x16 -> x24, waiting for transfers between devices: 96.1 us -> 113 us  [ring_step(): return lax.ppermute(value, 'dp', hops)]
    dynamic_update_slice x9 -> x17, local copies, waits for them, and re-layouts: 3.25 us -> 20.4 us  [put(): return lax.dynamic_update_slice(whole, value, (row, column))]
    unnamed x371 -> x353, local copies, waits for them, and re-layouts: 22.8 us -> 37.7 us
    all_gather x2 -> x4, waiting for transfers between devices: 12.7 us -> 0.04 us  [gathered(): return lax.all_gather(joined, 'dp', axis=0, tiled=True)]
  transfers between devices with their start and end apart: 68 -> 78, of which waited for: 29 -> 27; matrix products, arithmetic and copies ran while one was open for 28% -> 16% of each run, Pallas kernels for 16% -> 36%
where the time goes in v5:
time: 972 us; the launch traced here: 964 us
  Pallas kernels  342 us (35%)
  waiting for transfers between devices  320 us (33%)
  local copies, waits for them, and re-layouts  98.3 us (10%)
  other arithmetic  91.4 us (9%)
  starting transfers between devices  65 us (7%)
  between operations  33.2 us (3%)
    ppermute x48, waiting for transfers between devices, swap(): return lax.ppermute(value, axis, [(i, i ^ bit) for i in range(size)])  187 us
    ppermute x24, waiting for transfers between devices, ring_step(): return lax.ppermute(value, 'dp', hops)  113 us
    pallas_call x16, Pallas kernels, products_of(): pl.pallas_call(functools.partial(product_kernel, count, weight_dim), grid...  111 us
    pallas_call x8, Pallas kernels, weight_grad(): pl.pallas_call(functools.partial(rows_kernel, count), grid=(rows // step,...  68.3 us
    pallas_call x2, Pallas kernels, attend_back(): pl.pallas_call(functools.partial(attend_back_kernel, count, asked, groups...  63.7 us
    pallas_call x1, Pallas kernels, attend(): pl.pallas_call(functools.partial(attend_kernel, count), grid=(slots, grou...  54.8 us
    pallas_call x3, Pallas kernels, hidden_both(): pl.pallas_call(functools.partial(hidden_kernel, count), grid=(slots, wide...  44.1 us
    ppermute x48, starting transfers between devices, swap(): return lax.ppermute(value, axis, [(i, i ^ bit) for i in range(size)])  39.9 us
  transfers between devices with their start and end apart: 78, of which 27 were waited for; matrix products, arithmetic and copies ran while one was open for 16% of the time, Pallas kernels for 36%

profile of v5, /device:TPU:0, one launch (start us, length us, event | category | flops | bytes accessed | tf_op | source)
XLA Modules:
  0.0 963.8 jit_solution(4025998696604297520)
XLA Ops:
  29.1 18.4 %collective-permute-done.2 = bf16[4,2,1536]{2,1,0:T(2,128)(2,1)} collective-permute-done((bf16[4,2,1536]{2,1,0:T(2,128)(2,1)}, bf16[4,2,1536]{2,1,0:T(2,128)(2,1)}, u32[]{:S(2)}, u32[]{:S(2)}) %collective-permute-start.2) | collective-permute-done | bytes 24608 | tf_op jit(solution)/shard_map/ppermute | solution.py:44
  54.4 11.9 %collective-permute-done.5 = f32[4,2,4608]{2,1,0:T(2,128)} collective-permute-done((f32[4,2,4608]{2,1,0:T(2,128)}, f32[4,2,4608]{2,1,0:T(2,128)}, u32[]{:S(2)}, u32[]{:S(2)}) %collective-permute-start.5) | collective-permute-done | bytes 147488 | tf_op jit(solution)/shard_map/ppermute | solution.py:44
  96.3 25.5 %collective-permute-done.11.refs_2_ = bf16[2,256,1536]{2,1,0:T(8,128)(2,1)} collective-permute-done((bf16[2,256,1536]{2,1,0:T(8,128)(2,1)}, bf16[2,256,1536]{2,1,0:T(8,128)(2,1)}, u32[]{:S(2)}, u32[]{:S(2)}) %collective-permute-start.11) | collective-permute-done | bytes 1572896 | tf_op jit(solution)/shard_map/ppermute | solution.py:44
  126.9 11.0 %collective-permute-done.13 = bf16[192,768]{1,0:T(8,128)(2,1)S(1)} collective-permute-done((bf16[192,768]{1,0:T(8,128)(2,1)S(1)}, bf16[192,768]{1,0:T(8,128)(2,1)S(1)}, u32[]{:S(2)}, u32[]{:S(2)}) %collective-permute-start.13) | collective-permute-done | bytes 294944 | tf_op jit(solution)/shard_map/ppermute | solution.py:121
  145.8 14.6 %products.16 = (bf16[2,256,1152]{2,1,0:T(8,128)(2,1)S(1)}, bf16[2,256,1152]{2,1,0:T(8,128)(2,1)S(1)}, bf16[2,256,1152]{2,1,0:T(8,128)(2,1)S(1)}, bf16[2,256,1152]{2,1,0:T(8,128)(2,1)S(1)}) custom-call(bf16[2,256,1536]{2,1,0:T(8,128)(2,1)} %fusion.7.refs_0_, bf16[2,256,1536]{2,1,0:T(8,128)(2,1)} %copy-done.101, ...), custom_call_target="tpu_custom_call" | custom-call | bytes 1024 | tf_op jit(solution)/shard_map/products/pallas_call | solution.py:492
  161.4 7.0 products.17.refs_4_.refs_9_.refs_14_.refs_10_
  168.5 54.8 %attend.1 = (bf16[2,256,384]{2,1,0:T(8,128)(2,1)S(1)}, bf16[2,256,384]{2,1,0:T(8,128)(2,1)S(1)}, bf16[2,256,384]{2,1,0:T(8,128)(2,1)S(1)}, bf16[2,256,384]{2,1,0...) custom-call(bf16[2,256,1152]{2,1,0:T(8,128)(2,1)S(1)} %get-tuple-ele, ...), custom_call_target="tpu_custom_call" | custom-call | flops 17051860992 | bytes 7237632 | tf_op jit(solution)/shard_map/attend/pallas_call | solution.py:329
  242.6 29.9 %collective-permute-done.21 = bf16[2,256,1536]{2,1,0:T(8,128)(2,1)} collective-permute-done((bf16[2,256,1536]{2,1,0:T(8,128)(2,1)}, bf16[2,256,1536]{2,1,0:T(8,128)(2,1)}, u32[]{:S(2)}, u32[]{:S(2)}) %collective-permute-start.21) | collective-permute-done | bytes 1572896 | tf_op jit(solution)/shard_map/ppermute | solution.py:44
  283.4 22.9 %collective-permute-done.25.refs_2_ = bf16[2,256,1536]{2,1,0:T(8,128)(2,1)} collective-permute-done((bf16[2,256,1536]{2,1,0:T(8,128)(2,1)S(1)}, bf16[2,256,1536]{2,1,0:T(8,128)(2,1)}, u32[]{:S(2)}, u32[]{:S(2)}) %collective-permute-start.25) | collective-permute-done | bytes 1572896 | tf_op jit(solution)/shard_map/ppermute | solution.py:44
  306.8 32.3 %collective-permute-done.27.refs_0_.refs_2_ = bf16[2,256,1536]{2,1,0:T(8,128)(2,1)} collective-permute-done((bf16[2,256,1536]{2,1,0:T(8,128)(2,1)S(1)}, bf16[2,256,1536]{2,1,0:T(8,128)(2,1)}, u32[]{:S(2)}, u32[]{:S(2)}) %collective-permute-start.27) | collective-permute-done | bytes 1572896 | tf_op jit(solution)/shard_map/ppermute | solution.py:44
  346.8 17.0 %hidden_both.3 = (bf16[2,256,1536]{2,1,0:T(8,128)(2,1)S(1)}, bf16[2,256,1536]{2,1,0:T(8,128)(2,1)S(1)}, bf16[2,256,1536]{2,1,0:T(8,128)(2,1)S(1)}, bf16[2,256,1536]{2,1,0:T(8,128)(2,1)}) custom-call(bf16[2,256,1536]{2,1,0:T(8,128)(2,1)} %copy-done.10, bf16[2,256,1536]{2,1,0:T(8,128)(2,1)} %copy-done.30, bf16[2,256,1536]{2,1,0:T(8,128)(2,1)} %copy-done.8, ...), custom_call_target="tpu_custom_call" | custom-call | bytes 1024 | tf_op jit(solution)/shard_map/hidden_both/pallas_call | solution.py:544
  366.1 17.6 %hidden_both.4 = (bf16[2,256,1536]{2,1,0:T(8,128)(2,1)S(1)}, bf16[2,256,1536]{2,1,0:T(8,128)(2,1)S(1)}, bf16[2,256,1536]{2,1,0:T(8,128)(2,1)S(1)}, bf16[2,256,1536]{2,1,0:T(8,128)(2,1)}) custom-call(bf16[2,256,1536]{2,1,0:T(8,128)(2,1)} %collective-permute-done.27.refs_0_.refs_2_, bf16[2,256,1536]{2,1,0:T(8,128)(2,1)} %collective-permute-done.28.refs_1_.refs_3_, ...), custom_call_target="tpu_custom_call" | custom-call | bytes 1024 | tf_op jit(solution)/shard_map/hidden_both/pallas_call | solution.py:544
  388.0 8.9 products.20
  409.5 9.1 products.21
  434.1 15.3 %weight_grad.8.refs_8_ = bf16[1536,3072]{1,0:T(8,128)(2,1)} custom-call(bf16[2,256,1536]{2,1,0:T(8,128)(2,1)S(1)} %copy-done.9, bf16[2,256,1536]{2,1,0:T(8,128)(2,1)S(1)} %copy-done.33, bf16[2,256,1536]{2,1,0:T(8,128)(2,1)} %collective-permute-done.25.refs_2_, bf16[2,256,1536]{2,1,0:T(8,128)(2,1)} %collective-permute-done.31.refs_3_, ...), custom_call_target="tpu_custom_call" | custom-call | bytes 1024 | tf_op jit(solution)/shard_map/weight_grad/pallas_call | solution.py:426
  449.4 15.2 %weight_grad.9 = bf16[1536,3072]{1,0:T(8,128)(2,1)} custom-call(bf16[2,256,1536]{2,1,0:T(8,128)(2,1)S(1)} %copy-done.11, bf16[2,256,1536]{2,1,0:T(8,128)(2,1)S(1)} %copy-done.31, bf16[2,256,1536]{2,1,0:T(8,128)(2,1)} %collective-permute-done.27.refs_0_.refs_2_, ...), custom_call_target="tpu_custom_call", output_to_operand_aliasing={{}: (8, {})} | custom-call | bytes 1024 | tf_op jit(solution)/shard_map/weight_grad/pallas_call | solution.py:426
  485.0 9.5 hidden_both.5
  494.5 7.1 products.25
  506.5 9.5 products.22
  540.2 9.4 products.26
  564.4 14.5 %collective-permute-done.44 = bf16[2,154,1536]{2,0,1:T(2,128)(2,1)S(1)} collective-permute-done((bf16[2,154,1536]{2,0,1:T(2,128)(2,1)S(1)}, bf16[2,154,1536]{2,0,1:T(2,128)(2,1)S(1)}, u32[]{:S(2)}, u32[]{:S(2)}) %collective-permute-start.44) | collective-permute-done | bytes 946208 | tf_op jit(solution)/shard_map/ppermute | solution.py:44
  591.1 47.8 %attend_back.2 = (bf16[2,256,384]{2,1,0:T(8,128)(2,1)S(1)}, bf16[2,256,384]{2,1,0:T(8,128)(2,1)S(1)}, bf16[2,256,384]{2,1,0:T(8,128)(2,1)S(1)}, bf16[2,256,384]{...) custom-call(bf16[2,256,1152]{2,1,0:T(8,128)(2,1)S(1)} %copy-done.61, ...), custom_call_target="tpu_custom_call" | custom-call | flops 42629652480 | bytes 12665856 | tf_op jit(solution)/shard_map/attend_back/pallas_call | solution.py:378
  661.5 15.9 %attend_back.3 = (bf16[2,256,1152]{2,1,0:T(8,128)(2,1)S(1)}, bf16[2,256,1152]{2,1,0:T(8,128)(2,1)S(1)}, bf16[2,256,1152]{2,1,0:T(8,128)(2,1)}, bf16[2,256,1152]{2,1,0:T(8,128)(2,1)}, bf16[2,154,1152]{2,1,0:T(8,128)(2,1)S(1)}) custom-call(bf16[2,256,1152]{2,1,0:T(8,128)(2,1)} %copy-done.60, bf16[2,256,1152]{2,1,0:T(8,128)(2,1)} %copy-done.62, ...), custom_call_target="tpu_custom_call" | custom-call | flops 17051860992 | bytes 7237632 | tf_op jit(solution)/shard_map/attend_back/pallas_call | solution.py:378
  680.9 11.6 %weight_grad.12.refs_2_ = bf16[1536,3072]{1,0:T(8,128)(2,1)} custom-call(bf16[2,256,1536]{2,1,0:T(8,128)(2,1)} %fusion.7.refs_0_, bf16[2,256,1536]{2,1,0:T(8,128)(2,1)} %copy-done.101, bf16[2,256,1536]{2,1,0:T(8,128)(2,1)} %collective-permute-done.11.refs_2_, bf16[2,256,1536]{2,1,0:T(8,128)(2,1)} %copy-done.102, ...), custom_call_target="tpu_custom_call" | custom-call | bytes 1024 | tf_op jit(solution)/shard_map/weight_grad/pallas_call | solution.py:426
  697.4 7.2 weight_grad.14.refs_2_
  733.9 9.4 products.29
  760.0 8.0 products.30
  779.5 31.5 %collective-permute-done.58 = bf16[192,3072]{1,0:T(8,128)(2,1)S(1)} collective-permute-done((bf16[192,3072]{1,0:T(8,128)(2,1)}, bf16[192,3072]{1,0:T(8,128)(2,1)S(1)}, u32[]{:S(2)}, u32[]{:S(2)}) %collective-permute-start.58) | collective-permute-done | bytes 1179680 | tf_op jit(solution)/shard_map/ppermute | solution.py:121
  811.0 24.4 %collective-permute-done.59 = bf16[192,3072]{1,0:T(8,128)(2,1)} collective-permute-done((bf16[192,3072]{1,0:T(8,128)(2,1)S(1)}, bf16[192,3072]{1,0:T(8,128)(2,1)}, u32[]{:S(2)}, u32[]{:S(2)}) %collective-permute-start.59) | collective-permute-done | bytes 1179680 | tf_op jit(solution)/shard_map/ppermute | solution.py:121
  845.9 32.2 %collective-permute-done.60 = bf16[192,3072]{1,0:T(8,128)(2,1)S(1)} collective-permute-done((bf16[192,3072]{1,0:T(8,128)(2,1)S(1)}, bf16[192,3072]{1,0:T(8,128)(2,1)S(1)}, u32[]{:S(2)}, u32[]{:S(2)}) %collective-permute-start.60) | collective-permute-done | bytes 1179680 | tf_op jit(solution)/shard_map/ppermute | solution.py:121
  920.9 8.1 collective-permute-done.71
  933.7 18.5 %reduce-scatter.3.cloned.1.call-done = bf16[192,3072]{1,0:T(8,128)(2,1)} async-done(((bf16[1536,3072]{1,0:T(8,128)(2,1)}), bf16[192,3072]{1,0:T(8,128)(2,1)}) %reduce-scatter.3.cloned.1.call-update) | async-done | bytes 1179664 | tf_op jit(solution)/shard_map/reduce_scatter | solution.py:651
  (667 shorter events, 354.6 us)
Async XLA Ops:
  7.2 138.6 %all-gather.5.cloned.1.call-start = ((), (), s32[]{:S(2)}) async-start(), calls=%async_computation.2 | async-start | bytes 7962624 | tf_op jit(solution)/shard_map/all_gather | solution.py:604
  10.4 336.4 %all-gather.7.cloned.1.call-start = ((), (), s32[]{:S(2)}) async-start(), calls=%async_computation.3 | async-start | bytes 5308416 | tf_op jit(solution)/shard_map/all_gather | solution.py:604
  11.1 335.7 %all-gather.9.cloned.1.call-start = ((), (), s32[]{:S(2)}) async-start(), calls=%async_computation.4 | async-start | bytes 5308416 | tf_op jit(solution)/shard_map/all_gather | solution.py:604
  95.8 386.8 %all-gather.11.cloned.1.call-start = ((), (), s32[]{:S(2)}) async-start(), calls=%async_computation.5 | async-start | bytes 5308416 | tf_op jit(solution)/shard_map/all_gather | solution.py:604
  96.2 43.9 %collective-permute-start.10 = (bf16[2,256,1536]{2,1,0:T(8,128)(2,1)}, bf16[2,256,1536]{2,1,0:T(8,128)(2,1)S(1)}, u32[]{:S(2)}, u32[]{:S(2)}) collective-permute-start(bf16[2,256,1536]{2,1,0:T(8,128)(2,1)} %fusion.7.refs_0_), channel_id=1, source_target_pairs={{0,1},{1,0},{2,3},{3,2},{4,5},{5,4},{6,7},{7,6},{8,9},{9,8},{10,11... | collective-permute-start | bytes 4718600 | tf_op jit(solution)/shard_map/ppermute | solution.py:44
  140.1 83.4 %collective-permute-start.17 = (bf16[192,1536]{1,0:T(8,128)(2,1)}, bf16[192,1536]{1,0:T(8,128)(2,1)}, u32[]{:S(2)}, u32[]{:S(2)}) collective-permute-start(bf16[192,1536]{1,0:T(8,128)(2,1)} %param.28), channel_id=1, source_target_pairs={{0,8},{8,16},{16,24},{24,28},{28,20},{20,12},{12,4},{4,0},{1,9},{9... | collective-permute-start | bytes 1769480 | tf_op jit(solution)/shard_map/ppermute | solution.py:121
  140.5 83.0 %collective-permute-start.18 = (bf16[192,1536]{1,0:T(8,128)(2,1)}, bf16[192,1536]{1,0:T(8,128)(2,1)}, u32[]{:S(2)}, u32[]{:S(2)}) collective-permute-start(bf16[192,1536]{1,0:T(8,128)(2,1)} %param.28), channel_id=1, source_target_pairs={{0,4},{8,0},{16,8},{24,16},{28,24},{20,28},{12,20},{4,12},{1,5},{9... | collective-permute-start | bytes 1769480 | tf_op jit(solution)/shard_map/ppermute | solution.py:121
  142.8 80.6 %collective-permute-start.15 = (bf16[192,384]{1,0:T(8,128)(2,1)}, bf16[192,384]{1,0:T(8,128)(2,1)S(1)}, u32[]{:S(2)}, u32[]{:S(2)}) collective-permute-start(bf16[192,384]{1,0:T(8,128)(2,1)} %slice.195), channel_id=1, source_target_pairs={{0,8},{8,16},{16,24},{24,28},{28,20},{20,12},{12,4},{4,0},{1,9},{9... | collective-permute-start | bytes 442376 | tf_op jit(solution)/shard_map/ppermute | solution.py:121
  143.9 79.6 %collective-permute-start.16 = (bf16[192,384]{1,0:T(8,128)(2,1)}, bf16[192,384]{1,0:T(8,128)(2,1)}, u32[]{:S(2)}, u32[]{:S(2)}) collective-permute-start(bf16[192,384]{1,0:T(8,128)(2,1)} %slice.196), channel_id=1, source_target_pairs={{0,4},{8,0},{16,8},{24,16},{28,24},{20,28},{12,20},{4,12},{1,5},{9... | collective-permute-start | bytes 442376 | tf_op jit(solution)/shard_map/ppermute | solution.py:121
  236.5 693.2 %reduce-scatter.5.cloned.1.call-start = ((), (), s32[]{:S(2)}) async-start(), calls=%async_computation.7 | async-start | bytes 10616832 | tf_op jit(solution)/shard_map/reduce_scatter | solution.py:651
  239.8 66.4 %collective-permute-start.25 = (bf16[2,256,1536]{2,1,0:T(8,128)(2,1)S(1)}, bf16[2,256,1536]{2,1,0:T(8,128)(2,1)}, u32[]{:S(2)}, u32[]{:S(2)}) collective-permute-start(bf16[2,256,1536]{2,1,0:T(8,128)(2,1)S(1)} %multiply_convert_fusion.2.refs_2_.refs_0_), channel_id=1, source_target_pairs={{0,2},{1,3},{2,0},{3,1},{4,6},{5,7},{6,4},{7,5},{8,10},{9,11},{10,... | collective-permute-start | bytes 4718600 | tf_op jit(solution)/shard_map/ppermute | solution.py:44
  278.4 60.6 %collective-permute-start.27 = (bf16[2,256,1536]{2,1,0:T(8,128)(2,1)S(1)}, bf16[2,256,1536]{2,1,0:T(8,128)(2,1)}, u32[]{:S(2)}, u32[]{:S(2)}) collective-permute-start(bf16[2,256,1536]{2,1,0:T(8,128)(2,1)S(1)} %add_convert_fusion.3.refs_0_), channel_id=1, source_target_pairs={{0,2},{1,3},{2,0},{3,1},{4,6},{5,7},{6,4},{7,5},{8,10},{9,11},{10,... | collective-permute-start | bytes 4718600 | tf_op jit(solution)/shard_map/ppermute | solution.py:44
  283.3 56.7 %collective-permute-start.41 = (f32[2,154,1536]{2,0,1:T(2,128)S(1)}, f32[2,154,1536]{2,0,1:T(2,128)S(1)}, u32[]{:S(2)}, u32[]{:S(2)}) collective-permute-start(f32[2,154,1536]{2,0,1:T(2,128)S(1)} %copy.74), channel_id=1, source_target_pairs={{0,1},{1,0},{2,3},{3,2},{4,5},{5,4},{6,7},{7,6},{8,9},{9,8},{10,11... | collective-permute-start | bytes 5677064 | tf_op jit(solution)/shard_map/ppermute | solution.py:44
  344.0 61.4 %collective-permute-start.42 = (bf16[2,154,1536]{2,0,1:T(2,128)(2,1)}, bf16[2,154,1536]{2,0,1:T(2,128)(2,1)}, u32[]{:S(2)}, u32[]{:S(2)}) collective-permute-start(bf16[2,154,1536]{2,0,1:T(2,128)(2,1)} %copy.76), channel_id=1, source_target_pairs={{0,2},{1,3},{2,0},{3,1},{4,6},{5,7},{6,4},{7,5},{8,10},{9,11},{10,... | collective-permute-start | bytes 2838536 | tf_op jit(solution)/shard_map/ppermute | solution.py:44
  418.6 50.0 %collective-permute-start.32 = (bf16[2,256,1536]{2,1,0:T(8,128)(2,1)S(1)}, bf16[2,256,1536]{2,1,0:T(8,128)(2,1)}, u32[]{:S(2)}, u32[]{:S(2)}) collective-permute-start(bf16[2,256,1536]{2,1,0:T(8,128)(2,1)S(1)} %get-tuple-element.225), channel_id=1, source_target_pairs={{0,1},{1,0},{2,3},{3,2},{4,5},{5,4},{6,7},{7,6},{8,9},{9,8},{10,11... | collective-permute-start | bytes 4718600 | tf_op jit(solution)/shard_map/ppermute | solution.py:44
  422.1 46.4 %collective-permute-start.34 = (bf16[2,256,1536]{2,1,0:T(8,128)(2,1)}, bf16[2,256,1536]{2,1,0:T(8,128)(2,1)}, u32[]{:S(2)}, u32[]{:S(2)}) collective-permute-start(bf16[2,256,1536]{2,1,0:T(8,128)(2,1)} %add_convert_fusion.2), channel_id=1, source_target_pairs={{0,2},{1,3},{2,0},{3,1},{4,6},{5,7},{6,4},{7,5},{8,10},{9,11},{10,... | collective-permute-start | bytes 4718600 | tf_op jit(solution)/shard_map/ppermute | solution.py:44
  430.2 42.5 %collective-permute-start.35 = (bf16[192,768]{1,0:T(8,128)(2,1)}, bf16[192,768]{1,0:T(8,128)(2,1)}, u32[]{:S(2)}, u32[]{:S(2)}) collective-permute-start(bf16[192,768]{1,0:T(8,128)(2,1)} %slice.200), channel_id=1, source_target_pairs={{0,8},{8,16},{16,24},{24,28},{28,20},{20,12},{12,4},{4,0},{1,9},{9... | collective-permute-start | bytes 884744 | tf_op jit(solution)/shard_map/ppermute | solution.py:121
  464.6 487.6 %reduce-scatter.3.cloned.1.call-start = ((), (), s32[]{:S(2)}) async-start(), calls=%async_computation.6 | async-start | bytes 10616832 | tf_op jit(solution)/shard_map/reduce_scatter | solution.py:651
  505.7 46.6 %collective-permute-start.43 = (f32[2,154,1536]{2,0,1:T(2,128)}, f32[2,154,1536]{2,0,1:T(2,128)}, u32[]{:S(2)}, u32[]{:S(2)}) collective-permute-start(f32[2,154,1536]{2,0,1:T(2,128)} %copy.79), channel_id=1, source_target_pairs={{0,1},{1,0},{2,3},{3,2},{4,5},{5,4},{6,7},{7,6},{8,9},{9,8},{10,11... | collective-permute-start | bytes 5677064 | tf_op jit(solution)/shard_map/ppermute | solution.py:44
  505.7 46.3 %collective-permute-start.38 = (bf16[2,256,1536]{2,1,0:T(8,128)(2,1)S(1)}, bf16[2,256,1536]{2,1,0:T(8,128)(2,1)}, u32[]{:S(2)}, u32[]{:S(2)}) collective-permute-start(bf16[2,256,1536]{2,1,0:T(8,128)(2,1)S(1)} %multiply_convert_fusion.1.refs_0_), channel_id=1, source_target_pairs={{0,2},{1,3},{2,0},{3,1},{4,6},{5,7},{6,4},{7,5},{8,10},{9,11},{10,... | collective-permute-start | bytes 4718600 | tf_op jit(solution)/shard_map/ppermute | solution.py:44
  527.0 54.9 %collective-permute-start.37 = (bf16[2,256,1536]{2,1,0:T(8,128)(2,1)S(1)}, bf16[2,256,1536]{2,1,0:T(8,128)(2,1)S(1)}, u32[]{:S(2)}, u32[]{:S(2)}) collective-permute-start(bf16[2,256,1536]{2,1,0:T(8,128)(2,1)S(1)} %multiply_convert_fusion.1.refs_0_), channel_id=1, source_target_pairs={{0,1},{1,0},{2,3},{3,2},{4,5},{5,4},{6,7},{7,6},{8,9},{9,8},{10,11... | collective-permute-start | bytes 4718600 | tf_op jit(solution)/shard_map/ppermute | solution.py:44
  552.0 86.9 %collective-permute-start.45 = (bf16[2,256,1536]{2,1,0:T(8,128)(2,1)}, bf16[2,256,1536]{2,1,0:T(8,128)(2,1)}, u32[]{:S(2)}, u32[]{:S(2)}) collective-permute-start(bf16[2,256,1536]{2,1,0:T(8,128)(2,1)} %get-tuple-element.289), channel_id=1, source_target_pairs={{0,1},{1,0},{2,3},{3,2},{4,5},{5,4},{6,7},{7,6},{8,9},{9,8},{10,11... | collective-permute-start | bytes 4718600 | tf_op jit(solution)/shard_map/ppermute | solution.py:44
  560.1 85.2 %collective-permute-start.47 = (bf16[192,1536]{1,0:T(8,128)(2,1)}, bf16[192,1536]{1,0:T(8,128)(2,1)}, u32[]{:S(2)}, u32[]{:S(2)}) collective-permute-start(bf16[192,1536]{1,0:T(8,128)(2,1)} %get-tuple-element.418), channel_id=1, source_target_pairs={{0,8},{8,16},{16,24},{24,28},{28,20},{20,12},{12,4},{4,0},{1,9},{9... | collective-permute-start | bytes 1769480 | tf_op jit(solution)/shard_map/ppermute | solution.py:121
  578.9 66.5 %collective-permute-start.48 = (bf16[192,1536]{1,0:T(8,128)(2,1)}, bf16[192,1536]{1,0:T(8,128)(2,1)}, u32[]{:S(2)}, u32[]{:S(2)}) collective-permute-start(bf16[192,1536]{1,0:T(8,128)(2,1)} %get-tuple-element.417), channel_id=1, source_target_pairs={{0,4},{8,0},{16,8},{24,16},{28,24},{20,28},{12,20},{4,12},{1,5},{9... | collective-permute-start | bytes 1769480 | tf_op jit(solution)/shard_map/ppermute | solution.py:121
  582.0 56.9 %collective-permute-start.46 = (bf16[2,256,1536]{2,1,0:T(8,128)(2,1)}, bf16[2,256,1536]{2,1,0:T(8,128)(2,1)S(1)}, u32[]{:S(2)}, u32[]{:S(2)}) collective-permute-start(bf16[2,256,1536]{2,1,0:T(8,128)(2,1)} %add_convert_fusion.1), channel_id=1, source_target_pairs={{0,2},{1,3},{2,0},{3,1},{4,6},{5,7},{6,4},{7,5},{8,10},{9,11},{10,... | collective-permute-start | bytes 4718600 | tf_op jit(solution)/shard_map/ppermute | solution.py:44
  584.0 62.9 %collective-permute-start.50 = (bf16[2,154,1536]{2,0,1:T(2,128)(2,1)}, bf16[2,154,1536]{2,0,1:T(2,128)(2,1)}, u32[]{:S(2)}, u32[]{:S(2)}) collective-permute-start(bf16[2,154,1536]{2,0,1:T(2,128)(2,1)} %copy.85), channel_id=1, source_target_pairs={{0,2},{1,3},{2,0},{3,1},{4,6},{5,7},{6,4},{7,5},{8,10},{9,11},{10,... | collective-permute-start | bytes 2838536 | tf_op jit(solution)/shard_map/ppermute | solution.py:44
  659.5 48.8 %collective-permute-start.51 = (bf16[192,3072]{1,0:T(8,128)(2,1)}, bf16[192,3072]{1,0:T(8,128)(2,1)}, u32[]{:S(2)}, u32[]{:S(2)}) collective-permute-start(bf16[192,3072]{1,0:T(8,128)(2,1)} %get-tuple-element.416), channel_id=1, source_target_pairs={{0,8},{8,16},{16,24},{24,28},{28,20},{20,12},{12,4},{4,0},{1,9},{9... | collective-permute-start | bytes 3538952 | tf_op jit(solution)/shard_map/ppermute | solution.py:121
  660.6 47.7 %collective-permute-start.52 = (bf16[192,3072]{1,0:T(8,128)(2,1)S(1)}, bf16[192,3072]{1,0:T(8,128)(2,1)}, u32[]{:S(2)}, u32[]{:S(2)}) collective-permute-start(bf16[192,3072]{1,0:T(8,128)(2,1)S(1)} %get-tuple-element.415), channel_id=1, source_target_pairs={{0,4},{8,0},{16,8},{24,16},{28,24},{20,28},{12,20},{4,12},{1,5},{9... | collective-permute-start | bytes 3538952 | tf_op jit(solution)/shard_map/ppermute | solution.py:121
  757.9 53.0 %collective-permute-start.58 = (bf16[192,3072]{1,0:T(8,128)(2,1)}, bf16[192,3072]{1,0:T(8,128)(2,1)S(1)}, u32[]{:S(2)}, u32[]{:S(2)}) collective-permute-start(bf16[192,3072]{1,0:T(8,128)(2,1)} %get-tuple-element.414), channel_id=1, source_target_pairs={{0,8},{8,16},{16,24},{24,28},{28,20},{20,12},{12,4},{4,0},{1,9},{9... | collective-permute-start | bytes 3538952 | tf_op jit(solution)/shard_map/ppermute | solution.py:121
  759.4 75.9 %collective-permute-start.59 = (bf16[192,3072]{1,0:T(8,128)(2,1)S(1)}, bf16[192,3072]{1,0:T(8,128)(2,1)}, u32[]{:S(2)}, u32[]{:S(2)}) collective-permute-start(bf16[192,3072]{1,0:T(8,128)(2,1)S(1)} %get-tuple-element.413), channel_id=1, source_target_pairs={{0,4},{8,0},{16,8},{24,16},{28,24},{20,28},{12,20},{4,12},{1,5},{9... | collective-permute-start | bytes 3538952 | tf_op jit(solution)/shard_map/ppermute | solution.py:121
  768.0 77.2 %collective-permute-start.53 = (bf16[2,256,1536]{2,1,0:T(8,128)(2,1)S(1)}, bf16[2,256,1536]{2,1,0:T(8,128)(2,1)S(1)}, u32[]{:S(2)}, u32[]{:S(2)}) collective-permute-start(bf16[2,256,1536]{2,1,0:T(8,128)(2,1)S(1)} %get-tuple-element.315), channel_id=1, source_target_pairs={{0,1},{1,0},{2,3},{3,2},{4,5},{5,4},{6,7},{7,6},{8,9},{9,8},{10,11... | collective-permute-start | bytes 4718600 | tf_op jit(solution)/shard_map/ppermute | solution.py:44
  769.9 75.3 %collective-permute-start.55 = (bf16[2,256,1536]{2,1,0:T(8,128)(2,1)S(1)}, bf16[2,256,1536]{2,1,0:T(8,128)(2,1)S(1)}, u32[]{:S(2)}, u32[]{:S(2)}) collective-permute-start(bf16[2,256,1536]{2,1,0:T(8,128)(2,1)S(1)} %add_convert_fusion), channel_id=1, source_target_pairs={{0,2},{1,3},{2,0},{3,1},{4,6},{5,7},{6,4},{7,5},{8,10},{9,11},{10,... | collective-permute-start | bytes 4718600 | tf_op jit(solution)/shard_map/ppermute | solution.py:44
  (212 other events, 3570.3 us)
Sparse Core Ops, SparseCore 0:
  10.8 129.5 all-gather.4
  142.5 84.8 all-gather.6
  229.6 90.6 all-gather.8
  322.3 87.8 all-gather.10
  464.7 175.0 reduce-scatter.4
  746.1 206.0 reduce-scatter.2

commit v6 on v5

--- a/solution.py
+++ b/solution.py
@@ -53,13 +53,20 @@
     return bits
 
 
-def gather_pieces(value, size, axis="tensor", gate=None):
+def gather_start(value, size, axis="tensor"):
     have = {0: value}
-    for bit in reversed(bits_of(size)):
-        if bit == 1 and gate is not None:
-            have = after(have, gate)
+    for bit in reversed(bits_of(size)[1:]):
         have.update({k ^ bit: swap(v, bit, size, axis) for k, v in list(have.items())})
+    return have
+
+
+def gather_end(have, size, axis="tensor"):
+    have = have | {k ^ 1: swap(v, 1, size, axis) for k, v in have.items()}
     return [have[k] for k in range(size)]
+
+
+def gather_pieces(value, size, axis="tensor"):
+    return gather_end(gather_start(value, size, axis), size, axis)
 
 
 def gather_stack(value, size, axis):
@@ -218,27 +225,20 @@
         outs[index][0] = jnp.concatenate(halves, axis=0).T.astype(BF16)
 
 
-def attend_back_kernel(count, asked, groups, last, *refs):
-    refs = list(refs)
-
-    def take(number):
-        return [refs.pop(0) for _ in range(number)]
-
-    keys, values = take(count), take(count)
-    queries, upstreams, sums = take(asked), take(asked), take(asked)
-    if last:
-        before = take(2)
-        query_grads = take(count - asked)
-        outs = take(count)
-    else:
-        outs = take(asked)
-        totals = take(2)
-    key_all, value_all, key_grad, value_grad = refs
+def attend_back_kernel(count, groups, *refs):
+    queries, keys, values = refs[:count], refs[count : 2 * count], refs[2 * count : 3 * count]
+    upstreams = refs[3 * count : 4 * count]
+    sums = refs[4 * count : 5 * count]
+    outs = refs[5 * count : 6 * count]
+    key_all, value_all, key_grad, value_grad = refs[6 * count :]
     load_rows(keys, key_all)
     load_rows(values, value_all)
     pair = pl.program_id(1)
     scale = jnp.asarray(HEAD**-0.5, BF16)
-    for index in range(asked):
+    query_lanes = pl.ds(pl.multiple_of(pair * LANES, LANES), LANES)
+    key_lanes = pl.ds(pl.multiple_of((groups + pair) * LANES, LANES), LANES)
+    value_lanes = pl.ds(pl.multiple_of((2 * groups + pair) * LANES, LANES), LANES)
+    for index in range(count):
         query = queries[index][0] * scale
         upstream = upstreams[index][0]
         halves = []
@@ -252,10 +252,7 @@
             product = weights * along
             score_grad = (product - weights * jnp.sum(product, axis=0, keepdims=True)).astype(BF16)
             key_part = dot(score_grad, query_half, 1, 0)
-            if index == 0 and half == 0 and last:
-                value_grad[...] = before[1][0, 0] + value_part
-                key_grad[...] = before[0][0, 0] + key_part
-            elif index == 0 and half == 0:
+            if index == 0 and half == 0:
                 value_grad[...] = value_part
                 key_grad[...] = key_part
             else:
@@ -263,25 +260,13 @@
                 key_grad[...] += key_part
             mixed = dot(key_all[...], score_grad, 0, 0)
             halves.append(mixed[half * HEAD : (half + 1) * HEAD])
-        query_grad = (jnp.concatenate(halves, axis=0).T * HEAD**-0.5).astype(BF16)
-        if last:
-            lanes = pl.ds(pl.multiple_of(pair * LANES, LANES), LANES)
-            outs[count - asked + index][0, :, lanes] = query_grad
-        else:
-            outs[index][0] = query_grad
-    if not last:
-        totals[0][0, 0] = key_grad[...]
-        totals[1][0, 0] = value_grad[...]
-        return
-    for index, query_grad in enumerate(query_grads):
-        lanes = pl.ds(pl.multiple_of(pair * LANES, LANES), LANES)
-        outs[index][0, :, lanes] = query_grad[0]
+        query_grad = jnp.concatenate(halves, axis=0).T * HEAD**-0.5
+        outs[index][0, :, query_lanes] = query_grad.astype(BF16)
     start = 0
-    for out in outs:
-        rows = out.shape[1]
-        for number, grad in ((1, key_grad), (2, value_grad)):
-            lanes = pl.ds(pl.multiple_of((number * groups + pair) * LANES, LANES), LANES)
-            out[0, :, lanes] = grad[start : start + rows, :].astype(BF16)
+    for index in range(count):
+        rows = outs[index].shape[1]
+        outs[index][0, :, key_lanes] = key_grad[start : start + rows, :].astype(BF16)
+        outs[index][0, :, value_lanes] = value_grad[start : start + rows, :].astype(BF16)
         start += rows
 
 
@@ -344,51 +329,35 @@
     return [narrow(out, 1, width) for out in outs[:count]], outs[count:]
 
 
-def attend_back(parts, asked, upstreams, sums, before=None):
+def attend_back(parts, upstreams, sums):
     slots = parts[0].shape[0]
     width = parts[0].shape[2] // 3
     parts = [widen(part, 3) for part in parts]
     upstreams = [widen(part, 1) for part in upstreams]
-    last = before is not None
     count = len(parts)
-    queries = parts[-asked:] if last else parts[:asked]
     wide = parts[0].shape[2] // 3
     groups = wide // LANES
     total = sum(part.shape[1] for part in parts)
-    whole = pl.BlockSpec((1, 1, total, LANES), lambda s, p: (s, p, 0, 0))
-    ins = lane_blocks(parts, groups) + lane_blocks(parts, 2 * groups) + lane_blocks(queries, 0)
-    ins += lane_blocks(upstreams, 0)
-    ins += [pl.BlockSpec((1, 1, 2, part.shape[1]), lambda s, p: (s, p, 0, 0)) for part in queries]
-    operands = [*parts, *parts, *queries, *upstreams, *sums]
-    if last:
-        query_grads, totals = before
-        ins += [whole, whole] + lane_blocks(query_grads, 0)
-        operands += [*totals, *query_grads]
-        out_specs = [
+    outs = pl.pallas_call(
+        functools.partial(attend_back_kernel, count, groups),
+        grid=(slots, groups),
+        in_specs=lane_blocks(parts, 0)
+        + lane_blocks(parts, groups)
+        + lane_blocks(parts, 2 * groups)
+        + lane_blocks(upstreams, 0)
+        + [
+            pl.BlockSpec((1, 1, 2, part.shape[1]), lambda s, p: (s, p, 0, 0)) for part in parts
+        ],
+        out_specs=[
             pl.BlockSpec((1, part.shape[1], 3 * wide), lambda s, p: (s, 0, 0)) for part in parts
-        ]
-        out_shape = [
-            jax.ShapeDtypeStruct((slots, part.shape[1], 3 * wide), BF16) for part in parts
-        ]
-    else:
-        out_specs = lane_blocks(queries, 0) + [whole, whole]
-        out_shape = [
-            jax.ShapeDtypeStruct((slots, part.shape[1], wide), BF16) for part in queries
-        ] + [jax.ShapeDtypeStruct((slots, groups, total, LANES), F32)] * 2
-    outs = pl.pallas_call(
-        functools.partial(attend_back_kernel, count, asked, groups, last),
-        grid=(slots, groups),
-        in_specs=ins,
-        out_specs=out_specs,
-        out_shape=out_shape,
+        ],
+        out_shape=[jax.ShapeDtypeStruct((slots, part.shape[1], 3 * wide), BF16) for part in parts],
         scratch_shapes=[pltpu.VMEM((total, LANES), BF16)] * 2 + [pltpu.VMEM((total, LANES), F32)] * 2,
         compiler_params=pltpu.CompilerParams(vmem_limit_bytes=48 * 1024 * 1024),
-        cost_estimate=attention_cost(slots, total, wide, 2 if last else 5),
+        cost_estimate=attention_cost(slots, total, wide, 5),
         name="attend_back",
-    )(*operands)
-    if last:
-        return [narrow(out, 3, width) for out in outs]
-    return outs[:asked], outs[asked:]
+    )(*parts, *parts, *parts, *upstreams, *sums)
+    return [narrow(out, 3, width) for out in outs]
 
 
 def rows_kernel(count, *refs):
@@ -456,22 +425,30 @@
     return array[:, start : start + wide]
 
 
+def row_blocks(ref):
+    slots, rows, columns = ref.shape
+    if rows % 16 == 0:
+        return [(slice(None), ref[...].reshape(slots * rows, columns))]
+    return [(slice(slot, slot + 1), ref[slot]) for slot in range(slots)]
+
+
+def store_rows(ref, place, value):
+    slots = ref.shape[0] if place == slice(None) else 1
+    ref[place] = value.reshape(slots, -1, value.shape[-1]).astype(ref.dtype)
+
+
 def product_kernel(count, weight_dim, *refs):
-    pieces, weight, outs, rows_all = refs[:count], refs[count], refs[count + 1 : -1], refs[-1]
-
-    @pl.when(pl.program_id(1) == 0)
-    def _():
-        load_rows(pieces, rows_all)
-
-    total = dot(rows_all[...], weight[...], 1, weight_dim)
-    start = 0
-    for out in outs:
-        rows = out.shape[1]
-        out[0] = total[start : start + rows].astype(out.dtype)
-        start += rows
-
-
-def products_of(pieces, weight, weight_dim, kinds):
+    pieces, weight, outs = refs[:count], refs[count], refs[count + 1 :]
+    for piece, out in zip(pieces, outs):
+        for place, rows in row_blocks(piece):
+            store_rows(out, place, dot(rows, weight[...], 1, weight_dim))
+
+
+def whole_block(array):
+    return pl.BlockSpec(array.shape, lambda j: (0, 0, 0), pipeline_mode=pl.Buffered(1))
+
+
+def products_of(pieces, weight, weight_dim, kinds, late=False):
     array, start, wide = weight
     if not fits(weight) or (weight_dim and start % wide):
         return [
@@ -480,32 +457,31 @@
         ]
     count = len(pieces)
     slots, _, depth = pieces[0].shape
-    total = sum(piece.shape[1] for piece in pieces)
     if weight_dim:
         result = array.shape[0]
         tile = tile_of(result, 0, 768)
-        block = pl.BlockSpec((tile, wide), lambda s, j: (j, start // wide))
+        block = pl.BlockSpec((tile, wide), lambda j: (j, start // wide))
     else:
         result = wide
         tile = tile_of(wide, start, 768)
-        block = pl.BlockSpec((depth, tile), lambda s, j: (0, start // tile + j))
+        block = pl.BlockSpec((depth, tile), lambda j: (0, start // tile + j))
+    rows = slots * sum(piece.shape[1] for piece in pieces)
+    cost = pl.CostEstimate(
+        flops=4 * rows * depth * result, transcendentals=0, bytes_accessed=4 * rows * result
+    )
     return pl.pallas_call(
         functools.partial(product_kernel, count, weight_dim),
-        grid=(slots, result // tile),
-        in_specs=[
-            pl.BlockSpec((1, piece.shape[1], depth), lambda s, j: (s, 0, 0)) for piece in pieces
-        ]
-        + [block],
+        grid=(result // tile,),
+        in_specs=[whole_block(piece) for piece in pieces] + [block],
         out_specs=[
-            pl.BlockSpec((1, piece.shape[1], tile), lambda s, j: (s, 0, j)) for piece in pieces
+            pl.BlockSpec((slots, piece.shape[1], tile), lambda j: (0, 0, j)) for piece in pieces
         ],
         out_shape=[
             jax.ShapeDtypeStruct((slots, piece.shape[1], result), kind)
             for piece, kind in zip(pieces, kinds)
         ],
-        scratch_shapes=[pltpu.VMEM((total, depth), BF16)],
         compiler_params=LIMIT,
-        cost_estimate=NO_COST,
+        cost_estimate=cost if late else NO_COST,
         name="products",
     )(*pieces, array)
 
@@ -514,15 +490,18 @@
     pieces, downs, up, down = refs[:count], refs[count : 2 * count], refs[2 * count], refs[2 * count + 1]
     actives, grads = refs[2 * count + 2 : 3 * count + 2], refs[3 * count + 2 :]
     for piece, upstream, active, grad in zip(pieces, downs, actives, grads):
-        hidden = dot(piece[0], up[...], 1, 0)
-        active_grad = dot(upstream[0], down[...], 1, 0)
-        square = hidden * hidden
-        scale = (2 / math.pi) ** 0.5
-        bend = jnp.tanh(hidden * (scale + scale * 0.044715 * square))
-        half = 0.5 + 0.5 * bend
-        slope = half + hidden * (0.5 - 0.5 * bend * bend) * (scale + scale * 0.134145 * square)
-        active[0] = (hidden * half).astype(BF16)
-        grad[0] = (active_grad * slope).astype(BF16)
+        for (place, rows), (_, above) in zip(row_blocks(piece), row_blocks(upstream)):
+            hidden = dot(rows, up[...], 1, 0)
+            active_grad = dot(above, down[...], 1, 0)
+            square = hidden * hidden
+            scale = (2 / math.pi) ** 0.5
+            bend = jnp.tanh(hidden * (scale + scale * 0.044715 * square))
+            half = 0.5 + 0.5 * bend
+            slope = half + hidden * (0.5 - 0.5 * bend * bend) * (
+                scale + scale * 0.134145 * square
+            )
+            store_rows(active, place, hidden * half)
+            store_rows(grad, place, active_grad * slope)
 
 
 def hidden_both(pieces, downs, up, down):
@@ -540,18 +519,16 @@
     slots, _, depth = pieces[0].shape
     wide = up[2]
     tile = tile_of(wide, math.gcd(up[1], down[1]), 512)
-    rows = [pl.BlockSpec((1, piece.shape[1], depth), lambda s, j: (s, 0, 0)) for piece in pieces]
     outs = pl.pallas_call(
         functools.partial(hidden_kernel, count),
-        grid=(slots, wide // tile),
-        in_specs=rows
-        + rows
+        grid=(wide // tile,),
+        in_specs=[whole_block(piece) for piece in (*pieces, *downs)]
         + [
-            pl.BlockSpec((depth, tile), lambda s, j, o=block[1] // tile: (0, o + j))
+            pl.BlockSpec((depth, tile), lambda j, o=block[1] // tile: (0, o + j))
             for block in (up, down)
         ],
         out_specs=[
-            pl.BlockSpec((1, piece.shape[1], tile), lambda s, j: (s, 0, j)) for piece in pieces
+            pl.BlockSpec((slots, piece.shape[1], tile), lambda j: (0, 0, j)) for piece in pieces
         ]
         * 2,
         out_shape=[
@@ -608,7 +585,6 @@
     )
     image_up = gathered(image_hidden_in)
     image_down = gathered(image_hidden_out.T)
-    text_down = gathered(text_hidden_out.T)
     out_ring = ring_gather(
         jnp.concatenate([image_attention_out.T, text_attention_out.T], axis=1), group_count
     )
@@ -619,8 +595,6 @@
     cond_full = condition.astype(F32)
     activated_low = jax.nn.silu(cond_full).astype(BF16)
     activated_all = gather_stack(activated_low, group_count, "dp").reshape(-1, model)
-    activated_all, out_hop = lax.optimization_barrier((activated_all, out_hop))
-    out_hop = out_ring.send(out_hop)
     activated_own = lax.dynamic_slice_in_dim(activated_all, group_rank * share, share, 1)
     all_slots = activated_own.shape[0]
     mod_parts = jnp.concatenate(
@@ -644,22 +618,20 @@
     half = size // 2
     near_kinds = [F32] + [BF16] * (half - 1)
 
-    def gathered_rows(values, gate=None):
-        return gather_pieces(values, size, gate=gate)
-
     def scattered(grad):
         return lax.psum_scatter(grad, "dp", scatter_dimension=0, tiled=True).astype(F32)
 
-    def row_products(pieces, weight, weight_dim):
-        far = products_of(pieces[half:], weight, weight_dim, near_kinds)
-        near = products_of(after(pieces[:half], far), weight, weight_dim, near_kinds)
+    def row_products(pieces, weight, weight_dim, late=False):
+        far = products_of(pieces[half:], weight, weight_dim, near_kinds, late)
+        near = products_of(after(pieces[:half], far), weight, weight_dim, near_kinds, late)
         return [*near, *far]
 
-    def image_sum(pieces, weight, weight_dim):
-        return scatter_end(*scatter_start(row_products(pieces, weight, weight_dim), size), size)
-
-    def text_sum(piece, weight, weight_dim):
-        (product,) = products_of([piece], weight, weight_dim, [F32])
+    def image_sum(pieces, weight, weight_dim, late=False):
+        products = row_products(pieces, weight, weight_dim, late)
+        return scatter_end(*scatter_start(products, size), size)
+
+    def text_sum(piece, weight, weight_dim, late=False):
+        (product,) = products_of([piece], weight, weight_dim, [F32], late)
         return scatter_end(*text_start(product, size), size)
 
     def modulated(values, mod, shift, scale):
@@ -681,20 +653,25 @@
 
     normed_one, inverse_one, image_first = modulated(tokens[0], mods[0], 0, 1)
     text_normed_one, text_inverse_one, text_first = modulated(tokens[1], mods[1], 0, 1)
-    first_pieces = gathered_rows(image_first)
+    first_pieces = gather_pieces(image_first, size)
     first_pieces, out_hop = lax.optimization_barrier((first_pieces, out_hop))
-    for _ in range(group_count // 2 - 3):
+    out_hop = out_ring.send(out_hop)
+    for _ in range(group_count // 2 - 4):
         out_hop = out_ring.send(out_hop)
     packed = products_of(first_pieces, weight_in[0], 0, low_kinds)
     text_packed = products_of([text_first], weight_in[1], 0, [BF16])
-    parts = [*packed, *text_packed]
     down_rows = [
         (outgoing[stream] * spread(mods[stream][:, 5])).astype(BF16) for stream in range(2)
     ]
-    up_ring = ring_gather(after(text_hidden_in, first_pieces), group_count)
+    down_have = gather_start(after(down_rows[0], first_pieces), size)
+    parts, out_hop = after(([*packed, *text_packed], out_hop), down_have)
+    out_hop = out_ring.send(out_hop)
+    up_ring = ring_gather(
+        after(jnp.concatenate([text_hidden_in, text_hidden_out.T], axis=1), parts), group_count
+    )
     up_hop = next(up_ring)
     attended, sums = attend(parts)
-    down_pieces = gathered_rows(after(down_rows[0], first_pieces), attended)
+    down_pieces = gather_end(after(down_have, attended), size)
     attended, out_hop, up_hop = lax.optimization_barrier((attended, out_hop, up_hop))
     both_out = out_ring.send(out_hop)
     up_hop = up_ring.send(up_hop)
@@ -707,7 +684,7 @@
     text_branch = text_sum(attended_parts[1][0], weight_out[1], 1)
     middle = tokens[0] + spread(mods[0][:, 2]) * branch
     normed_two, inverse_two, image_second = modulated(middle, mods[0], 3, 4)
-    second_pieces = gathered_rows(image_second)
+    second_pieces = gather_pieces(image_second, size)
     up_weight, down_weight = (image_up, 0, units), (image_down, 0, units)
     near = hidden_both(second_pieces[:half], down_pieces[:half], up_weight, down_weight)
     far_pieces, up_hop = after((second_pieces[half:], up_hop), near)
@@ -716,53 +693,44 @@
     active = [*near[0], *far[0]]
     hidden_grad = [*near[1], *far[1]]
     kept, sent = scatter_start(row_products(hidden_grad, up_weight, 1), size)
-    image_mlp_grad = weight_grad(
-        after([(down_pieces, active), (second_pieces, hidden_grad)], sent)
-    )
-    second_grad, up_hop = after((scatter_end(kept, sent, size), up_hop), image_mlp_grad)
-    image_mlp = scattered(image_mlp_grad)
-    middle_grad, low, shift_two_grad, scale_two_grad = second_back(
-        0, second_grad, normed_two, inverse_two
-    )
-    gate_one_grad = jnp.sum(middle_grad * branch, axis=1)
-
     for _ in range(group_count // 2 - 4):
         up_hop = up_ring.send(up_hop)
-    text_up, text_down = after((up_ring.send(up_hop), text_down), low)
-    up_weight, text_down_weight = (text_up, 0, units), (text_down, 0, units)
+    up_hop = after(up_hop, sent)
+    text_both = up_ring.send(up_hop)
+
+    text_up_weight, text_down_weight = (text_both, 0, units), (text_both, units, units)
     text_middle = tokens[1] + spread(mods[1][:, 2]) * text_branch
     text_normed_two, text_inverse_two, text_second = modulated(text_middle, mods[1], 3, 4)
     text_active, text_hidden_grad = hidden_both(
-        [text_second], [down_rows[1]], up_weight, text_down_weight
-    )
-    (text_product,) = products_of(text_hidden_grad, up_weight, 1, [F32])
-    text_kept, text_sent = text_start(text_product, size)
+        [text_second], [down_rows[1]], text_up_weight, text_down_weight
+    )
+    (text_product,) = products_of(text_hidden_grad, text_up_weight, 1, [F32])
+    text_second_grad = scatter_end(*text_start(text_product, size), size)
+    image_mlp_grad = weight_grad(
+        after([(down_pieces, active), (second_pieces, hidden_grad)], sent)
+    )
+    second_grad = after(scatter_end(kept, sent, size), image_mlp_grad, text_product)
+    image_mlp = scattered(after(image_mlp_grad, second_grad))
+    middle_grad, low, shift_two_grad, scale_two_grad = second_back(
+        0, second_grad, normed_two, inverse_two
+    )
+    gate_one_grad = jnp.sum(middle_grad * branch, axis=1)
+
+    branch_grads = gather_pieces(low, size)
     text_mlp_grad = weight_grad(
-        after([([down_rows[1]], text_active), ([text_second], text_hidden_grad)], text_product)
-    )
-    text_ring = ring_scatter(text_mlp_grad, group_count)
-    text_hop = next(text_ring)
-
-    two_kept, two_sent = scatter_start(
-        row_products(after(active, low), down_weight, 1), size
-    )
-    branch_grads = gathered_rows(low)
-    branch_grads = after(branch_grads, two_sent)
-    upstreams = products_of(branch_grads, weight_out[0], 0, low_kinds)
-    upstreams = after(upstreams, text_sent, text_mlp_grad)
-    first_part = attend_back(parts, size, upstreams, sums[:-1])
-    text_second_grad = scatter_end(text_kept, text_sent, size)
-    branch_two = scatter_end(two_kept, two_sent, size)
-    first_part, text_second_grad, branch_two, text_hop = lax.optimization_barrier(
-        (first_part, text_second_grad, branch_two, text_hop)
-    )
-    text_hop = text_ring.send(text_hop)
+        after([([down_rows[1]], text_active), ([text_second], text_hidden_grad)], low)
+    )
+    upstreams = products_of(after(branch_grads, text_mlp_grad), weight_out[0], 0, low_kinds)
     text_middle_grad, text_low, text_shift_two_grad, text_scale_two_grad = second_back(
         1, text_second_grad, text_normed_two, text_inverse_two
     )
     text_gate_one_grad = jnp.sum(text_middle_grad * text_branch, axis=1)
     text_upstream = products_of([text_low], weight_out[1], 0, [BF16])
-    packed_grads = attend_back(parts, 1, text_upstream, sums[-1:], first_part)
+    text_ring = ring_scatter(after(text_mlp_grad, branch_grads), group_count)
+    text_hop = next(text_ring)
+    packed_grads = attend_back(parts, [*upstreams, *text_upstream], sums)
+    packed_grads, text_hop = lax.optimization_barrier((packed_grads, text_hop))
+    text_hop = text_ring.send(text_hop)
     attention_grad = weight_grad(
         [
             (first_pieces, packed_grads[:-1]),
@@ -772,7 +740,9 @@
         ]
     )
     attention_sum = scattered(attention_grad)
-    packed_grads, text_hop = after((packed_grads, text_hop), attention_grad)
+    packed_grads, text_hop, active, text_active = after(
+        (packed_grads, text_hop, active, text_active), attention_grad
+    )
     text_hop = text_ring.send(text_hop)
 
     def first_back(stream, first_grad, normed, inverse, middle_grad):
@@ -789,9 +759,10 @@
         gate_two_grad = jnp.sum(outgoing[stream] * branch_two, axis=1)
         return (result * alive).astype(BF16), gate_two_grad
 
-    first_grad = image_sum(packed_grads[:-1], weight_in[0], 1)
-    text_first_grad = text_sum(packed_grads[-1], weight_in[1], 1)
-    text_branch_two = text_sum(text_active[0], text_down_weight, 1)
+    first_grad = image_sum(packed_grads[:-1], weight_in[0], 1, True)
+    text_first_grad = text_sum(packed_grads[-1], weight_in[1], 1, True)
+    branch_two = image_sum(active, down_weight, 1, True)
+    text_branch_two = text_sum(text_active[0], text_down_weight, 1, True)
     text_first_grad, text_hop = lax.optimization_barrier((text_first_grad, text_hop))
     text_hop = text_ring.send(text_hop)
     for _ in range(group_count // 2 - 4):

time: 972 us -> 959 us (0.987)
  Pallas kernels: 342 us -> 317 us
  waiting for transfers between devices: 320 us -> 334 us
  starting transfers between devices: 65 us -> 78.1 us
    ppermute x48, waiting for transfers between devices: 187 us -> 299 us  [swap(): return lax.ppermute(value, axis, [(i, i ^ bit) for i in range(size)])]
    ppermute x24, waiting for transfers between devices: 113 us -> 34.7 us  [ring_step(): return lax.ppermute(value, 'dp', hops)]
    reduce_scatter x2, waiting for transfers between devices: 18.5 us -> 0.01 us  [scattered(): lax.psum_scatter(grad, 'dp', scatter_dimension=0, tiled=True).astype(F32)]
    pallas_call x16, Pallas kernels: 111 us -> 95.1 us  [products_of(): pl.pallas_call(functools.partial(product_kernel, count, weight_dim), grid...]
    unnamed x353 -> x305, local copies, waits for them, and re-layouts: 37.7 us -> 26 us
    pallas_call x5 -> x4, Pallas kernels: 108 us -> 98 us  [the longest x1 58 us: attend_back(): pl.pallas_call(functools.partial(attend_back_kernel, count, groups), grid...]
  transfers between devices with their start and end apart: 78 -> 77, of which waited for: 27 -> 32; matrix products, arithmetic and copies ran while one was open for 16% -> 16% of each run, Pallas kernels for 36% -> 31%
where the time goes in v6:
time: 959 us; the launch traced here: 949 us
  waiting for transfers between devices  334 us (35%)
  Pallas kernels  317 us (33%)
  local copies, waits for them, and re-layouts  89.2 us (9%)
  other arithmetic  86.4 us (9%)
  starting transfers between devices  78.1 us (8%)
  between operations  32 us (3%)
    ppermute x48, waiting for transfers between devices, swap(): return lax.ppermute(value, axis, [(i, i ^ bit) for i in range(size)])  299 us
    pallas_call x16, Pallas kernels, products_of(): pl.pallas_call(functools.partial(product_kernel, count, weight_dim), grid...  95.1 us
    pallas_call x8, Pallas kernels, weight_grad(): pl.pallas_call(functools.partial(rows_kernel, count), grid=(rows // step,...  68.8 us
    pallas_call x1, Pallas kernels, attend_back(): pl.pallas_call(functools.partial(attend_back_kernel, count, groups), grid...  58 us
    pallas_call x1, Pallas kernels, attend(): pl.pallas_call(functools.partial(attend_kernel, count), grid=(slots, grou...  54.8 us
    ppermute x48, starting transfers between devices, swap(): return lax.ppermute(value, axis, [(i, i ^ bit) for i in range(size)])  44 us
    pallas_call x3, Pallas kernels, hidden_both(): pl.pallas_call(functools.partial(hidden_kernel, count), grid=(wide // til...  40 us
    ppermute x24, waiting for transfers between devices, ring_step(): return lax.ppermute(value, 'dp', hops)  34.7 us
  transfers between devices with their start and end apart: 77, of which 32 were waited for; matrix products, arithmetic and copies ran while one was open for 16% of the time, Pallas kernels for 31%

profile of v6, /device:TPU:0, one launch (start us, length us, event | category | flops | bytes accessed | tf_op | source)
XLA Modules:
  0.0 949.4 jit_solution(11961386109767111023)
XLA Ops:
  28.1 7.4 collective-permute-done.2
  40.3 13.3 %collective-permute-done.3 = f32[4,2,4608]{2,1,0:T(2,128)} collective-permute-done((f32[4,2,4608]{2,1,0:T(2,128)}, f32[4,2,4608]{2,1,0:T(2,128)}, u32[]{:S(2)}, u32[]{:S(2)}) %collective-permute-start.3) | collective-permute-done | bytes 147488 | tf_op jit(solution)/shard_map/ppermute | solution.py:44
  54.7 7.8 collective-permute-start.4
  82.9 34.4 %collective-permute-done.9.refs_2_ = bf16[2,256,1536]{2,1,0:T(8,128)(2,1)} collective-permute-done((bf16[2,256,1536]{2,1,0:T(8,128)(2,1)}, bf16[2,256,1536]{2,1,0:T(8,128)(2,1)}, u32[]{:S(2)}, u32[]{:S(2)}) %collective-permute-start.9) | collective-permute-done | bytes 1572896 | tf_op jit(solution)/shard_map/ppermute | solution.py:44
  123.0 10.1 %collective-permute-done.11 = bf16[192,768]{1,0:T(8,128)(2,1)} collective-permute-done((bf16[192,768]{1,0:T(8,128)(2,1)}, bf16[192,768]{1,0:T(8,128)(2,1)}, u32[]{:S(2)}, u32[]{:S(2)}) %collective-permute-start.11) | collective-permute-done | bytes 294944 | tf_op jit(solution)/shard_map/ppermute | solution.py:128
  145.4 14.5 %products.16 = (bf16[2,256,1152]{2,1,0:T(8,128)(2,1)S(1)}, bf16[2,256,1152]{2,1,0:T(8,128)(2,1)S(1)}, bf16[2,256,1152]{2,1,0:T(8,128)(2,1)S(1)}, bf16[2,256,1152]{2,1,0:T(8,128)(2,1)S(1)}) custom-call(bf16[2,256,1536]{2,1,0:T(8,128)(2,1)} %fusion.7.refs_0_, bf16[2,256,1536]{2,1,0:T(8,128)(2,1)} %copy-done.95, ...), custom_call_target="tpu_custom_call" | custom-call | bytes 1024 | tf_op jit(solution)/shard_map/products/pallas_call | solution.py:472
  166.0 7.9 collective-permute-done.15.refs_2_
  180.2 54.8 %attend.1 = (bf16[2,256,384]{2,1,0:T(8,128)(2,1)S(1)}, bf16[2,256,384]{2,1,0:T(8,128)(2,1)S(1)}, bf16[2,256,384]{2,1,0:T(8,128)(2,1)S(1)}, bf16[2,256,384]{2,1,0...) custom-call(bf16[2,256,1152]{2,1,0:T(8,128)(2,1)S(1)} %get-tuple-ele, ...), custom_call_target="tpu_custom_call" | custom-call | flops 17051860992 | bytes 7237632 | tf_op jit(solution)/shard_map/attend/pallas_call | solution.py:314
  261.3 29.5 %collective-permute-done.22 = bf16[2,256,1536]{2,1,0:T(8,128)(2,1)S(1)} collective-permute-done((bf16[2,256,1536]{2,1,0:T(8,128)(2,1)}, bf16[2,256,1536]{2,1,0:T(8,128)(2,1)S(1)}, u32[]{:S(2)}, u32[]{:S(2)}) %collective-permute-start.22) | collective-permute-done | bytes 1572896 | tf_op jit(solution)/shard_map/ppermute | solution.py:44
  307.4 33.8 %collective-permute-done.27.refs_0_.refs_2_ = bf16[2,256,1536]{2,1,0:T(8,128)(2,1)} collective-permute-done((bf16[2,256,1536]{2,1,0:T(8,128)(2,1)}, bf16[2,256,1536]{2,1,0:T(8,128)(2,1)}, u32[]{:S(2)}, u32[]{:S(2)}) %collective-permute-start.27) | collective-permute-done | bytes 1572896 | tf_op jit(solution)/shard_map/ppermute | solution.py:44
  343.4 16.9 %collective-permute-done.36 = bf16[2,154,1536]{2,0,1:T(2,128)(2,1)S(1)} collective-permute-done((bf16[2,154,1536]{2,0,1:T(2,128)(2,1)S(1)}, bf16[2,154,1536]{2,0,1:T(2,128)(2,1)S(1)}, u32[]{:S(2)}, u32[]{:S(2)}) %collective-permute-start.36) | collective-permute-done | bytes 946208 | tf_op jit(solution)/shard_map/ppermute | solution.py:44
  373.3 16.2 %hidden_both.3 = (bf16[2,256,1536]{2,1,0:T(8,128)(2,1)S(1)}, bf16[2,256,1536]{2,1,0:T(8,128)(2,1)S(1)}, bf16[2,256,1536]{2,1,0:T(8,128)(2,1)S(1)}, bf16[2,256,1536]{2,1,0:T(8,128)(2,1)}) custom-call(bf16[2,256,1536]{2,1,0:T(8,128)(2,1)} %add_convert_fusion.3.refs_0_, bf16[2,256,1536]{2,1,0:T(8,128)(2,1)} %collective-permute-done.25.refs_1_, ...), custom_call_target="tpu_custom_call" | custom-call | bytes 1024 | tf_op jit(solution)/shard_map/hidden_both/pallas_call | solution.py:522
  390.7 17.1 %hidden_both.4 = (bf16[2,256,1536]{2,1,0:T(8,128)(2,1)S(1)}, bf16[2,256,1536]{2,1,0:T(8,128)(2,1)S(1)}, bf16[2,256,1536]{2,1,0:T(8,128)(2,1)S(1)}, bf16[2,256,1536]{2,1,0:T(8,128)(2,1)}) custom-call(bf16[2,256,1536]{2,1,0:T(8,128)(2,1)} %collective-permute-done.27.refs_0_.refs_2_, bf16[2,256,1536]{2,1,0:T(8,128)(2,1)} %collective-permute-done.28.refs_1_.refs_3_, ...), custom_call_target="tpu_custom_call" | custom-call | bytes 1024 | tf_op jit(solution)/shard_map/hidden_both/pallas_call | solution.py:522
  410.3 7.9 products.20
  423.7 8.2 products.21
  447.8 8.7 collective-permute-done.38
  473.9 15.1 %weight_grad.8.refs_8_ = bf16[1536,3072]{1,0:T(8,128)(2,1)} custom-call(bf16[2,256,1536]{2,1,0:T(8,128)(2,1)} %multiply_convert_fusion.2.refs_2_.refs_0_, bf16[2,256,1536]{2,1,0:T(8,128)(2,1)S(1)} %copy-done.19, bf16[2,256,1536]{2,1,0:T(8,128)(2,1)} %collective-permute-done.15.refs_2_, bf16[2,256,1536]{2,1,0:T(8,128)(2,1)} %collective-permute-done.31.refs_3_, ...), custom_call_target="tpu_custom_call" | custom-call | bytes 1024 | tf_op jit(solution)/shard_map/weight_grad/pallas_call | solution.py:395
  489.0 15.2 %weight_grad.9 = bf16[1536,3072]{1,0:T(8,128)(2,1)} custom-call(bf16[2,256,1536]{2,1,0:T(8,128)(2,1)} %add_convert_fusion.3.refs_0_, bf16[2,256,1536]{2,1,0:T(8,128)(2,1)} %collective-permute-done.25.refs_1_, bf16[2,256,1536]{2,1,0:T(8,128)(2,1)} %collective-permute-done.27.refs_0_.refs_2_, ...), custom_call_target="tpu_custom_call", output_to_operand_aliasing={{}: (8, {})} | custom-call | bytes 1024 | tf_op jit(solution)/shard_map/weight_grad/pallas_call | solution.py:395
  541.2 39.3 %collective-permute-done.43 = bf16[2,154,1536]{2,0,1:T(2,128)(2,1)} collective-permute-done((bf16[2,154,1536]{2,0,1:T(2,128)(2,1)}, bf16[2,154,1536]{2,0,1:T(2,128)(2,1)}, u32[]{:S(2)}, u32[]{:S(2)}) %collective-permute-start.43) | collective-permute-done | bytes 946208 | tf_op jit(solution)/shard_map/ppermute | solution.py:44
  597.1 58.0 %attend_back.1 = (bf16[2,256,1152]{2,1,0:T(8,128)(2,1)S(1)}, bf16[2,256,1152]{2,1,0:T(8,128)(2,1)S(1)}, bf16[2,256,1152]{2,1,0:T(8,128)(2,1)}, bf16[2,256,1152]{2,1,0:T(8,128)(2,1)}, bf16[2,154,1152]{2,1,0:T(8,128)(2,1)S(1)}) custom-call(bf16[2,256,1152]{2,1,0:T(8,128)(2,1)} %copy-done.59, bf16[2,256,1152]{2,1,0:T(8,128)(2,1)} %copy-done.60, ...), custom_call_target="tpu_custom_call" | custom-call | flops 42629652480 | bytes 12665856 | tf_op jit(solution)/shard_map/attend_back/pallas_call | solution.py:341
  680.3 12.0 %weight_grad.12.refs_2_ = bf16[1536,3072]{1,0:T(8,128)(2,1)} custom-call(bf16[2,256,1536]{2,1,0:T(8,128)(2,1)} %fusion.7.refs_0_, bf16[2,256,1536]{2,1,0:T(8,128)(2,1)} %copy-done.95, bf16[2,256,1536]{2,1,0:T(8,128)(2,1)} %collective-permute-done.9.refs_2_, bf16[2,256,1536]{2,1,0:T(8,128)(2,1)} %copy-done.96, ...), custom_call_target="tpu_custom_call" | custom-call | bytes 1024 | tf_op jit(solution)/shard_map/weight_grad/pallas_call | solution.py:395
  697.2 7.5 weight_grad.14.refs_2_
  730.4 8.1 products.26
  738.6 6.9 products.29
  746.0 8.0 products.27
  754.0 7.0 products.30
  773.1 18.0 %collective-permute-done.52 = bf16[2,154,1536]{2,0,1:T(2,128)(2,1)S(1)} collective-permute-done((bf16[2,154,1536]{2,0,1:T(2,128)(2,1)S(1)}, bf16[2,154,1536]{2,0,1:T(2,128)(2,1)S(1)}, u32[]{:S(2)}, u32[]{:S(2)}) %collective-permute-start.52) | collective-permute-done | bytes 946208 | tf_op jit(solution)/shard_map/ppermute | solution.py:44
  795.6 15.4 %collective-permute-done.57 = bf16[2,154,1536]{2,0,1:T(2,128)(2,1)S(1)} collective-permute-done((bf16[2,154,1536]{2,0,1:T(2,128)(2,1)S(1)}, bf16[2,154,1536]{2,0,1:T(2,128)(2,1)S(1)}, u32[]{:S(2)}, u32[]{:S(2)}) %collective-permute-start.57) | collective-permute-done | bytes 946208 | tf_op jit(solution)/shard_map/ppermute | solution.py:44
  822.8 8.8 collective-permute-start.61
  831.9 16.4 %collective-permute-done.50 = bf16[2,256,1536]{2,1,0:T(8,128)(2,1)S(1)} collective-permute-done((bf16[2,256,1536]{2,1,0:T(8,128)(2,1)S(1)}, bf16[2,256,1536]{2,1,0:T(8,128)(2,1)S(1)}, u32[]{:S(2)}, u32[]{:S(2)}) %collective-permute-start.50) | collective-permute-done | bytes 1572896 | tf_op jit(solution)/shard_map/ppermute | solution.py:44
  850.9 30.0 %collective-permute-done.55 = bf16[2,256,1536]{2,1,0:T(8,128)(2,1)S(1)} collective-permute-done((bf16[2,256,1536]{2,1,0:T(8,128)(2,1)S(1)}, bf16[2,256,1536]{2,1,0:T(8,128)(2,1)S(1)}, u32[]{:S(2)}, u32[]{:S(2)}) %collective-permute-start.55) | collective-permute-done | bytes 1572896 | tf_op jit(solution)/shard_map/ppermute | solution.py:44
  902.2 10.2 %collective-permute-done.66 = bf16[4,2,2,6,384]{4,1,3,2,0:T(2,128)(2,1)S(1)} collective-permute-done((bf16[4,2,2,6,384]{4,1,3,2,0:T(2,128)(2,1)S(1)}, bf16[4,2,2,6,384]{4,1,3,2,0:T(2,128)(2,1)S(1)}, u32[]{:S(2)}, u32[]{:S(2)}) %collective-permute-start.66) | collective-permute-done | bytes 73760 | tf_op jit(solution)/shard_map/ppermute | solution.py:44
  (615 shorter events, 353.2 us)
Async XLA Ops:
  7.2 138.2 %all-gather.4.cloned.1.call-start = ((), (), s32[]{:S(2)}) async-start(), calls=%async_computation.2 | async-start | bytes 7962624 | tf_op jit(solution)/shard_map/all_gather | solution.py:581
  10.4 362.9 %all-gather.6.cloned.1.call-start = ((), (), s32[]{:S(2)}) async-start(), calls=%async_computation.3 | async-start | bytes 5308416 | tf_op jit(solution)/shard_map/all_gather | solution.py:581
  18.8 59.6 %collective-permute-start.7 = (bf16[192,768]{1,0:T(8,128)(2,1)}, bf16[192,768]{1,0:T(8,128)(2,1)}, u32[]{:S(2)}, u32[]{:S(2)}) collective-permute-start(bf16[192,768]{1,0:T(8,128)(2,1)} %get-tuple-element.415), channel_id=1, source_target_pairs={{0,4},{8,0},{16,8},{24,16},{28,24},{20,28},{12,20},{4,12},{1,5},{9... | collective-permute-start | bytes 884744 | tf_op jit(solution)/shard_map/ppermute | solution.py:128
  20.2 58.1 %collective-permute-start.6 = (bf16[192,768]{1,0:T(8,128)(2,1)}, bf16[192,768]{1,0:T(8,128)(2,1)}, u32[]{:S(2)}, u32[]{:S(2)}) collective-permute-start(bf16[192,768]{1,0:T(8,128)(2,1)} %get-tuple-element.415), channel_id=1, source_target_pairs={{0,8},{8,16},{16,24},{24,28},{28,20},{20,12},{12,4},{4,0},{1,9},{9... | collective-permute-start | bytes 884744 | tf_op jit(solution)/shard_map/ppermute | solution.py:128
  20.8 352.4 %all-gather.8.cloned.1.call-start = ((), (), s32[]{:S(2)}) async-start(), calls=%async_computation.4 | async-start | bytes 5308416 | tf_op jit(solution)/shard_map/all_gather | solution.py:581
  82.8 54.3 %collective-permute-start.8 = (bf16[2,256,1536]{2,1,0:T(8,128)(2,1)}, bf16[2,256,1536]{2,1,0:T(8,128)(2,1)S(1)}, u32[]{:S(2)}, u32[]{:S(2)}) collective-permute-start(bf16[2,256,1536]{2,1,0:T(8,128)(2,1)} %fusion.7.refs_0_), channel_id=1, source_target_pairs={{0,1},{1,0},{2,3},{3,2},{4,5},{5,4},{6,7},{7,6},{8,9},{9,8},{10,11... | collective-permute-start | bytes 4718600 | tf_op jit(solution)/shard_map/ppermute | solution.py:44
  173.8 68.1 %collective-permute-start.19 = (bf16[192,3072]{1,0:T(8,128)(2,1)S(1)}, bf16[192,3072]{1,0:T(8,128)(2,1)S(1)}, u32[]{:S(2)}, u32[]{:S(2)}) collective-permute-start(bf16[192,3072]{1,0:T(8,128)(2,1)S(1)} %copy-done.98), channel_id=1, source_target_pairs={{0,4},{8,0},{16,8},{24,16},{28,24},{20,28},{12,20},{4,12},{1,5},{9... | collective-permute-start | bytes 3538952 | tf_op jit(solution)/shard_map/ppermute | solution.py:128
  174.8 67.1 %collective-permute-start.18 = (bf16[192,3072]{1,0:T(8,128)(2,1)S(1)}, bf16[192,3072]{1,0:T(8,128)(2,1)}, u32[]{:S(2)}, u32[]{:S(2)}) collective-permute-start(bf16[192,3072]{1,0:T(8,128)(2,1)S(1)} %copy-done.98), channel_id=1, source_target_pairs={{0,8},{8,16},{16,24},{24,28},{28,20},{20,12},{12,4},{4,0},{1,9},{9... | collective-permute-start | bytes 3538952 | tf_op jit(solution)/shard_map/ppermute | solution.py:128
  177.7 64.2 %collective-permute-start.17 = (bf16[192,384]{1,0:T(8,128)(2,1)S(1)}, bf16[192,384]{1,0:T(8,128)(2,1)S(1)}, u32[]{:S(2)}, u32[]{:S(2)}) collective-permute-start(bf16[192,384]{1,0:T(8,128)(2,1)S(1)} %slice.197), channel_id=1, source_target_pairs={{0,4},{8,0},{16,8},{24,16},{28,24},{20,28},{12,20},{4,12},{1,5},{9... | collective-permute-start | bytes 442376 | tf_op jit(solution)/shard_map/ppermute | solution.py:128
  178.8 63.1 %collective-permute-start.16 = (bf16[192,384]{1,0:T(8,128)(2,1)S(1)}, bf16[192,384]{1,0:T(8,128)(2,1)S(1)}, u32[]{:S(2)}, u32[]{:S(2)}) collective-permute-start(bf16[192,384]{1,0:T(8,128)(2,1)S(1)} %slice.196), channel_id=1, source_target_pairs={{0,8},{8,16},{16,24},{24,28},{28,20},{20,12},{12,4},{4,0},{1,9},{9... | collective-permute-start | bytes 442376 | tf_op jit(solution)/shard_map/ppermute | solution.py:128
  245.4 689.1 %reduce-scatter.5.cloned.1.call-start = ((), (), s32[]{:S(2)}) async-start(), calls=%async_computation.6 | async-start | bytes 10616832 | tf_op jit(solution)/shard_map/reduce_scatter | solution.py:622
  306.6 53.8 %collective-permute-start.36 = (bf16[2,154,1536]{2,0,1:T(2,128)(2,1)S(1)}, bf16[2,154,1536]{2,0,1:T(2,128)(2,1)S(1)}, u32[]{:S(2)}, u32[]{:S(2)}) collective-permute-start(bf16[2,154,1536]{2,0,1:T(2,128)(2,1)S(1)} %copy.76), channel_id=1, source_target_pairs={{0,2},{1,3},{2,0},{3,1},{4,6},{5,7},{6,4},{7,5},{8,10},{9,11},{10,... | collective-permute-start | bytes 2838536 | tf_op jit(solution)/shard_map/ppermute | solution.py:44
  307.2 66.1 %collective-permute-start.25 = (bf16[2,256,1536]{2,1,0:T(8,128)(2,1)}, bf16[2,256,1536]{2,1,0:T(8,128)(2,1)}, u32[]{:S(2)}, u32[]{:S(2)}) collective-permute-start(bf16[2,256,1536]{2,1,0:T(8,128)(2,1)} %add_convert_fusion.3.refs_0_), channel_id=1, source_target_pairs={{0,1},{1,0},{2,3},{3,2},{4,5},{5,4},{6,7},{7,6},{8,9},{9,8},{10,11... | collective-permute-start | bytes 4718600 | tf_op jit(solution)/shard_map/ppermute | solution.py:44
  341.2 49.4 %collective-permute-start.28 = (bf16[2,256,1536]{2,1,0:T(8,128)(2,1)}, bf16[2,256,1536]{2,1,0:T(8,128)(2,1)}, u32[]{:S(2)}, u32[]{:S(2)}) collective-permute-start(bf16[2,256,1536]{2,1,0:T(8,128)(2,1)} %collective-permute-done.27.refs_0_.refs_2_), channel_id=1, source_target_pairs={{0,1},{1,0},{2,3},{3,2},{4,5},{5,4},{6,7},{7,6},{8,9},{9,8},{10,11... | collective-permute-start | bytes 4718600 | tf_op jit(solution)/shard_map/ppermute | solution.py:44
  341.2 49.4 %collective-permute-start.31 = (bf16[2,256,1536]{2,1,0:T(8,128)(2,1)}, bf16[2,256,1536]{2,1,0:T(8,128)(2,1)}, u32[]{:S(2)}, u32[]{:S(2)}) collective-permute-start(bf16[2,256,1536]{2,1,0:T(8,128)(2,1)} %collective-permute-done.15.refs_2_), channel_id=1, source_target_pairs={{0,1},{1,0},{2,3},{3,2},{4,5},{5,4},{6,7},{7,6},{8,9},{9,8},{10,11... | collective-permute-start | bytes 4718600 | tf_op jit(solution)/shard_map/ppermute | solution.py:44
  341.7 48.9 %collective-permute-start.29 = (bf16[192,3072]{1,0:T(8,128)(2,1)}, bf16[192,3072]{1,0:T(8,128)(2,1)}, u32[]{:S(2)}, u32[]{:S(2)}) collective-permute-start(bf16[192,3072]{1,0:T(8,128)(2,1)} %collective-permute-done.23), channel_id=1, source_target_pairs={{0,8},{8,16},{16,24},{24,28},{28,20},{20,12},{12,4},{4,0},{1,9},{9... | collective-permute-start | bytes 3538952 | tf_op jit(solution)/shard_map/ppermute | solution.py:128
  431.9 72.3 %collective-permute-start.32 = (bf16[2,256,1536]{2,1,0:T(8,128)(2,1)}, bf16[2,256,1536]{2,1,0:T(8,128)(2,1)}, u32[]{:S(2)}, u32[]{:S(2)}) collective-permute-start(bf16[2,256,1536]{2,1,0:T(8,128)(2,1)} %get-tuple-element.221), channel_id=1, source_target_pairs={{0,1},{1,0},{2,3},{3,2},{4,5},{5,4},{6,7},{7,6},{8,9},{9,8},{10,11... | collective-permute-start | bytes 4718600 | tf_op jit(solution)/shard_map/ppermute | solution.py:44
  434.9 69.3 %collective-permute-start.34 = (bf16[2,256,1536]{2,1,0:T(8,128)(2,1)}, bf16[2,256,1536]{2,1,0:T(8,128)(2,1)}, u32[]{:S(2)}, u32[]{:S(2)}) collective-permute-start(bf16[2,256,1536]{2,1,0:T(8,128)(2,1)} %add_convert_fusion.2), channel_id=1, source_target_pairs={{0,2},{1,3},{2,0},{3,1},{4,6},{5,7},{6,4},{7,5},{8,10},{9,11},{10,... | collective-permute-start | bytes 4718600 | tf_op jit(solution)/shard_map/ppermute | solution.py:44
  509.4 428.9 %reduce-scatter.3.cloned.1.call-start = ((), (), s32[]{:S(2)}) async-start(), calls=%async_computation.5 | async-start | bytes 10616832 | tf_op jit(solution)/shard_map/reduce_scatter | solution.py:622
  522.9 60.7 %collective-permute-start.40 = (bf16[2,256,1536]{2,1,0:T(8,128)(2,1)}, bf16[2,256,1536]{2,1,0:T(8,128)(2,1)}, u32[]{:S(2)}, u32[]{:S(2)}) collective-permute-start(bf16[2,256,1536]{2,1,0:T(8,128)(2,1)} %multiply_convert_fusion.1.refs_0_), channel_id=1, source_target_pairs={{0,2},{1,3},{2,0},{3,1},{4,6},{5,7},{6,4},{7,5},{8,10},{9,11},{10,... | collective-permute-start | bytes 4718600 | tf_op jit(solution)/shard_map/ppermute | solution.py:44
  526.8 53.6 %collective-permute-start.43 = (bf16[2,154,1536]{2,0,1:T(2,128)(2,1)}, bf16[2,154,1536]{2,0,1:T(2,128)(2,1)}, u32[]{:S(2)}, u32[]{:S(2)}) collective-permute-start(bf16[2,154,1536]{2,0,1:T(2,128)(2,1)} %copy.81), channel_id=1, source_target_pairs={{0,2},{1,3},{2,0},{3,1},{4,6},{5,7},{6,4},{7,5},{8,10},{9,11},{10,... | collective-permute-start | bytes 2838536 | tf_op jit(solution)/shard_map/ppermute | solution.py:44
  528.1 58.5 %collective-permute-start.39 = (bf16[2,256,1536]{2,1,0:T(8,128)(2,1)}, bf16[2,256,1536]{2,1,0:T(8,128)(2,1)S(1)}, u32[]{:S(2)}, u32[]{:S(2)}) collective-permute-start(bf16[2,256,1536]{2,1,0:T(8,128)(2,1)} %multiply_convert_fusion.1.refs_0_), channel_id=1, source_target_pairs={{0,1},{1,0},{2,3},{3,2},{4,5},{5,4},{6,7},{7,6},{8,9},{9,8},{10,11... | collective-permute-start | bytes 4718600 | tf_op jit(solution)/shard_map/ppermute | solution.py:44
  588.8 66.3 %collective-permute-start.45 = (bf16[192,1536]{1,0:T(8,128)(2,1)S(1)}, bf16[192,1536]{1,0:T(8,128)(2,1)S(1)}, u32[]{:S(2)}, u32[]{:S(2)}) collective-permute-start(bf16[192,1536]{1,0:T(8,128)(2,1)S(1)} %get-tuple-element.402), channel_id=1, source_target_pairs={{0,4},{8,0},{16,8},{24,16},{28,24},{20,28},{12,20},{4,12},{1,5},{9... | collective-permute-start | bytes 1769480 | tf_op jit(solution)/shard_map/ppermute | solution.py:128
  589.5 65.6 %collective-permute-start.44 = (bf16[192,1536]{1,0:T(8,128)(2,1)S(1)}, bf16[192,1536]{1,0:T(8,128)(2,1)S(1)}, u32[]{:S(2)}, u32[]{:S(2)}) collective-permute-start(bf16[192,1536]{1,0:T(8,128)(2,1)S(1)} %get-tuple-element.403), channel_id=1, source_target_pairs={{0,8},{8,16},{16,24},{24,28},{28,20},{20,12},{12,4},{4,0},{1,9},{9... | collective-permute-start | bytes 1769480 | tf_op jit(solution)/shard_map/ppermute | solution.py:128
  659.7 48.6 %collective-permute-start.47 = (bf16[192,3072]{1,0:T(8,128)(2,1)}, bf16[192,3072]{1,0:T(8,128)(2,1)}, u32[]{:S(2)}, u32[]{:S(2)}) collective-permute-start(bf16[192,3072]{1,0:T(8,128)(2,1)} %get-tuple-element.400), channel_id=1, source_target_pairs={{0,4},{8,0},{16,8},{24,16},{28,24},{20,28},{12,20},{4,12},{1,5},{9... | collective-permute-start | bytes 3538952 | tf_op jit(solution)/shard_map/ppermute | solution.py:128
  729.8 84.2 %collective-permute-start.59 = (bf16[192,3072]{1,0:T(8,128)(2,1)}, bf16[192,3072]{1,0:T(8,128)(2,1)}, u32[]{:S(2)}, u32[]{:S(2)}) collective-permute-start(bf16[192,3072]{1,0:T(8,128)(2,1)} %get-tuple-element.398), channel_id=1, source_target_pairs={{0,4},{8,0},{16,8},{24,16},{28,24},{20,28},{12,20},{4,12},{1,5},{9... | collective-permute-start | bytes 3538952 | tf_op jit(solution)/shard_map/ppermute | solution.py:128
  761.0 54.2 %collective-permute-start.58 = (bf16[192,3072]{1,0:T(8,128)(2,1)}, bf16[192,3072]{1,0:T(8,128)(2,1)S(1)}, u32[]{:S(2)}, u32[]{:S(2)}) collective-permute-start(bf16[192,3072]{1,0:T(8,128)(2,1)} %get-tuple-element.399), channel_id=1, source_target_pairs={{0,8},{8,16},{16,24},{24,28},{28,20},{20,12},{12,4},{4,0},{1,9},{9... | collective-permute-start | bytes 3538952 | tf_op jit(solution)/shard_map/ppermute | solution.py:128
  764.3 67.3 %collective-permute-start.48 = (bf16[2,256,1536]{2,1,0:T(8,128)(2,1)S(1)}, bf16[2,256,1536]{2,1,0:T(8,128)(2,1)S(1)}, u32[]{:S(2)}, u32[]{:S(2)}) collective-permute-start(bf16[2,256,1536]{2,1,0:T(8,128)(2,1)S(1)} %get-tuple-element.287), channel_id=1, source_target_pairs={{0,1},{1,0},{2,3},{3,2},{4,5},{5,4},{6,7},{7,6},{8,9},{9,8},{10,11... | collective-permute-start | bytes 4718600 | tf_op jit(solution)/shard_map/ppermute | solution.py:44
  791.1 59.7 %collective-permute-start.53 = (bf16[2,256,1536]{2,1,0:T(8,128)(2,1)S(1)}, bf16[2,256,1536]{2,1,0:T(8,128)(2,1)S(1)}, u32[]{:S(2)}, u32[]{:S(2)}) collective-permute-start(bf16[2,256,1536]{2,1,0:T(8,128)(2,1)S(1)} %get-tuple-element.298), channel_id=1, source_target_pairs={{0,1},{1,0},{2,3},{3,2},{4,5},{5,4},{6,7},{7,6},{8,9},{9,8},{10,11... | collective-permute-start | bytes 4718600 | tf_op jit(solution)/shard_map/ppermute | solution.py:44
  814.0 66.9 %collective-permute-start.55 = (bf16[2,256,1536]{2,1,0:T(8,128)(2,1)S(1)}, bf16[2,256,1536]{2,1,0:T(8,128)(2,1)S(1)}, u32[]{:S(2)}, u32[]{:S(2)}) collective-permute-start(bf16[2,256,1536]{2,1,0:T(8,128)(2,1)S(1)} %add_convert_fusion), channel_id=1, source_target_pairs={{0,2},{1,3},{2,0},{3,1},{4,6},{5,7},{6,4},{7,5},{8,10},{9,11},{10,... | collective-permute-start | bytes 4718600 | tf_op jit(solution)/shard_map/ppermute | solution.py:44
  822.8 58.8 %collective-permute-start.61 = (bf16[192,3072]{1,0:T(8,128)(2,1)S(1)}, bf16[192,3072]{1,0:T(8,128)(2,1)S(1)}, u32[]{:S(2)}, u32[]{:S(2)}) collective-permute-start(bf16[192,3072]{1,0:T(8,128)(2,1)S(1)} %get-tuple-element.396), channel_id=1, source_target_pairs={{0,4},{8,0},{16,8},{24,16},{28,24},{20,28},{12,20},{4,12},{1,5},{9... | collective-permute-start | bytes 3538952 | tf_op jit(solution)/shard_map/ppermute | solution.py:128
  831.7 49.9 %collective-permute-start.60 = (bf16[192,3072]{1,0:T(8,128)(2,1)S(1)}, bf16[192,3072]{1,0:T(8,128)(2,1)S(1)}, u32[]{:S(2)}, u32[]{:S(2)}) collective-permute-start(bf16[192,3072]{1,0:T(8,128)(2,1)S(1)} %get-tuple-element.397), channel_id=1, source_target_pairs={{0,8},{8,16},{16,24},{24,28},{28,20},{20,12},{12,4},{4,0},{1,9},{9... | collective-permute-start | bytes 3538952 | tf_op jit(solution)/shard_map/ppermute | solution.py:128
  (187 other events, 3539.4 us)
Sparse Core Ops, SparseCore 0:
  10.8 126.6 all-gather.3
  139.6 101.8 all-gather.5
  245.6 98.5 all-gather.7
  509.5 181.9 reduce-scatter.4
  708.4 206.0 reduce-scatter.2

commit v7 on v6

--- a/solution.py
+++ b/solution.py
@@ -128,27 +128,64 @@
     return lax.ppermute(value, "dp", hops)
 
 
+def place_kernel(sizes, *refs):
+    count = len(sizes)
+    rows, blocks, out, sems = refs[0], refs[1 : count + 1], refs[count + 1], refs[count + 2]
+    copies = []
+    for index, (share, start, wide) in enumerate(sizes):
+        row = pl.multiple_of(rows[index], 16)
+        copies.append(
+            pltpu.make_async_copy(
+                blocks[index],
+                out.at[pl.ds(row, share), pl.ds(start, wide)],
+                sems.at[index],
+            )
+        )
+        copies[-1].start()
+    for copy in copies:
+        copy.wait()
+
+
+def place_blocks(blocks, rows, starts, shape):
+    sizes = [(*block.shape, start) for block, start in zip(blocks, starts)]
+    sizes = [(share, start, wide) for share, wide, start in sizes]
+    anywhere = pl.BlockSpec(memory_space=pl.ANY)
+    return pl.pallas_call(
+        functools.partial(place_kernel, sizes),
+        grid_spec=pltpu.PrefetchScalarGridSpec(
+            num_scalar_prefetch=1,
+            grid=(1,),
+            in_specs=[anywhere] * len(blocks),
+            out_specs=anywhere,
+            scratch_shapes=[pltpu.SemaphoreType.DMA((len(blocks),))],
+        ),
+        out_shape=jax.ShapeDtypeStruct(shape, BF16),
+        cost_estimate=pl.CostEstimate(flops=0, transcendentals=0, bytes_accessed=1024),
+        name="place_blocks",
+    )(jnp.stack(rows).astype(jnp.int32), *blocks)
+
+
 def ring_gather(block, count):
     share, wide = block.shape
     half = wide // 2 // LANES * LANES
     place = ring_place(lax.axis_index("dp"), count)
-    whole = jnp.zeros((count * share, wide), block.dtype)
-
-    def put(whole, value, offset, column):
-        row = ring_member(place + offset, count) * share
-        return lax.dynamic_update_slice(whole, value, (row, column))
-
-    whole = put(whole, block, 0, 0)
+    blocks, offsets, starts = [block], [0], [0]
     behind = ahead = block
     for hop in range(1, count // 2):
         behind = ring_step(behind, 1, count)
         ahead = ring_step(ahead, -1, count)
         behind, ahead = yield behind, ahead
-        whole = put(put(whole, behind, -hop, 0), ahead, hop, 0)
+        blocks += [behind, ahead]
+        offsets += [-hop, hop]
+        starts += [0, 0]
     behind = ring_step(behind[:, :half], 1, count)
     ahead = ring_step(ahead[:, half:], -1, count)
     behind, ahead = yield behind, ahead
-    yield put(put(whole, behind, -(count // 2), 0), ahead, count // 2, half)
+    blocks += [behind, ahead]
+    offsets += [-(count // 2), count // 2]
+    starts += [0, half]
+    rows = [ring_member(place + offset, count) * share for offset in offsets]
+    yield place_blocks(blocks, rows, starts, (count * share, wide))
 
 
 def ring_scatter(grad, count):
@@ -580,16 +617,16 @@
         joined = blocks[0] if len(blocks) == 1 else jnp.concatenate(blocks, axis=1)
         return lax.all_gather(joined, "dp", axis=0, tiled=True)
 
-    packed_in = gathered(
-        image_attention_in.reshape(share, 3 * width), text_attention_in.reshape(share, 3 * width)
+    packed_first = gathered(
+        image_attention_in.reshape(share, 3 * width),
+        text_attention_in.reshape(share, 3 * width),
+        image_attention_out.T,
+        text_attention_out.T,
     )
     image_up = gathered(image_hidden_in)
     image_down = gathered(image_hidden_out.T)
-    out_ring = ring_gather(
-        jnp.concatenate([image_attention_out.T, text_attention_out.T], axis=1), group_count
-    )
-    out_hop = next(out_ring)
-    weight_in = ((packed_in, 0, 3 * width), (packed_in, 3 * width, 3 * width))
+    weight_in = ((packed_first, 0, 3 * width), (packed_first, 3 * width, 3 * width))
+    weight_out = ((packed_first, 6 * width, width), (packed_first, 7 * width, width))
 
     alive = (jnp.arange(slots) < group_size[0]).astype(F32)[:, None, None]
     cond_full = condition.astype(F32)
@@ -608,8 +645,6 @@
     modulations = lax.all_gather(
         mod_own.reshape(slots, 2, 6, width), "tensor", axis=3, tiled=True
     )
-    modulations, out_hop = lax.optimization_barrier((modulations, out_hop))
-    out_hop = out_ring.send(out_hop)
     mods = (modulations[:, 0], modulations[:, 1])
 
     tokens = (image_tokens.astype(F32), text_tokens.astype(F32))
@@ -654,37 +689,30 @@
     normed_one, inverse_one, image_first = modulated(tokens[0], mods[0], 0, 1)
     text_normed_one, text_inverse_one, text_first = modulated(tokens[1], mods[1], 0, 1)
     first_pieces = gather_pieces(image_first, size)
-    first_pieces, out_hop = lax.optimization_barrier((first_pieces, out_hop))
-    out_hop = out_ring.send(out_hop)
-    for _ in range(group_count // 2 - 4):
-        out_hop = out_ring.send(out_hop)
     packed = products_of(first_pieces, weight_in[0], 0, low_kinds)
     text_packed = products_of([text_first], weight_in[1], 0, [BF16])
     down_rows = [
         (outgoing[stream] * spread(mods[stream][:, 5])).astype(BF16) for stream in range(2)
     ]
     down_have = gather_start(after(down_rows[0], first_pieces), size)
-    parts, out_hop = after(([*packed, *text_packed], out_hop), down_have)
-    out_hop = out_ring.send(out_hop)
+    parts = after([*packed, *text_packed], down_have)
     up_ring = ring_gather(
         after(jnp.concatenate([text_hidden_in, text_hidden_out.T], axis=1), parts), group_count
     )
     up_hop = next(up_ring)
     attended, sums = attend(parts)
     down_pieces = gather_end(after(down_have, attended), size)
-    attended, out_hop, up_hop = lax.optimization_barrier((attended, out_hop, up_hop))
-    both_out = out_ring.send(out_hop)
+    attended, up_hop = lax.optimization_barrier((attended, up_hop))
     up_hop = up_ring.send(up_hop)
-    weight_out = ((both_out, 0, width), (both_out, width, width))
     attended_parts = (attended[:-1], attended[-1:])
 
     branch = image_sum(attended_parts[0], weight_out[0], 1)
     branch, up_hop = lax.optimization_barrier((branch, up_hop))
     up_hop = up_ring.send(up_hop)
-    text_branch = text_sum(attended_parts[1][0], weight_out[1], 1)
     middle = tokens[0] + spread(mods[0][:, 2]) * branch
     normed_two, inverse_two, image_second = modulated(middle, mods[0], 3, 4)
     second_pieces = gather_pieces(image_second, size)
+    text_branch = text_sum(after(attended_parts[1][0], second_pieces), weight_out[1], 1)
     up_weight, down_weight = (image_up, 0, units), (image_down, 0, units)
     near = hidden_both(second_pieces[:half], down_pieces[:half], up_weight, down_weight)
     far_pieces, up_hop = after((second_pieces[half:], up_hop), near)
@@ -716,6 +744,7 @@
     )
     gate_one_grad = jnp.sum(middle_grad * branch, axis=1)
 
+    low = after(low, text_second_grad)
     branch_grads = gather_pieces(low, size)
     text_mlp_grad = weight_grad(
         after([([down_rows[1]], text_active), ([text_second], text_hidden_grad)], low)
@@ -764,8 +793,7 @@
     branch_two = image_sum(active, down_weight, 1, True)
     text_branch_two = text_sum(text_active[0], text_down_weight, 1, True)
     text_first_grad, text_hop = lax.optimization_barrier((text_first_grad, text_hop))
-    text_hop = text_ring.send(text_hop)
-    for _ in range(group_count // 2 - 4):
+    for _ in range(group_count // 2 - 3):
         text_hop = text_ring.send(text_hop)
     first_grad, text_hop = lax.optimization_barrier((first_grad, text_hop))
     text_mlp = text_ring.send(text_hop)
@@ -824,10 +852,9 @@
     activated_part = sum_all(activated_part, size, "tensor").reshape(group_count, slots, share)
     activated_rows = gather_stack(activated_part, group_count, "dp")
     activated_rows = jnp.stack([activated_rows[k, k] for k in range(group_count)])
-    group_order = group_rank ^ jnp.arange(group_count)
     activated_grad = jnp.concatenate(
         [
-            lax.dynamic_index_in_dim(activated_rows, group_order[k], 0, keepdims=False)
+            lax.dynamic_index_in_dim(activated_rows, group_rank ^ k, 0, keepdims=False)
             for k in range(group_count)
         ],
         axis=1,

time: 959 us -> 1210 us (1.26)
  Pallas kernels: 317 us -> 607 us
  local copies, waits for them, and re-layouts: 89.2 us -> 70.9 us
  waiting for transfers between devices: 334 us -> 352 us
  starting transfers between devices: 78.1 us -> 61.4 us
  between operations: 32 us -> 17 us
    pallas_call x0 -> x1, Pallas kernels: none -> 288 us  [place_blocks(): pl.pallas_call(functools.partial(place_kernel, sizes), grid_spec=pltpu.Pr...]
    all_gather x3, waiting for transfers between devices: 0.02 us -> 45.7 us  [gathered(): return lax.all_gather(joined, 'dp', axis=0, tiled=True)]
    dynamic_update_slice x17 -> x0, local copies, waits for them, and re-layouts: 23 us -> none  [put(): return lax.dynamic_update_slice(whole, value, (row, column))]
    ppermute x48, waiting for transfers between devices: 299 us -> 279 us  [swap(): return lax.ppermute(value, axis, [(i, i ^ bit) for i in range(size)])]
    ppermute x24 -> x16, starting transfers between devices: 33.9 us -> 24.5 us  [ring_step(): return lax.ppermute(value, 'dp', hops)]
    ppermute x24 -> x16, waiting for transfers between devices: 34.7 us -> 26.7 us  [ring_step(): return lax.ppermute(value, 'dp', hops)]
    unnamed x305 -> x371, local copies, waits for them, and re-layouts: 26 us -> 33.7 us
  transfers between devices with their start and end apart: 77 -> 69, of which waited for: 32 -> 29; matrix products, arithmetic and copies ran while one was open for 16% -> 10% of each run, Pallas kernels for 31% -> 50%
where the time goes in v7:
time: 1210 us; the launch traced here: 1200 us
  Pallas kernels  607 us (50%)
  waiting for transfers between devices  352 us (29%)
  other arithmetic  84.5 us (7%)
  local copies, waits for them, and re-layouts  70.9 us (6%)
  starting transfers between devices  61.4 us (5%)
  between operations  17 us (1%)
    pallas_call x1, Pallas kernels, place_blocks(): pl.pallas_call(functools.partial(place_kernel, sizes), grid_spec=pltpu.Pr...  288 us
    ppermute x48, waiting for transfers between devices, swap(): return lax.ppermute(value, axis, [(i, i ^ bit) for i in range(size)])  279 us
    pallas_call x16, Pallas kernels, products_of(): pl.pallas_call(functools.partial(product_kernel, count, weight_dim), grid...  98.9 us
    pallas_call x8, Pallas kernels, weight_grad(): pl.pallas_call(functools.partial(rows_kernel, count), grid=(rows // step,...  68.1 us
    pallas_call x1, Pallas kernels, attend_back(): pl.pallas_call(functools.partial(attend_back_kernel, count, groups), grid...  57.7 us
    pallas_call x1, Pallas kernels, attend(): pl.pallas_call(functools.partial(attend_kernel, count), grid=(slots, grou...  54.8 us
    all_gather x3, waiting for transfers between devices, gathered(): return lax.all_gather(joined, 'dp', axis=0, tiled=True)  45.7 us
    pallas_call x3, Pallas kernels, hidden_both(): pl.pallas_call(functools.partial(hidden_kernel, count), grid=(wide // til...  39.2 us
  transfers between devices with their start and end apart: 69, of which 29 were waited for; matrix products, arithmetic and copies ran while one was open for 10% of the time, Pallas kernels for 50%

profile of v7, /device:TPU:0, one launch (start us, length us, event | category | flops | bytes accessed | tf_op | source)
XLA Modules:
  0.0 1203.7 jit_solution(14672400163637508941)
XLA Ops:
  31.3 15.4 %collective-permute-done.3 = f32[4,2,4608]{2,1,0:T(2,128)S(1)} collective-permute-done((f32[4,2,4608]{2,1,0:T(2,128)S(1)}, f32[4,2,4608]{2,1,0:T(2,128)S(1)}, u32[]{:S(2)}, u32[]{:S(2)}) %collective-permute-start.3) | collective-permute-done | bytes 147488 | tf_op jit(solution)/shard_map/ppermute | solution.py:44
  47.9 8.4 collective-permute-done.4
  70.6 35.2 %collective-permute-done.7.refs_2_ = bf16[2,256,1536]{2,1,0:T(8,128)(2,1)S(1)} collective-permute-done((bf16[2,256,1536]{2,1,0:T(8,128)(2,1)}, bf16[2,256,1536]{2,1,0:T(8,128)(2,1)S(1)}, u32[]{:S(2)}, u32[]{:S(2)}) %collective-permute-start.7) | collective-permute-done | bytes 1572896 | tf_op jit(solution)/shard_map/ppermute | solution.py:44
  113.3 45.7 %all-gather.4.cloned.1.call-done.refs_4_.refs_1_.refs_2_ = bf16[1536,3072]{1,0:T(8,128)(2,1)} async-done(((bf16[192,3072]{1,0:T(8,128)(2,1)}), bf16[1536,3072]{1,0:T(8,128)(2,1)}) %all-gather.4.cloned.1.call-update) | async-done | bytes 9437200 | tf_op jit(solution)/shard_map/all_gather | solution.py:618
  159.1 13.9 %products.16 = (bf16[2,256,1152]{2,1,0:T(8,128)(2,1)S(1)}, bf16[2,256,1152]{2,1,0:T(8,128)(2,1)S(1)}, bf16[2,256,1152]{2,1,0:T(8,128)(2,1)S(1)}, bf16[2,256,1152]{2,1,0:T(8,128)(2,1)S(1)}) custom-call(bf16[2,256,1536]{2,1,0:T(8,128)(2,1)} %fusion.7.refs_0_, bf16[2,256,1536]{2,1,0:T(8,128)(2,1)} %copy-done.104, bf16[2,256,1536]{2,1,0:T(8,128)(2,1)} %copy-done.103, ...), custom_call_target="tpu_custom_call" | custom-call | bytes 1024 | tf_op jit(solution)/shard_map/products/pallas_call | solution.py:509
  181.3 54.8 %attend.1 = (bf16[2,256,384]{2,1,0:T(8,128)(2,1)S(1)}, bf16[2,256,384]{2,1,0:T(8,128)(2,1)S(1)}, bf16[2,256,384]{2,1,0:T(8,128)(2,1)S(1)}, bf16[2,256,384]{2,1,0...) custom-call(bf16[2,256,1152]{2,1,0:T(8,128)(2,1)S(1)} %get-tuple-ele, ...), custom_call_target="tpu_custom_call" | custom-call | flops 17051860992 | bytes 7237632 | tf_op jit(solution)/shard_map/attend/pallas_call | solution.py:351
  253.5 33.3 %collective-permute-done.14 = bf16[2,256,1536]{2,1,0:T(8,128)(2,1)} collective-permute-done((bf16[2,256,1536]{2,1,0:T(8,128)(2,1)}, bf16[2,256,1536]{2,1,0:T(8,128)(2,1)}, u32[]{:S(2)}, u32[]{:S(2)}) %collective-permute-start.14) | collective-permute-done | bytes 1572896 | tf_op jit(solution)/shard_map/ppermute | solution.py:44
  290.4 8.3 collective-permute-done.16.refs_5_
  301.9 34.4 %collective-permute-done.19.refs_0_.refs_2_ = bf16[2,256,1536]{2,1,0:T(8,128)(2,1)S(1)} collective-permute-done((bf16[2,256,1536]{2,1,0:T(8,128)(2,1)S(1)}, bf16[2,256,1536]{2,1,0:T(8,128)(2,1)S(1)}, u32[]{:S(2)}, u32[]{:S(2)}) %collective-permute-start.19) | collective-permute-done | bytes 1572896 | tf_op jit(solution)/shard_map/ppermute | solution.py:44
  348.7 16.1 %hidden_both.3 = (bf16[2,256,1536]{2,1,0:T(8,128)(2,1)S(1)}, bf16[2,256,1536]{2,1,0:T(8,128)(2,1)S(1)}, bf16[2,256,1536]{2,1,0:T(8,128)(2,1)S(1)}, bf16[2,256,1536]{2,1,0:T(8,128)(2,1)}) custom-call(bf16[2,256,1536]{2,1,0:T(8,128)(2,1)} %copy-done.4, bf16[2,256,1536]{2,1,0:T(8,128)(2,1)} %copy-done.20, bf16[2,256,1536]{2,1,0:T(8,128)(2,1)} %copy-done.2, ...), custom_call_target="tpu_custom_call" | custom-call | bytes 1024 | tf_op jit(solution)/shard_map/hidden_both/pallas_call | solution.py:559
  367.2 8.0 collective-permute-done.21.refs_6_
  375.3 16.0 %hidden_both.4 = (bf16[2,256,1536]{2,1,0:T(8,128)(2,1)S(1)}, bf16[2,256,1536]{2,1,0:T(8,128)(2,1)S(1)}, bf16[2,256,1536]{2,1,0:T(8,128)(2,1)S(1)}, bf16[2,256,1536]{2,1,0:T(8,128)(2,1)}) custom-call(bf16[2,256,1536]{2,1,0:T(8,128)(2,1)} %copy-done.18, bf16[2,256,1536]{2,1,0:T(8,128)(2,1)} %copy-done.107, ...), custom_call_target="tpu_custom_call" | custom-call | bytes 1024 | tf_op jit(solution)/shard_map/hidden_both/pallas_call | solution.py:559
  394.9 8.2 products.20
  414.3 8.4 products.21
  429.9 287.9 %place_blocks.1.refs_2_.refs_3_.refs_1_ = bf16[1536,3072]{1,0:T(8,128)(2,1)} custom-call(s32[9]{0:T(128)} %stack.109.refs_0_, bf16[192,3072]{1,0:T(8,128)(2,1)} %pad_maximum_fusion.1.refs_1_, bf16[192,3072]{1,0:T(8,128)(2,1)} %copy-done.118, bf16[192,3072]{1,0:T(8,128)(2,1)} %copy-done.117, bf16[192,3072]{1,0:T(8,128)(2,1)} %collective-permute-done.15.refs_4_, ...), custom_call_target="tpu_custom_call" | custom-call | bytes 1024 | tf_op jit(solution)/shard_map/place_blocks/pallas_call | solution.py:153
  717.9 15.3 %weight_grad.8.refs_8_ = bf16[1536,3072]{1,0:T(8,128)(2,1)} custom-call(bf16[2,256,1536]{2,1,0:T(8,128)(2,1)S(1)} %copy-done.3, bf16[2,256,1536]{2,1,0:T(8,128)(2,1)} %collective-permute-done.18.refs_3_.refs_1_, bf16[2,256,1536]{2,1,0:T(8,128)(2,1)} %collective-permute-done.9.refs_2_, bf16[2,256,1536]{2,1,0:T(8,128)(2,1)} %collective-permute-done.23.refs_3_, ...), custom_call_target="tpu_custom_call" | custom-call | bytes 1024 | tf_op jit(solution)/shard_map/weight_grad/pallas_call | solution.py:432
  733.2 15.2 %weight_grad.9 = bf16[1536,3072]{1,0:T(8,128)(2,1)} custom-call(bf16[2,256,1536]{2,1,0:T(8,128)(2,1)S(1)} %copy-done.5, bf16[2,256,1536]{2,1,0:T(8,128)(2,1)S(1)} %copy-done.21, bf16[2,256,1536]{2,1,0:T(8,128)(2,1)S(1)} %copy-done.19, bf16[2,256,1536]{2,1,0:T(8,128)(2,1)} %copy-done.107, ...), custom_call_target="tpu_custom_call", output_to_operand_aliasing={{}: (8, {})} | custom-call | bytes 1024 | tf_op jit(solution)/shard_map/weight_grad/pallas_call | solution.py:432
  753.9 7.2 hidden_both.5
  787.0 18.4 %collective-permute-done.32 = bf16[2,154,1536]{2,0,1:T(2,128)(2,1)S(1)} collective-permute-done((bf16[2,154,1536]{2,0,1:T(2,128)(2,1)S(1)}, bf16[2,154,1536]{2,0,1:T(2,128)(2,1)S(1)}, u32[]{:S(2)}, u32[]{:S(2)}) %collective-permute-start.32) | collective-permute-done | bytes 946208 | tf_op jit(solution)/shard_map/ppermute | solution.py:44
  821.6 23.1 %collective-permute-done.34.refs_2_ = bf16[2,256,1536]{2,1,0:T(8,128)(2,1)} collective-permute-done((bf16[2,256,1536]{2,1,0:T(8,128)(2,1)S(1)}, bf16[2,256,1536]{2,1,0:T(8,128)(2,1)}, u32[]{:S(2)}, u32[]{:S(2)}) %collective-permute-start.34) | collective-permute-done | bytes 1572896 | tf_op jit(solution)/shard_map/ppermute | solution.py:44
  862.0 57.7 %attend_back.1 = (bf16[2,256,1152]{2,1,0:T(8,128)(2,1)S(1)}, bf16[2,256,1152]{2,1,0:T(8,128)(2,1)S(1)}, bf16[2,256,1152]{2,1,0:T(8,128)(2,1)}, bf16[2,256,1152]{2,1,0:T(8,128)(2,1)}, bf16[2,154,1152]{2,1,0:T(8,128)(2,1)S(1)}) custom-call(bf16[2,256,1152]{2,1,0:T(8,128)(2,1)} %copy-done.59, bf16[2,256,1152]{2,1,0:T(8,128)(2,1)} %copy-done.60, ...), custom_call_target="tpu_custom_call" | custom-call | flops 42629652480 | bytes 12665856 | tf_op jit(solution)/shard_map/attend_back/pallas_call | solution.py:378
  931.6 11.6 weight_grad.12.refs_2_
  948.1 7.2 weight_grad.14.refs_2_
  958.9 7.1 collective-permute-done.39
  987.8 8.0 products.26
  1003.4 8.0 products.27
  1011.4 7.1 products.30
  1031.8 16.5 %collective-permute-done.44 = bf16[2,154,1536]{2,0,1:T(2,128)(2,1)S(1)} collective-permute-done((bf16[2,154,1536]{2,0,1:T(2,128)(2,1)S(1)}, bf16[2,154,1536]{2,0,1:T(2,128)(2,1)S(1)}, u32[]{:S(2)}, u32[]{:S(2)}) %collective-permute-start.44) | collective-permute-done | bytes 946208 | tf_op jit(solution)/shard_map/ppermute | solution.py:44
  1052.8 15.2 %collective-permute-done.49 = bf16[2,154,1536]{2,0,1:T(2,128)(2,1)S(1)} collective-permute-done((bf16[2,154,1536]{2,0,1:T(2,128)(2,1)S(1)}, bf16[2,154,1536]{2,0,1:T(2,128)(2,1)S(1)}, u32[]{:S(2)}, u32[]{:S(2)}) %collective-permute-start.49) | collective-permute-done | bytes 946208 | tf_op jit(solution)/shard_map/ppermute | solution.py:44
  1079.9 8.2 collective-permute-start.53
  1088.6 16.7 %collective-permute-done.42 = bf16[2,256,1536]{2,1,0:T(8,128)(2,1)S(1)} collective-permute-done((bf16[2,256,1536]{2,1,0:T(8,128)(2,1)S(1)}, bf16[2,256,1536]{2,1,0:T(8,128)(2,1)S(1)}, u32[]{:S(2)}, u32[]{:S(2)}) %collective-permute-start.42) | collective-permute-done | bytes 1572896 | tf_op jit(solution)/shard_map/ppermute | solution.py:44
  1109.5 28.2 %collective-permute-done.47 = bf16[2,256,1536]{2,1,0:T(8,128)(2,1)S(1)} collective-permute-done((bf16[2,256,1536]{2,1,0:T(8,128)(2,1)S(1)}, bf16[2,256,1536]{2,1,0:T(8,128)(2,1)S(1)}, u32[]{:S(2)}, u32[]{:S(2)}) %collective-permute-start.47) | collective-permute-done | bytes 1572896 | tf_op jit(solution)/shard_map/ppermute | solution.py:44
  (643 shorter events, 322.0 us)
Async XLA Ops:
  7.2 151.9 %all-gather.4.cloned.1.call-start = ((), (), s32[]{:S(2)}) async-start(), calls=%async_computation.2 | async-start | bytes 10616832 | tf_op jit(solution)/shard_map/all_gather | solution.py:618
  11.7 337.1 %all-gather.6.cloned.1.call-start = ((), (), s32[]{:S(2)}) async-start(), calls=%async_computation.3 | async-start | bytes 5308416 | tf_op jit(solution)/shard_map/all_gather | solution.py:618
  70.4 278.3 %all-gather.8.cloned.1.call-start = ((), (), s32[]{:S(2)}) async-start(), calls=%async_computation.4 | async-start | bytes 5308416 | tf_op jit(solution)/shard_map/all_gather | solution.py:618
  70.4 38.2 %collective-permute-start.6 = (bf16[2,256,1536]{2,1,0:T(8,128)(2,1)}, bf16[2,256,1536]{2,1,0:T(8,128)(2,1)S(1)}, u32[]{:S(2)}, u32[]{:S(2)}) collective-permute-start(bf16[2,256,1536]{2,1,0:T(8,128)(2,1)} %fusion.7.refs_0_), channel_id=1, source_target_pairs={{0,1},{1,0},{2,3},{3,2},{4,5},{5,4},{6,7},{7,6},{8,9},{9,8},{10,11... | collective-permute-start | bytes 4718600 | tf_op jit(solution)/shard_map/ppermute | solution.py:44
  109.1 69.9 %collective-permute-start.9 = (bf16[2,256,1536]{2,1,0:T(8,128)(2,1)S(1)}, bf16[2,256,1536]{2,1,0:T(8,128)(2,1)}, u32[]{:S(2)}, u32[]{:S(2)}) collective-permute-start(bf16[2,256,1536]{2,1,0:T(8,128)(2,1)S(1)} %multiply_convert_fusion.2.refs_2_.refs_0_), channel_id=1, source_target_pairs={{0,2},{1,3},{2,0},{3,1},{4,6},{5,7},{6,4},{7,5},{8,10},{9,11},{10,... | collective-permute-start | bytes 4718600 | tf_op jit(solution)/shard_map/ppermute | solution.py:44
  179.1 60.1 %collective-permute-start.11 = (bf16[192,3072]{1,0:T(8,128)(2,1)S(1)}, bf16[192,3072]{1,0:T(8,128)(2,1)S(1)}, u32[]{:S(2)}, u32[]{:S(2)}) collective-permute-start(bf16[192,3072]{1,0:T(8,128)(2,1)S(1)} %copy-done.109), channel_id=1, source_target_pairs={{0,4},{8,0},{16,8},{24,16},{28,24},{20,28},{12,20},{4,12},{1,5},{9... | collective-permute-start | bytes 3538952 | tf_op jit(solution)/shard_map/ppermute | solution.py:128
  179.7 59.5 %collective-permute-start.10 = (bf16[192,3072]{1,0:T(8,128)(2,1)S(1)}, bf16[192,3072]{1,0:T(8,128)(2,1)S(1)}, u32[]{:S(2)}, u32[]{:S(2)}) collective-permute-start(bf16[192,3072]{1,0:T(8,128)(2,1)S(1)} %copy-done.109), channel_id=1, source_target_pairs={{0,8},{8,16},{16,24},{24,28},{28,20},{20,12},{12,4},{4,0},{1,9},{9... | collective-permute-start | bytes 3538952 | tf_op jit(solution)/shard_map/ppermute | solution.py:128
  251.2 937.8 %reduce-scatter.5.cloned.1.call-start = ((), (), s32[]{:S(2)}) async-start(), calls=%async_computation.6 | async-start | bytes 10616832 | tf_op jit(solution)/shard_map/reduce_scatter | solution.py:657
  251.2 39.1 %collective-permute-start.15 = (bf16[192,3072]{1,0:T(8,128)(2,1)}, bf16[192,3072]{1,0:T(8,128)(2,1)}, u32[]{:S(2)}, u32[]{:S(2)}) collective-permute-start(bf16[192,3072]{1,0:T(8,128)(2,1)} %copy-done.118), channel_id=1, source_target_pairs={{0,8},{8,16},{16,24},{24,28},{28,20},{20,12},{12,4},{4,0},{1,9},{9... | collective-permute-start | bytes 3538952 | tf_op jit(solution)/shard_map/ppermute | solution.py:128
  251.4 47.3 %collective-permute-start.16 = (bf16[192,3072]{1,0:T(8,128)(2,1)}, bf16[192,3072]{1,0:T(8,128)(2,1)}, u32[]{:S(2)}, u32[]{:S(2)}) collective-permute-start(bf16[192,3072]{1,0:T(8,128)(2,1)} %copy-done.117), channel_id=1, source_target_pairs={{0,4},{8,0},{16,8},{24,16},{28,24},{20,28},{12,20},{4,12},{1,5},{9... | collective-permute-start | bytes 3538952 | tf_op jit(solution)/shard_map/ppermute | solution.py:128
  336.7 38.5 %collective-permute-start.23 = (bf16[2,256,1536]{2,1,0:T(8,128)(2,1)}, bf16[2,256,1536]{2,1,0:T(8,128)(2,1)}, u32[]{:S(2)}, u32[]{:S(2)}) collective-permute-start(bf16[2,256,1536]{2,1,0:T(8,128)(2,1)} %collective-permute-done.9.refs_2_), channel_id=1, source_target_pairs={{0,1},{1,0},{2,3},{3,2},{4,5},{5,4},{6,7},{7,6},{8,9},{9,8},{10,11... | collective-permute-start | bytes 4718600 | tf_op jit(solution)/shard_map/ppermute | solution.py:44
  346.6 56.7 %collective-permute-start.27 = (f32[2,154,1536]{2,0,1:T(2,128)}, f32[2,154,1536]{2,0,1:T(2,128)}, u32[]{:S(2)}, u32[]{:S(2)}) collective-permute-start(f32[2,154,1536]{2,0,1:T(2,128)} %copy.74), channel_id=1, source_target_pairs={{0,1},{1,0},{2,3},{3,2},{4,5},{5,4},{6,7},{7,6},{8,9},{9,8},{10,11... | collective-permute-start | bytes 5677064 | tf_op jit(solution)/shard_map/ppermute | solution.py:44
  407.1 341.3 %collective-permute-start.28 = (bf16[2,154,1536]{2,0,1:T(2,128)(2,1)}, bf16[2,154,1536]{2,0,1:T(2,128)(2,1)}, u32[]{:S(2)}, u32[]{:S(2)}) collective-permute-start(bf16[2,154,1536]{2,0,1:T(2,128)(2,1)} %copy.76), channel_id=1, source_target_pairs={{0,2},{1,3},{2,0},{3,1},{4,6},{5,7},{6,4},{7,5},{8,10},{9,11},{10,... | collective-permute-start | bytes 2838536 | tf_op jit(solution)/shard_map/ppermute | solution.py:44
  422.6 345.8 %collective-permute-start.24 = (bf16[2,256,1536]{2,1,0:T(8,128)(2,1)}, bf16[2,256,1536]{2,1,0:T(8,128)(2,1)}, u32[]{:S(2)}, u32[]{:S(2)}) collective-permute-start(bf16[2,256,1536]{2,1,0:T(8,128)(2,1)} %get-tuple-element.197), channel_id=1, source_target_pairs={{0,1},{1,0},{2,3},{3,2},{4,5},{5,4},{6,7},{7,6},{8,9},{9,8},{10,11... | collective-permute-start | bytes 4718600 | tf_op jit(solution)/shard_map/ppermute | solution.py:44
  425.7 342.7 %collective-permute-start.26 = (bf16[2,256,1536]{2,1,0:T(8,128)(2,1)}, bf16[2,256,1536]{2,1,0:T(8,128)(2,1)}, u32[]{:S(2)}, u32[]{:S(2)}) collective-permute-start(bf16[2,256,1536]{2,1,0:T(8,128)(2,1)} %add_convert_fusion.2), channel_id=1, source_target_pairs={{0,2},{1,3},{2,0},{3,1},{4,6},{5,7},{6,4},{7,5},{8,10},{9,11},{10,... | collective-permute-start | bytes 4718600 | tf_op jit(solution)/shard_map/ppermute | solution.py:44
  772.5 420.1 %reduce-scatter.3.cloned.1.call-start = ((), (), s32[]{:S(2)}) async-start(), calls=%async_computation.5 | async-start | bytes 10616832 | tf_op jit(solution)/shard_map/reduce_scatter | solution.py:657
  808.7 42.8 %collective-permute-start.33 = (bf16[2,256,1536]{2,1,0:T(8,128)(2,1)S(1)}, bf16[2,256,1536]{2,1,0:T(8,128)(2,1)S(1)}, u32[]{:S(2)}, u32[]{:S(2)}) collective-permute-start(bf16[2,256,1536]{2,1,0:T(8,128)(2,1)S(1)} %multiply_convert_fusion.1.refs_0_), channel_id=1, source_target_pairs={{0,1},{1,0},{2,3},{3,2},{4,5},{5,4},{6,7},{7,6},{8,9},{9,8},{10,11... | collective-permute-start | bytes 4718600 | tf_op jit(solution)/shard_map/ppermute | solution.py:44
  853.8 66.0 %collective-permute-start.37 = (bf16[192,1536]{1,0:T(8,128)(2,1)S(1)}, bf16[192,1536]{1,0:T(8,128)(2,1)S(1)}, u32[]{:S(2)}, u32[]{:S(2)}) collective-permute-start(bf16[192,1536]{1,0:T(8,128)(2,1)S(1)} %get-tuple-element.380), channel_id=1, source_target_pairs={{0,4},{8,0},{16,8},{24,16},{28,24},{20,28},{12,20},{4,12},{1,5},{9... | collective-permute-start | bytes 1769480 | tf_op jit(solution)/shard_map/ppermute | solution.py:128
  853.9 65.9 %collective-permute-start.36 = (bf16[192,1536]{1,0:T(8,128)(2,1)S(1)}, bf16[192,1536]{1,0:T(8,128)(2,1)S(1)}, u32[]{:S(2)}, u32[]{:S(2)}) collective-permute-start(bf16[192,1536]{1,0:T(8,128)(2,1)S(1)} %get-tuple-element.381), channel_id=1, source_target_pairs={{0,8},{8,16},{16,24},{24,28},{28,20},{20,12},{12,4},{4,0},{1,9},{9... | collective-permute-start | bytes 1769480 | tf_op jit(solution)/shard_map/ppermute | solution.py:128
  924.2 41.9 %collective-permute-start.39 = (bf16[192,3072]{1,0:T(8,128)(2,1)}, bf16[192,3072]{1,0:T(8,128)(2,1)}, u32[]{:S(2)}, u32[]{:S(2)}) collective-permute-start(bf16[192,3072]{1,0:T(8,128)(2,1)} %get-tuple-element.378), channel_id=1, source_target_pairs={{0,4},{8,0},{16,8},{24,16},{28,24},{20,28},{12,20},{4,12},{1,5},{9... | collective-permute-start | bytes 3538952 | tf_op jit(solution)/shard_map/ppermute | solution.py:128
  924.4 41.7 %collective-permute-start.38 = (bf16[192,3072]{1,0:T(8,128)(2,1)}, bf16[192,3072]{1,0:T(8,128)(2,1)}, u32[]{:S(2)}, u32[]{:S(2)}) collective-permute-start(bf16[192,3072]{1,0:T(8,128)(2,1)} %get-tuple-element.379), channel_id=1, source_target_pairs={{0,8},{8,16},{16,24},{24,28},{28,20},{20,12},{12,4},{4,0},{1,9},{9... | collective-permute-start | bytes 3538952 | tf_op jit(solution)/shard_map/ppermute | solution.py:128
  973.9 47.4 %collective-permute-start.43 = (f32[2,154,1536]{2,0,1:T(2,128)}, f32[2,154,1536]{2,0,1:T(2,128)}, u32[]{:S(2)}, u32[]{:S(2)}) collective-permute-start(f32[2,154,1536]{2,0,1:T(2,128)} %copy.83), channel_id=1, source_target_pairs={{0,1},{1,0},{2,3},{3,2},{4,5},{5,4},{6,7},{7,6},{8,9},{9,8},{10,11... | collective-permute-start | bytes 5677064 | tf_op jit(solution)/shard_map/ppermute | solution.py:44
  980.9 43.5 %collective-permute-start.48 = (f32[2,154,1536]{2,0,1:T(2,128)}, f32[2,154,1536]{2,0,1:T(2,128)}, u32[]{:S(2)}, u32[]{:S(2)}) collective-permute-start(f32[2,154,1536]{2,0,1:T(2,128)} %copy.87), channel_id=1, source_target_pairs={{0,1},{1,0},{2,3},{3,2},{4,5},{5,4},{6,7},{7,6},{8,9},{9,8},{10,11... | collective-permute-start | bytes 5677064 | tf_op jit(solution)/shard_map/ppermute | solution.py:44
  986.3 85.3 %collective-permute-start.51 = (bf16[192,3072]{1,0:T(8,128)(2,1)}, bf16[192,3072]{1,0:T(8,128)(2,1)}, u32[]{:S(2)}, u32[]{:S(2)}) collective-permute-start(bf16[192,3072]{1,0:T(8,128)(2,1)} %get-tuple-element.376), channel_id=1, source_target_pairs={{0,4},{8,0},{16,8},{24,16},{28,24},{20,28},{12,20},{4,12},{1,5},{9... | collective-permute-start | bytes 3538952 | tf_op jit(solution)/shard_map/ppermute | solution.py:128
  1018.6 53.7 %collective-permute-start.50 = (bf16[192,3072]{1,0:T(8,128)(2,1)}, bf16[192,3072]{1,0:T(8,128)(2,1)S(1)}, u32[]{:S(2)}, u32[]{:S(2)}) collective-permute-start(bf16[192,3072]{1,0:T(8,128)(2,1)} %get-tuple-element.377), channel_id=1, source_target_pairs={{0,8},{8,16},{16,24},{24,28},{28,20},{20,12},{12,4},{4,0},{1,9},{9... | collective-permute-start | bytes 3538952 | tf_op jit(solution)/shard_map/ppermute | solution.py:128
  1021.4 67.0 %collective-permute-start.40 = (bf16[2,256,1536]{2,1,0:T(8,128)(2,1)S(1)}, bf16[2,256,1536]{2,1,0:T(8,128)(2,1)S(1)}, u32[]{:S(2)}, u32[]{:S(2)}) collective-permute-start(bf16[2,256,1536]{2,1,0:T(8,128)(2,1)S(1)} %get-tuple-element.265), channel_id=1, source_target_pairs={{0,1},{1,0},{2,3},{3,2},{4,5},{5,4},{6,7},{7,6},{8,9},{9,8},{10,11... | collective-permute-start | bytes 4718600 | tf_op jit(solution)/shard_map/ppermute | solution.py:44
  1029.1 39.0 %collective-permute-start.49 = (bf16[2,154,1536]{2,0,1:T(2,128)(2,1)S(1)}, bf16[2,154,1536]{2,0,1:T(2,128)(2,1)S(1)}, u32[]{:S(2)}, u32[]{:S(2)}) collective-permute-start(bf16[2,154,1536]{2,0,1:T(2,128)(2,1)S(1)} %copy.89), channel_id=1, source_target_pairs={{0,2},{1,3},{2,0},{3,1},{4,6},{5,7},{6,4},{7,5},{8,10},{9,11},{10,... | collective-permute-start | bytes 2838536 | tf_op jit(solution)/shard_map/ppermute | solution.py:44
  1048.3 61.2 %collective-permute-start.45 = (bf16[2,256,1536]{2,1,0:T(8,128)(2,1)S(1)}, bf16[2,256,1536]{2,1,0:T(8,128)(2,1)S(1)}, u32[]{:S(2)}, u32[]{:S(2)}) collective-permute-start(bf16[2,256,1536]{2,1,0:T(8,128)(2,1)S(1)} %get-tuple-element.276), channel_id=1, source_target_pairs={{0,1},{1,0},{2,3},{3,2},{4,5},{5,4},{6,7},{7,6},{8,9},{9,8},{10,11... | collective-permute-start | bytes 4718600 | tf_op jit(solution)/shard_map/ppermute | solution.py:44
  1068.0 37.3 %collective-permute-start.42 = (bf16[2,256,1536]{2,1,0:T(8,128)(2,1)S(1)}, bf16[2,256,1536]{2,1,0:T(8,128)(2,1)S(1)}, u32[]{:S(2)}, u32[]{:S(2)}) collective-permute-start(bf16[2,256,1536]{2,1,0:T(8,128)(2,1)S(1)} %add_convert_fusion.1), channel_id=1, source_target_pairs={{0,2},{1,3},{2,0},{3,1},{4,6},{5,7},{6,4},{7,5},{8,10},{9,11},{10,... | collective-permute-start | bytes 4718600 | tf_op jit(solution)/shard_map/ppermute | solution.py:44
  1071.6 66.1 %collective-permute-start.47 = (bf16[2,256,1536]{2,1,0:T(8,128)(2,1)S(1)}, bf16[2,256,1536]{2,1,0:T(8,128)(2,1)S(1)}, u32[]{:S(2)}, u32[]{:S(2)}) collective-permute-start(bf16[2,256,1536]{2,1,0:T(8,128)(2,1)S(1)} %add_convert_fusion), channel_id=1, source_target_pairs={{0,2},{1,3},{2,0},{3,1},{4,6},{5,7},{6,4},{7,5},{8,10},{9,11},{10,... | collective-permute-start | bytes 4718600 | tf_op jit(solution)/shard_map/ppermute | solution.py:44
  1079.9 58.4 %collective-permute-start.53 = (bf16[192,3072]{1,0:T(8,128)(2,1)S(1)}, bf16[192,3072]{1,0:T(8,128)(2,1)S(1)}, u32[]{:S(2)}, u32[]{:S(2)}) collective-permute-start(bf16[192,3072]{1,0:T(8,128)(2,1)S(1)} %get-tuple-element.374), channel_id=1, source_target_pairs={{0,4},{8,0},{16,8},{24,16},{28,24},{20,28},{12,20},{4,12},{1,5},{9... | collective-permute-start | bytes 3538952 | tf_op jit(solution)/shard_map/ppermute | solution.py:128
  1088.4 50.0 %collective-permute-start.52 = (bf16[192,3072]{1,0:T(8,128)(2,1)S(1)}, bf16[192,3072]{1,0:T(8,128)(2,1)S(1)}, u32[]{:S(2)}, u32[]{:S(2)}) collective-permute-start(bf16[192,3072]{1,0:T(8,128)(2,1)S(1)} %get-tuple-element.375), channel_id=1, source_target_pairs={{0,8},{8,16},{16,24},{24,28},{28,20},{20,12},{12,4},{4,0},{1,9},{9... | collective-permute-start | bytes 3538952 | tf_op jit(solution)/shard_map/ppermute | solution.py:128
  (212 other events, 2804.3 us)
Sparse Core Ops, SparseCore 0:
  11.8 147.2 all-gather.3
  161.3 93.3 all-gather.5
  256.8 90.3 all-gather.7
  772.7 179.4 reduce-scatter.4
  959.0 204.9 reduce-scatter.2

commit v8 on v6

--- a/solution.py
+++ b/solution.py
@@ -128,27 +128,58 @@
     return lax.ppermute(value, "dp", hops)
 
 
+def place_kernel(steps, order, *refs):
+    out = refs[-1]
+    for step, (inputs, starts) in enumerate(steps):
+
+        @pl.when(pl.program_id(0) == step)
+        def _():
+            for index, start in zip(inputs, starts):
+                out[:, start : start + refs[index].shape[1]] = refs[index][...]
+
+
+def place_blocks(blocks, steps, order, wide):
+    share = blocks[0].shape[0]
+    return pl.pallas_call(
+        functools.partial(place_kernel, steps),
+        grid_spec=pltpu.PrefetchScalarGridSpec(
+            num_scalar_prefetch=1,
+            grid=(len(steps),),
+            in_specs=[
+                pl.BlockSpec(block.shape, lambda s, order: (0, 0), pipeline_mode=pl.Buffered(1))
+                for block in blocks
+            ],
+            out_specs=pl.BlockSpec((share, wide), lambda s, order: (order[s], 0)),
+        ),
+        out_shape=jax.ShapeDtypeStruct((len(steps) * share, wide), BF16),
+        compiler_params=pltpu.CompilerParams(vmem_limit_bytes=48 * 1024 * 1024),
+        cost_estimate=pl.CostEstimate(flops=0, transcendentals=0, bytes_accessed=1024),
+        name="place_blocks",
+    )(jnp.stack(order).astype(jnp.int32), *blocks)
+
+
 def ring_gather(block, count):
-    share, wide = block.shape
+    wide = block.shape[1]
     half = wide // 2 // LANES * LANES
     place = ring_place(lax.axis_index("dp"), count)
-    whole = jnp.zeros((count * share, wide), block.dtype)
-
-    def put(whole, value, offset, column):
-        row = ring_member(place + offset, count) * share
-        return lax.dynamic_update_slice(whole, value, (row, column))
-
-    whole = put(whole, block, 0, 0)
+    blocks, offsets, steps = [block], [0], [((0,), (0,))]
     behind = ahead = block
     for hop in range(1, count // 2):
         behind = ring_step(behind, 1, count)
         ahead = ring_step(ahead, -1, count)
         behind, ahead = yield behind, ahead
-        whole = put(put(whole, behind, -hop, 0), ahead, hop, 0)
+        blocks += [behind, ahead]
+        offsets += [-hop, hop]
+        steps += [((2 * hop - 1,), (0,)), ((2 * hop,), (0,))]
     behind = ring_step(behind[:, :half], 1, count)
     ahead = ring_step(ahead[:, half:], -1, count)
     behind, ahead = yield behind, ahead
-    yield put(put(whole, behind, -(count // 2), 0), ahead, count // 2, half)
+    blocks += [behind, ahead]
+    offsets.append(count // 2)
+    steps.append(((count - 1, count), (0, half)))
+    yield place_blocks(
+        blocks, steps, [ring_member(place + offset, count) for offset in offsets], wide
+    )
 
 
 def ring_scatter(grad, count):
@@ -583,13 +614,13 @@
     packed_in = gathered(
         image_attention_in.reshape(share, 3 * width), text_attention_in.reshape(share, 3 * width)
     )
+    both_out = gathered(image_attention_out.T, text_attention_out.T)
     image_up = gathered(image_hidden_in)
-    image_down = gathered(image_hidden_out.T)
-    out_ring = ring_gather(
-        jnp.concatenate([image_attention_out.T, text_attention_out.T], axis=1), group_count
-    )
-    out_hop = next(out_ring)
+    packed_text = gathered(text_hidden_in, text_hidden_out.T)
+    down_ring = ring_gather(image_hidden_out.T, group_count)
+    down_hop = next(down_ring)
     weight_in = ((packed_in, 0, 3 * width), (packed_in, 3 * width, 3 * width))
+    weight_out = ((both_out, 0, width), (both_out, width, width))
 
     alive = (jnp.arange(slots) < group_size[0]).astype(F32)[:, None, None]
     cond_full = condition.astype(F32)
@@ -608,8 +639,8 @@
     modulations = lax.all_gather(
         mod_own.reshape(slots, 2, 6, width), "tensor", axis=3, tiled=True
     )
-    modulations, out_hop = lax.optimization_barrier((modulations, out_hop))
-    out_hop = out_ring.send(out_hop)
+    modulations, down_hop = lax.optimization_barrier((modulations, down_hop))
+    down_hop = down_ring.send(down_hop)
     mods = (modulations[:, 0], modulations[:, 1])
 
     tokens = (image_tokens.astype(F32), text_tokens.astype(F32))
@@ -654,49 +685,37 @@
     normed_one, inverse_one, image_first = modulated(tokens[0], mods[0], 0, 1)
     text_normed_one, text_inverse_one, text_first = modulated(tokens[1], mods[1], 0, 1)
     first_pieces = gather_pieces(image_first, size)
-    first_pieces, out_hop = lax.optimization_barrier((first_pieces, out_hop))
-    out_hop = out_ring.send(out_hop)
+    first_pieces, down_hop = lax.optimization_barrier((first_pieces, down_hop))
+    down_hop = down_ring.send(down_hop)
     for _ in range(group_count // 2 - 4):
-        out_hop = out_ring.send(out_hop)
+        down_hop = down_ring.send(down_hop)
     packed = products_of(first_pieces, weight_in[0], 0, low_kinds)
     text_packed = products_of([text_first], weight_in[1], 0, [BF16])
     down_rows = [
         (outgoing[stream] * spread(mods[stream][:, 5])).astype(BF16) for stream in range(2)
     ]
     down_have = gather_start(after(down_rows[0], first_pieces), size)
-    parts, out_hop = after(([*packed, *text_packed], out_hop), down_have)
-    out_hop = out_ring.send(out_hop)
-    up_ring = ring_gather(
-        after(jnp.concatenate([text_hidden_in, text_hidden_out.T], axis=1), parts), group_count
-    )
-    up_hop = next(up_ring)
+    parts, down_hop = after(([*packed, *text_packed], down_hop), down_have)
+    down_hop = down_ring.send(down_hop)
     attended, sums = attend(parts)
     down_pieces = gather_end(after(down_have, attended), size)
-    attended, out_hop, up_hop = lax.optimization_barrier((attended, out_hop, up_hop))
-    both_out = out_ring.send(out_hop)
-    up_hop = up_ring.send(up_hop)
-    weight_out = ((both_out, 0, width), (both_out, width, width))
+    attended, down_hop = lax.optimization_barrier((attended, down_hop))
+    image_down = down_ring.send(down_hop)
     attended_parts = (attended[:-1], attended[-1:])
 
     branch = image_sum(attended_parts[0], weight_out[0], 1)
-    branch, up_hop = lax.optimization_barrier((branch, up_hop))
-    up_hop = up_ring.send(up_hop)
-    text_branch = text_sum(attended_parts[1][0], weight_out[1], 1)
     middle = tokens[0] + spread(mods[0][:, 2]) * branch
     normed_two, inverse_two, image_second = modulated(middle, mods[0], 3, 4)
     second_pieces = gather_pieces(image_second, size)
+    text_branch = text_sum(after(attended_parts[1][0], second_pieces), weight_out[1], 1)
     up_weight, down_weight = (image_up, 0, units), (image_down, 0, units)
     near = hidden_both(second_pieces[:half], down_pieces[:half], up_weight, down_weight)
-    far_pieces, up_hop = after((second_pieces[half:], up_hop), near)
-    up_hop = up_ring.send(up_hop)
+    far_pieces = after(second_pieces[half:], near)
     far = hidden_both(far_pieces, down_pieces[half:], up_weight, down_weight)
     active = [*near[0], *far[0]]
     hidden_grad = [*near[1], *far[1]]
     kept, sent = scatter_start(row_products(hidden_grad, up_weight, 1), size)
-    for _ in range(group_count // 2 - 4):
-        up_hop = up_ring.send(up_hop)
-    up_hop = after(up_hop, sent)
-    text_both = up_ring.send(up_hop)
+    text_both = after(packed_text, sent)
 
     text_up_weight, text_down_weight = (text_both, 0, units), (text_both, units, units)
     text_middle = tokens[1] + spread(mods[1][:, 2]) * text_branch
@@ -716,6 +735,7 @@
     )
     gate_one_grad = jnp.sum(middle_grad * branch, axis=1)
 
+    low = after(low, text_second_grad)
     branch_grads = gather_pieces(low, size)
     text_mlp_grad = weight_grad(
         after([([down_rows[1]], text_active), ([text_second], text_hidden_grad)], low)
@@ -735,15 +755,21 @@
         [
             (first_pieces, packed_grads[:-1]),
             ([text_first], packed_grads[-1:]),
-            (branch_grads, attended_parts[0]),
-            ([text_low], attended_parts[1]),
         ]
     )
     attention_sum = scattered(attention_grad)
+    out_grad = weight_grad(
+        after(
+            [(branch_grads, attended_parts[0]), ([text_low], attended_parts[1])], attention_grad
+        )
+    )
     packed_grads, text_hop, active, text_active = after(
         (packed_grads, text_hop, active, text_active), attention_grad
     )
+    text_hop, image_mlp = lax.optimization_barrier((text_hop, image_mlp))
     text_hop = text_ring.send(text_hop)
+    out_ring = ring_scatter(after(out_grad, image_mlp), group_count)
+    out_hop = next(out_ring)
 
     def first_back(stream, first_grad, normed, inverse, middle_grad):
         mod = mods[stream]
@@ -763,12 +789,17 @@
     text_first_grad = text_sum(packed_grads[-1], weight_in[1], 1, True)
     branch_two = image_sum(active, down_weight, 1, True)
     text_branch_two = text_sum(text_active[0], text_down_weight, 1, True)
-    text_first_grad, text_hop = lax.optimization_barrier((text_first_grad, text_hop))
-    text_hop = text_ring.send(text_hop)
-    for _ in range(group_count // 2 - 4):
+    text_first_grad, text_hop, out_hop = lax.optimization_barrier(
+        (text_first_grad, text_hop, out_hop)
+    )
+    for _ in range(group_count // 2 - 3):
         text_hop = text_ring.send(text_hop)
-    first_grad, text_hop = lax.optimization_barrier((first_grad, text_hop))
+    out_hop = out_ring.send(out_hop)
+    first_grad, text_hop, out_hop = lax.optimization_barrier((first_grad, text_hop, out_hop))
     text_mlp = text_ring.send(text_hop)
+    for _ in range(group_count // 2 - 1):
+        out_hop = out_ring.send(out_hop)
+    out_sum = out_hop
     input_grads = [None, None]
     input_grads[0], shift_one_grad, scale_one_grad = first_back(
         0, first_grad, normed_one, inverse_one, middle_grad
@@ -824,10 +855,9 @@
     activated_part = sum_all(activated_part, size, "tensor").reshape(group_count, slots, share)
     activated_rows = gather_stack(activated_part, group_count, "dp")
     activated_rows = jnp.stack([activated_rows[k, k] for k in range(group_count)])
-    group_order = group_rank ^ jnp.arange(group_count)
     activated_grad = jnp.concatenate(
         [
-            lax.dynamic_index_in_dim(activated_rows, group_order[k], 0, keepdims=False)
+            lax.dynamic_index_in_dim(activated_rows, group_rank ^ k, 0, keepdims=False)
             for k in range(group_count)
         ],
         axis=1,
@@ -842,12 +872,12 @@
         condition_gradient,
         image_ada,
         attention_sum[:, : 3 * width].reshape(share, 3, width),
-        attention_sum[:, 6 * width : 7 * width].T,
+        out_sum[:, :width].T,
         image_mlp[:, units:],
         image_mlp[:, :units].T,
         text_ada,
-        attention_sum[:, 3 * width : 6 * width].reshape(share, 3, width),
-        attention_sum[:, 7 * width :].T,
+        attention_sum[:, 3 * width :].reshape(share, 3, width),
+        out_sum[:, width:].T,
         text_mlp[:, units:],
         text_mlp[:, :units].T,
     )

time: 959 us -> 967 us (level)
  waiting for transfers between devices: 334 us -> 376 us
  starting transfers between devices: 78.1 us -> 59.2 us
  between operations: 32 us -> 17 us
    ppermute x24, waiting for transfers between devices: 34.7 us -> 65 us  [ring_step(): return lax.ppermute(value, 'dp', hops)]
    dynamic_update_slice x17 -> x0, local copies, waits for them, and re-layouts: 23 us -> none  [put(): return lax.dynamic_update_slice(whole, value, (row, column))]
    unnamed x305 -> x363, local copies, waits for them, and re-layouts: 26 us -> 46.8 us
    ppermute x48, waiting for transfers between devices: 299 us -> 311 us  [swap(): return lax.ppermute(value, axis, [(i, i ^ bit) for i in range(size)])]
    ppermute x48, starting transfers between devices: 44 us -> 34.2 us  [swap(): return lax.ppermute(value, axis, [(i, i ^ bit) for i in range(size)])]
  transfers between devices with their start and end apart: 77 -> 78, of which waited for: 32 -> 35; matrix products, arithmetic and copies ran while one was open for 16% -> 13% of each run, Pallas kernels for 31% -> 33%
where the time goes in v8:
time: 967 us; the launch traced here: 958 us
  waiting for transfers between devices  376 us (39%)
  Pallas kernels  320 us (33%)
  other arithmetic  88.5 us (9%)
  local copies, waits for them, and re-layouts  82.8 us (9%)
  starting transfers between devices  59.2 us (6%)
  between operations  17 us (2%)
    ppermute x48, waiting for transfers between devices, swap(): return lax.ppermute(value, axis, [(i, i ^ bit) for i in range(size)])  311 us
    pallas_call x16, Pallas kernels, products_of(): pl.pallas_call(functools.partial(product_kernel, count, weight_dim), grid...  95.3 us
    pallas_call x8, Pallas kernels, weight_grad(): pl.pallas_call(functools.partial(rows_kernel, count), grid=(rows // step,...  67.3 us
    ppermute x24, waiting for transfers between devices, ring_step(): return lax.ppermute(value, 'dp', hops)  65 us
    pallas_call x1, Pallas kernels, attend_back(): pl.pallas_call(functools.partial(attend_back_kernel, count, groups), grid...  58.2 us
    pallas_call x1, Pallas kernels, attend(): pl.pallas_call(functools.partial(attend_kernel, count), grid=(slots, grou...  54.8 us
    unnamed x363, local copies, waits for them, and re-layouts  46.8 us
    pallas_call x3, Pallas kernels, hidden_both(): pl.pallas_call(functools.partial(hidden_kernel, count), grid=(wide // til...  39.4 us
  transfers between devices with their start and end apart: 78, of which 35 were waited for; matrix products, arithmetic and copies ran while one was open for 13% of the time, Pallas kernels for 33%

profile of v8, /device:TPU:0, one launch (start us, length us, event | category | flops | bytes accessed | tf_op | source)
XLA Modules:
  0.0 958.0 jit_solution(9592153623243797711)
XLA Ops:
  27.7 34.9 %collective-permute-done.2 = bf16[4,2,1536]{2,1,0:T(2,128)(2,1)S(1)} collective-permute-done((bf16[4,2,1536]{2,1,0:T(2,128)(2,1)S(1)}, bf16[4,2,1536]{2,1,0:T(2,128)(2,1)S(1)}, u32[]{:S(2)}, u32[]{:S(2)}) %collective-permute-start.2) | collective-permute-done | bytes 24608 | tf_op jit(solution)/shard_map/ppermute | solution.py:44
  68.1 5.9 collective-permute-done.3
  75.7 8.5 collective-permute-done.4
  100.0 35.2 %collective-permute-done.9.refs_2_ = bf16[2,256,1536]{2,1,0:T(8,128)(2,1)} collective-permute-done((bf16[2,256,1536]{2,1,0:T(8,128)(2,1)}, bf16[2,256,1536]{2,1,0:T(8,128)(2,1)}, u32[]{:S(2)}, u32[]{:S(2)}) %collective-permute-start.9) | collective-permute-done | bytes 1572896 | tf_op jit(solution)/shard_map/ppermute | solution.py:44
  142.4 13.8 %collective-permute-done.11.refs_3_ = bf16[192,1536]{1,0:T(8,128)(2,1)S(1)} collective-permute-done((bf16[192,1536]{1,0:T(8,128)(2,1)S(1)}, bf16[192,1536]{1,0:T(8,128)(2,1)S(1)}, u32[]{:S(2)}, u32[]{:S(2)}) %collective-permute-start.11) | collective-permute-done | bytes 589856 | tf_op jit(solution)/shard_map/ppermute | solution.py:128
  165.7 14.5 %products.16 = (bf16[2,256,1152]{2,1,0:T(8,128)(2,1)S(1)}, bf16[2,256,1152]{2,1,0:T(8,128)(2,1)S(1)}, bf16[2,256,1152]{2,1,0:T(8,128)(2,1)S(1)}, bf16[2,256,1152]{2,1,0:T(8,128)(2,1)S(1)}) custom-call(bf16[2,256,1536]{2,1,0:T(8,128)(2,1)} %fusion.7.refs_0_, bf16[2,256,1536]{2,1,0:T(8,128)(2,1)} %collective-permute-done.8.refs_1_, ...), custom_call_target="tpu_custom_call" | custom-call | bytes 1024 | tf_op jit(solution)/shard_map/products/pallas_call | solution.py:503
  186.2 8.3 collective-permute-done.14.refs_6_
  198.2 54.8 %attend.1 = (bf16[2,256,384]{2,1,0:T(8,128)(2,1)S(1)}, bf16[2,256,384]{2,1,0:T(8,128)(2,1)S(1)}, bf16[2,256,384]{2,1,0:T(8,128)(2,1)S(1)}, bf16[2,256,384]{2,1,0...) custom-call(bf16[2,256,1152]{2,1,0:T(8,128)(2,1)S(1)} %get-tuple-ele, ...), custom_call_target="tpu_custom_call" | custom-call | flops 17051860992 | bytes 7237632 | tf_op jit(solution)/shard_map/attend/pallas_call | solution.py:345
  268.3 33.8 %collective-permute-done.20 = bf16[2,256,1536]{2,1,0:T(8,128)(2,1)S(1)} collective-permute-done((bf16[2,256,1536]{2,1,0:T(8,128)(2,1)S(1)}, bf16[2,256,1536]{2,1,0:T(8,128)(2,1)S(1)}, u32[]{:S(2)}, u32[]{:S(2)}) %collective-permute-start.20) | collective-permute-done | bytes 1572896 | tf_op jit(solution)/shard_map/ppermute | solution.py:44
  306.8 33.8 %collective-permute-done.23.refs_0_.refs_2_ = bf16[2,256,1536]{2,1,0:T(8,128)(2,1)S(1)} collective-permute-done((bf16[2,256,1536]{2,1,0:T(8,128)(2,1)S(1)}, bf16[2,256,1536]{2,1,0:T(8,128)(2,1)S(1)}, u32[]{:S(2)}, u32[]{:S(2)}) %collective-permute-start.23) | collective-permute-done | bytes 1572896 | tf_op jit(solution)/shard_map/ppermute | solution.py:44
  363.5 16.0 %hidden_both.3 = (bf16[2,256,1536]{2,1,0:T(8,128)(2,1)S(1)}, bf16[2,256,1536]{2,1,0:T(8,128)(2,1)S(1)}, bf16[2,256,1536]{2,1,0:T(8,128)(2,1)S(1)}, bf16[2,256,1536]{2,1,0:T(8,128)(2,1)}) custom-call(bf16[2,256,1536]{2,1,0:T(8,128)(2,1)} %copy-done.10, bf16[2,256,1536]{2,1,0:T(8,128)(2,1)} %copy-done.24, ...), custom_call_target="tpu_custom_call" | custom-call | bytes 1024 | tf_op jit(solution)/shard_map/hidden_both/pallas_call | solution.py:553
  381.9 16.5 %hidden_both.4 = (bf16[2,256,1536]{2,1,0:T(8,128)(2,1)S(1)}, bf16[2,256,1536]{2,1,0:T(8,128)(2,1)S(1)}, bf16[2,256,1536]{2,1,0:T(8,128)(2,1)S(1)}, bf16[2,256,1536]{2,1,0:T(8,128)(2,1)}) custom-call(bf16[2,256,1536]{2,1,0:T(8,128)(2,1)} %copy-done.22, bf16[2,256,1536]{2,1,0:T(8,128)(2,1)} %collective-permute-done.24.refs_1_.refs_3_, ...), custom_call_target="tpu_custom_call" | custom-call | bytes 1024 | tf_op jit(solution)/shard_map/hidden_both/pallas_call | solution.py:553
  402.1 8.0 products.20
  416.1 8.3 products.21
  426.3 15.4 %weight_grad.8.refs_8_ = bf16[1536,3072]{1,0:T(8,128)(2,1)} custom-call(bf16[2,256,1536]{2,1,0:T(8,128)(2,1)} %multiply_convert_fusion.2.refs_2_.refs_0_, bf16[2,256,1536]{2,1,0:T(8,128)(2,1)} %collective-permute-done.22.refs_3_.refs_1_, bf16[2,256,1536]{2,1,0:T(8,128)(2,1)} %collective-permute-done.15.refs_2_, ...), custom_call_target="tpu_custom_call" | custom-call | bytes 1024 | tf_op jit(solution)/shard_map/weight_grad/pallas_call | solution.py:426
  441.7 15.2 %weight_grad.9 = bf16[1536,3072]{1,0:T(8,128)(2,1)} custom-call(bf16[2,256,1536]{2,1,0:T(8,128)(2,1)S(1)} %copy-done.11, bf16[2,256,1536]{2,1,0:T(8,128)(2,1)S(1)} %copy-done.25, bf16[2,256,1536]{2,1,0:T(8,128)(2,1)S(1)} %copy-done.23, bf16[2,256,1536]{2,1,0:T(8,128)(2,1)} %collective-permute-done.24.refs_1_.refs_3_, ...), custom_call_target="tpu_custom_call", output_to_operand_aliasing={{}: (8, {})} | custom-call | bytes 1024 | tf_op jit(solution)/shard_map/weight_grad/pallas_call | solution.py:426
  463.0 6.8 hidden_both.5
  499.0 16.3 %collective-permute-done.32 = bf16[2,154,1536]{2,0,1:T(2,128)(2,1)S(1)} collective-permute-done((bf16[2,154,1536]{2,0,1:T(2,128)(2,1)S(1)}, bf16[2,154,1536]{2,0,1:T(2,128)(2,1)S(1)}, u32[]{:S(2)}, u32[]{:S(2)}) %collective-permute-start.32) | collective-permute-done | bytes 946208 | tf_op jit(solution)/shard_map/ppermute | solution.py:44
  533.1 21.4 %collective-permute-done.34.refs_2_ = bf16[2,256,1536]{2,1,0:T(8,128)(2,1)} collective-permute-done((bf16[2,256,1536]{2,1,0:T(8,128)(2,1)}, bf16[2,256,1536]{2,1,0:T(8,128)(2,1)}, u32[]{:S(2)}, u32[]{:S(2)}) %collective-permute-start.34) | collective-permute-done | bytes 1572896 | tf_op jit(solution)/shard_map/ppermute | solution.py:44
  563.7 6.3 products.24
  570.0 58.2 %attend_back.1 = (bf16[2,256,1152]{2,1,0:T(8,128)(2,1)S(1)}, bf16[2,256,1152]{2,1,0:T(8,128)(2,1)S(1)}, bf16[2,256,1152]{2,1,0:T(8,128)(2,1)}, bf16[2,256,1152]{2,1,0:T(8,128)(2,1)}, bf16[2,154,1152]{2,1,0:T(8,128)(2,1)S(1)}) custom-call(bf16[2,256,1152]{2,1,0:T(8,128)(2,1)} %copy-done.73, bf16[2,256,1152]{2,1,0:T(8,128)(2,1)} %copy-done.74, ...), custom_call_target="tpu_custom_call" | custom-call | flops 42629652480 | bytes 12665856 | tf_op jit(solution)/shard_map/attend_back/pallas_call | solution.py:372
  638.5 11.7 %weight_grad.12.refs_2_ = bf16[1536,2304]{1,0:T(8,128)(2,1)} custom-call(bf16[2,256,1536]{2,1,0:T(8,128)(2,1)} %fusion.7.refs_0_, bf16[2,256,1536]{2,1,0:T(8,128)(2,1)} %collective-permute-done.8.refs_1_, bf16[2,256,1536]{2,1,0:T(8,128)(2,1)} %collective-permute-done.9.refs_2_, bf16[2,256,1536]{2,1,0:T(8,128)(2,1)} %collective-permute-done.10.refs_3_, ...), custom_call_target="tpu_custom_call" | custom-call | bytes 1024 | tf_op jit(solution)/shard_map/weight_grad/pallas_call | solution.py:426
  660.4 7.4 weight_grad.14.refs_2_
  676.2 7.8 products.26
  683.9 6.8 products.29
  698.3 7.9 products.27
  715.0 6.8 products.30
  734.6 47.8 %collective-permute-done.49 = bf16[2,154,1536]{2,0,1:T(2,128)(2,1)S(1)} collective-permute-done((bf16[2,154,1536]{2,0,1:T(2,128)(2,1)S(1)}, bf16[2,154,1536]{2,0,1:T(2,128)(2,1)S(1)}, u32[]{:S(2)}, u32[]{:S(2)}) %collective-permute-start.49) | collective-permute-done | bytes 946208 | tf_op jit(solution)/shard_map/ppermute | solution.py:44
  785.7 17.0 %collective-permute-done.44 = bf16[2,154,1536]{2,0,1:T(2,128)(2,1)S(1)} collective-permute-done((bf16[2,154,1536]{2,0,1:T(2,128)(2,1)S(1)}, bf16[2,154,1536]{2,0,1:T(2,128)(2,1)S(1)}, u32[]{:S(2)}, u32[]{:S(2)}) %collective-permute-start.44) | collective-permute-done | bytes 946208 | tf_op jit(solution)/shard_map/ppermute | solution.py:44
  816.2 19.7 %collective-permute-done.42 = bf16[2,256,1536]{2,1,0:T(8,128)(2,1)} collective-permute-done((bf16[2,256,1536]{2,1,0:T(8,128)(2,1)}, bf16[2,256,1536]{2,1,0:T(8,128)(2,1)}, u32[]{:S(2)}, u32[]{:S(2)}) %collective-permute-start.42) | collective-permute-done | bytes 1572896 | tf_op jit(solution)/shard_map/ppermute | solution.py:44
  865.2 19.6 %collective-permute-done.56 = bf16[192,768]{1,0:T(8,128)(2,1)} collective-permute-done((bf16[192,768]{1,0:T(8,128)(2,1)}, bf16[192,768]{1,0:T(8,128)(2,1)}, u32[]{:S(2)}, u32[]{:S(2)}) %collective-permute-start.56) | collective-permute-done | bytes 294944 | tf_op jit(solution)/shard_map/ppermute | solution.py:128
  937.3 5.8 collective-permute-done.70
  (658 shorter events, 350.8 us)
Async XLA Ops:
  7.2 158.5 %all-gather.5.cloned.1.call-start = ((), (), s32[]{:S(2)}) async-start(), calls=%async_computation.2 | async-start | bytes 7962624 | tf_op jit(solution)/shard_map/all_gather | solution.py:612
  10.5 245.8 %all-gather.7.cloned.1.call-start = ((), (), s32[]{:S(2)}) async-start(), calls=%async_computation.3 | async-start | bytes 2654208 | tf_op jit(solution)/shard_map/all_gather | solution.py:612
  11.3 352.3 %all-gather.9.cloned.1.call-start = ((), (), s32[]{:S(2)}) async-start(), calls=%async_computation.4 | async-start | bytes 5308416 | tf_op jit(solution)/shard_map/all_gather | solution.py:612
  14.4 411.8 %all-gather.11.cloned.1.call-start = ((), (), s32[]{:S(2)}) async-start(), calls=%async_computation.5 | async-start | bytes 10616832 | tf_op jit(solution)/shard_map/all_gather | solution.py:612
  18.2 76.7 %collective-permute-start.6 = (bf16[192,1536]{1,0:T(8,128)(2,1)S(1)}, bf16[192,1536]{1,0:T(8,128)(2,1)S(1)}, u32[]{:S(2)}, u32[]{:S(2)}) collective-permute-start(bf16[192,1536]{1,0:T(8,128)(2,1)S(1)} %bitcast.187), channel_id=1, source_target_pairs={{0,8},{8,16},{16,24},{24,28},{28,20},{20,12},{12,4},{4,0},{1,9},{9... | collective-permute-start | bytes 1769480 | tf_op jit(solution)/shard_map/ppermute | solution.py:128
  18.3 76.6 %collective-permute-start.7 = (bf16[192,1536]{1,0:T(8,128)(2,1)S(1)}, bf16[192,1536]{1,0:T(8,128)(2,1)S(1)}, u32[]{:S(2)}, u32[]{:S(2)}) collective-permute-start(bf16[192,1536]{1,0:T(8,128)(2,1)S(1)} %bitcast.188), channel_id=1, source_target_pairs={{0,4},{8,0},{16,8},{24,16},{28,24},{20,28},{12,20},{4,12},{1,5},{9... | collective-permute-start | bytes 1769480 | tf_op jit(solution)/shard_map/ppermute | solution.py:128
  20.3 42.4 %collective-permute-start.2 = (bf16[4,2,1536]{2,1,0:T(2,128)(2,1)S(1)}, bf16[4,2,1536]{2,1,0:T(2,128)(2,1)S(1)}, u32[]{:S(2)}, u32[]{:S(2)}) collective-permute-start(bf16[4,2,1536]{2,1,0:T(2,128)(2,1)S(1)} %pad_maximum_fusion.11), channel_id=1, source_target_pairs={{0,16},{4,20},{8,24},{12,28},{16,0},{20,4},{24,8},{28,12},{1,17},{... | collective-permute-start | bytes 73736 | tf_op jit(solution)/shard_map/ppermute | solution.py:44
  98.1 37.1 %collective-permute-start.9 = (bf16[2,256,1536]{2,1,0:T(8,128)(2,1)}, bf16[2,256,1536]{2,1,0:T(8,128)(2,1)}, u32[]{:S(2)}, u32[]{:S(2)}) collective-permute-start(bf16[2,256,1536]{2,1,0:T(8,128)(2,1)} %fusion.7.refs_0_), channel_id=1, source_target_pairs={{0,2},{1,3},{2,0},{3,1},{4,6},{5,7},{6,4},{7,5},{8,10},{9,11},{10,... | collective-permute-start | bytes 4718600 | tf_op jit(solution)/shard_map/ppermute | solution.py:44
  99.9 60.3 %collective-permute-start.8 = (bf16[2,256,1536]{2,1,0:T(8,128)(2,1)}, bf16[2,256,1536]{2,1,0:T(8,128)(2,1)}, u32[]{:S(2)}, u32[]{:S(2)}) collective-permute-start(bf16[2,256,1536]{2,1,0:T(8,128)(2,1)} %fusion.7.refs_0_), channel_id=1, source_target_pairs={{0,1},{1,0},{2,3},{3,2},{4,5},{5,4},{6,7},{7,6},{8,9},{9,8},{10,11... | collective-permute-start | bytes 4718600 | tf_op jit(solution)/shard_map/ppermute | solution.py:44
  136.3 672.3 %reduce-scatter.3.cloned.1.call-start = ((), (), s32[]{:S(2)}) async-start(), calls=%async_computation.6 | async-start | bytes 10616832 | tf_op jit(solution)/shard_map/reduce_scatter | solution.py:653
  195.9 59.6 %collective-permute-start.16 = (bf16[192,768]{1,0:T(8,128)(2,1)S(1)}, bf16[192,768]{1,0:T(8,128)(2,1)S(1)}, u32[]{:S(2)}, u32[]{:S(2)}) collective-permute-start(bf16[192,768]{1,0:T(8,128)(2,1)S(1)} %slice.172), channel_id=1, source_target_pairs={{0,8},{8,16},{16,24},{24,28},{28,20},{20,12},{12,4},{4,0},{1,9},{9... | collective-permute-start | bytes 884744 | tf_op jit(solution)/shard_map/ppermute | solution.py:128
  196.0 59.5 %collective-permute-start.17 = (bf16[192,768]{1,0:T(8,128)(2,1)S(1)}, bf16[192,768]{1,0:T(8,128)(2,1)S(1)}, u32[]{:S(2)}, u32[]{:S(2)}) collective-permute-start(bf16[192,768]{1,0:T(8,128)(2,1)S(1)} %slice.173), channel_id=1, source_target_pairs={{0,4},{8,0},{16,8},{24,16},{28,24},{20,28},{12,20},{4,12},{1,5},{9... | collective-permute-start | bytes 884744 | tf_op jit(solution)/shard_map/ppermute | solution.py:128
  265.8 36.4 %collective-permute-start.20 = (bf16[2,256,1536]{2,1,0:T(8,128)(2,1)S(1)}, bf16[2,256,1536]{2,1,0:T(8,128)(2,1)S(1)}, u32[]{:S(2)}, u32[]{:S(2)}) collective-permute-start(bf16[2,256,1536]{2,1,0:T(8,128)(2,1)S(1)} %add_convert_fusion.4), channel_id=1, source_target_pairs={{0,2},{1,3},{2,0},{3,1},{4,6},{5,7},{6,4},{7,5},{8,10},{9,11},{10,... | collective-permute-start | bytes 4718600 | tf_op jit(solution)/shard_map/ppermute | solution.py:44
  341.1 40.8 %collective-permute-start.25 = (bf16[2,256,1536]{2,1,0:T(8,128)(2,1)}, bf16[2,256,1536]{2,1,0:T(8,128)(2,1)}, u32[]{:S(2)}, u32[]{:S(2)}) collective-permute-start(bf16[2,256,1536]{2,1,0:T(8,128)(2,1)} %collective-permute-done.15.refs_2_), channel_id=1, source_target_pairs={{0,1},{1,0},{2,3},{3,2},{4,5},{5,4},{6,7},{7,6},{8,9},{9,8},{10,11... | collective-permute-start | bytes 4718600 | tf_op jit(solution)/shard_map/ppermute | solution.py:44
  351.7 58.8 %collective-permute-start.29 = (f32[2,154,1536]{2,0,1:T(2,128)}, f32[2,154,1536]{2,0,1:T(2,128)}, u32[]{:S(2)}, u32[]{:S(2)}) collective-permute-start(f32[2,154,1536]{2,0,1:T(2,128)} %copy.73), channel_id=1, source_target_pairs={{0,1},{1,0},{2,3},{3,2},{4,5},{5,4},{6,7},{7,6},{8,9},{9,8},{10,11... | collective-permute-start | bytes 5677064 | tf_op jit(solution)/shard_map/ppermute | solution.py:44
  414.3 42.6 %collective-permute-start.30 = (bf16[2,154,1536]{2,0,1:T(2,128)(2,1)}, bf16[2,154,1536]{2,0,1:T(2,128)(2,1)}, u32[]{:S(2)}, u32[]{:S(2)}) collective-permute-start(bf16[2,154,1536]{2,0,1:T(2,128)(2,1)} %copy.75), channel_id=1, source_target_pairs={{0,2},{1,3},{2,0},{3,1},{4,6},{5,7},{6,4},{7,5},{8,10},{9,11},{10,... | collective-permute-start | bytes 2838536 | tf_op jit(solution)/shard_map/ppermute | solution.py:44
  424.3 53.7 %collective-permute-start.26 = (bf16[2,256,1536]{2,1,0:T(8,128)(2,1)}, bf16[2,256,1536]{2,1,0:T(8,128)(2,1)}, u32[]{:S(2)}, u32[]{:S(2)}) collective-permute-start(bf16[2,256,1536]{2,1,0:T(8,128)(2,1)} %get-tuple-element.226), channel_id=1, source_target_pairs={{0,1},{1,0},{2,3},{3,2},{4,5},{5,4},{6,7},{7,6},{8,9},{9,8},{10,11... | collective-permute-start | bytes 4718600 | tf_op jit(solution)/shard_map/ppermute | solution.py:44
  426.0 52.1 %collective-permute-start.28 = (bf16[2,256,1536]{2,1,0:T(8,128)(2,1)}, bf16[2,256,1536]{2,1,0:T(8,128)(2,1)}, u32[]{:S(2)}, u32[]{:S(2)}) collective-permute-start(bf16[2,256,1536]{2,1,0:T(8,128)(2,1)} %add_convert_fusion.2), channel_id=1, source_target_pairs={{0,2},{1,3},{2,0},{3,1},{4,6},{5,7},{6,4},{7,5},{8,10},{9,11},{10,... | collective-permute-start | bytes 4718600 | tf_op jit(solution)/shard_map/ppermute | solution.py:44
  482.2 379.5 %reduce-scatter.5.cloned.1.call-start = ((), (), s32[]{:S(2)}) async-start(), calls=%async_computation.7 | async-start | bytes 7962624 | tf_op jit(solution)/shard_map/reduce_scatter | solution.py:653
  520.0 39.3 %collective-permute-start.33 = (bf16[2,256,1536]{2,1,0:T(8,128)(2,1)}, bf16[2,256,1536]{2,1,0:T(8,128)(2,1)S(1)}, u32[]{:S(2)}, u32[]{:S(2)}) collective-permute-start(bf16[2,256,1536]{2,1,0:T(8,128)(2,1)} %multiply_convert_fusion.1.refs_0_), channel_id=1, source_target_pairs={{0,1},{1,0},{2,3},{3,2},{4,5},{5,4},{6,7},{7,6},{8,9},{9,8},{10,11... | collective-permute-start | bytes 4718600 | tf_op jit(solution)/shard_map/ppermute | solution.py:44
  561.5 66.7 %collective-permute-start.36 = (bf16[192,1536]{1,0:T(8,128)(2,1)S(1)}, bf16[192,1536]{1,0:T(8,128)(2,1)S(1)}, u32[]{:S(2)}, u32[]{:S(2)}) collective-permute-start(bf16[192,1536]{1,0:T(8,128)(2,1)S(1)} %get-tuple-element.425), channel_id=1, source_target_pairs={{0,8},{8,16},{16,24},{24,28},{28,20},{20,12},{12,4},{4,0},{1,9},{9... | collective-permute-start | bytes 1769480 | tf_op jit(solution)/shard_map/ppermute | solution.py:128
  561.7 66.6 %collective-permute-start.37 = (bf16[192,1536]{1,0:T(8,128)(2,1)S(1)}, bf16[192,1536]{1,0:T(8,128)(2,1)S(1)}, u32[]{:S(2)}, u32[]{:S(2)}) collective-permute-start(bf16[192,1536]{1,0:T(8,128)(2,1)S(1)} %get-tuple-element.424), channel_id=1, source_target_pairs={{0,4},{8,0},{16,8},{24,16},{28,24},{20,28},{12,20},{4,12},{1,5},{9... | collective-permute-start | bytes 1769480 | tf_op jit(solution)/shard_map/ppermute | solution.py:128
  632.6 41.6 %collective-permute-start.38 = (bf16[192,3072]{1,0:T(8,128)(2,1)}, bf16[192,3072]{1,0:T(8,128)(2,1)}, u32[]{:S(2)}, u32[]{:S(2)}) collective-permute-start(bf16[192,3072]{1,0:T(8,128)(2,1)} %get-tuple-element.423), channel_id=1, source_target_pairs={{0,8},{8,16},{16,24},{24,28},{28,20},{20,12},{12,4},{4,0},{1,9},{9... | collective-permute-start | bytes 3538952 | tf_op jit(solution)/shard_map/ppermute | solution.py:128
  632.7 43.4 %collective-permute-start.39 = (bf16[192,3072]{1,0:T(8,128)(2,1)}, bf16[192,3072]{1,0:T(8,128)(2,1)}, u32[]{:S(2)}, u32[]{:S(2)}) collective-permute-start(bf16[192,3072]{1,0:T(8,128)(2,1)} %get-tuple-element.422), channel_id=1, source_target_pairs={{0,4},{8,0},{16,8},{24,16},{28,24},{20,28},{12,20},{4,12},{1,5},{9... | collective-permute-start | bytes 3538952 | tf_op jit(solution)/shard_map/ppermute | solution.py:128
  683.9 46.0 %collective-permute-start.41 = (bf16[2,256,1536]{2,1,0:T(8,128)(2,1)S(1)}, bf16[2,256,1536]{2,1,0:T(8,128)(2,1)}, u32[]{:S(2)}, u32[]{:S(2)}) collective-permute-start(bf16[2,256,1536]{2,1,0:T(8,128)(2,1)S(1)} %get-tuple-element.287), channel_id=1, source_target_pairs={{0,1},{1,0},{2,3},{3,2},{4,5},{5,4},{6,7},{7,6},{8,9},{9,8},{10,11... | collective-permute-start | bytes 4718600 | tf_op jit(solution)/shard_map/ppermute | solution.py:44
  706.2 109.9 %collective-permute-start.40 = (bf16[2,256,1536]{2,1,0:T(8,128)(2,1)S(1)}, bf16[2,256,1536]{2,1,0:T(8,128)(2,1)}, u32[]{:S(2)}, u32[]{:S(2)}) collective-permute-start(bf16[2,256,1536]{2,1,0:T(8,128)(2,1)S(1)} %get-tuple-element.291), channel_id=1, source_target_pairs={{0,1},{1,0},{2,3},{3,2},{4,5},{5,4},{6,7},{7,6},{8,9},{9,8},{10,11... | collective-permute-start | bytes 4718600 | tf_op jit(solution)/shard_map/ppermute | solution.py:44
  721.8 84.5 %collective-permute-start.45 = (bf16[2,256,1536]{2,1,0:T(8,128)(2,1)S(1)}, bf16[2,256,1536]{2,1,0:T(8,128)(2,1)S(1)}, u32[]{:S(2)}, u32[]{:S(2)}) collective-permute-start(bf16[2,256,1536]{2,1,0:T(8,128)(2,1)S(1)} %get-tuple-element.302), channel_id=1, source_target_pairs={{0,1},{1,0},{2,3},{3,2},{4,5},{5,4},{6,7},{7,6},{8,9},{9,8},{10,11... | collective-permute-start | bytes 4718600 | tf_op jit(solution)/shard_map/ppermute | solution.py:44
  724.9 81.4 %collective-permute-start.47 = (bf16[2,256,1536]{2,1,0:T(8,128)(2,1)S(1)}, bf16[2,256,1536]{2,1,0:T(8,128)(2,1)S(1)}, u32[]{:S(2)}, u32[]{:S(2)}) collective-permute-start(bf16[2,256,1536]{2,1,0:T(8,128)(2,1)S(1)} %add_convert_fusion), channel_id=1, source_target_pairs={{0,2},{1,3},{2,0},{3,1},{4,6},{5,7},{6,4},{7,5},{8,10},{9,11},{10,... | collective-permute-start | bytes 4718600 | tf_op jit(solution)/shard_map/ppermute | solution.py:44
  727.9 54.6 %collective-permute-start.49 = (bf16[2,154,1536]{2,0,1:T(2,128)(2,1)S(1)}, bf16[2,154,1536]{2,0,1:T(2,128)(2,1)S(1)}, u32[]{:S(2)}, u32[]{:S(2)}) collective-permute-start(bf16[2,154,1536]{2,0,1:T(2,128)(2,1)S(1)} %copy.88), channel_id=1, source_target_pairs={{0,2},{1,3},{2,0},{3,1},{4,6},{5,7},{6,4},{7,5},{8,10},{9,11},{10,... | collective-permute-start | bytes 2838536 | tf_op jit(solution)/shard_map/ppermute | solution.py:44
  730.0 72.8 %collective-permute-start.44 = (bf16[2,154,1536]{2,0,1:T(2,128)(2,1)S(1)}, bf16[2,154,1536]{2,0,1:T(2,128)(2,1)S(1)}, u32[]{:S(2)}, u32[]{:S(2)}) collective-permute-start(bf16[2,154,1536]{2,0,1:T(2,128)(2,1)S(1)} %copy.84), channel_id=1, source_target_pairs={{0,2},{1,3},{2,0},{3,1},{4,6},{5,7},{6,4},{7,5},{8,10},{9,11},{10,... | collective-permute-start | bytes 2838536 | tf_op jit(solution)/shard_map/ppermute | solution.py:44
  782.4 53.4 %collective-permute-start.42 = (bf16[2,256,1536]{2,1,0:T(8,128)(2,1)}, bf16[2,256,1536]{2,1,0:T(8,128)(2,1)}, u32[]{:S(2)}, u32[]{:S(2)}) collective-permute-start(bf16[2,256,1536]{2,1,0:T(8,128)(2,1)} %add_convert_fusion.1), channel_id=1, source_target_pairs={{0,2},{1,3},{2,0},{3,1},{4,6},{5,7},{6,4},{7,5},{8,10},{9,11},{10,... | collective-permute-start | bytes 4718600 | tf_op jit(solution)/shard_map/ppermute | solution.py:44
  892.2 41.7 %collective-permute-start.68 = (bf16[192,768]{1,0:T(8,128)(2,1)}, bf16[192,768]{1,0:T(8,128)(2,1)}, u32[]{:S(2)}, u32[]{:S(2)}) collective-permute-start(bf16[192,768]{1,0:T(8,128)(2,1)} %add_convert_fusion.15), channel_id=1, source_target_pairs={{0,8},{8,16},{16,24},{24,28},{28,20},{20,12},{12,4},{4,0},{1,9},{9... | collective-permute-start | bytes 884744 | tf_op jit(solution)/shard_map/ppermute | solution.py:128
  (217 other events, 2918.5 us)
Sparse Core Ops, SparseCore 0:
  10.8 125.7 all-gather.4
  139.4 58.3 all-gather.6
  199.9 79.7 all-gather.8
  282.3 136.1 all-gather.10
  482.3 183.3 reduce-scatter.2
  669.2 135.9 reduce-scatter.4

commit v9 on v5

--- a/solution.py
+++ b/solution.py
@@ -53,13 +53,23 @@
     return bits
 
 
-def gather_pieces(value, size, axis="tensor", gate=None):
+def gather_start(value, size, axis="tensor"):
     have = {0: value}
-    for bit in reversed(bits_of(size)):
-        if bit == 1 and gate is not None:
-            have = after(have, gate)
+    for bit in reversed(bits_of(size)[1:]):
         have.update({k ^ bit: swap(v, bit, size, axis) for k, v in list(have.items())})
-    return [have[k] for k in range(size)]
+    return have
+
+
+def gather_end(have, size, first=0, axis="tensor"):
+    have = have | {k ^ 1: swap(v, 1, size, axis) for k, v in have.items()}
+    return [have[k] for k in range(first, first + len(have))]
+
+
+def gather_pieces(value, size, reach=None, axis="tensor"):
+    have = {0: value}
+    for bit in reversed(bits_of(reach or size)):
+        have.update({k ^ bit: swap(v, bit, size, axis) for k, v in list(have.items())})
+    return [have[k] for k in sorted(have)]
 
 
 def gather_stack(value, size, axis):
@@ -119,29 +129,6 @@
     ring = ring_of(count)
     hops = [(ring[i], ring[(i + way) % count]) for i in range(count)]
     return lax.ppermute(value, "dp", hops)
-
-
-def ring_gather(block, count):
-    share, wide = block.shape
-    half = wide // 2 // LANES * LANES
-    place = ring_place(lax.axis_index("dp"), count)
-    whole = jnp.zeros((count * share, wide), block.dtype)
-
-    def put(whole, value, offset, column):
-        row = ring_member(place + offset, count) * share
-        return lax.dynamic_update_slice(whole, value, (row, column))
-
-    whole = put(whole, block, 0, 0)
-    behind = ahead = block
-    for hop in range(1, count // 2):
-        behind = ring_step(behind, 1, count)
-        ahead = ring_step(ahead, -1, count)
-        behind, ahead = yield behind, ahead
-        whole = put(put(whole, behind, -hop, 0), ahead, hop, 0)
-    behind = ring_step(behind[:, :half], 1, count)
-    ahead = ring_step(ahead[:, half:], -1, count)
-    behind, ahead = yield behind, ahead
-    yield put(put(whole, behind, -(count // 2), 0), ahead, count // 2, half)
 
 
 def ring_scatter(grad, count):
@@ -456,22 +443,30 @@
     return array[:, start : start + wide]
 
 
+def row_blocks(ref):
+    slots, rows, columns = ref.shape
+    if rows % 16 == 0:
+        return [(slice(None), ref[...].reshape(slots * rows, columns))]
+    return [(slice(slot, slot + 1), ref[slot]) for slot in range(slots)]
+
+
+def store_rows(ref, place, value):
+    slots = ref.shape[0] if place == slice(None) else 1
+    ref[place] = value.reshape(slots, -1, value.shape[-1]).astype(ref.dtype)
+
+
 def product_kernel(count, weight_dim, *refs):
-    pieces, weight, outs, rows_all = refs[:count], refs[count], refs[count + 1 : -1], refs[-1]
-
-    @pl.when(pl.program_id(1) == 0)
-    def _():
-        load_rows(pieces, rows_all)
-
-    total = dot(rows_all[...], weight[...], 1, weight_dim)
-    start = 0
-    for out in outs:
-        rows = out.shape[1]
-        out[0] = total[start : start + rows].astype(out.dtype)
-        start += rows
-
-
-def products_of(pieces, weight, weight_dim, kinds):
+    pieces, weight, outs = refs[:count], refs[count], refs[count + 1 :]
+    for piece, out in zip(pieces, outs):
+        for place, rows in row_blocks(piece):
+            store_rows(out, place, dot(rows, weight[...], 1, weight_dim))
+
+
+def whole_block(array):
+    return pl.BlockSpec(array.shape, lambda j: (0, 0, 0), pipeline_mode=pl.Buffered(1))
+
+
+def products_of(pieces, weight, weight_dim, kinds, late=False):
     array, start, wide = weight
     if not fits(weight) or (weight_dim and start % wide):
         return [
@@ -480,32 +475,31 @@
         ]
     count = len(pieces)
     slots, _, depth = pieces[0].shape
-    total = sum(piece.shape[1] for piece in pieces)
     if weight_dim:
         result = array.shape[0]
         tile = tile_of(result, 0, 768)
-        block = pl.BlockSpec((tile, wide), lambda s, j: (j, start // wide))
+        block = pl.BlockSpec((tile, wide), lambda j: (j, start // wide))
     else:
         result = wide
         tile = tile_of(wide, start, 768)
-        block = pl.BlockSpec((depth, tile), lambda s, j: (0, start // tile + j))
+        block = pl.BlockSpec((depth, tile), lambda j: (0, start // tile + j))
+    rows = slots * sum(piece.shape[1] for piece in pieces)
+    cost = pl.CostEstimate(
+        flops=4 * rows * depth * result, transcendentals=0, bytes_accessed=4 * rows * result
+    )
     return pl.pallas_call(
         functools.partial(product_kernel, count, weight_dim),
-        grid=(slots, result // tile),
-        in_specs=[
-            pl.BlockSpec((1, piece.shape[1], depth), lambda s, j: (s, 0, 0)) for piece in pieces
-        ]
-        + [block],
+        grid=(result // tile,),
+        in_specs=[whole_block(piece) for piece in pieces] + [block],
         out_specs=[
-            pl.BlockSpec((1, piece.shape[1], tile), lambda s, j: (s, 0, j)) for piece in pieces
+            pl.BlockSpec((slots, piece.shape[1], tile), lambda j: (0, 0, j)) for piece in pieces
         ],
         out_shape=[
             jax.ShapeDtypeStruct((slots, piece.shape[1], result), kind)
             for piece, kind in zip(pieces, kinds)
         ],
-        scratch_shapes=[pltpu.VMEM((total, depth), BF16)],
         compiler_params=LIMIT,
-        cost_estimate=NO_COST,
+        cost_estimate=cost if late else NO_COST,
         name="products",
     )(*pieces, array)
 
@@ -514,15 +508,18 @@
     pieces, downs, up, down = refs[:count], refs[count : 2 * count], refs[2 * count], refs[2 * count + 1]
     actives, grads = refs[2 * count + 2 : 3 * count + 2], refs[3 * count + 2 :]
     for piece, upstream, active, grad in zip(pieces, downs, actives, grads):
-        hidden = dot(piece[0], up[...], 1, 0)
-        active_grad = dot(upstream[0], down[...], 1, 0)
-        square = hidden * hidden
-        scale = (2 / math.pi) ** 0.5
-        bend = jnp.tanh(hidden * (scale + scale * 0.044715 * square))
-        half = 0.5 + 0.5 * bend
-        slope = half + hidden * (0.5 - 0.5 * bend * bend) * (scale + scale * 0.134145 * square)
-        active[0] = (hidden * half).astype(BF16)
-        grad[0] = (active_grad * slope).astype(BF16)
+        for (place, rows), (_, above) in zip(row_blocks(piece), row_blocks(upstream)):
+            hidden = dot(rows, up[...], 1, 0)
+            active_grad = dot(above, down[...], 1, 0)
+            square = hidden * hidden
+            scale = (2 / math.pi) ** 0.5
+            bend = jnp.tanh(hidden * (scale + scale * 0.044715 * square))
+            half = 0.5 + 0.5 * bend
+            slope = half + hidden * (0.5 - 0.5 * bend * bend) * (
+                scale + scale * 0.134145 * square
+            )
+            store_rows(active, place, hidden * half)
+            store_rows(grad, place, active_grad * slope)
 
 
 def hidden_both(pieces, downs, up, down):
@@ -540,18 +537,16 @@
     slots, _, depth = pieces[0].shape
     wide = up[2]
     tile = tile_of(wide, math.gcd(up[1], down[1]), 512)
-    rows = [pl.BlockSpec((1, piece.shape[1], depth), lambda s, j: (s, 0, 0)) for piece in pieces]
     outs = pl.pallas_call(
         functools.partial(hidden_kernel, count),
-        grid=(slots, wide // tile),
-        in_specs=rows
-        + rows
+        grid=(wide // tile,),
+        in_specs=[whole_block(piece) for piece in (*pieces, *downs)]
         + [
-            pl.BlockSpec((depth, tile), lambda s, j, o=block[1] // tile: (0, o + j))
+            pl.BlockSpec((depth, tile), lambda j, o=block[1] // tile: (0, o + j))
             for block in (up, down)
         ],
         out_specs=[
-            pl.BlockSpec((1, piece.shape[1], tile), lambda s, j: (s, 0, j)) for piece in pieces
+            pl.BlockSpec((slots, piece.shape[1], tile), lambda j: (0, 0, j)) for piece in pieces
         ]
         * 2,
         out_shape=[
@@ -603,24 +598,22 @@
         joined = blocks[0] if len(blocks) == 1 else jnp.concatenate(blocks, axis=1)
         return lax.all_gather(joined, "dp", axis=0, tiled=True)
 
-    packed_in = gathered(
-        image_attention_in.reshape(share, 3 * width), text_attention_in.reshape(share, 3 * width)
+    packed_first = gathered(
+        image_attention_in.reshape(share, 3 * width),
+        text_attention_in.reshape(share, 3 * width),
+        image_attention_out.T,
+        text_attention_out.T,
     )
     image_up = gathered(image_hidden_in)
     image_down = gathered(image_hidden_out.T)
-    text_down = gathered(text_hidden_out.T)
-    out_ring = ring_gather(
-        jnp.concatenate([image_attention_out.T, text_attention_out.T], axis=1), group_count
-    )
-    out_hop = next(out_ring)
-    weight_in = ((packed_in, 0, 3 * width), (packed_in, 3 * width, 3 * width))
+    packed_text = gathered(text_hidden_in, text_hidden_out.T)
+    weight_in = ((packed_first, 0, 3 * width), (packed_first, 3 * width, 3 * width))
+    weight_out = ((packed_first, 6 * width, width), (packed_first, 7 * width, width))
 
     alive = (jnp.arange(slots) < group_size[0]).astype(F32)[:, None, None]
     cond_full = condition.astype(F32)
     activated_low = jax.nn.silu(cond_full).astype(BF16)
     activated_all = gather_stack(activated_low, group_count, "dp").reshape(-1, model)
-    activated_all, out_hop = lax.optimization_barrier((activated_all, out_hop))
-    out_hop = out_ring.send(out_hop)
     activated_own = lax.dynamic_slice_in_dim(activated_all, group_rank * share, share, 1)
     all_slots = activated_own.shape[0]
     mod_parts = jnp.concatenate(
@@ -634,8 +627,6 @@
     modulations = lax.all_gather(
         mod_own.reshape(slots, 2, 6, width), "tensor", axis=3, tiled=True
     )
-    modulations, out_hop = lax.optimization_barrier((modulations, out_hop))
-    out_hop = out_ring.send(out_hop)
     mods = (modulations[:, 0], modulations[:, 1])
 
     tokens = (image_tokens.astype(F32), text_tokens.astype(F32))
@@ -644,22 +635,20 @@
     half = size // 2
     near_kinds = [F32] + [BF16] * (half - 1)
 
-    def gathered_rows(values, gate=None):
-        return gather_pieces(values, size, gate=gate)
-
     def scattered(grad):
         return lax.psum_scatter(grad, "dp", scatter_dimension=0, tiled=True).astype(F32)
 
-    def row_products(pieces, weight, weight_dim):
-        far = products_of(pieces[half:], weight, weight_dim, near_kinds)
-        near = products_of(after(pieces[:half], far), weight, weight_dim, near_kinds)
+    def row_products(pieces, weight, weight_dim, late=False):
+        far = products_of(pieces[half:], weight, weight_dim, near_kinds, late)
+        near = products_of(after(pieces[:half], far), weight, weight_dim, near_kinds, late)
         return [*near, *far]
 
-    def image_sum(pieces, weight, weight_dim):
-        return scatter_end(*scatter_start(row_products(pieces, weight, weight_dim), size), size)
-
-    def text_sum(piece, weight, weight_dim):
-        (product,) = products_of([piece], weight, weight_dim, [F32])
+    def image_sum(pieces, weight, weight_dim, late=False):
+        products = row_products(pieces, weight, weight_dim, late)
+        return scatter_end(*scatter_start(products, size), size)
+
+    def text_sum(piece, weight, weight_dim, late=False):
+        (product,) = products_of([piece], weight, weight_dim, [F32], late)
         return scatter_end(*text_start(product, size), size)
 
     def modulated(values, mod, shift, scale):
@@ -681,81 +670,71 @@
 
     normed_one, inverse_one, image_first = modulated(tokens[0], mods[0], 0, 1)
     text_normed_one, text_inverse_one, text_first = modulated(tokens[1], mods[1], 0, 1)
-    first_pieces = gathered_rows(image_first)
-    first_pieces, out_hop = lax.optimization_barrier((first_pieces, out_hop))
-    for _ in range(group_count // 2 - 3):
-        out_hop = out_ring.send(out_hop)
+    first_pieces = gather_pieces(image_first, size)
     packed = products_of(first_pieces, weight_in[0], 0, low_kinds)
     text_packed = products_of([text_first], weight_in[1], 0, [BF16])
-    parts = [*packed, *text_packed]
     down_rows = [
         (outgoing[stream] * spread(mods[stream][:, 5])).astype(BF16) for stream in range(2)
     ]
-    up_ring = ring_gather(after(text_hidden_in, first_pieces), group_count)
-    up_hop = next(up_ring)
+    down_have = gather_start(after(down_rows[0], first_pieces), size)
+    parts = after([*packed, *text_packed], down_have)
     attended, sums = attend(parts)
-    down_pieces = gathered_rows(after(down_rows[0], first_pieces), attended)
-    attended, out_hop, up_hop = lax.optimization_barrier((attended, out_hop, up_hop))
-    both_out = out_ring.send(out_hop)
-    up_hop = up_ring.send(up_hop)
-    weight_out = ((both_out, 0, width), (both_out, width, width))
+    down_pieces = gather_end(after(down_have, attended), size)
     attended_parts = (attended[:-1], attended[-1:])
 
     branch = image_sum(attended_parts[0], weight_out[0], 1)
-    branch, up_hop = lax.optimization_barrier((branch, up_hop))
-    up_hop = up_ring.send(up_hop)
-    text_branch = text_sum(attended_parts[1][0], weight_out[1], 1)
     middle = tokens[0] + spread(mods[0][:, 2]) * branch
     normed_two, inverse_two, image_second = modulated(middle, mods[0], 3, 4)
-    second_pieces = gathered_rows(image_second)
     up_weight, down_weight = (image_up, 0, units), (image_down, 0, units)
-    near = hidden_both(second_pieces[:half], down_pieces[:half], up_weight, down_weight)
-    far_pieces, up_hop = after((second_pieces[half:], up_hop), near)
-    up_hop = up_ring.send(up_hop)
+    near_pieces = gather_pieces(image_second, size, half)
+    far_have = gather_start(image_second, size)
+    near = hidden_both(near_pieces, down_pieces[:half], up_weight, down_weight)
+    far_have = {k: v for k, v in far_have.items() if k >= half}
+    far_pieces = gather_end(after(far_have, near), size, half)
+    second_pieces = [*near_pieces, *far_pieces]
     far = hidden_both(far_pieces, down_pieces[half:], up_weight, down_weight)
+    text_branch = text_sum(after(attended_parts[1][0], far_pieces), weight_out[1], 1)
     active = [*near[0], *far[0]]
-    hidden_grad = [*near[1], *far[1]]
+    hidden_grad = after([*near[1], *far[1]], text_branch)
     kept, sent = scatter_start(row_products(hidden_grad, up_weight, 1), size)
     image_mlp_grad = weight_grad(
         after([(down_pieces, active), (second_pieces, hidden_grad)], sent)
     )
-    second_grad, up_hop = after((scatter_end(kept, sent, size), up_hop), image_mlp_grad)
-    image_mlp = scattered(image_mlp_grad)
+    second_grad = after(scatter_end(kept, sent, size), image_mlp_grad)
+    image_mlp = scattered(after(image_mlp_grad, second_grad))
     middle_grad, low, shift_two_grad, scale_two_grad = second_back(
         0, second_grad, normed_two, inverse_two
     )
     gate_one_grad = jnp.sum(middle_grad * branch, axis=1)
 
-    for _ in range(group_count // 2 - 4):
-        up_hop = up_ring.send(up_hop)
-    text_up, text_down = after((up_ring.send(up_hop), text_down), low)
-    up_weight, text_down_weight = (text_up, 0, units), (text_down, 0, units)
+    low_have = gather_start(low, size)
+    two_products = row_products(after(active, low), down_weight, 1)
+    two_kept, two_sent = scatter_start(two_products, size)
+    low_have = after(low_have, two_products)
+    branch_grads = gather_end(low_have, size)
+
+    text_both = after(packed_text, low_have)
+    text_up_weight, text_down_weight = (text_both, 0, units), (text_both, units, units)
     text_middle = tokens[1] + spread(mods[1][:, 2]) * text_branch
     text_normed_two, text_inverse_two, text_second = modulated(text_middle, mods[1], 3, 4)
     text_active, text_hidden_grad = hidden_both(
-        [text_second], [down_rows[1]], up_weight, text_down_weight
-    )
-    (text_product,) = products_of(text_hidden_grad, up_weight, 1, [F32])
+        [text_second], [down_rows[1]], text_up_weight, text_down_weight
+    )
+    (text_product,) = products_of(text_hidden_grad, text_up_weight, 1, [F32])
     text_kept, text_sent = text_start(text_product, size)
     text_mlp_grad = weight_grad(
         after([([down_rows[1]], text_active), ([text_second], text_hidden_grad)], text_product)
     )
-    text_ring = ring_scatter(text_mlp_grad, group_count)
+    (text_two,) = products_of(after(text_active, text_product), text_down_weight, 1, [F32])
+
+    upstreams = products_of(branch_grads, weight_out[0], 0, low_kinds)
+    upstreams = after(upstreams, text_sent, text_mlp_grad, text_two)
+    text_ring = ring_scatter(after(text_mlp_grad, branch_grads), group_count)
     text_hop = next(text_ring)
-
-    two_kept, two_sent = scatter_start(
-        row_products(after(active, low), down_weight, 1), size
-    )
-    branch_grads = gathered_rows(low)
-    branch_grads = after(branch_grads, two_sent)
-    upstreams = products_of(branch_grads, weight_out[0], 0, low_kinds)
-    upstreams = after(upstreams, text_sent, text_mlp_grad)
     first_part = attend_back(parts, size, upstreams, sums[:-1])
-    text_second_grad = scatter_end(text_kept, text_sent, size)
-    branch_two = scatter_end(two_kept, two_sent, size)
-    first_part, text_second_grad, branch_two, text_hop = lax.optimization_barrier(
-        (first_part, text_second_grad, branch_two, text_hop)
-    )
+    branch_two = scatter_end(after(two_kept, first_part), two_sent, size)
+    text_second_grad = scatter_end(after(text_kept, first_part), text_sent, size)
+    first_part, branch_two, text_hop = lax.optimization_barrier((first_part, branch_two, text_hop))
     text_hop = text_ring.send(text_hop)
     text_middle_grad, text_low, text_shift_two_grad, text_scale_two_grad = second_back(
         1, text_second_grad, text_normed_two, text_inverse_two
@@ -772,7 +751,7 @@
         ]
     )
     attention_sum = scattered(attention_grad)
-    packed_grads, text_hop = after((packed_grads, text_hop), attention_grad)
+    packed_grads, text_hop, text_two = after((packed_grads, text_hop, text_two), attention_grad)
     text_hop = text_ring.send(text_hop)
 
     def first_back(stream, first_grad, normed, inverse, middle_grad):
@@ -789,12 +768,11 @@
         gate_two_grad = jnp.sum(outgoing[stream] * branch_two, axis=1)
         return (result * alive).astype(BF16), gate_two_grad
 
-    first_grad = image_sum(packed_grads[:-1], weight_in[0], 1)
-    text_first_grad = text_sum(packed_grads[-1], weight_in[1], 1)
-    text_branch_two = text_sum(text_active[0], text_down_weight, 1)
+    first_grad = image_sum(packed_grads[:-1], weight_in[0], 1, True)
+    text_first_grad = text_sum(packed_grads[-1], weight_in[1], 1, True)
+    text_branch_two = scatter_end(*text_start(text_two, size), size)
     text_first_grad, text_hop = lax.optimization_barrier((text_first_grad, text_hop))
-    text_hop = text_ring.send(text_hop)
-    for _ in range(group_count // 2 - 4):
+    for _ in range(group_count // 2 - 3):
         text_hop = text_ring.send(text_hop)
     first_grad, text_hop = lax.optimization_barrier((first_grad, text_hop))
     text_mlp = text_ring.send(text_hop)
@@ -853,10 +831,9 @@
     activated_part = sum_all(activated_part, size, "tensor").reshape(group_count, slots, share)
     activated_rows = gather_stack(activated_part, group_count, "dp")
     activated_rows = jnp.stack([activated_rows[k, k] for k in range(group_count)])
-    group_order = group_rank ^ jnp.arange(group_count)
     activated_grad = jnp.concatenate(
         [
-            lax.dynamic_index_in_dim(activated_rows, group_order[k], 0, keepdims=False)
+            lax.dynamic_index_in_dim(activated_rows, group_rank ^ k, 0, keepdims=False)
             for k in range(group_count)
         ],
         axis=1,

time: 972 us -> 888 us (0.914)
  local copies, waits for them, and re-layouts: 98.3 us -> 48.4 us
  between operations: 33.2 us -> 17.1 us
  Pallas kernels: 342 us -> 327 us
  waiting for transfers between devices: 320 us -> 335 us
    all_gather x4, waiting for transfers between devices: 0.04 us -> 78.3 us  [gathered(): return lax.all_gather(joined, 'dp', axis=0, tiled=True)]
    ppermute x24 -> x8, waiting for transfers between devices: 113 us -> 62.8 us  [ring_step(): return lax.ppermute(value, 'dp', hops)]
    dynamic_update_slice x17 -> x0, local copies, waits for them, and re-layouts: 20.4 us -> none  [put(): return lax.dynamic_update_slice(whole, value, (row, column))]
    unnamed x353 -> x313, local copies, waits for them, and re-layouts: 37.7 us -> 21.1 us
    ppermute x24 -> x8, starting transfers between devices: 24.4 us -> 8.49 us  [ring_step(): return lax.ppermute(value, 'dp', hops)]
    ppermute x48, waiting for transfers between devices: 187 us -> 176 us  [swap(): return lax.ppermute(value, axis, [(i, i ^ bit) for i in range(size)])]
    pallas_call x16, Pallas kernels: 111 us -> 101 us  [products_of(): pl.pallas_call(functools.partial(product_kernel, count, weight_dim), grid...]
  transfers between devices with their start and end apart: 78 -> 62, of which waited for: 27 -> 30; matrix products, arithmetic and copies ran while one was open for 16% -> 13% of each run, Pallas kernels for 36% -> 37%
where the time goes in v9:
time: 888 us; the launch traced here: 882 us
  waiting for transfers between devices  335 us (38%)
  Pallas kernels  327 us (37%)
  other arithmetic  85.9 us (10%)
  starting transfers between devices  56.9 us (6%)
  local copies, waits for them, and re-layouts  48.4 us (5%)
  between operations  17.1 us (2%)
    ppermute x48, waiting for transfers between devices, swap(): return lax.ppermute(value, axis, [(i, i ^ bit) for i in range(size)])  176 us
    pallas_call x16, Pallas kernels, products_of(): pl.pallas_call(functools.partial(product_kernel, count, weight_dim), grid...  101 us
    all_gather x4, waiting for transfers between devices, gathered(): return lax.all_gather(joined, 'dp', axis=0, tiled=True)  78.3 us
    pallas_call x8, Pallas kernels, weight_grad(): pl.pallas_call(functools.partial(rows_kernel, count), grid=(rows // step,...  68.7 us
    pallas_call x2, Pallas kernels, attend_back(): pl.pallas_call(functools.partial(attend_back_kernel, count, asked, groups...  64 us
    ppermute x8, waiting for transfers between devices, ring_step(): return lax.ppermute(value, 'dp', hops)  62.8 us
    pallas_call x1, Pallas kernels, attend(): pl.pallas_call(functools.partial(attend_kernel, count), grid=(slots, grou...  54.8 us
    ppermute x48, starting transfers between devices, swap(): return lax.ppermute(value, axis, [(i, i ^ bit) for i in range(size)])  48.1 us
  transfers between devices with their start and end apart: 62, of which 30 were waited for; matrix products, arithmetic and copies ran while one was open for 13% of the time, Pallas kernels for 37%

profile of v9, /device:TPU:0, one launch (start us, length us, event | category | flops | bytes accessed | tf_op | source)
XLA Modules:
  0.0 881.6 jit_solution(4103596072286913037)
XLA Ops:
  32.1 14.7 %collective-permute-done.3 = f32[4,2,4608]{2,1,0:T(2,128)S(1)} collective-permute-done((f32[4,2,4608]{2,1,0:T(2,128)S(1)}, f32[4,2,4608]{2,1,0:T(2,128)S(1)}, u32[]{:S(2)}, u32[]{:S(2)}) %collective-permute-start.3) | collective-permute-done | bytes 147488 | tf_op jit(solution)/shard_map/ppermute | solution.py:44
  48.0 8.3 collective-permute-done.4
  68.2 35.1 %collective-permute-done.7.refs_2_ = bf16[2,256,1536]{2,1,0:T(8,128)(2,1)S(1)} collective-permute-done((bf16[2,256,1536]{2,1,0:T(8,128)(2,1)S(1)}, bf16[2,256,1536]{2,1,0:T(8,128)(2,1)S(1)}, u32[]{:S(2)}, u32[]{:S(2)}) %collective-permute-start.7) | collective-permute-done | bytes 1572896 | tf_op jit(solution)/shard_map/ppermute | solution.py:44
  109.8 49.3 %all-gather.5.cloned.1.call-done.refs_4_.refs_1_.refs_2_ = bf16[1536,3072]{1,0:T(8,128)(2,1)} async-done(((bf16[192,3072]{1,0:T(8,128)(2,1)}), bf16[1536,3072]{1,0:T(8,128)(2,1)}) %all-gather.5.cloned.1.call-update) | async-done | bytes 9437200 | tf_op jit(solution)/shard_map/all_gather | solution.py:599
  159.1 14.4 %products.16 = (bf16[2,256,1152]{2,1,0:T(8,128)(2,1)S(1)}, bf16[2,256,1152]{2,1,0:T(8,128)(2,1)S(1)}, bf16[2,256,1152]{2,1,0:T(8,128)(2,1)S(1)}, bf16[2,256,1152]{2,1,0:T(8,128)(2,1)S(1)}) custom-call(bf16[2,256,1536]{2,1,0:T(8,128)(2,1)} %copy-done.86, bf16[2,256,1536]{2,1,0:T(8,128)(2,1)} %copy-done.100, bf16[2,256,1536]{2,1,0:T(8,128)(2,1)} %copy-done.99, ...), custom_call_target="tpu_custom_call" | custom-call | bytes 1024 | tf_op jit(solution)/shard_map/products/pallas_call | solution.py:490
  179.5 54.8 %attend.1 = (bf16[2,256,384]{2,1,0:T(8,128)(2,1)S(1)}, bf16[2,256,384]{2,1,0:T(8,128)(2,1)S(1)}, bf16[2,256,384]{2,1,0:T(8,128)(2,1)S(1)}, bf16[2,256,384]{2,1,0...) custom-call(bf16[2,256,1152]{2,1,0:T(8,128)(2,1)S(1)} %get-tuple-ele, ...), custom_call_target="tpu_custom_call" | custom-call | flops 17051860992 | bytes 7237632 | tf_op jit(solution)/shard_map/attend/pallas_call | solution.py:316
  251.3 34.9 %collective-permute-done.12 = bf16[2,256,1536]{2,1,0:T(8,128)(2,1)S(1)} collective-permute-done((bf16[2,256,1536]{2,1,0:T(8,128)(2,1)S(1)}, bf16[2,256,1536]{2,1,0:T(8,128)(2,1)S(1)}, u32[]{:S(2)}, u32[]{:S(2)}) %collective-permute-start.12) | collective-permute-done | bytes 1572896 | tf_op jit(solution)/shard_map/ppermute | solution.py:44
  290.6 29.0 %all-gather.9.cloned.1.call-done.refs_5_.refs_2_ = bf16[1536,1536]{1,0:T(8,128)(2,1)} async-done(((bf16[192,1536]{1,0:T(8,128)(2,1)}), bf16[1536,1536]{1,0:T(8,128)(2,1)}) %all-gather.9.cloned.1.call-update) | async-done | bytes 4718608 | tf_op jit(solution)/shard_map/all_gather | solution.py:599
  319.6 16.0 %hidden_both.3 = (bf16[2,256,1536]{2,1,0:T(8,128)(2,1)S(1)}, bf16[2,256,1536]{2,1,0:T(8,128)(2,1)S(1)}, bf16[2,256,1536]{2,1,0:T(8,128)(2,1)S(1)}, bf16[2,256,1536]{2,1,0:T(8,128)(2,1)}) custom-call(bf16[2,256,1536]{2,1,0:T(8,128)(2,1)} %copy-done.4, bf16[2,256,1536]{2,1,0:T(8,128)(2,1)} %collective-permute-done.13.refs_1_, bf16[2,256,1536]{2,1,0:T(8,128)(2,1)} %copy-done.2, ...), custom_call_target="tpu_custom_call" | custom-call | bytes 1024 | tf_op jit(solution)/shard_map/hidden_both/pallas_call | solution.py:540
  354.1 16.1 %hidden_both.4 = (bf16[2,256,1536]{2,1,0:T(8,128)(2,1)S(1)}, bf16[2,256,1536]{2,1,0:T(8,128)(2,1)S(1)}, bf16[2,256,1536]{2,1,0:T(8,128)(2,1)S(1)}, bf16[2,256,1536]{2,1,0:T(8,128)(2,1)}) custom-call(bf16[2,256,1536]{2,1,0:T(8,128)(2,1)} %collective-permute-done.15.refs_0_.refs_2_, bf16[2,256,1536]{2,1,0:T(8,128)(2,1)} %copy-done.102, ...), custom_call_target="tpu_custom_call" | custom-call | bytes 1024 | tf_op jit(solution)/shard_map/hidden_both/pallas_call | solution.py:540
  377.1 8.1 products.21
  385.2 8.0 products.22
  397.0 15.2 %weight_grad.8.refs_8_ = bf16[1536,3072]{1,0:T(8,128)(2,1)} custom-call(bf16[2,256,1536]{2,1,0:T(8,128)(2,1)S(1)} %copy-done.3, bf16[2,256,1536]{2,1,0:T(8,128)(2,1)} %collective-permute-done.14.refs_3_.refs_1_, bf16[2,256,1536]{2,1,0:T(8,128)(2,1)} %collective-permute-done.9.refs_2_, bf16[2,256,1536]{2,1,0:T(8,128)(2,1)} %copy-done.103, ...), custom_call_target="tpu_custom_call" | custom-call | bytes 1024 | tf_op jit(solution)/shard_map/weight_grad/pallas_call | solution.py:413
  412.2 15.2 %weight_grad.9 = bf16[1536,3072]{1,0:T(8,128)(2,1)} custom-call(bf16[2,256,1536]{2,1,0:T(8,128)(2,1)S(1)} %copy-done.5, bf16[2,256,1536]{2,1,0:T(8,128)(2,1)} %collective-permute-done.13.refs_1_, bf16[2,256,1536]{2,1,0:T(8,128)(2,1)} %collective-permute-done.15.refs_0_.refs_2_, bf16[2,256,1536]{2,1,0:T(8,128)(2,1)} %copy-done.102, ...), custom_call_target="tpu_custom_call", output_to_operand_aliasing={{}: (8, {})} | custom-call | bytes 1024 | tf_op jit(solution)/shard_map/weight_grad/pallas_call | solution.py:413
  450.7 8.1 products.23
  460.3 8.1 products.24
  470.2 14.5 %collective-permute-done.23.refs_2_ = bf16[2,256,1536]{2,1,0:T(8,128)(2,1)} collective-permute-done((bf16[2,256,1536]{2,1,0:T(8,128)(2,1)S(1)}, bf16[2,256,1536]{2,1,0:T(8,128)(2,1)}, u32[]{:S(2)}, u32[]{:S(2)}) %collective-permute-start.23) | collective-permute-done | bytes 1572896 | tf_op jit(solution)/shard_map/ppermute | solution.py:44
  484.7 6.6 hidden_both.5
  532.5 6.1 products.25
  542.5 47.9 %attend_back.2 = (bf16[2,256,384]{2,1,0:T(8,128)(2,1)S(1)}, bf16[2,256,384]{2,1,0:T(8,128)(2,1)S(1)}, bf16[2,256,384]{2,1,0:T(8,128)(2,1)S(1)}, bf16[2,256,384]{...) custom-call(bf16[2,256,1152]{2,1,0:T(8,128)(2,1)S(1)} %copy-done.56, ...), custom_call_target="tpu_custom_call" | custom-call | flops 42629652480 | bytes 12665856 | tf_op jit(solution)/shard_map/attend_back/pallas_call | solution.py:365
  609.3 16.0 %attend_back.3 = (bf16[2,256,1152]{2,1,0:T(8,128)(2,1)S(1)}, bf16[2,256,1152]{2,1,0:T(8,128)(2,1)S(1)}, bf16[2,256,1152]{2,1,0:T(8,128)(2,1)}, bf16[2,256,1152]{2,1,0:T(8,128)(2,1)}, bf16[2,154,1152]{2,1,0:T(8,128)(2,1)S(1)}) custom-call(bf16[2,256,1152]{2,1,0:T(8,128)(2,1)} %copy-done.55, bf16[2,256,1152]{2,1,0:T(8,128)(2,1)} %copy-done.57, ...), custom_call_target="tpu_custom_call" | custom-call | flops 17051860992 | bytes 7237632 | tf_op jit(solution)/shard_map/attend_back/pallas_call | solution.py:365
  628.8 11.6 %weight_grad.12.refs_2_ = bf16[1536,3072]{1,0:T(8,128)(2,1)} custom-call(bf16[2,256,1536]{2,1,0:T(8,128)(2,1)} %copy-done.86, bf16[2,256,1536]{2,1,0:T(8,128)(2,1)} %copy-done.100, bf16[2,256,1536]{2,1,0:T(8,128)(2,1)} %copy-done.99, bf16[2,256,1536]{2,1,0:T(8,128)(2,1)} %copy-done.101, bf16[2,256,1152]{2,1,0:T(8,128)(2,1)S(1)} %get-tuple-element.275.refs_4_.refs_0_, ...), custom_call_target="tpu_custom_call" | custom-call | bytes 1024 | tf_op jit(solution)/shard_map/weight_grad/pallas_call | solution.py:413
  645.4 7.5 weight_grad.14.refs_2_
  663.7 6.7 products.29
  680.3 7.3 products.30
  695.1 18.3 %collective-permute-done.41 = bf16[2,154,1536]{2,0,1:T(2,128)(2,1)S(1)} collective-permute-done((bf16[2,154,1536]{2,0,1:T(2,128)(2,1)S(1)}, bf16[2,154,1536]{2,0,1:T(2,128)(2,1)S(1)}, u32[]{:S(2)}, u32[]{:S(2)}) %collective-permute-start.41) | collective-permute-done | bytes 946208 | tf_op jit(solution)/shard_map/ppermute | solution.py:44
  715.7 13.1 %collective-permute-done.42 = bf16[192,3072]{1,0:T(8,128)(2,1)} collective-permute-done((bf16[192,3072]{1,0:T(8,128)(2,1)}, bf16[192,3072]{1,0:T(8,128)(2,1)}, u32[]{:S(2)}, u32[]{:S(2)}) %collective-permute-start.42) | collective-permute-done | bytes 1179680 | tf_op jit(solution)/shard_map/ppermute | solution.py:131
  728.7 24.8 %collective-permute-done.43 = bf16[192,3072]{1,0:T(8,128)(2,1)} collective-permute-done((bf16[192,3072]{1,0:T(8,128)(2,1)}, bf16[192,3072]{1,0:T(8,128)(2,1)}, u32[]{:S(2)}, u32[]{:S(2)}) %collective-permute-start.43) | collective-permute-done | bytes 1179680 | tf_op jit(solution)/shard_map/ppermute | solution.py:131
  760.3 6.2 collective-permute-done.36
  774.6 21.9 %collective-permute-done.44 = bf16[192,3072]{1,0:T(8,128)(2,1)S(1)} collective-permute-done((bf16[192,3072]{1,0:T(8,128)(2,1)S(1)}, bf16[192,3072]{1,0:T(8,128)(2,1)S(1)}, u32[]{:S(2)}, u32[]{:S(2)}) %collective-permute-start.44) | collective-permute-done | bytes 1179680 | tf_op jit(solution)/shard_map/ppermute | solution.py:131
  839.3 9.3 %collective-permute-done.55 = f32[4,8,2,192]{3,2,1,0:T(2,128)S(1)} collective-permute-done((f32[4,8,2,192]{3,2,1,0:T(2,128)S(1)}, f32[4,8,2,192]{3,2,1,0:T(2,128)S(1)}, u32[]{:S(2)}, u32[]{:S(2)}) %collective-permute-start.55) | collective-permute-done | bytes 49184 | tf_op jit(solution)/shard_map/ppermute | solution.py:44
  853.3 16.7 %reduce-scatter.3.cloned.1.call-done = bf16[192,3072]{1,0:T(8,128)(2,1)} async-done(((bf16[1536,3072]{1,0:T(8,128)(2,1)}), bf16[192,3072]{1,0:T(8,128)(2,1)}) %reduce-scatter.3.cloned.1.call-update) | async-done | bytes 1179664 | tf_op jit(solution)/shard_map/reduce_scatter | solution.py:639
  (569 shorter events, 294.4 us)
Async XLA Ops:
  7.2 151.9 %all-gather.5.cloned.1.call-start = ((), (), s32[]{:S(2)}) async-start(), calls=%async_computation.2 | async-start | bytes 10616832 | tf_op jit(solution)/shard_map/all_gather | solution.py:599
  11.7 279.0 %all-gather.7.cloned.1.call-start = ((), (), s32[]{:S(2)}) async-start(), calls=%async_computation.3 | async-start | bytes 5308416 | tf_op jit(solution)/shard_map/all_gather | solution.py:599
  12.4 307.2 %all-gather.9.cloned.1.call-start = ((), (), s32[]{:S(2)}) async-start(), calls=%async_computation.4 | async-start | bytes 5308416 | tf_op jit(solution)/shard_map/all_gather | solution.py:599
  19.3 465.4 %all-gather.11.cloned.1.call-start = ((), (), s32[]{:S(2)}) async-start(), calls=%async_computation.5 | async-start | bytes 10616832 | tf_op jit(solution)/shard_map/all_gather | solution.py:599
  66.6 36.7 %collective-permute-start.7 = (bf16[2,256,1536]{2,1,0:T(8,128)(2,1)S(1)}, bf16[2,256,1536]{2,1,0:T(8,128)(2,1)S(1)}, u32[]{:S(2)}, u32[]{:S(2)}) collective-permute-start(bf16[2,256,1536]{2,1,0:T(8,128)(2,1)S(1)} %fusion.7.refs_0_), channel_id=1, source_target_pairs={{0,2},{1,3},{2,0},{3,1},{4,6},{5,7},{6,4},{7,5},{8,10},{9,11},{10,... | collective-permute-start | bytes 4718600 | tf_op jit(solution)/shard_map/ppermute | solution.py:44
  68.2 37.8 %collective-permute-start.6 = (bf16[2,256,1536]{2,1,0:T(8,128)(2,1)S(1)}, bf16[2,256,1536]{2,1,0:T(8,128)(2,1)S(1)}, u32[]{:S(2)}, u32[]{:S(2)}) collective-permute-start(bf16[2,256,1536]{2,1,0:T(8,128)(2,1)S(1)} %fusion.7.refs_0_), channel_id=1, source_target_pairs={{0,1},{1,0},{2,3},{3,2},{4,5},{5,4},{6,7},{7,6},{8,9},{9,8},{10,11... | collective-permute-start | bytes 4718600 | tf_op jit(solution)/shard_map/ppermute | solution.py:44
  106.7 72.7 %collective-permute-start.9 = (bf16[2,256,1536]{2,1,0:T(8,128)(2,1)S(1)}, bf16[2,256,1536]{2,1,0:T(8,128)(2,1)}, u32[]{:S(2)}, u32[]{:S(2)}) collective-permute-start(bf16[2,256,1536]{2,1,0:T(8,128)(2,1)S(1)} %multiply_convert_fusion.2.refs_2_.refs_0_), channel_id=1, source_target_pairs={{0,2},{1,3},{2,0},{3,1},{4,6},{5,7},{6,4},{7,5},{8,10},{9,11},{10,... | collective-permute-start | bytes 4718600 | tf_op jit(solution)/shard_map/ppermute | solution.py:44
  242.1 607.3 %reduce-scatter.5.cloned.1.call-start = ((), (), s32[]{:S(2)}) async-start(), calls=%async_computation.7 | async-start | bytes 10616832 | tf_op jit(solution)/shard_map/reduce_scatter | solution.py:639
  249.7 36.5 %collective-permute-start.12 = (bf16[2,256,1536]{2,1,0:T(8,128)(2,1)S(1)}, bf16[2,256,1536]{2,1,0:T(8,128)(2,1)S(1)}, u32[]{:S(2)}, u32[]{:S(2)}) collective-permute-start(bf16[2,256,1536]{2,1,0:T(8,128)(2,1)S(1)} %add_convert_fusion.4), channel_id=1, source_target_pairs={{0,2},{1,3},{2,0},{3,1},{4,6},{5,7},{6,4},{7,5},{8,10},{9,11},{10,... | collective-permute-start | bytes 4718600 | tf_op jit(solution)/shard_map/ppermute | solution.py:44
  251.3 68.3 %collective-permute-start.14 = (bf16[2,256,1536]{2,1,0:T(8,128)(2,1)S(1)}, bf16[2,256,1536]{2,1,0:T(8,128)(2,1)}, u32[]{:S(2)}, u32[]{:S(2)}) collective-permute-start(bf16[2,256,1536]{2,1,0:T(8,128)(2,1)S(1)} %multiply_convert_fusion.2.refs_2_.refs_0_), channel_id=1, source_target_pairs={{0,1},{1,0},{2,3},{3,2},{4,5},{5,4},{6,7},{7,6},{8,9},{9,8},{10,11... | collective-permute-start | bytes 4718600 | tf_op jit(solution)/shard_map/ppermute | solution.py:44
  289.1 30.5 %collective-permute-start.13 = (bf16[2,256,1536]{2,1,0:T(8,128)(2,1)S(1)}, bf16[2,256,1536]{2,1,0:T(8,128)(2,1)}, u32[]{:S(2)}, u32[]{:S(2)}) collective-permute-start(bf16[2,256,1536]{2,1,0:T(8,128)(2,1)S(1)} %add_convert_fusion.3.refs_0_), channel_id=1, source_target_pairs={{0,1},{1,0},{2,3},{3,2},{4,5},{5,4},{6,7},{7,6},{8,9},{9,8},{10,11... | collective-permute-start | bytes 4718600 | tf_op jit(solution)/shard_map/ppermute | solution.py:44
  289.1 47.6 %collective-permute-start.15 = (bf16[2,256,1536]{2,1,0:T(8,128)(2,1)S(1)}, bf16[2,256,1536]{2,1,0:T(8,128)(2,1)}, u32[]{:S(2)}, u32[]{:S(2)}) collective-permute-start(bf16[2,256,1536]{2,1,0:T(8,128)(2,1)S(1)} %add_convert_fusion.3.refs_0_), channel_id=1, source_target_pairs={{0,2},{1,3},{2,0},{3,1},{4,6},{5,7},{6,4},{7,5},{8,10},{9,11},{10,... | collective-permute-start | bytes 4718600 | tf_op jit(solution)/shard_map/ppermute | solution.py:44
  393.2 34.2 %collective-permute-start.20 = (bf16[2,256,1536]{2,1,0:T(8,128)(2,1)S(1)}, bf16[2,256,1536]{2,1,0:T(8,128)(2,1)S(1)}, u32[]{:S(2)}, u32[]{:S(2)}) collective-permute-start(bf16[2,256,1536]{2,1,0:T(8,128)(2,1)S(1)} %get-tuple-element.192), channel_id=1, source_target_pairs={{0,1},{1,0},{2,3},{3,2},{4,5},{5,4},{6,7},{7,6},{8,9},{9,8},{10,11... | collective-permute-start | bytes 4718600 | tf_op jit(solution)/shard_map/ppermute | solution.py:44
  395.4 36.6 %collective-permute-start.22 = (bf16[2,256,1536]{2,1,0:T(8,128)(2,1)}, bf16[2,256,1536]{2,1,0:T(8,128)(2,1)}, u32[]{:S(2)}, u32[]{:S(2)}) collective-permute-start(bf16[2,256,1536]{2,1,0:T(8,128)(2,1)} %add_convert_fusion.2), channel_id=1, source_target_pairs={{0,2},{1,3},{2,0},{3,1},{4,6},{5,7},{6,4},{7,5},{8,10},{9,11},{10,... | collective-permute-start | bytes 4718600 | tf_op jit(solution)/shard_map/ppermute | solution.py:44
  436.8 433.2 %reduce-scatter.3.cloned.1.call-start = ((), (), s32[]{:S(2)}) async-start(), calls=%async_computation.6 | async-start | bytes 10616832 | tf_op jit(solution)/shard_map/reduce_scatter | solution.py:639
  449.1 35.6 %collective-permute-start.23 = (bf16[2,256,1536]{2,1,0:T(8,128)(2,1)S(1)}, bf16[2,256,1536]{2,1,0:T(8,128)(2,1)}, u32[]{:S(2)}, u32[]{:S(2)}) collective-permute-start(bf16[2,256,1536]{2,1,0:T(8,128)(2,1)S(1)} %multiply_convert_fusion.1.refs_0_), channel_id=1, source_target_pairs={{0,2},{1,3},{2,0},{3,1},{4,6},{5,7},{6,4},{7,5},{8,10},{9,11},{10,... | collective-permute-start | bytes 4718600 | tf_op jit(solution)/shard_map/ppermute | solution.py:44
  458.8 50.1 %collective-permute-start.28 = (bf16[2,256,1536]{2,1,0:T(8,128)(2,1)}, bf16[2,256,1536]{2,1,0:T(8,128)(2,1)}, u32[]{:S(2)}, u32[]{:S(2)}) collective-permute-start(bf16[2,256,1536]{2,1,0:T(8,128)(2,1)} %get-tuple-element.217), channel_id=1, source_target_pairs={{0,1},{1,0},{2,3},{3,2},{4,5},{5,4},{6,7},{7,6},{8,9},{9,8},{10,11... | collective-permute-start | bytes 4718600 | tf_op jit(solution)/shard_map/ppermute | solution.py:44
  468.3 56.2 %collective-permute-start.27 = (bf16[2,256,1536]{2,1,0:T(8,128)(2,1)}, bf16[2,256,1536]{2,1,0:T(8,128)(2,1)}, u32[]{:S(2)}, u32[]{:S(2)}) collective-permute-start(bf16[2,256,1536]{2,1,0:T(8,128)(2,1)} %get-tuple-element.221), channel_id=1, source_target_pairs={{0,1},{1,0},{2,3},{3,2},{4,5},{5,4},{6,7},{7,6},{8,9},{9,8},{10,11... | collective-permute-start | bytes 4718600 | tf_op jit(solution)/shard_map/ppermute | solution.py:44
  501.8 36.9 %collective-permute-start.26 = (f32[2,154,1536]{2,0,1:T(2,128)}, f32[2,154,1536]{2,0,1:T(2,128)}, u32[]{:S(2)}, u32[]{:S(2)}) collective-permute-start(f32[2,154,1536]{2,0,1:T(2,128)} %copy.79), channel_id=1, source_target_pairs={{0,1},{1,0},{2,3},{3,2},{4,5},{5,4},{6,7},{7,6},{8,9},{9,8},{10,11... | collective-permute-start | bytes 5677064 | tf_op jit(solution)/shard_map/ppermute | solution.py:44
  512.3 78.2 %collective-permute-start.29 = (bf16[2,256,1536]{2,1,0:T(8,128)(2,1)}, bf16[2,256,1536]{2,1,0:T(8,128)(2,1)}, u32[]{:S(2)}, u32[]{:S(2)}) collective-permute-start(bf16[2,256,1536]{2,1,0:T(8,128)(2,1)} %add_convert_fusion.1), channel_id=1, source_target_pairs={{0,2},{1,3},{2,0},{3,1},{4,6},{5,7},{6,4},{7,5},{8,10},{9,11},{10,... | collective-permute-start | bytes 4718600 | tf_op jit(solution)/shard_map/ppermute | solution.py:44
  530.5 62.0 %collective-permute-start.30 = (bf16[192,1536]{1,0:T(8,128)(2,1)}, bf16[192,1536]{1,0:T(8,128)(2,1)}, u32[]{:S(2)}, u32[]{:S(2)}) collective-permute-start(bf16[192,1536]{1,0:T(8,128)(2,1)} %get-tuple-element.385), channel_id=1, source_target_pairs={{0,8},{8,16},{16,24},{24,28},{28,20},{20,12},{12,4},{4,0},{1,9},{9... | collective-permute-start | bytes 1769480 | tf_op jit(solution)/shard_map/ppermute | solution.py:131
  531.5 61.0 %collective-permute-start.31 = (bf16[192,1536]{1,0:T(8,128)(2,1)}, bf16[192,1536]{1,0:T(8,128)(2,1)}, u32[]{:S(2)}, u32[]{:S(2)}) collective-permute-start(bf16[192,1536]{1,0:T(8,128)(2,1)} %get-tuple-element.384), channel_id=1, source_target_pairs={{0,4},{8,0},{16,8},{24,16},{28,24},{20,28},{12,20},{4,12},{1,5},{9... | collective-permute-start | bytes 1769480 | tf_op jit(solution)/shard_map/ppermute | solution.py:131
  542.0 60.3 %collective-permute-start.32 = (bf16[2,154,1536]{2,0,1:T(2,128)(2,1)S(1)}, bf16[2,154,1536]{2,0,1:T(2,128)(2,1)S(1)}, u32[]{:S(2)}, u32[]{:S(2)}) collective-permute-start(bf16[2,154,1536]{2,0,1:T(2,128)(2,1)S(1)} %copy.81), channel_id=1, source_target_pairs={{0,2},{1,3},{2,0},{3,1},{4,6},{5,7},{6,4},{7,5},{8,10},{9,11},{10,... | collective-permute-start | bytes 2838536 | tf_op jit(solution)/shard_map/ppermute | solution.py:44
  596.6 60.0 %collective-permute-start.33 = (bf16[192,3072]{1,0:T(8,128)(2,1)}, bf16[192,3072]{1,0:T(8,128)(2,1)}, u32[]{:S(2)}, u32[]{:S(2)}) collective-permute-start(bf16[192,3072]{1,0:T(8,128)(2,1)} %get-tuple-element.383), channel_id=1, source_target_pairs={{0,8},{8,16},{16,24},{24,28},{28,20},{20,12},{12,4},{4,0},{1,9},{9... | collective-permute-start | bytes 3538952 | tf_op jit(solution)/shard_map/ppermute | solution.py:131
  598.2 59.6 %collective-permute-start.34 = (bf16[192,3072]{1,0:T(8,128)(2,1)}, bf16[192,3072]{1,0:T(8,128)(2,1)}, u32[]{:S(2)}, u32[]{:S(2)}) collective-permute-start(bf16[192,3072]{1,0:T(8,128)(2,1)} %get-tuple-element.382), channel_id=1, source_target_pairs={{0,4},{8,0},{16,8},{24,16},{28,24},{20,28},{12,20},{4,12},{1,5},{9... | collective-permute-start | bytes 3538952 | tf_op jit(solution)/shard_map/ppermute | solution.py:131
  675.5 53.2 %collective-permute-start.42 = (bf16[192,3072]{1,0:T(8,128)(2,1)}, bf16[192,3072]{1,0:T(8,128)(2,1)}, u32[]{:S(2)}, u32[]{:S(2)}) collective-permute-start(bf16[192,3072]{1,0:T(8,128)(2,1)} %get-tuple-element.381), channel_id=1, source_target_pairs={{0,8},{8,16},{16,24},{24,28},{28,20},{20,12},{12,4},{4,0},{1,9},{9... | collective-permute-start | bytes 3538952 | tf_op jit(solution)/shard_map/ppermute | solution.py:131
  677.1 76.5 %collective-permute-start.43 = (bf16[192,3072]{1,0:T(8,128)(2,1)}, bf16[192,3072]{1,0:T(8,128)(2,1)}, u32[]{:S(2)}, u32[]{:S(2)}) collective-permute-start(bf16[192,3072]{1,0:T(8,128)(2,1)} %get-tuple-element.380), channel_id=1, source_target_pairs={{0,4},{8,0},{16,8},{24,16},{28,24},{20,28},{12,20},{4,12},{1,5},{9... | collective-permute-start | bytes 3538952 | tf_op jit(solution)/shard_map/ppermute | solution.py:131
  687.6 86.1 %collective-permute-start.37 = (bf16[2,256,1536]{2,1,0:T(8,128)(2,1)S(1)}, bf16[2,256,1536]{2,1,0:T(8,128)(2,1)S(1)}, u32[]{:S(2)}, u32[]{:S(2)}) collective-permute-start(bf16[2,256,1536]{2,1,0:T(8,128)(2,1)S(1)} %get-tuple-element.278), channel_id=1, source_target_pairs={{0,1},{1,0},{2,3},{3,2},{4,5},{5,4},{6,7},{7,6},{8,9},{9,8},{10,11... | collective-permute-start | bytes 4718600 | tf_op jit(solution)/shard_map/ppermute | solution.py:44
  693.3 80.5 %collective-permute-start.39 = (bf16[2,256,1536]{2,1,0:T(8,128)(2,1)S(1)}, bf16[2,256,1536]{2,1,0:T(8,128)(2,1)S(1)}, u32[]{:S(2)}, u32[]{:S(2)}) collective-permute-start(bf16[2,256,1536]{2,1,0:T(8,128)(2,1)S(1)} %add_convert_fusion), channel_id=1, source_target_pairs={{0,2},{1,3},{2,0},{3,1},{4,6},{5,7},{6,4},{7,5},{8,10},{9,11},{10,... | collective-permute-start | bytes 4718600 | tf_op jit(solution)/shard_map/ppermute | solution.py:44
  713.4 53.1 %collective-permute-start.36 = (bf16[2,154,1536]{2,0,1:T(2,128)(2,1)S(1)}, bf16[2,154,1536]{2,0,1:T(2,128)(2,1)S(1)}, u32[]{:S(2)}, u32[]{:S(2)}) collective-permute-start(bf16[2,154,1536]{2,0,1:T(2,128)(2,1)S(1)} %copy.85), channel_id=1, source_target_pairs={{0,2},{1,3},{2,0},{3,1},{4,6},{5,7},{6,4},{7,5},{8,10},{9,11},{10,... | collective-permute-start | bytes 2838536 | tf_op jit(solution)/shard_map/ppermute | solution.py:44
  756.8 39.7 %collective-permute-start.44 = (bf16[192,3072]{1,0:T(8,128)(2,1)S(1)}, bf16[192,3072]{1,0:T(8,128)(2,1)S(1)}, u32[]{:S(2)}, u32[]{:S(2)}) collective-permute-start(bf16[192,3072]{1,0:T(8,128)(2,1)S(1)} %get-tuple-element.379), channel_id=1, source_target_pairs={{0,8},{8,16},{16,24},{24,28},{28,20},{20,12},{12,4},{4,0},{1,9},{9... | collective-permute-start | bytes 3538952 | tf_op jit(solution)/shard_map/ppermute | solution.py:131
  756.9 41.4 %collective-permute-start.45 = (bf16[192,3072]{1,0:T(8,128)(2,1)S(1)}, bf16[192,3072]{1,0:T(8,128)(2,1)S(1)}, u32[]{:S(2)}, u32[]{:S(2)}) collective-permute-start(bf16[192,3072]{1,0:T(8,128)(2,1)S(1)} %get-tuple-element.378), channel_id=1, source_target_pairs={{0,4},{8,0},{16,8},{24,16},{28,24},{20,28},{12,20},{4,12},{1,5},{9... | collective-permute-start | bytes 3538952 | tf_op jit(solution)/shard_map/ppermute | solution.py:131
  (176 other events, 2712.4 us)
Sparse Core Ops, SparseCore 0:
  11.8 147.2 all-gather.4
  161.3 78.0 all-gather.6
  241.6 78.0 all-gather.8
  322.2 136.1 all-gather.10
  461.9 195.2 reduce-scatter.4
  660.7 209.2 reduce-scatter.2

commit v10 on v9

--- a/solution.py
+++ b/solution.py
@@ -129,6 +129,60 @@
     ring = ring_of(count)
     hops = [(ring[i], ring[(i + way) % count]) for i in range(count)]
     return lax.ppermute(value, "dp", hops)
+
+
+def place_kernel(steps, order, *refs):
+    out = refs[-1]
+    for step, (inputs, starts) in enumerate(steps):
+
+        @pl.when(pl.program_id(0) == step)
+        def _():
+            for index, start in zip(inputs, starts):
+                out[:, start : start + refs[index].shape[1]] = refs[index][...]
+
+
+def place_blocks(blocks, steps, order, wide):
+    share = blocks[0].shape[0]
+    return pl.pallas_call(
+        functools.partial(place_kernel, steps),
+        grid_spec=pltpu.PrefetchScalarGridSpec(
+            num_scalar_prefetch=1,
+            grid=(len(steps),),
+            in_specs=[
+                pl.BlockSpec(block.shape, lambda s, order: (0, 0), pipeline_mode=pl.Buffered(1))
+                for block in blocks
+            ],
+            out_specs=pl.BlockSpec((share, wide), lambda s, order: (order[s], 0)),
+        ),
+        out_shape=jax.ShapeDtypeStruct((len(steps) * share, wide), BF16),
+        compiler_params=pltpu.CompilerParams(vmem_limit_bytes=48 * 1024 * 1024),
+        cost_estimate=pl.CostEstimate(flops=0, transcendentals=0, bytes_accessed=1024),
+        name="place_blocks",
+    )(jnp.stack(order).astype(jnp.int32), *blocks)
+
+
+def ring_gather(block, count):
+    wide = block.shape[1]
+    half = wide // 2 // LANES * LANES
+    place = ring_place(lax.axis_index("dp"), count)
+    blocks, offsets, steps = [block], [0], [((0,), (0,))]
+    behind = ahead = block
+    for hop in range(1, count // 2):
+        behind = ring_step(behind, 1, count)
+        ahead = ring_step(ahead, -1, count)
+        behind, ahead = yield behind, ahead
+        blocks += [behind, ahead]
+        offsets += [-hop, hop]
+        steps += [((2 * hop - 1,), (0,)), ((2 * hop,), (0,))]
+    behind = ring_step(behind[:, :half], 1, count)
+    ahead = ring_step(ahead[:, half:], -1, count)
+    behind, ahead = yield behind, ahead
+    blocks += [behind, ahead]
+    offsets.append(count // 2)
+    steps.append(((count - 1, count), (0, half)))
+    yield place_blocks(
+        blocks, steps, [ring_member(place + offset, count) for offset in offsets], wide
+    )
 
 
 def ring_scatter(grad, count):
@@ -605,7 +659,6 @@
         text_attention_out.T,
     )
     image_up = gathered(image_hidden_in)
-    image_down = gathered(image_hidden_out.T)
     packed_text = gathered(text_hidden_in, text_hidden_out.T)
     weight_in = ((packed_first, 0, 3 * width), (packed_first, 3 * width, 3 * width))
     weight_out = ((packed_first, 6 * width, width), (packed_first, 7 * width, width))
@@ -627,6 +680,8 @@
     modulations = lax.all_gather(
         mod_own.reshape(slots, 2, 6, width), "tensor", axis=3, tiled=True
     )
+    down_ring = ring_gather(after(image_hidden_out.T, modulations), group_count)
+    down_hop = next(down_ring)
     mods = (modulations[:, 0], modulations[:, 1])
 
     tokens = (image_tokens.astype(F32), text_tokens.astype(F32))
@@ -671,18 +726,27 @@
     normed_one, inverse_one, image_first = modulated(tokens[0], mods[0], 0, 1)
     text_normed_one, text_inverse_one, text_first = modulated(tokens[1], mods[1], 0, 1)
     first_pieces = gather_pieces(image_first, size)
+    first_pieces, down_hop = lax.optimization_barrier((first_pieces, down_hop))
+    down_hop = down_ring.send(down_hop)
+    for _ in range(group_count // 2 - 4):
+        down_hop = down_ring.send(down_hop)
     packed = products_of(first_pieces, weight_in[0], 0, low_kinds)
     text_packed = products_of([text_first], weight_in[1], 0, [BF16])
     down_rows = [
         (outgoing[stream] * spread(mods[stream][:, 5])).astype(BF16) for stream in range(2)
     ]
     down_have = gather_start(after(down_rows[0], first_pieces), size)
-    parts = after([*packed, *text_packed], down_have)
+    parts, down_hop = after(([*packed, *text_packed], down_hop), down_have)
+    down_hop = down_ring.send(down_hop)
     attended, sums = attend(parts)
+    attended, down_hop = lax.optimization_barrier((attended, down_hop))
+    down_hop = down_ring.send(down_hop)
     down_pieces = gather_end(after(down_have, attended), size)
     attended_parts = (attended[:-1], attended[-1:])
 
     branch = image_sum(attended_parts[0], weight_out[0], 1)
+    branch, down_hop = lax.optimization_barrier((branch, down_hop))
+    image_down = down_ring.send(down_hop)
     middle = tokens[0] + spread(mods[0][:, 2]) * branch
     normed_two, inverse_two, image_second = modulated(middle, mods[0], 3, 4)
     up_weight, down_weight = (image_up, 0, units), (image_down, 0, units)
@@ -693,7 +757,7 @@
     far_pieces = gather_end(after(far_have, near), size, half)
     second_pieces = [*near_pieces, *far_pieces]
     far = hidden_both(far_pieces, down_pieces[half:], up_weight, down_weight)
-    text_branch = text_sum(after(attended_parts[1][0], far_pieces), weight_out[1], 1)
+    text_branch = text_sum(after(attended_parts[1][0], image_second), weight_out[1], 1)
     active = [*near[0], *far[0]]
     hidden_grad = after([*near[1], *far[1]], text_branch)
     kept, sent = scatter_start(row_products(hidden_grad, up_weight, 1), size)
@@ -710,10 +774,7 @@
     low_have = gather_start(low, size)
     two_products = row_products(after(active, low), down_weight, 1)
     two_kept, two_sent = scatter_start(two_products, size)
-    low_have = after(low_have, two_products)
-    branch_grads = gather_end(low_have, size)
-
-    text_both = after(packed_text, low_have)
+    text_both = after(packed_text, low)
     text_up_weight, text_down_weight = (text_both, 0, units), (text_both, units, units)
     text_middle = tokens[1] + spread(mods[1][:, 2]) * text_branch
     text_normed_two, text_inverse_two, text_second = modulated(text_middle, mods[1], 3, 4)
@@ -722,14 +783,22 @@
     )
     (text_product,) = products_of(text_hidden_grad, text_up_weight, 1, [F32])
     text_kept, text_sent = text_start(text_product, size)
-    text_mlp_grad = weight_grad(
-        after([([down_rows[1]], text_active), ([text_second], text_hidden_grad)], text_product)
-    )
-    (text_two,) = products_of(after(text_active, text_product), text_down_weight, 1, [F32])
+    low_have = after(low_have, two_products, text_product)
+    branch_grads = gather_end(low_have, size)
 
     upstreams = products_of(branch_grads, weight_out[0], 0, low_kinds)
-    upstreams = after(upstreams, text_sent, text_mlp_grad, text_two)
-    text_ring = ring_scatter(after(text_mlp_grad, branch_grads), group_count)
+    ring_grad = weight_grad(
+        after(
+            [
+                ([down_rows[1]], text_active),
+                ([text_second], text_hidden_grad),
+                (branch_grads, attended_parts[0]),
+            ],
+            branch_grads,
+        )
+    )
+    upstreams = after(upstreams, text_sent, ring_grad)
+    text_ring = ring_scatter(ring_grad, group_count)
     text_hop = next(text_ring)
     first_part = attend_back(parts, size, upstreams, sums[:-1])
     branch_two = scatter_end(after(two_kept, first_part), two_sent, size)
@@ -742,17 +811,17 @@
     text_gate_one_grad = jnp.sum(text_middle_grad * text_branch, axis=1)
     text_upstream = products_of([text_low], weight_out[1], 0, [BF16])
     packed_grads = attend_back(parts, 1, text_upstream, sums[-1:], first_part)
+    packed_grads, text_hop = lax.optimization_barrier((packed_grads, text_hop))
+    text_hop = text_ring.send(text_hop)
     attention_grad = weight_grad(
         [
             (first_pieces, packed_grads[:-1]),
             ([text_first], packed_grads[-1:]),
-            (branch_grads, attended_parts[0]),
             ([text_low], attended_parts[1]),
         ]
     )
     attention_sum = scattered(attention_grad)
-    packed_grads, text_hop, text_two = after((packed_grads, text_hop, text_two), attention_grad)
-    text_hop = text_ring.send(text_hop)
+    packed_grads, text_active = after((packed_grads, text_active), attention_grad)
 
     def first_back(stream, first_grad, normed, inverse, middle_grad):
         mod = mods[stream]
@@ -770,7 +839,7 @@
 
     first_grad = image_sum(packed_grads[:-1], weight_in[0], 1, True)
     text_first_grad = text_sum(packed_grads[-1], weight_in[1], 1, True)
-    text_branch_two = scatter_end(*text_start(text_two, size), size)
+    text_branch_two = text_sum(text_active[0], text_down_weight, 1, True)
     text_first_grad, text_hop = lax.optimization_barrier((text_first_grad, text_hop))
     for _ in range(group_count // 2 - 3):
         text_hop = text_ring.send(text_hop)
@@ -848,13 +917,13 @@
         condition_gradient,
         image_ada,
         attention_sum[:, : 3 * width].reshape(share, 3, width),
-        attention_sum[:, 6 * width : 7 * width].T,
+        text_mlp[:, 2 * units :].T,
         image_mlp[:, units:],
         image_mlp[:, :units].T,
         text_ada,
         attention_sum[:, 3 * width : 6 * width].reshape(share, 3, width),
-        attention_sum[:, 7 * width :].T,
-        text_mlp[:, units:],
+        attention_sum[:, 6 * width :].T,
+        text_mlp[:, units : 2 * units],
         text_mlp[:, :units].T,
     )
 

time: 888 us -> 933 us (1.051)
  waiting for transfers between devices: 335 us -> 364 us
  local copies, waits for them, and re-layouts: 48.4 us -> 63.6 us
    ppermute x8 -> x16, waiting for transfers between devices: 62.8 us -> 138 us  [ring_step(): return lax.ppermute(value, 'dp', hops)]
    all_gather x4 -> x3, waiting for transfers between devices: 78.3 us -> 24.6 us  [gathered(): return lax.all_gather(joined, 'dp', axis=0, tiled=True)]
    ppermute x48, waiting for transfers between devices: 176 us -> 202 us  [swap(): return lax.ppermute(value, axis, [(i, i ^ bit) for i in range(size)])]
    reduce_scatter x2, waiting for transfers between devices: 16.7 us -> 0.01 us  [scattered(): lax.psum_scatter(grad, 'dp', scatter_dimension=0, tiled=True).astype(F32)]
    ppermute x8 -> x16, starting transfers between devices: 8.49 us -> 19.2 us  [ring_step(): return lax.ppermute(value, 'dp', hops)]
    unnamed x313 -> x327, local copies, waits for them, and re-layouts: 21.1 us -> 30.4 us
  transfers between devices with their start and end apart: 62 -> 69, of which waited for: 30 -> 25; matrix products, arithmetic and copies ran while one was open for 13% -> 12% of each run, Pallas kernels for 37% -> 36%
where the time goes in v10:
time: 933 us; the launch traced here: 924 us
  waiting for transfers between devices  364 us (39%)
  Pallas kernels  330 us (35%)
  other arithmetic  79.3 us (8%)
  local copies, waits for them, and re-layouts  63.6 us (7%)
  starting transfers between devices  58.2 us (6%)
  between operations  17.2 us (2%)
    ppermute x48, waiting for transfers between devices, swap(): return lax.ppermute(value, axis, [(i, i ^ bit) for i in range(size)])  202 us
    ppermute x16, waiting for transfers between devices, ring_step(): return lax.ppermute(value, 'dp', hops)  138 us
    pallas_call x16, Pallas kernels, products_of(): pl.pallas_call(functools.partial(product_kernel, count, weight_dim), grid...  98.2 us
    pallas_call x8, Pallas kernels, weight_grad(): pl.pallas_call(functools.partial(rows_kernel, count), grid=(rows // step,...  68.2 us
    pallas_call x2, Pallas kernels, attend_back(): pl.pallas_call(functools.partial(attend_back_kernel, count, asked, groups...  64.3 us
    pallas_call x1, Pallas kernels, attend(): pl.pallas_call(functools.partial(attend_kernel, count), grid=(slots, grou...  54.8 us
    pallas_call x3, Pallas kernels, hidden_both(): pl.pallas_call(functools.partial(hidden_kernel, count), grid=(wide // til...  39.1 us
    ppermute x48, starting transfers between devices, swap(): return lax.ppermute(value, axis, [(i, i ^ bit) for i in range(size)])  38.8 us
  transfers between devices with their start and end apart: 69, of which 25 were waited for; matrix products, arithmetic and copies ran while one was open for 12% of the time, Pallas kernels for 36%

profile of v10, /device:TPU:0, one launch (start us, length us, event | category | flops | bytes accessed | tf_op | source)
XLA Modules:
  0.0 924.2 jit_solution(17805199781306192860)
XLA Ops:
  31.2 15.4 %collective-permute-done.3 = f32[4,2,4608]{2,1,0:T(2,128)S(1)} collective-permute-done((f32[4,2,4608]{2,1,0:T(2,128)S(1)}, f32[4,2,4608]{2,1,0:T(2,128)S(1)}, u32[]{:S(2)}, u32[]{:S(2)}) %collective-permute-start.3) | collective-permute-done | bytes 147488 | tf_op jit(solution)/shard_map/ppermute | solution.py:44
  47.9 8.4 collective-permute-done.4
  69.3 35.4 %collective-permute-done.7.refs_2_ = bf16[2,256,1536]{2,1,0:T(8,128)(2,1)} collective-permute-done((bf16[2,256,1536]{2,1,0:T(8,128)(2,1)}, bf16[2,256,1536]{2,1,0:T(8,128)(2,1)}, u32[]{:S(2)}, u32[]{:S(2)}) %collective-permute-start.7) | collective-permute-done | bytes 1572896 | tf_op jit(solution)/shard_map/ppermute | solution.py:44
  110.7 42.0 %collective-permute-done.10.refs_2_ = bf16[192,1536]{1,0:T(8,128)(2,1)} collective-permute-done((bf16[192,1536]{1,0:T(8,128)(2,1)S(1)}, bf16[192,1536]{1,0:T(8,128)(2,1)}, u32[]{:S(2)}, u32[]{:S(2)}) %collective-permute-start.10) | collective-permute-done | bytes 589856 | tf_op jit(solution)/shard_map/ppermute | solution.py:131
  156.5 24.6 %all-gather.4.cloned.1.call-done.refs_4_.refs_1_.refs_2_ = bf16[1536,3072]{1,0:T(8,128)(2,1)} async-done(((bf16[192,3072]{1,0:T(8,128)(2,1)}), bf16[1536,3072]{1,0:T(8,128)(2,1)}) %all-gather.4.cloned.1.call-update) | async-done | bytes 9437200 | tf_op jit(solution)/shard_map/all_gather | solution.py:653
  181.1 13.9 %products.16 = (bf16[2,256,1152]{2,1,0:T(8,128)(2,1)S(1)}, bf16[2,256,1152]{2,1,0:T(8,128)(2,1)S(1)}, bf16[2,256,1152]{2,1,0:T(8,128)(2,1)S(1)}, bf16[2,256,1152]{2,1,0:T(8,128)(2,1)S(1)}) custom-call(bf16[2,256,1536]{2,1,0:T(8,128)(2,1)} %fusion.7.refs_0_, bf16[2,256,1536]{2,1,0:T(8,128)(2,1)} %collective-permute-done.6.refs_1_, ...), custom_call_target="tpu_custom_call" | custom-call | bytes 1024 | tf_op jit(solution)/shard_map/products/pallas_call | solution.py:544
  203.2 54.8 %attend.1 = (bf16[2,256,384]{2,1,0:T(8,128)(2,1)S(1)}, bf16[2,256,384]{2,1,0:T(8,128)(2,1)S(1)}, bf16[2,256,384]{2,1,0:T(8,128)(2,1)S(1)}, bf16[2,256,384]{2,1,0...) custom-call(bf16[2,256,1152]{2,1,0:T(8,128)(2,1)S(1)} %get-tuple-ele, ...), custom_call_target="tpu_custom_call" | custom-call | flops 17051860992 | bytes 7237632 | tf_op jit(solution)/shard_map/attend/pallas_call | solution.py:370
  270.8 32.2 %collective-permute-done.18 = bf16[2,256,1536]{2,1,0:T(8,128)(2,1)S(1)} collective-permute-done((bf16[2,256,1536]{2,1,0:T(8,128)(2,1)S(1)}, bf16[2,256,1536]{2,1,0:T(8,128)(2,1)S(1)}, u32[]{:S(2)}, u32[]{:S(2)}) %collective-permute-start.18) | collective-permute-done | bytes 1572896 | tf_op jit(solution)/shard_map/ppermute | solution.py:44
  327.5 16.0 %hidden_both.3 = (bf16[2,256,1536]{2,1,0:T(8,128)(2,1)S(1)}, bf16[2,256,1536]{2,1,0:T(8,128)(2,1)S(1)}, bf16[2,256,1536]{2,1,0:T(8,128)(2,1)S(1)}, bf16[2,256,1536]{2,1,0:T(8,128)(2,1)}) custom-call(bf16[2,256,1536]{2,1,0:T(8,128)(2,1)} %add_convert_fusion.3.refs_0_, bf16[2,256,1536]{2,1,0:T(8,128)(2,1)} %collective-permute-done.21.refs_1_, ...), custom_call_target="tpu_custom_call" | custom-call | bytes 1024 | tf_op jit(solution)/shard_map/hidden_both/pallas_call | solution.py:594
  343.5 8.3 collective-permute-done.23.refs_0_.refs_2_
  356.2 21.9 %collective-permute-done.27 = bf16[2,154,1536]{2,0,1:T(2,128)(2,1)S(1)} collective-permute-done((bf16[2,154,1536]{2,0,1:T(2,128)(2,1)S(1)}, bf16[2,154,1536]{2,0,1:T(2,128)(2,1)S(1)}, u32[]{:S(2)}, u32[]{:S(2)}) %collective-permute-start.27) | collective-permute-done | bytes 946208 | tf_op jit(solution)/shard_map/ppermute | solution.py:44
  384.0 15.9 %hidden_both.4 = (bf16[2,256,1536]{2,1,0:T(8,128)(2,1)S(1)}, bf16[2,256,1536]{2,1,0:T(8,128)(2,1)S(1)}, bf16[2,256,1536]{2,1,0:T(8,128)(2,1)S(1)}, bf16[2,256,1536]{2,1,0:T(8,128)(2,1)}) custom-call(bf16[2,256,1536]{2,1,0:T(8,128)(2,1)} %collective-permute-done.23.refs_0_.refs_2_, bf16[2,256,1536]{2,1,0:T(8,128)(2,1)} %copy-done.98, ...), custom_call_target="tpu_custom_call" | custom-call | bytes 1024 | tf_op jit(solution)/shard_map/hidden_both/pallas_call | solution.py:594
  404.2 8.1 products.21
  412.4 8.0 products.22
  424.0 15.1 %weight_grad.8.refs_8_ = bf16[1536,3072]{1,0:T(8,128)(2,1)} custom-call(bf16[2,256,1536]{2,1,0:T(8,128)(2,1)S(1)} %copy-done.1, bf16[2,256,1536]{2,1,0:T(8,128)(2,1)} %collective-permute-done.22.refs_3_.refs_1_, bf16[2,256,1536]{2,1,0:T(8,128)(2,1)} %collective-permute-done.13.refs_2_, bf16[2,256,1536]{2,1,0:T(8,128)(2,1)} %collective-permute-done.25.refs_3_, ...), custom_call_target="tpu_custom_call" | custom-call | bytes 1024 | tf_op jit(solution)/shard_map/weight_grad/pallas_call | solution.py:467
  439.2 15.2 %weight_grad.9 = bf16[1536,3072]{1,0:T(8,128)(2,1)} custom-call(bf16[2,256,1536]{2,1,0:T(8,128)(2,1)} %add_convert_fusion.3.refs_0_, bf16[2,256,1536]{2,1,0:T(8,128)(2,1)} %collective-permute-done.21.refs_1_, bf16[2,256,1536]{2,1,0:T(8,128)(2,1)} %collective-permute-done.23.refs_0_.refs_2_, ...), custom_call_target="tpu_custom_call", output_to_operand_aliasing={{}: (8, {})} | custom-call | bytes 1024 | tf_op jit(solution)/shard_map/weight_grad/pallas_call | solution.py:467
  477.0 8.1 products.23
  486.5 8.1 products.24
  495.8 7.2 hidden_both.5
  504.0 6.0 products.25
  537.1 7.2 weight_grad.12
  555.1 48.3 %attend_back.2 = (bf16[2,256,384]{2,1,0:T(8,128)(2,1)S(1)}, bf16[2,256,384]{2,1,0:T(8,128)(2,1)S(1)}, bf16[2,256,384]{2,1,0:T(8,128)(2,1)S(1)}, bf16[2,256,384]{...) custom-call(bf16[2,256,1152]{2,1,0:T(8,128)(2,1)S(1)} %copy-done.56, ...), custom_call_target="tpu_custom_call" | custom-call | flops 42629652480 | bytes 12665856 | tf_op jit(solution)/shard_map/attend_back/pallas_call | solution.py:419
  618.9 16.0 %attend_back.3 = (bf16[2,256,1152]{2,1,0:T(8,128)(2,1)S(1)}, bf16[2,256,1152]{2,1,0:T(8,128)(2,1)S(1)}, bf16[2,256,1152]{2,1,0:T(8,128)(2,1)}, bf16[2,256,1152]{2,1,0:T(8,128)(2,1)}, bf16[2,154,1152]{2,1,0:T(8,128)(2,1)S(1)}) custom-call(bf16[2,256,1152]{2,1,0:T(8,128)(2,1)} %copy-done.55, bf16[2,256,1152]{2,1,0:T(8,128)(2,1)} %copy-done.57, ...), custom_call_target="tpu_custom_call" | custom-call | flops 17051860992 | bytes 7237632 | tf_op jit(solution)/shard_map/attend_back/pallas_call | solution.py:419
  634.9 27.9 %collective-permute-done.42 = bf16[192,3456]{1,0:T(8,128)(2,1)S(1)} collective-permute-done((bf16[192,3456]{1,0:T(8,128)(2,1)S(1)}, bf16[192,3456]{1,0:T(8,128)(2,1)S(1)}, u32[]{:S(2)}, u32[]{:S(2)}) %collective-permute-start.42) | collective-permute-done | bytes 1327136 | tf_op jit(solution)/shard_map/ppermute | solution.py:131
  666.3 11.6 %weight_grad.13.refs_2_ = bf16[1536,2688]{1,0:T(8,128)(2,1)} custom-call(bf16[2,256,1536]{2,1,0:T(8,128)(2,1)} %fusion.7.refs_0_, bf16[2,256,1536]{2,1,0:T(8,128)(2,1)} %collective-permute-done.6.refs_1_, bf16[2,256,1536]{2,1,0:T(8,128)(2,1)} %collective-permute-done.7.refs_2_, bf16[2,256,1536]{2,1,0:T(8,128)(2,1)} %collective-permute-done.8.refs_3_, ...), custom_call_target="tpu_custom_call" | custom-call | bytes 1024 | tf_op jit(solution)/shard_map/weight_grad/pallas_call | solution.py:467
  693.3 7.1 products.29
  715.1 7.0 products.30
  731.2 18.4 %collective-permute-done.49 = bf16[2,154,1536]{2,0,1:T(2,128)(2,1)S(1)} collective-permute-done((bf16[2,154,1536]{2,0,1:T(2,128)(2,1)S(1)}, bf16[2,154,1536]{2,0,1:T(2,128)(2,1)S(1)}, u32[]{:S(2)}, u32[]{:S(2)}) %collective-permute-start.49) | collective-permute-done | bytes 946208 | tf_op jit(solution)/shard_map/ppermute | solution.py:44
  753.2 23.1 %collective-permute-done.51 = bf16[192,3456]{1,0:T(8,128)(2,1)} collective-permute-done((bf16[192,3456]{1,0:T(8,128)(2,1)}, bf16[192,3456]{1,0:T(8,128)(2,1)}, u32[]{:S(2)}, u32[]{:S(2)}) %collective-permute-start.51) | collective-permute-done | bytes 1327136 | tf_op jit(solution)/shard_map/ppermute | solution.py:131
  778.2 24.5 %collective-permute-done.44 = bf16[2,154,1536]{2,0,1:T(2,128)(2,1)S(1)} collective-permute-done((bf16[2,154,1536]{2,0,1:T(2,128)(2,1)S(1)}, bf16[2,154,1536]{2,0,1:T(2,128)(2,1)S(1)}, u32[]{:S(2)}, u32[]{:S(2)}) %collective-permute-start.44) | collective-permute-done | bytes 946208 | tf_op jit(solution)/shard_map/ppermute | solution.py:44
  814.9 43.7 %collective-permute-done.53 = bf16[192,3456]{1,0:T(8,128)(2,1)S(1)} collective-permute-done((bf16[192,3456]{1,0:T(8,128)(2,1)S(1)}, bf16[192,3456]{1,0:T(8,128)(2,1)S(1)}, u32[]{:S(2)}, u32[]{:S(2)}) %collective-permute-start.53) | collective-permute-done | bytes 1327136 | tf_op jit(solution)/shard_map/ppermute | solution.py:131
  878.6 8.4 collective-permute-done.58
  (603 shorter events, 299.2 us)
Async XLA Ops:
  7.2 173.9 %all-gather.4.cloned.1.call-start = ((), (), s32[]{:S(2)}) async-start(), calls=%async_computation.2 | async-start | bytes 10616832 | tf_op jit(solution)/shard_map/all_gather | solution.py:653
  11.7 315.8 %all-gather.6.cloned.1.call-start = ((), (), s32[]{:S(2)}) async-start(), calls=%async_computation.3 | async-start | bytes 5308416 | tf_op jit(solution)/shard_map/all_gather | solution.py:653
  18.6 477.2 %all-gather.8.cloned.1.call-start = ((), (), s32[]{:S(2)}) async-start(), calls=%async_computation.4 | async-start | bytes 10616832 | tf_op jit(solution)/shard_map/all_gather | solution.py:653
  67.7 37.0 %collective-permute-start.7 = (bf16[2,256,1536]{2,1,0:T(8,128)(2,1)}, bf16[2,256,1536]{2,1,0:T(8,128)(2,1)}, u32[]{:S(2)}, u32[]{:S(2)}) collective-permute-start(bf16[2,256,1536]{2,1,0:T(8,128)(2,1)} %fusion.7.refs_0_), channel_id=1, source_target_pairs={{0,2},{1,3},{2,0},{3,1},{4,6},{5,7},{6,4},{7,5},{8,10},{9,11},{10,... | collective-permute-start | bytes 4718600 | tf_op jit(solution)/shard_map/ppermute | solution.py:44
  69.2 83.6 %collective-permute-start.6 = (bf16[2,256,1536]{2,1,0:T(8,128)(2,1)}, bf16[2,256,1536]{2,1,0:T(8,128)(2,1)}, u32[]{:S(2)}, u32[]{:S(2)}) collective-permute-start(bf16[2,256,1536]{2,1,0:T(8,128)(2,1)} %fusion.7.refs_0_), channel_id=1, source_target_pairs={{0,1},{1,0},{2,3},{3,2},{4,5},{5,4},{6,7},{7,6},{8,9},{9,8},{10,11... | collective-permute-start | bytes 4718600 | tf_op jit(solution)/shard_map/ppermute | solution.py:44
  104.7 48.1 %collective-permute-start.8 = (bf16[2,256,1536]{2,1,0:T(8,128)(2,1)}, bf16[2,256,1536]{2,1,0:T(8,128)(2,1)}, u32[]{:S(2)}, u32[]{:S(2)}) collective-permute-start(bf16[2,256,1536]{2,1,0:T(8,128)(2,1)} %collective-permute-done.7.refs_2_), channel_id=1, source_target_pairs={{0,1},{1,0},{2,3},{3,2},{4,5},{5,4},{6,7},{7,6},{8,9},{9,8},{10,11... | collective-permute-start | bytes 4718600 | tf_op jit(solution)/shard_map/ppermute | solution.py:44
  105.9 803.6 %reduce-scatter.5.cloned.1.call-start = ((), (), s32[]{:S(2)}) async-start(), calls=%async_computation.6 | async-start | bytes 10616832 | tf_op jit(solution)/shard_map/reduce_scatter | solution.py:694
  106.8 46.0 %collective-permute-start.10 = (bf16[192,1536]{1,0:T(8,128)(2,1)S(1)}, bf16[192,1536]{1,0:T(8,128)(2,1)}, u32[]{:S(2)}, u32[]{:S(2)}) collective-permute-start(bf16[192,1536]{1,0:T(8,128)(2,1)S(1)} %bitcast.187), channel_id=1, source_target_pairs={{0,4},{8,0},{16,8},{24,16},{28,24},{20,28},{12,20},{4,12},{1,5},{9... | collective-permute-start | bytes 1769480 | tf_op jit(solution)/shard_map/ppermute | solution.py:131
  108.3 44.5 %collective-permute-start.9 = (bf16[192,1536]{1,0:T(8,128)(2,1)S(1)}, bf16[192,1536]{1,0:T(8,128)(2,1)}, u32[]{:S(2)}, u32[]{:S(2)}) collective-permute-start(bf16[192,1536]{1,0:T(8,128)(2,1)S(1)} %bitcast.188), channel_id=1, source_target_pairs={{0,8},{8,16},{16,24},{24,28},{28,20},{20,12},{12,4},{4,0},{1,9},{9... | collective-permute-start | bytes 1769480 | tf_op jit(solution)/shard_map/ppermute | solution.py:131
  152.8 47.3 %collective-permute-start.13 = (bf16[2,256,1536]{2,1,0:T(8,128)(2,1)S(1)}, bf16[2,256,1536]{2,1,0:T(8,128)(2,1)}, u32[]{:S(2)}, u32[]{:S(2)}) collective-permute-start(bf16[2,256,1536]{2,1,0:T(8,128)(2,1)S(1)} %multiply_convert_fusion.2.refs_2_.refs_0_), channel_id=1, source_target_pairs={{0,2},{1,3},{2,0},{3,1},{4,6},{5,7},{6,4},{7,5},{8,10},{9,11},{10,... | collective-permute-start | bytes 4718600 | tf_op jit(solution)/shard_map/ppermute | solution.py:44
  153.3 46.8 %collective-permute-start.11 = (bf16[192,1536]{1,0:T(8,128)(2,1)}, bf16[192,1536]{1,0:T(8,128)(2,1)}, u32[]{:S(2)}, u32[]{:S(2)}) collective-permute-start(bf16[192,1536]{1,0:T(8,128)(2,1)} %collective-permute-done.9.refs_1_), channel_id=1, source_target_pairs={{0,8},{8,16},{16,24},{24,28},{28,20},{20,12},{12,4},{4,0},{1,9},{9... | collective-permute-start | bytes 1769480 | tf_op jit(solution)/shard_map/ppermute | solution.py:131
  153.4 46.7 %collective-permute-start.12 = (bf16[192,1536]{1,0:T(8,128)(2,1)}, bf16[192,1536]{1,0:T(8,128)(2,1)}, u32[]{:S(2)}, u32[]{:S(2)}) collective-permute-start(bf16[192,1536]{1,0:T(8,128)(2,1)} %collective-permute-done.10.refs_2_), channel_id=1, source_target_pairs={{0,4},{8,0},{16,8},{24,16},{28,24},{20,28},{12,20},{4,12},{1,5},{9... | collective-permute-start | bytes 1769480 | tf_op jit(solution)/shard_map/ppermute | solution.py:131
  200.1 58.0 %collective-permute-start.14 = (bf16[192,1536]{1,0:T(8,128)(2,1)}, bf16[192,1536]{1,0:T(8,128)(2,1)S(1)}, u32[]{:S(2)}, u32[]{:S(2)}) collective-permute-start(bf16[192,1536]{1,0:T(8,128)(2,1)} %collective-permute-done.11.refs_3_), channel_id=1, source_target_pairs={{0,8},{8,16},{16,24},{24,28},{28,20},{20,12},{12,4},{4,0},{1,9},{9... | collective-permute-start | bytes 1769480 | tf_op jit(solution)/shard_map/ppermute | solution.py:131
  203.0 55.1 %collective-permute-start.15 = (bf16[192,1536]{1,0:T(8,128)(2,1)}, bf16[192,1536]{1,0:T(8,128)(2,1)S(1)}, u32[]{:S(2)}, u32[]{:S(2)}) collective-permute-start(bf16[192,1536]{1,0:T(8,128)(2,1)} %collective-permute-done.12.refs_4_), channel_id=1, source_target_pairs={{0,4},{8,0},{16,8},{24,16},{28,24},{20,28},{12,20},{4,12},{1,5},{9... | collective-permute-start | bytes 1769480 | tf_op jit(solution)/shard_map/ppermute | solution.py:131
  314.1 37.6 %collective-permute-start.26 = (f32[2,154,1536]{2,0,1:T(2,128)}, f32[2,154,1536]{2,0,1:T(2,128)}, u32[]{:S(2)}, u32[]{:S(2)}) collective-permute-start(f32[2,154,1536]{2,0,1:T(2,128)} %copy.74), channel_id=1, source_target_pairs={{0,1},{1,0},{2,3},{3,2},{4,5},{5,4},{6,7},{7,6},{8,9},{9,8},{10,11... | collective-permute-start | bytes 5677064 | tf_op jit(solution)/shard_map/ppermute | solution.py:44
  314.6 37.1 %collective-permute-start.23 = (bf16[2,256,1536]{2,1,0:T(8,128)(2,1)}, bf16[2,256,1536]{2,1,0:T(8,128)(2,1)}, u32[]{:S(2)}, u32[]{:S(2)}) collective-permute-start(bf16[2,256,1536]{2,1,0:T(8,128)(2,1)} %add_convert_fusion.3.refs_0_), channel_id=1, source_target_pairs={{0,2},{1,3},{2,0},{3,1},{4,6},{5,7},{6,4},{7,5},{8,10},{9,11},{10,... | collective-permute-start | bytes 4718600 | tf_op jit(solution)/shard_map/ppermute | solution.py:44
  316.2 66.7 %collective-permute-start.25 = (bf16[2,256,1536]{2,1,0:T(8,128)(2,1)}, bf16[2,256,1536]{2,1,0:T(8,128)(2,1)}, u32[]{:S(2)}, u32[]{:S(2)}) collective-permute-start(bf16[2,256,1536]{2,1,0:T(8,128)(2,1)} %collective-permute-done.13.refs_2_), channel_id=1, source_target_pairs={{0,1},{1,0},{2,3},{3,2},{4,5},{5,4},{6,7},{7,6},{8,9},{9,8},{10,11... | collective-permute-start | bytes 4718600 | tf_op jit(solution)/shard_map/ppermute | solution.py:44
  463.9 449.2 %reduce-scatter.3.cloned.1.call-start = ((), (), s32[]{:S(2)}) async-start(), calls=%async_computation.5 | async-start | bytes 9289728 | tf_op jit(solution)/shard_map/reduce_scatter | solution.py:694
  475.4 37.7 %collective-permute-start.31 = (bf16[2,256,1536]{2,1,0:T(8,128)(2,1)S(1)}, bf16[2,256,1536]{2,1,0:T(8,128)(2,1)}, u32[]{:S(2)}, u32[]{:S(2)}) collective-permute-start(bf16[2,256,1536]{2,1,0:T(8,128)(2,1)S(1)} %multiply_convert_fusion.1.refs_0_), channel_id=1, source_target_pairs={{0,2},{1,3},{2,0},{3,1},{4,6},{5,7},{6,4},{7,5},{8,10},{9,11},{10,... | collective-permute-start | bytes 4718600 | tf_op jit(solution)/shard_map/ppermute | solution.py:44
  518.2 91.7 %collective-permute-start.37 = (bf16[2,256,1536]{2,1,0:T(8,128)(2,1)}, bf16[2,256,1536]{2,1,0:T(8,128)(2,1)}, u32[]{:S(2)}, u32[]{:S(2)}) collective-permute-start(bf16[2,256,1536]{2,1,0:T(8,128)(2,1)} %add_convert_fusion.1), channel_id=1, source_target_pairs={{0,2},{1,3},{2,0},{3,1},{4,6},{5,7},{6,4},{7,5},{8,10},{9,11},{10,... | collective-permute-start | bytes 4718600 | tf_op jit(solution)/shard_map/ppermute | solution.py:44
  524.6 78.8 %collective-permute-start.40 = (bf16[2,154,1536]{2,0,1:T(2,128)(2,1)S(1)}, bf16[2,154,1536]{2,0,1:T(2,128)(2,1)S(1)}, u32[]{:S(2)}, u32[]{:S(2)}) collective-permute-start(bf16[2,154,1536]{2,0,1:T(2,128)(2,1)S(1)} %copy.81), channel_id=1, source_target_pairs={{0,2},{1,3},{2,0},{3,1},{4,6},{5,7},{6,4},{7,5},{8,10},{9,11},{10,... | collective-permute-start | bytes 2838536 | tf_op jit(solution)/shard_map/ppermute | solution.py:44
  551.3 60.6 %collective-permute-start.38 = (bf16[192,1664]{1,0:T(8,128)(2,1)S(1)}, bf16[192,1664]{1,0:T(8,128)(2,1)}, u32[]{:S(2)}, u32[]{:S(2)}) collective-permute-start(bf16[192,1664]{1,0:T(8,128)(2,1)S(1)} %constant_dynamic-slice_fusion), channel_id=1, source_target_pairs={{0,8},{8,16},{16,24},{24,28},{28,20},{20,12},{12,4},{4,0},{1,9},{9... | collective-permute-start | bytes 1916936 | tf_op jit(solution)/shard_map/ppermute | solution.py:131
  554.9 57.0 %collective-permute-start.39 = (bf16[192,1792]{1,0:T(8,128)(2,1)S(1)}, bf16[192,1792]{1,0:T(8,128)(2,1)S(1)}, u32[]{:S(2)}, u32[]{:S(2)}) collective-permute-start(bf16[192,1792]{1,0:T(8,128)(2,1)S(1)} %dynamic-slice.1), channel_id=1, source_target_pairs={{0,4},{8,0},{16,8},{24,16},{28,24},{20,28},{12,20},{4,12},{1,5},{9... | collective-permute-start | bytes 2064392 | tf_op jit(solution)/shard_map/ppermute | solution.py:131
  614.3 48.6 %collective-permute-start.42 = (bf16[192,3456]{1,0:T(8,128)(2,1)S(1)}, bf16[192,3456]{1,0:T(8,128)(2,1)S(1)}, u32[]{:S(2)}, u32[]{:S(2)}) collective-permute-start(bf16[192,3456]{1,0:T(8,128)(2,1)S(1)} %get-tuple-element.442), channel_id=1, source_target_pairs={{0,4},{8,0},{16,8},{24,16},{28,24},{20,28},{12,20},{4,12},{1,5},{9... | collective-permute-start | bytes 3981320 | tf_op jit(solution)/shard_map/ppermute | solution.py:131
  614.8 48.0 %collective-permute-start.41 = (bf16[192,3456]{1,0:T(8,128)(2,1)S(1)}, bf16[192,3456]{1,0:T(8,128)(2,1)S(1)}, u32[]{:S(2)}, u32[]{:S(2)}) collective-permute-start(bf16[192,3456]{1,0:T(8,128)(2,1)S(1)} %get-tuple-element.443), channel_id=1, source_target_pairs={{0,8},{8,16},{16,24},{24,28},{28,20},{20,12},{12,4},{4,0},{1,9},{9... | collective-permute-start | bytes 3981320 | tf_op jit(solution)/shard_map/ppermute | solution.py:131
  705.0 71.2 %collective-permute-start.51 = (bf16[192,3456]{1,0:T(8,128)(2,1)}, bf16[192,3456]{1,0:T(8,128)(2,1)}, u32[]{:S(2)}, u32[]{:S(2)}) collective-permute-start(bf16[192,3456]{1,0:T(8,128)(2,1)} %get-tuple-element.440), channel_id=1, source_target_pairs={{0,4},{8,0},{16,8},{24,16},{28,24},{20,28},{12,20},{4,12},{1,5},{9... | collective-permute-start | bytes 3981320 | tf_op jit(solution)/shard_map/ppermute | solution.py:131
  705.9 70.3 %collective-permute-start.50 = (bf16[192,3456]{1,0:T(8,128)(2,1)}, bf16[192,3456]{1,0:T(8,128)(2,1)}, u32[]{:S(2)}, u32[]{:S(2)}) collective-permute-start(bf16[192,3456]{1,0:T(8,128)(2,1)} %get-tuple-element.441), channel_id=1, source_target_pairs={{0,8},{8,16},{16,24},{24,28},{28,20},{20,12},{12,4},{4,0},{1,9},{9... | collective-permute-start | bytes 3981320 | tf_op jit(solution)/shard_map/ppermute | solution.py:131
  722.1 91.9 %collective-permute-start.45 = (bf16[2,256,1536]{2,1,0:T(8,128)(2,1)S(1)}, bf16[2,256,1536]{2,1,0:T(8,128)(2,1)S(1)}, u32[]{:S(2)}, u32[]{:S(2)}) collective-permute-start(bf16[2,256,1536]{2,1,0:T(8,128)(2,1)S(1)} %get-tuple-element.338), channel_id=1, source_target_pairs={{0,1},{1,0},{2,3},{3,2},{4,5},{5,4},{6,7},{7,6},{8,9},{9,8},{10,11... | collective-permute-start | bytes 4718600 | tf_op jit(solution)/shard_map/ppermute | solution.py:44
  729.1 84.9 %collective-permute-start.47 = (bf16[2,256,1536]{2,1,0:T(8,128)(2,1)S(1)}, bf16[2,256,1536]{2,1,0:T(8,128)(2,1)S(1)}, u32[]{:S(2)}, u32[]{:S(2)}) collective-permute-start(bf16[2,256,1536]{2,1,0:T(8,128)(2,1)S(1)} %add_convert_fusion), channel_id=1, source_target_pairs={{0,2},{1,3},{2,0},{3,1},{4,6},{5,7},{6,4},{7,5},{8,10},{9,11},{10,... | collective-permute-start | bytes 4718600 | tf_op jit(solution)/shard_map/ppermute | solution.py:44
  749.6 53.0 %collective-permute-start.44 = (bf16[2,154,1536]{2,0,1:T(2,128)(2,1)S(1)}, bf16[2,154,1536]{2,0,1:T(2,128)(2,1)S(1)}, u32[]{:S(2)}, u32[]{:S(2)}) collective-permute-start(bf16[2,154,1536]{2,0,1:T(2,128)(2,1)S(1)} %copy.85), channel_id=1, source_target_pairs={{0,2},{1,3},{2,0},{3,1},{4,6},{5,7},{6,4},{7,5},{8,10},{9,11},{10,... | collective-permute-start | bytes 2838536 | tf_op jit(solution)/shard_map/ppermute | solution.py:44
  811.6 47.0 %collective-permute-start.53 = (bf16[192,3456]{1,0:T(8,128)(2,1)S(1)}, bf16[192,3456]{1,0:T(8,128)(2,1)S(1)}, u32[]{:S(2)}, u32[]{:S(2)}) collective-permute-start(bf16[192,3456]{1,0:T(8,128)(2,1)S(1)} %get-tuple-element.438), channel_id=1, source_target_pairs={{0,4},{8,0},{16,8},{24,16},{28,24},{20,28},{12,20},{4,12},{1,5},{9... | collective-permute-start | bytes 3981320 | tf_op jit(solution)/shard_map/ppermute | solution.py:131
  813.4 46.1 %collective-permute-start.52 = (bf16[192,3456]{1,0:T(8,128)(2,1)S(1)}, bf16[192,3456]{1,0:T(8,128)(2,1)S(1)}, u32[]{:S(2)}, u32[]{:S(2)}) collective-permute-start(bf16[192,3456]{1,0:T(8,128)(2,1)S(1)} %get-tuple-element.439), channel_id=1, source_target_pairs={{0,8},{8,16},{16,24},{24,28},{28,20},{20,12},{12,4},{4,0},{1,9},{9... | collective-permute-start | bytes 3981320 | tf_op jit(solution)/shard_map/ppermute | solution.py:131
  (190 other events, 3311.1 us)
Sparse Core Ops, SparseCore 0:
  11.8 169.2 all-gather.3
  183.3 93.3 all-gather.5
  279.5 137.6 all-gather.7
  464.0 185.5 reduce-scatter.4
  707.2 180.6 reduce-scatter.2

commit v11 on v9

--- a/solution.py
+++ b/solution.py
@@ -485,7 +485,7 @@
         block = pl.BlockSpec((depth, tile), lambda j: (0, start // tile + j))
     rows = slots * sum(piece.shape[1] for piece in pieces)
     cost = pl.CostEstimate(
-        flops=4 * rows * depth * result, transcendentals=0, bytes_accessed=4 * rows * result
+        flops=12 * rows * depth * result, transcendentals=0, bytes_accessed=4 * rows * result
     )
     return pl.pallas_call(
         functools.partial(product_kernel, count, weight_dim),
@@ -710,10 +710,7 @@
     low_have = gather_start(low, size)
     two_products = row_products(after(active, low), down_weight, 1)
     two_kept, two_sent = scatter_start(two_products, size)
-    low_have = after(low_have, two_products)
-    branch_grads = gather_end(low_have, size)
-
-    text_both = after(packed_text, low_have)
+    text_both = after(packed_text, low)
     text_up_weight, text_down_weight = (text_both, 0, units), (text_both, units, units)
     text_middle = tokens[1] + spread(mods[1][:, 2]) * text_branch
     text_normed_two, text_inverse_two, text_second = modulated(text_middle, mods[1], 3, 4)
@@ -722,14 +719,22 @@
     )
     (text_product,) = products_of(text_hidden_grad, text_up_weight, 1, [F32])
     text_kept, text_sent = text_start(text_product, size)
-    text_mlp_grad = weight_grad(
-        after([([down_rows[1]], text_active), ([text_second], text_hidden_grad)], text_product)
-    )
-    (text_two,) = products_of(after(text_active, text_product), text_down_weight, 1, [F32])
+    low_have = after(low_have, two_products, text_product)
+    branch_grads = gather_end(low_have, size)
 
     upstreams = products_of(branch_grads, weight_out[0], 0, low_kinds)
-    upstreams = after(upstreams, text_sent, text_mlp_grad, text_two)
-    text_ring = ring_scatter(after(text_mlp_grad, branch_grads), group_count)
+    ring_grad = weight_grad(
+        after(
+            [
+                ([down_rows[1]], text_active),
+                ([text_second], text_hidden_grad),
+                (branch_grads, attended_parts[0]),
+            ],
+            branch_grads,
+        )
+    )
+    upstreams = after(upstreams, text_sent, ring_grad)
+    text_ring = ring_scatter(ring_grad, group_count)
     text_hop = next(text_ring)
     first_part = attend_back(parts, size, upstreams, sums[:-1])
     branch_two = scatter_end(after(two_kept, first_part), two_sent, size)
@@ -746,12 +751,13 @@
         [
             (first_pieces, packed_grads[:-1]),
             ([text_first], packed_grads[-1:]),
-            (branch_grads, attended_parts[0]),
             ([text_low], attended_parts[1]),
         ]
     )
     attention_sum = scattered(attention_grad)
-    packed_grads, text_hop, text_two = after((packed_grads, text_hop, text_two), attention_grad)
+    packed_grads, text_active, text_hop = after(
+        (packed_grads, text_active, text_hop), attention_grad
+    )
     text_hop = text_ring.send(text_hop)
 
     def first_back(stream, first_grad, normed, inverse, middle_grad):
@@ -770,12 +776,11 @@
 
     first_grad = image_sum(packed_grads[:-1], weight_in[0], 1, True)
     text_first_grad = text_sum(packed_grads[-1], weight_in[1], 1, True)
-    text_branch_two = scatter_end(*text_start(text_two, size), size)
-    text_first_grad, text_hop = lax.optimization_barrier((text_first_grad, text_hop))
-    for _ in range(group_count // 2 - 3):
+    text_branch_two = text_sum(text_active[0], text_down_weight, 1, True)
+    first_grad, text_hop = lax.optimization_barrier((first_grad, text_hop))
+    for _ in range(group_count // 2 - 2):
         text_hop = text_ring.send(text_hop)
-    first_grad, text_hop = lax.optimization_barrier((first_grad, text_hop))
-    text_mlp = text_ring.send(text_hop)
+    text_mlp = text_hop
     input_grads = [None, None]
     input_grads[0], shift_one_grad, scale_one_grad = first_back(
         0, first_grad, normed_one, inverse_one, middle_grad
@@ -848,13 +853,13 @@
         condition_gradient,
         image_ada,
         attention_sum[:, : 3 * width].reshape(share, 3, width),
-        attention_sum[:, 6 * width : 7 * width].T,
+        text_mlp[:, 2 * units :].T,
         image_mlp[:, units:],
         image_mlp[:, :units].T,
         text_ada,
         attention_sum[:, 3 * width : 6 * width].reshape(share, 3, width),
-        attention_sum[:, 7 * width :].T,
-        text_mlp[:, units:],
+        attention_sum[:, 6 * width :].T,
+        text_mlp[:, units : 2 * units],
         text_mlp[:, :units].T,
     )
 

time: 888 us -> 912 us (1.027)
  waiting for transfers between devices: 335 us -> 363 us
    ppermute x48, waiting for transfers between devices: 176 us -> 263 us  [swap(): return lax.ppermute(value, axis, [(i, i ^ bit) for i in range(size)])]
    ppermute x8, waiting for transfers between devices: 62.8 us -> 20.5 us  [ring_step(): return lax.ppermute(value, 'dp', hops)]
    reduce_scatter x2, waiting for transfers between devices: 16.7 us -> 0.01 us  [scattered(): lax.psum_scatter(grad, 'dp', scatter_dimension=0, tiled=True).astype(F32)]
    unnamed x313 -> x283, local copies, waits for them, and re-layouts: 21.1 us -> 22.4 us
  transfers between devices with their start and end apart: 62 -> 62, of which waited for: 30 -> 24; matrix products, arithmetic and copies ran while one was open for 13% -> 13% of each run, Pallas kernels for 37% -> 36%
where the time goes in v11:
time: 912 us; the launch traced here: 906 us
  waiting for transfers between devices  363 us (40%)
  Pallas kernels  327 us (36%)
  other arithmetic  85.1 us (9%)
  local copies, waits for them, and re-layouts  54.1 us (6%)
  starting transfers between devices  48.5 us (5%)
  between operations  16.9 us (2%)
    ppermute x48, waiting for transfers between devices, swap(): return lax.ppermute(value, axis, [(i, i ^ bit) for i in range(size)])  263 us
    pallas_call x16, Pallas kernels, products_of(): pl.pallas_call(functools.partial(product_kernel, count, weight_dim), grid...  100 us
    all_gather x4, waiting for transfers between devices, gathered(): return lax.all_gather(joined, 'dp', axis=0, tiled=True)  78.3 us
    pallas_call x8, Pallas kernels, weight_grad(): pl.pallas_call(functools.partial(rows_kernel, count), grid=(rows // step,...  68.2 us
    pallas_call x2, Pallas kernels, attend_back(): pl.pallas_call(functools.partial(attend_back_kernel, count, asked, groups...  64.9 us
    pallas_call x1, Pallas kernels, attend(): pl.pallas_call(functools.partial(attend_kernel, count), grid=(slots, grou...  54.8 us
    ppermute x48, starting transfers between devices, swap(): return lax.ppermute(value, axis, [(i, i ^ bit) for i in range(size)])  40.1 us
    pallas_call x3, Pallas kernels, hidden_both(): pl.pallas_call(functools.partial(hidden_kernel, count), grid=(wide // til...  39.3 us
  transfers between devices with their start and end apart: 62, of which 24 were waited for; matrix products, arithmetic and copies ran while one was open for 13% of the time, Pallas kernels for 36%

profile of v11, /device:TPU:0, one launch (start us, length us, event | category | flops | bytes accessed | tf_op | source)
XLA Modules:
  0.0 906.3 jit_solution(1171973416066420298)
XLA Ops:
  32.1 14.7 %collective-permute-done.3 = f32[4,2,4608]{2,1,0:T(2,128)S(1)} collective-permute-done((f32[4,2,4608]{2,1,0:T(2,128)S(1)}, f32[4,2,4608]{2,1,0:T(2,128)S(1)}, u32[]{:S(2)}, u32[]{:S(2)}) %collective-permute-start.3) | collective-permute-done | bytes 147488 | tf_op jit(solution)/shard_map/ppermute | solution.py:44
  48.0 8.3 collective-permute-done.4
  60.4 5.5 all_gather.15
  68.2 35.1 %collective-permute-done.7.refs_2_ = bf16[2,256,1536]{2,1,0:T(8,128)(2,1)S(1)} collective-permute-done((bf16[2,256,1536]{2,1,0:T(8,128)(2,1)S(1)}, bf16[2,256,1536]{2,1,0:T(8,128)(2,1)S(1)}, u32[]{:S(2)}, u32[]{:S(2)}) %collective-permute-start.7) | collective-permute-done | bytes 1572896 | tf_op jit(solution)/shard_map/ppermute | solution.py:44
  109.8 49.3 %all-gather.5.cloned.1.call-done.refs_4_.refs_1_.refs_2_ = bf16[1536,3072]{1,0:T(8,128)(2,1)} async-done(((bf16[192,3072]{1,0:T(8,128)(2,1)}), bf16[1536,3072]{1,0:T(8,128)(2,1)}) %all-gather.5.cloned.1.call-update) | async-done | bytes 9437200 | tf_op jit(solution)/shard_map/all_gather | solution.py:599
  159.1 14.1 %products.16 = (bf16[2,256,1152]{2,1,0:T(8,128)(2,1)S(1)}, bf16[2,256,1152]{2,1,0:T(8,128)(2,1)S(1)}, bf16[2,256,1152]{2,1,0:T(8,128)(2,1)S(1)}, bf16[2,256,1152]{2,1,0:T(8,128)(2,1)S(1)}) custom-call(bf16[2,256,1536]{2,1,0:T(8,128)(2,1)} %copy-done.76, bf16[2,256,1536]{2,1,0:T(8,128)(2,1)} %copy-done.90, bf16[2,256,1536]{2,1,0:T(8,128)(2,1)} %copy-done.89, ...), custom_call_target="tpu_custom_call" | custom-call | bytes 1024 | tf_op jit(solution)/shard_map/products/pallas_call | solution.py:490
  179.3 54.8 %attend.1 = (bf16[2,256,384]{2,1,0:T(8,128)(2,1)S(1)}, bf16[2,256,384]{2,1,0:T(8,128)(2,1)S(1)}, bf16[2,256,384]{2,1,0:T(8,128)(2,1)S(1)}, bf16[2,256,384]{2,1,0...) custom-call(bf16[2,256,1152]{2,1,0:T(8,128)(2,1)S(1)} %get-tuple-ele, ...), custom_call_target="tpu_custom_call" | custom-call | flops 17051860992 | bytes 7237632 | tf_op jit(solution)/shard_map/attend/pallas_call | solution.py:316
  251.4 34.9 %collective-permute-done.12 = bf16[2,256,1536]{2,1,0:T(8,128)(2,1)S(1)} collective-permute-done((bf16[2,256,1536]{2,1,0:T(8,128)(2,1)S(1)}, bf16[2,256,1536]{2,1,0:T(8,128)(2,1)S(1)}, u32[]{:S(2)}, u32[]{:S(2)}) %collective-permute-start.12) | collective-permute-done | bytes 1572896 | tf_op jit(solution)/shard_map/ppermute | solution.py:44
  290.7 29.0 %all-gather.9.cloned.1.call-done.refs_5_.refs_2_ = bf16[1536,1536]{1,0:T(8,128)(2,1)} async-done(((bf16[192,1536]{1,0:T(8,128)(2,1)}), bf16[1536,1536]{1,0:T(8,128)(2,1)}) %all-gather.9.cloned.1.call-update) | async-done | bytes 4718608 | tf_op jit(solution)/shard_map/all_gather | solution.py:599
  319.6 15.9 %hidden_both.3 = (bf16[2,256,1536]{2,1,0:T(8,128)(2,1)S(1)}, bf16[2,256,1536]{2,1,0:T(8,128)(2,1)S(1)}, bf16[2,256,1536]{2,1,0:T(8,128)(2,1)S(1)}, bf16[2,256,1536]{2,1,0:T(8,128)(2,1)}) custom-call(bf16[2,256,1536]{2,1,0:T(8,128)(2,1)} %copy-done.2, bf16[2,256,1536]{2,1,0:T(8,128)(2,1)} %collective-permute-done.13.refs_1_, bf16[2,256,1536]{2,1,0:T(8,128)(2,1)} %copy-done, ...), custom_call_target="tpu_custom_call" | custom-call | bytes 1024 | tf_op jit(solution)/shard_map/hidden_both/pallas_call | solution.py:540
  354.0 16.1 %hidden_both.4 = (bf16[2,256,1536]{2,1,0:T(8,128)(2,1)S(1)}, bf16[2,256,1536]{2,1,0:T(8,128)(2,1)S(1)}, bf16[2,256,1536]{2,1,0:T(8,128)(2,1)S(1)}, bf16[2,256,1536]{2,1,0:T(8,128)(2,1)}) custom-call(bf16[2,256,1536]{2,1,0:T(8,128)(2,1)} %collective-permute-done.15.refs_0_.refs_2_, bf16[2,256,1536]{2,1,0:T(8,128)(2,1)} %copy-done.92, ...), custom_call_target="tpu_custom_call" | custom-call | bytes 1024 | tf_op jit(solution)/shard_map/hidden_both/pallas_call | solution.py:540
  377.2 8.1 products.21
  385.3 8.1 products.22
  397.0 15.2 %weight_grad.8.refs_8_ = bf16[1536,3072]{1,0:T(8,128)(2,1)} custom-call(bf16[2,256,1536]{2,1,0:T(8,128)(2,1)S(1)} %copy-done.1, bf16[2,256,1536]{2,1,0:T(8,128)(2,1)} %collective-permute-done.14.refs_3_.refs_1_, bf16[2,256,1536]{2,1,0:T(8,128)(2,1)} %collective-permute-done.9.refs_2_, bf16[2,256,1536]{2,1,0:T(8,128)(2,1)} %copy-done.93, ...), custom_call_target="tpu_custom_call" | custom-call | bytes 1024 | tf_op jit(solution)/shard_map/weight_grad/pallas_call | solution.py:413
  412.2 15.2 %weight_grad.9 = bf16[1536,3072]{1,0:T(8,128)(2,1)} custom-call(bf16[2,256,1536]{2,1,0:T(8,128)(2,1)S(1)} %copy-done.3, bf16[2,256,1536]{2,1,0:T(8,128)(2,1)} %collective-permute-done.13.refs_1_, bf16[2,256,1536]{2,1,0:T(8,128)(2,1)} %collective-permute-done.15.refs_0_.refs_2_, bf16[2,256,1536]{2,1,0:T(8,128)(2,1)} %copy-done.92, ...), custom_call_target="tpu_custom_call", output_to_operand_aliasing={{}: (8, {})} | custom-call | bytes 1024 | tf_op jit(solution)/shard_map/weight_grad/pallas_call | solution.py:413
  450.5 8.1 products.23
  460.1 8.2 products.24
  470.0 7.3 hidden_both.5
  477.3 6.3 products.25
  499.9 5.3 weight_grad.10.refs_2_
  510.6 7.2 weight_grad.12
  517.8 5.6 products.26
  528.2 48.1 %attend_back.2 = (bf16[2,256,384]{2,1,0:T(8,128)(2,1)S(1)}, bf16[2,256,384]{2,1,0:T(8,128)(2,1)S(1)}, bf16[2,256,384]{2,1,0:T(8,128)(2,1)S(1)}, bf16[2,256,384]{...) custom-call(bf16[2,256,1152]{2,1,0:T(8,128)(2,1)S(1)} %copy-done.48, ...), custom_call_target="tpu_custom_call" | custom-call | flops 42629652480 | bytes 12665856 | tf_op jit(solution)/shard_map/attend_back/pallas_call | solution.py:365
  592.8 16.8 %attend_back.3 = (bf16[2,256,1152]{2,1,0:T(8,128)(2,1)S(1)}, bf16[2,256,1152]{2,1,0:T(8,128)(2,1)S(1)}, bf16[2,256,1152]{2,1,0:T(8,128)(2,1)}, bf16[2,256,1152]{2,1,0:T(8,128)(2,1)}, bf16[2,154,1152]{2,1,0:T(8,128)(2,1)S(1)}) custom-call(bf16[2,256,1152]{2,1,0:T(8,128)(2,1)} %copy-done.47, bf16[2,256,1152]{2,1,0:T(8,128)(2,1)} %copy-done.49, ...), custom_call_target="tpu_custom_call" | custom-call | flops 17051860992 | bytes 7237632 | tf_op jit(solution)/shard_map/attend_back/pallas_call | solution.py:365
  612.2 11.6 %weight_grad.13.refs_2_ = bf16[1536,2688]{1,0:T(8,128)(2,1)} custom-call(bf16[2,256,1536]{2,1,0:T(8,128)(2,1)} %copy-done.76, bf16[2,256,1536]{2,1,0:T(8,128)(2,1)} %copy-done.90, bf16[2,256,1536]{2,1,0:T(8,128)(2,1)} %copy-done.89, bf16[2,256,1536]{2,1,0:T(8,128)(2,1)} %copy-done.91, bf16[2,256,1152]{2,1,0:T(8,128)(2,1)S(1)} %get-tuple-element.284.refs_4_.refs_0_, ...), custom_call_target="tpu_custom_call" | custom-call | bytes 1024 | tf_op jit(solution)/shard_map/weight_grad/pallas_call | solution.py:413
  632.9 5.5 multiply_reduce_fusion
  638.4 20.5 %collective-permute-done.34 = bf16[192,3456]{1,0:T(8,128)(2,1)} collective-permute-done((bf16[192,3456]{1,0:T(8,128)(2,1)}, bf16[192,3456]{1,0:T(8,128)(2,1)}, u32[]{:S(2)}, u32[]{:S(2)}) %collective-permute-start.34) | collective-permute-done | bytes 1327136 | tf_op jit(solution)/shard_map/ppermute | solution.py:131
  681.2 6.7 products.29
  687.9 7.0 products.30
  702.5 18.3 %collective-permute-done.43 = bf16[2,154,1536]{2,0,1:T(2,128)(2,1)S(1)} collective-permute-done((bf16[2,154,1536]{2,0,1:T(2,128)(2,1)S(1)}, bf16[2,154,1536]{2,0,1:T(2,128)(2,1)S(1)}, u32[]{:S(2)}, u32[]{:S(2)}) %collective-permute-start.43) | collective-permute-done | bytes 946208 | tf_op jit(solution)/shard_map/ppermute | solution.py:44
  724.2 49.7 %collective-permute-done.36 = bf16[2,154,1536]{2,0,1:T(2,128)(2,1)S(1)} collective-permute-done((bf16[2,154,1536]{2,0,1:T(2,128)(2,1)S(1)}, bf16[2,154,1536]{2,0,1:T(2,128)(2,1)S(1)}, u32[]{:S(2)}, u32[]{:S(2)}) %collective-permute-start.36) | collective-permute-done | bytes 946208 | tf_op jit(solution)/shard_map/ppermute | solution.py:44
  803.9 60.4 %collective-permute-done.48 = bf16[4,2,2,6,384]{4,1,3,2,0:T(2,128)(2,1)S(1)} collective-permute-done((bf16[4,2,2,6,384]{4,1,3,2,0:T(2,128)(2,1)S(1)}, bf16[4,2,2,6,384]{4,1,3,2,0:T(2,128)(2,1)S(1)}, u32[]{:S(2)}, u32[]{:S(2)}) %collective-permute-start.48) | collective-permute-done | bytes 73760 | tf_op jit(solution)/shard_map/ppermute | solution.py:44
  (540 shorter events, 272.5 us)
Async XLA Ops:
  7.2 151.9 %all-gather.5.cloned.1.call-start = ((), (), s32[]{:S(2)}) async-start(), calls=%async_computation.2 | async-start | bytes 10616832 | tf_op jit(solution)/shard_map/all_gather | solution.py:599
  11.7 279.0 %all-gather.7.cloned.1.call-start = ((), (), s32[]{:S(2)}) async-start(), calls=%async_computation.3 | async-start | bytes 5308416 | tf_op jit(solution)/shard_map/all_gather | solution.py:599
  12.4 307.2 %all-gather.9.cloned.1.call-start = ((), (), s32[]{:S(2)}) async-start(), calls=%async_computation.4 | async-start | bytes 5308416 | tf_op jit(solution)/shard_map/all_gather | solution.py:599
  19.3 450.7 %all-gather.11.cloned.1.call-start = ((), (), s32[]{:S(2)}) async-start(), calls=%async_computation.5 | async-start | bytes 10616832 | tf_op jit(solution)/shard_map/all_gather | solution.py:599
  66.6 36.7 %collective-permute-start.7 = (bf16[2,256,1536]{2,1,0:T(8,128)(2,1)S(1)}, bf16[2,256,1536]{2,1,0:T(8,128)(2,1)S(1)}, u32[]{:S(2)}, u32[]{:S(2)}) collective-permute-start(bf16[2,256,1536]{2,1,0:T(8,128)(2,1)S(1)} %fusion.7.refs_0_), channel_id=1, source_target_pairs={{0,2},{1,3},{2,0},{3,1},{4,6},{5,7},{6,4},{7,5},{8,10},{9,11},{10,... | collective-permute-start | bytes 4718600 | tf_op jit(solution)/shard_map/ppermute | solution.py:44
  68.2 37.7 %collective-permute-start.6 = (bf16[2,256,1536]{2,1,0:T(8,128)(2,1)S(1)}, bf16[2,256,1536]{2,1,0:T(8,128)(2,1)S(1)}, u32[]{:S(2)}, u32[]{:S(2)}) collective-permute-start(bf16[2,256,1536]{2,1,0:T(8,128)(2,1)S(1)} %fusion.7.refs_0_), channel_id=1, source_target_pairs={{0,1},{1,0},{2,3},{3,2},{4,5},{5,4},{6,7},{7,6},{8,9},{9,8},{10,11... | collective-permute-start | bytes 4718600 | tf_op jit(solution)/shard_map/ppermute | solution.py:44
  106.7 72.5 %collective-permute-start.9 = (bf16[2,256,1536]{2,1,0:T(8,128)(2,1)S(1)}, bf16[2,256,1536]{2,1,0:T(8,128)(2,1)}, u32[]{:S(2)}, u32[]{:S(2)}) collective-permute-start(bf16[2,256,1536]{2,1,0:T(8,128)(2,1)S(1)} %multiply_convert_fusion.2.refs_2_.refs_0_), channel_id=1, source_target_pairs={{0,2},{1,3},{2,0},{3,1},{4,6},{5,7},{6,4},{7,5},{8,10},{9,11},{10,... | collective-permute-start | bytes 4718600 | tf_op jit(solution)/shard_map/ppermute | solution.py:44
  241.9 649.6 %reduce-scatter.5.cloned.1.call-start = ((), (), s32[]{:S(2)}) async-start(), calls=%async_computation.7 | async-start | bytes 10616832 | tf_op jit(solution)/shard_map/reduce_scatter | solution.py:639
  249.8 36.5 %collective-permute-start.12 = (bf16[2,256,1536]{2,1,0:T(8,128)(2,1)S(1)}, bf16[2,256,1536]{2,1,0:T(8,128)(2,1)S(1)}, u32[]{:S(2)}, u32[]{:S(2)}) collective-permute-start(bf16[2,256,1536]{2,1,0:T(8,128)(2,1)S(1)} %add_convert_fusion.4), channel_id=1, source_target_pairs={{0,2},{1,3},{2,0},{3,1},{4,6},{5,7},{6,4},{7,5},{8,10},{9,11},{10,... | collective-permute-start | bytes 4718600 | tf_op jit(solution)/shard_map/ppermute | solution.py:44
  251.3 68.3 %collective-permute-start.14 = (bf16[2,256,1536]{2,1,0:T(8,128)(2,1)S(1)}, bf16[2,256,1536]{2,1,0:T(8,128)(2,1)}, u32[]{:S(2)}, u32[]{:S(2)}) collective-permute-start(bf16[2,256,1536]{2,1,0:T(8,128)(2,1)S(1)} %multiply_convert_fusion.2.refs_2_.refs_0_), channel_id=1, source_target_pairs={{0,1},{1,0},{2,3},{3,2},{4,5},{5,4},{6,7},{7,6},{8,9},{9,8},{10,11... | collective-permute-start | bytes 4718600 | tf_op jit(solution)/shard_map/ppermute | solution.py:44
  289.2 30.5 %collective-permute-start.13 = (bf16[2,256,1536]{2,1,0:T(8,128)(2,1)S(1)}, bf16[2,256,1536]{2,1,0:T(8,128)(2,1)}, u32[]{:S(2)}, u32[]{:S(2)}) collective-permute-start(bf16[2,256,1536]{2,1,0:T(8,128)(2,1)S(1)} %add_convert_fusion.3.refs_0_), channel_id=1, source_target_pairs={{0,1},{1,0},{2,3},{3,2},{4,5},{5,4},{6,7},{7,6},{8,9},{9,8},{10,11... | collective-permute-start | bytes 4718600 | tf_op jit(solution)/shard_map/ppermute | solution.py:44
  289.2 47.5 %collective-permute-start.15 = (bf16[2,256,1536]{2,1,0:T(8,128)(2,1)S(1)}, bf16[2,256,1536]{2,1,0:T(8,128)(2,1)}, u32[]{:S(2)}, u32[]{:S(2)}) collective-permute-start(bf16[2,256,1536]{2,1,0:T(8,128)(2,1)S(1)} %add_convert_fusion.3.refs_0_), channel_id=1, source_target_pairs={{0,2},{1,3},{2,0},{3,1},{4,6},{5,7},{6,4},{7,5},{8,10},{9,11},{10,... | collective-permute-start | bytes 4718600 | tf_op jit(solution)/shard_map/ppermute | solution.py:44
  393.4 34.0 %collective-permute-start.20 = (bf16[2,256,1536]{2,1,0:T(8,128)(2,1)S(1)}, bf16[2,256,1536]{2,1,0:T(8,128)(2,1)S(1)}, u32[]{:S(2)}, u32[]{:S(2)}) collective-permute-start(bf16[2,256,1536]{2,1,0:T(8,128)(2,1)S(1)} %get-tuple-element.195), channel_id=1, source_target_pairs={{0,1},{1,0},{2,3},{3,2},{4,5},{5,4},{6,7},{7,6},{8,9},{9,8},{10,11... | collective-permute-start | bytes 4718600 | tf_op jit(solution)/shard_map/ppermute | solution.py:44
  395.5 36.6 %collective-permute-start.22 = (bf16[2,256,1536]{2,1,0:T(8,128)(2,1)}, bf16[2,256,1536]{2,1,0:T(8,128)(2,1)}, u32[]{:S(2)}, u32[]{:S(2)}) collective-permute-start(bf16[2,256,1536]{2,1,0:T(8,128)(2,1)} %add_convert_fusion.2), channel_id=1, source_target_pairs={{0,2},{1,3},{2,0},{3,1},{4,6},{5,7},{6,4},{7,5},{8,10},{9,11},{10,... | collective-permute-start | bytes 4718600 | tf_op jit(solution)/shard_map/ppermute | solution.py:44
  436.9 458.3 %reduce-scatter.3.cloned.1.call-start = ((), (), s32[]{:S(2)}) async-start(), calls=%async_computation.6 | async-start | bytes 9289728 | tf_op jit(solution)/shard_map/reduce_scatter | solution.py:639
  449.0 37.9 %collective-permute-start.23 = (bf16[2,256,1536]{2,1,0:T(8,128)(2,1)S(1)}, bf16[2,256,1536]{2,1,0:T(8,128)(2,1)}, u32[]{:S(2)}, u32[]{:S(2)}) collective-permute-start(bf16[2,256,1536]{2,1,0:T(8,128)(2,1)S(1)} %multiply_convert_fusion.1.refs_0_), channel_id=1, source_target_pairs={{0,2},{1,3},{2,0},{3,1},{4,6},{5,7},{6,4},{7,5},{8,10},{9,11},{10,... | collective-permute-start | bytes 4718600 | tf_op jit(solution)/shard_map/ppermute | solution.py:44
  458.6 28.7 %collective-permute-start.28 = (bf16[2,256,1536]{2,1,0:T(8,128)(2,1)}, bf16[2,256,1536]{2,1,0:T(8,128)(2,1)}, u32[]{:S(2)}, u32[]{:S(2)}) collective-permute-start(bf16[2,256,1536]{2,1,0:T(8,128)(2,1)} %get-tuple-element.220), channel_id=1, source_target_pairs={{0,1},{1,0},{2,3},{3,2},{4,5},{5,4},{6,7},{7,6},{8,9},{9,8},{10,11... | collective-permute-start | bytes 4718600 | tf_op jit(solution)/shard_map/ppermute | solution.py:44
  491.7 91.7 %collective-permute-start.29 = (bf16[2,256,1536]{2,1,0:T(8,128)(2,1)}, bf16[2,256,1536]{2,1,0:T(8,128)(2,1)}, u32[]{:S(2)}, u32[]{:S(2)}) collective-permute-start(bf16[2,256,1536]{2,1,0:T(8,128)(2,1)} %add_convert_fusion.1), channel_id=1, source_target_pairs={{0,2},{1,3},{2,0},{3,1},{4,6},{5,7},{6,4},{7,5},{8,10},{9,11},{10,... | collective-permute-start | bytes 4718600 | tf_op jit(solution)/shard_map/ppermute | solution.py:44
  498.3 78.0 %collective-permute-start.32 = (bf16[2,154,1536]{2,0,1:T(2,128)(2,1)S(1)}, bf16[2,154,1536]{2,0,1:T(2,128)(2,1)S(1)}, u32[]{:S(2)}, u32[]{:S(2)}) collective-permute-start(bf16[2,154,1536]{2,0,1:T(2,128)(2,1)S(1)} %copy.81), channel_id=1, source_target_pairs={{0,2},{1,3},{2,0},{3,1},{4,6},{5,7},{6,4},{7,5},{8,10},{9,11},{10,... | collective-permute-start | bytes 2838536 | tf_op jit(solution)/shard_map/ppermute | solution.py:44
  524.8 62.3 %collective-permute-start.30 = (bf16[192,1664]{1,0:T(8,128)(2,1)S(1)}, bf16[192,1664]{1,0:T(8,128)(2,1)}, u32[]{:S(2)}, u32[]{:S(2)}) collective-permute-start(bf16[192,1664]{1,0:T(8,128)(2,1)S(1)} %constant_dynamic-slice_fusion), channel_id=1, source_target_pairs={{0,8},{8,16},{16,24},{24,28},{28,20},{20,12},{12,4},{4,0},{1,9},{9... | collective-permute-start | bytes 1916936 | tf_op jit(solution)/shard_map/ppermute | solution.py:131
  526.8 60.3 %collective-permute-start.31 = (bf16[192,1792]{1,0:T(8,128)(2,1)S(1)}, bf16[192,1792]{1,0:T(8,128)(2,1)S(1)}, u32[]{:S(2)}, u32[]{:S(2)}) collective-permute-start(bf16[192,1792]{1,0:T(8,128)(2,1)S(1)} %dynamic-slice.1), channel_id=1, source_target_pairs={{0,4},{8,0},{16,8},{24,16},{28,24},{20,28},{12,20},{4,12},{1,5},{9... | collective-permute-start | bytes 2064392 | tf_op jit(solution)/shard_map/ppermute | solution.py:131
  590.8 68.1 %collective-permute-start.34 = (bf16[192,3456]{1,0:T(8,128)(2,1)}, bf16[192,3456]{1,0:T(8,128)(2,1)}, u32[]{:S(2)}, u32[]{:S(2)}) collective-permute-start(bf16[192,3456]{1,0:T(8,128)(2,1)} %get-tuple-element.389), channel_id=1, source_target_pairs={{0,4},{8,0},{16,8},{24,16},{28,24},{20,28},{12,20},{4,12},{1,5},{9... | collective-permute-start | bytes 3981320 | tf_op jit(solution)/shard_map/ppermute | solution.py:131
  591.7 67.3 %collective-permute-start.33 = (bf16[192,3456]{1,0:T(8,128)(2,1)}, bf16[192,3456]{1,0:T(8,128)(2,1)}, u32[]{:S(2)}, u32[]{:S(2)}) collective-permute-start(bf16[192,3456]{1,0:T(8,128)(2,1)} %get-tuple-element.390), channel_id=1, source_target_pairs={{0,8},{8,16},{16,24},{24,28},{28,20},{20,12},{12,4},{4,0},{1,9},{9... | collective-permute-start | bytes 3981320 | tf_op jit(solution)/shard_map/ppermute | solution.py:131
  666.8 33.7 %collective-permute-start.35 = (f32[2,154,1536]{2,0,1:T(2,128)}, f32[2,154,1536]{2,0,1:T(2,128)S(1)}, u32[]{:S(2)}, u32[]{:S(2)}) collective-permute-start(f32[2,154,1536]{2,0,1:T(2,128)} %copy.83), channel_id=1, source_target_pairs={{0,1},{1,0},{2,3},{3,2},{4,5},{5,4},{6,7},{7,6},{8,9},{9,8},{10,11... | collective-permute-start | bytes 5677064 | tf_op jit(solution)/shard_map/ppermute | solution.py:44
  679.1 99.1 %collective-permute-start.41 = (bf16[192,3456]{1,0:T(8,128)(2,1)}, bf16[192,3456]{1,0:T(8,128)(2,1)}, u32[]{:S(2)}, u32[]{:S(2)}) collective-permute-start(bf16[192,3456]{1,0:T(8,128)(2,1)} %get-tuple-element.387), channel_id=1, source_target_pairs={{0,4},{8,0},{16,8},{24,16},{28,24},{20,28},{12,20},{4,12},{1,5},{9... | collective-permute-start | bytes 3981320 | tf_op jit(solution)/shard_map/ppermute | solution.py:131
  680.2 98.0 %collective-permute-start.40 = (bf16[192,3456]{1,0:T(8,128)(2,1)}, bf16[192,3456]{1,0:T(8,128)(2,1)}, u32[]{:S(2)}, u32[]{:S(2)}) collective-permute-start(bf16[192,3456]{1,0:T(8,128)(2,1)} %get-tuple-element.388), channel_id=1, source_target_pairs={{0,8},{8,16},{16,24},{24,28},{28,20},{20,12},{12,4},{4,0},{1,9},{9... | collective-permute-start | bytes 3981320 | tf_op jit(solution)/shard_map/ppermute | solution.py:131
  694.9 81.4 %collective-permute-start.37 = (bf16[2,256,1536]{2,1,0:T(8,128)(2,1)S(1)}, bf16[2,256,1536]{2,1,0:T(8,128)(2,1)S(1)}, u32[]{:S(2)}, u32[]{:S(2)}) collective-permute-start(bf16[2,256,1536]{2,1,0:T(8,128)(2,1)S(1)} %get-tuple-element.287), channel_id=1, source_target_pairs={{0,1},{1,0},{2,3},{3,2},{4,5},{5,4},{6,7},{7,6},{8,9},{9,8},{10,11... | collective-permute-start | bytes 4718600 | tf_op jit(solution)/shard_map/ppermute | solution.py:44
  700.5 75.9 %collective-permute-start.39 = (bf16[2,256,1536]{2,1,0:T(8,128)(2,1)S(1)}, bf16[2,256,1536]{2,1,0:T(8,128)(2,1)S(1)}, u32[]{:S(2)}, u32[]{:S(2)}) collective-permute-start(bf16[2,256,1536]{2,1,0:T(8,128)(2,1)S(1)} %add_convert_fusion), channel_id=1, source_target_pairs={{0,2},{1,3},{2,0},{3,1},{4,6},{5,7},{6,4},{7,5},{8,10},{9,11},{10,... | collective-permute-start | bytes 4718600 | tf_op jit(solution)/shard_map/ppermute | solution.py:44
  720.9 53.0 %collective-permute-start.36 = (bf16[2,154,1536]{2,0,1:T(2,128)(2,1)S(1)}, bf16[2,154,1536]{2,0,1:T(2,128)(2,1)S(1)}, u32[]{:S(2)}, u32[]{:S(2)}) collective-permute-start(bf16[2,154,1536]{2,0,1:T(2,128)(2,1)S(1)} %copy.85), channel_id=1, source_target_pairs={{0,2},{1,3},{2,0},{3,1},{4,6},{5,7},{6,4},{7,5},{8,10},{9,11},{10,... | collective-permute-start | bytes 2838536 | tf_op jit(solution)/shard_map/ppermute | solution.py:44
  795.5 91.0 %collective-permute-start.54 = (bf16[192,3456]{1,0:T(8,128)(2,1)S(1)}, bf16[192,3456]{1,0:T(8,128)(2,1)}, u32[]{:S(2)}, u32[]{:S(2)}) collective-permute-start(bf16[192,3456]{1,0:T(8,128)(2,1)S(1)} %get-tuple-element.385), channel_id=1, source_target_pairs={{0,8},{8,16},{16,24},{24,28},{28,20},{20,12},{12,4},{4,0},{1,9},{9... | collective-permute-start | bytes 3981320 | tf_op jit(solution)/shard_map/ppermute | solution.py:131
  796.8 89.7 %collective-permute-start.55 = (bf16[192,3456]{1,0:T(8,128)(2,1)S(1)}, bf16[192,3456]{1,0:T(8,128)(2,1)}, u32[]{:S(2)}, u32[]{:S(2)}) collective-permute-start(bf16[192,3456]{1,0:T(8,128)(2,1)S(1)} %get-tuple-element.386), channel_id=1, source_target_pairs={{0,4},{8,0},{16,8},{24,16},{28,24},{20,28},{12,20},{4,12},{1,5},{9... | collective-permute-start | bytes 3981320 | tf_op jit(solution)/shard_map/ppermute | solution.py:131
  799.2 65.2 %collective-permute-start.48 = (bf16[4,2,2,6,384]{4,1,3,2,0:T(2,128)(2,1)S(1)}, bf16[4,2,2,6,384]{4,1,3,2,0:T(2,128)(2,1)S(1)}, u32[]{:S(2)}, u32[]{:S(2)}) collective-permute-start(bf16[4,2,2,6,384]{4,1,3,2,0:T(2,128)(2,1)S(1)} %pad_maximum_fusion.4), channel_id=1, source_target_pairs={{0,16},{4,20},{8,24},{12,28},{16,0},{20,4},{24,8},{28,12},{1,17},{... | collective-permute-start | bytes 221192 | tf_op jit(solution)/shard_map/ppermute | solution.py:44
  (161 other events, 2735.0 us)
Sparse Core Ops, SparseCore 0:
  11.8 147.2 all-gather.4
  161.3 78.0 all-gather.6
  241.6 78.0 all-gather.8
  322.2 136.1 all-gather.10
  461.9 197.7 reduce-scatter.4
  663.2 197.6 reduce-scatter.2

commit v12 on v9

--- a/solution.py
+++ b/solution.py
@@ -604,8 +604,7 @@
         image_attention_out.T,
         text_attention_out.T,
     )
-    image_up = gathered(image_hidden_in)
-    image_down = gathered(image_hidden_out.T)
+    packed_image = gathered(image_hidden_in, image_hidden_out.T)
     packed_text = gathered(text_hidden_in, text_hidden_out.T)
     weight_in = ((packed_first, 0, 3 * width), (packed_first, 3 * width, 3 * width))
     weight_out = ((packed_first, 6 * width, width), (packed_first, 7 * width, width))
@@ -685,7 +684,7 @@
     branch = image_sum(attended_parts[0], weight_out[0], 1)
     middle = tokens[0] + spread(mods[0][:, 2]) * branch
     normed_two, inverse_two, image_second = modulated(middle, mods[0], 3, 4)
-    up_weight, down_weight = (image_up, 0, units), (image_down, 0, units)
+    up_weight, down_weight = (packed_image, 0, units), (packed_image, units, units)
     near_pieces = gather_pieces(image_second, size, half)
     far_have = gather_start(image_second, size)
     near = hidden_both(near_pieces, down_pieces[:half], up_weight, down_weight)

time: 888 us -> 872 us (0.982)
  waiting for transfers between devices: 335 us -> 320 us
    all_gather x4 -> x3, waiting for transfers between devices: 78.3 us -> 56.4 us  [gathered(): return lax.all_gather(joined, 'dp', axis=0, tiled=True)]
    ppermute x48, waiting for transfers between devices: 176 us -> 195 us  [swap(): return lax.ppermute(value, axis, [(i, i ^ bit) for i in range(size)])]
    reduce_scatter x2, waiting for transfers between devices: 16.7 us -> 4.78 us  [scattered(): lax.psum_scatter(grad, 'dp', scatter_dimension=0, tiled=True).astype(F32)]
    unnamed x313 -> x317, local copies, waits for them, and re-layouts: 21.1 us -> 22.5 us
  transfers between devices with their start and end apart: 62 -> 61, of which waited for: 30 -> 30; matrix products, arithmetic and copies ran while one was open for 13% -> 13% of each run, Pallas kernels for 37% -> 38%
where the time goes in v12:
time: 872 us; the launch traced here: 866 us
  Pallas kernels  327 us (38%)
  waiting for transfers between devices  320 us (37%)
  other arithmetic  86.5 us (10%)
  starting transfers between devices  54.5 us (6%)
  local copies, waits for them, and re-layouts  49.9 us (6%)
  between operations  16.8 us (2%)
    ppermute x48, waiting for transfers between devices, swap(): return lax.ppermute(value, axis, [(i, i ^ bit) for i in range(size)])  195 us
    pallas_call x16, Pallas kernels, products_of(): pl.pallas_call(functools.partial(product_kernel, count, weight_dim), grid...  101 us
    pallas_call x8, Pallas kernels, weight_grad(): pl.pallas_call(functools.partial(rows_kernel, count), grid=(rows // step,...  68.8 us
    pallas_call x2, Pallas kernels, attend_back(): pl.pallas_call(functools.partial(attend_back_kernel, count, asked, groups...  63.9 us
    ppermute x8, waiting for transfers between devices, ring_step(): return lax.ppermute(value, 'dp', hops)  63.5 us
    all_gather x3, waiting for transfers between devices, gathered(): return lax.all_gather(joined, 'dp', axis=0, tiled=True)  56.4 us
    pallas_call x1, Pallas kernels, attend(): pl.pallas_call(functools.partial(attend_kernel, count), grid=(slots, grou...  54.8 us
    ppermute x48, starting transfers between devices, swap(): return lax.ppermute(value, axis, [(i, i ^ bit) for i in range(size)])  45.8 us
  transfers between devices with their start and end apart: 61, of which 30 were waited for; matrix products, arithmetic and copies ran while one was open for 13% of the time, Pallas kernels for 38%

profile of v12, /device:TPU:0, one launch (start us, length us, event | category | flops | bytes accessed | tf_op | source)
XLA Modules:
  0.0 866.0 jit_solution(12979582660881425563)
XLA Ops:
  32.7 14.6 %collective-permute-done.3 = f32[4,2,4608]{2,1,0:T(2,128)S(1)} collective-permute-done((f32[4,2,4608]{2,1,0:T(2,128)S(1)}, f32[4,2,4608]{2,1,0:T(2,128)S(1)}, u32[]{:S(2)}, u32[]{:S(2)}) %collective-permute-start.3) | collective-permute-done | bytes 147488 | tf_op jit(solution)/shard_map/ppermute | solution.py:44
  48.2 8.5 collective-permute-done.4
  68.8 35.0 %collective-permute-done.7.refs_2_ = bf16[2,256,1536]{2,1,0:T(8,128)(2,1)S(1)} collective-permute-done((bf16[2,256,1536]{2,1,0:T(8,128)(2,1)S(1)}, bf16[2,256,1536]{2,1,0:T(8,128)(2,1)S(1)}, u32[]{:S(2)}, u32[]{:S(2)}) %collective-permute-start.7) | collective-permute-done | bytes 1572896 | tf_op jit(solution)/shard_map/ppermute | solution.py:44
  110.3 48.8 %all-gather.4.cloned.1.call-done.refs_4_.refs_1_.refs_2_ = bf16[1536,3072]{1,0:T(8,128)(2,1)} async-done(((bf16[192,3072]{1,0:T(8,128)(2,1)}), bf16[1536,3072]{1,0:T(8,128)(2,1)}) %all-gather.4.cloned.1.call-update) | async-done | bytes 9437200 | tf_op jit(solution)/shard_map/all_gather | solution.py:599
  159.1 14.4 %products.16 = (bf16[2,256,1152]{2,1,0:T(8,128)(2,1)S(1)}, bf16[2,256,1152]{2,1,0:T(8,128)(2,1)S(1)}, bf16[2,256,1152]{2,1,0:T(8,128)(2,1)S(1)}, bf16[2,256,1152]{2,1,0:T(8,128)(2,1)S(1)}) custom-call(bf16[2,256,1536]{2,1,0:T(8,128)(2,1)} %copy-done.86, bf16[2,256,1536]{2,1,0:T(8,128)(2,1)} %copy-done.100, bf16[2,256,1536]{2,1,0:T(8,128)(2,1)} %copy-done.99, ...), custom_call_target="tpu_custom_call" | custom-call | bytes 1024 | tf_op jit(solution)/shard_map/products/pallas_call | solution.py:490
  179.5 54.8 %attend.1 = (bf16[2,256,384]{2,1,0:T(8,128)(2,1)S(1)}, bf16[2,256,384]{2,1,0:T(8,128)(2,1)S(1)}, bf16[2,256,384]{2,1,0:T(8,128)(2,1)S(1)}, bf16[2,256,384]{2,1,0...) custom-call(bf16[2,256,1152]{2,1,0:T(8,128)(2,1)S(1)} %get-tuple-ele, ...), custom_call_target="tpu_custom_call" | custom-call | flops 17051860992 | bytes 7237632 | tf_op jit(solution)/shard_map/attend/pallas_call | solution.py:316
  251.2 35.0 %collective-permute-done.12 = bf16[2,256,1536]{2,1,0:T(8,128)(2,1)S(1)} collective-permute-done((bf16[2,256,1536]{2,1,0:T(8,128)(2,1)S(1)}, bf16[2,256,1536]{2,1,0:T(8,128)(2,1)S(1)}, u32[]{:S(2)}, u32[]{:S(2)}) %collective-permute-start.12) | collective-permute-done | bytes 1572896 | tf_op jit(solution)/shard_map/ppermute | solution.py:44
  290.5 7.6 all-gather.6.cloned.1.call-done.refs_4_.refs_5_.refs_2_
  298.1 16.0 %hidden_both.3 = (bf16[2,256,1536]{2,1,0:T(8,128)(2,1)S(1)}, bf16[2,256,1536]{2,1,0:T(8,128)(2,1)S(1)}, bf16[2,256,1536]{2,1,0:T(8,128)(2,1)S(1)}, bf16[2,256,1536]{2,1,0:T(8,128)(2,1)}) custom-call(bf16[2,256,1536]{2,1,0:T(8,128)(2,1)} %copy-done.4, bf16[2,256,1536]{2,1,0:T(8,128)(2,1)} %collective-permute-done.13.refs_1_, bf16[2,256,1536]{2,1,0:T(8,128)(2,1)} %copy-done.2, ...), custom_call_target="tpu_custom_call" | custom-call | bytes 1024 | tf_op jit(solution)/shard_map/hidden_both/pallas_call | solution.py:540
  315.3 10.7 %collective-permute-done.15.refs_0_.refs_2_ = bf16[2,256,1536]{2,1,0:T(8,128)(2,1)} collective-permute-done((bf16[2,256,1536]{2,1,0:T(8,128)(2,1)S(1)}, bf16[2,256,1536]{2,1,0:T(8,128)(2,1)}, u32[]{:S(2)}, u32[]{:S(2)}) %collective-permute-start.15) | collective-permute-done | bytes 1572896 | tf_op jit(solution)/shard_map/ppermute | solution.py:44
  343.4 16.2 %hidden_both.4 = (bf16[2,256,1536]{2,1,0:T(8,128)(2,1)S(1)}, bf16[2,256,1536]{2,1,0:T(8,128)(2,1)S(1)}, bf16[2,256,1536]{2,1,0:T(8,128)(2,1)S(1)}, bf16[2,256,1536]{2,1,0:T(8,128)(2,1)}) custom-call(bf16[2,256,1536]{2,1,0:T(8,128)(2,1)} %collective-permute-done.15.refs_0_.refs_2_, bf16[2,256,1536]{2,1,0:T(8,128)(2,1)} %copy-done.102, ...), custom_call_target="tpu_custom_call" | custom-call | bytes 1024 | tf_op jit(solution)/shard_map/hidden_both/pallas_call | solution.py:540
  366.3 7.9 products.21
  374.3 8.0 products.22
  385.8 15.2 %weight_grad.8.refs_8_ = bf16[1536,3072]{1,0:T(8,128)(2,1)} custom-call(bf16[2,256,1536]{2,1,0:T(8,128)(2,1)S(1)} %copy-done.3, bf16[2,256,1536]{2,1,0:T(8,128)(2,1)} %collective-permute-done.14.refs_3_.refs_1_, bf16[2,256,1536]{2,1,0:T(8,128)(2,1)} %collective-permute-done.9.refs_2_, bf16[2,256,1536]{2,1,0:T(8,128)(2,1)} %copy-done.103, ...), custom_call_target="tpu_custom_call" | custom-call | bytes 1024 | tf_op jit(solution)/shard_map/weight_grad/pallas_call | solution.py:413
  401.1 15.2 %weight_grad.9 = bf16[1536,3072]{1,0:T(8,128)(2,1)} custom-call(bf16[2,256,1536]{2,1,0:T(8,128)(2,1)S(1)} %copy-done.5, bf16[2,256,1536]{2,1,0:T(8,128)(2,1)} %collective-permute-done.13.refs_1_, bf16[2,256,1536]{2,1,0:T(8,128)(2,1)} %collective-permute-done.15.refs_0_.refs_2_, bf16[2,256,1536]{2,1,0:T(8,128)(2,1)} %copy-done.102, ...), custom_call_target="tpu_custom_call", output_to_operand_aliasing={{}: (8, {})} | custom-call | bytes 1024 | tf_op jit(solution)/shard_map/weight_grad/pallas_call | solution.py:413
  439.6 8.2 products.23
  449.2 8.1 products.24
  459.1 14.6 %collective-permute-done.23.refs_2_ = bf16[2,256,1536]{2,1,0:T(8,128)(2,1)} collective-permute-done((bf16[2,256,1536]{2,1,0:T(8,128)(2,1)S(1)}, bf16[2,256,1536]{2,1,0:T(8,128)(2,1)}, u32[]{:S(2)}, u32[]{:S(2)}) %collective-permute-start.23) | collective-permute-done | bytes 1572896 | tf_op jit(solution)/shard_map/ppermute | solution.py:44
  473.7 6.6 hidden_both.5
  521.7 6.2 products.25
  531.7 47.9 %attend_back.2 = (bf16[2,256,384]{2,1,0:T(8,128)(2,1)S(1)}, bf16[2,256,384]{2,1,0:T(8,128)(2,1)S(1)}, bf16[2,256,384]{2,1,0:T(8,128)(2,1)S(1)}, bf16[2,256,384]{...) custom-call(bf16[2,256,1152]{2,1,0:T(8,128)(2,1)S(1)} %copy-done.56, ...), custom_call_target="tpu_custom_call" | custom-call | flops 42629652480 | bytes 12665856 | tf_op jit(solution)/shard_map/attend_back/pallas_call | solution.py:365
  598.3 16.0 %attend_back.3 = (bf16[2,256,1152]{2,1,0:T(8,128)(2,1)S(1)}, bf16[2,256,1152]{2,1,0:T(8,128)(2,1)S(1)}, bf16[2,256,1152]{2,1,0:T(8,128)(2,1)}, bf16[2,256,1152]{2,1,0:T(8,128)(2,1)}, bf16[2,154,1152]{2,1,0:T(8,128)(2,1)S(1)}) custom-call(bf16[2,256,1152]{2,1,0:T(8,128)(2,1)} %copy-done.55, bf16[2,256,1152]{2,1,0:T(8,128)(2,1)} %copy-done.57, ...), custom_call_target="tpu_custom_call" | custom-call | flops 17051860992 | bytes 7237632 | tf_op jit(solution)/shard_map/attend_back/pallas_call | solution.py:365
  617.8 11.7 %weight_grad.12.refs_2_ = bf16[1536,3072]{1,0:T(8,128)(2,1)} custom-call(bf16[2,256,1536]{2,1,0:T(8,128)(2,1)} %copy-done.86, bf16[2,256,1536]{2,1,0:T(8,128)(2,1)} %copy-done.100, bf16[2,256,1536]{2,1,0:T(8,128)(2,1)} %copy-done.99, bf16[2,256,1536]{2,1,0:T(8,128)(2,1)} %copy-done.101, bf16[2,256,1152]{2,1,0:T(8,128)(2,1)S(1)} %get-tuple-element.275.refs_4_.refs_0_, ...), custom_call_target="tpu_custom_call" | custom-call | bytes 1024 | tf_op jit(solution)/shard_map/weight_grad/pallas_call | solution.py:413
  634.4 7.5 weight_grad.14.refs_2_
  652.8 6.7 products.29
  669.2 7.3 products.30
  684.0 18.3 %collective-permute-done.41 = bf16[2,154,1536]{2,0,1:T(2,128)(2,1)S(1)} collective-permute-done((bf16[2,154,1536]{2,0,1:T(2,128)(2,1)S(1)}, bf16[2,154,1536]{2,0,1:T(2,128)(2,1)S(1)}, u32[]{:S(2)}, u32[]{:S(2)}) %collective-permute-start.41) | collective-permute-done | bytes 946208 | tf_op jit(solution)/shard_map/ppermute | solution.py:44
  704.5 12.0 %collective-permute-done.42 = bf16[192,3072]{1,0:T(8,128)(2,1)} collective-permute-done((bf16[192,3072]{1,0:T(8,128)(2,1)}, bf16[192,3072]{1,0:T(8,128)(2,1)}, u32[]{:S(2)}, u32[]{:S(2)}) %collective-permute-start.42) | collective-permute-done | bytes 1179680 | tf_op jit(solution)/shard_map/ppermute | solution.py:131
  716.5 24.8 %collective-permute-done.43 = bf16[192,3072]{1,0:T(8,128)(2,1)} collective-permute-done((bf16[192,3072]{1,0:T(8,128)(2,1)}, bf16[192,3072]{1,0:T(8,128)(2,1)}, u32[]{:S(2)}, u32[]{:S(2)}) %collective-permute-start.43) | collective-permute-done | bytes 1179680 | tf_op jit(solution)/shard_map/ppermute | solution.py:131
  747.9 7.5 collective-permute-done.36
  763.4 26.7 %collective-permute-done.44 = bf16[192,3072]{1,0:T(8,128)(2,1)S(1)} collective-permute-done((bf16[192,3072]{1,0:T(8,128)(2,1)S(1)}, bf16[192,3072]{1,0:T(8,128)(2,1)S(1)}, u32[]{:S(2)}, u32[]{:S(2)}) %collective-permute-start.44) | collective-permute-done | bytes 1179680 | tf_op jit(solution)/shard_map/ppermute | solution.py:131
  838.4 6.9 collective-permute-done.55
  (571 shorter events, 304.6 us)
Async XLA Ops:
  7.2 151.9 %all-gather.4.cloned.1.call-start = ((), (), s32[]{:S(2)}) async-start(), calls=%async_computation.2 | async-start | bytes 10616832 | tf_op jit(solution)/shard_map/all_gather | solution.py:599
  11.7 286.5 %all-gather.6.cloned.1.call-start = ((), (), s32[]{:S(2)}) async-start(), calls=%async_computation.3 | async-start | bytes 10616832 | tf_op jit(solution)/shard_map/all_gather | solution.py:599
  12.9 460.8 %all-gather.8.cloned.1.call-start = ((), (), s32[]{:S(2)}) async-start(), calls=%async_computation.4 | async-start | bytes 10616832 | tf_op jit(solution)/shard_map/all_gather | solution.py:599
  67.1 36.7 %collective-permute-start.7 = (bf16[2,256,1536]{2,1,0:T(8,128)(2,1)S(1)}, bf16[2,256,1536]{2,1,0:T(8,128)(2,1)S(1)}, u32[]{:S(2)}, u32[]{:S(2)}) collective-permute-start(bf16[2,256,1536]{2,1,0:T(8,128)(2,1)S(1)} %fusion.7.refs_0_), channel_id=1, source_target_pairs={{0,2},{1,3},{2,0},{3,1},{4,6},{5,7},{6,4},{7,5},{8,10},{9,11},{10,... | collective-permute-start | bytes 4718600 | tf_op jit(solution)/shard_map/ppermute | solution.py:44
  68.7 37.6 %collective-permute-start.6 = (bf16[2,256,1536]{2,1,0:T(8,128)(2,1)S(1)}, bf16[2,256,1536]{2,1,0:T(8,128)(2,1)S(1)}, u32[]{:S(2)}, u32[]{:S(2)}) collective-permute-start(bf16[2,256,1536]{2,1,0:T(8,128)(2,1)S(1)} %fusion.7.refs_0_), channel_id=1, source_target_pairs={{0,1},{1,0},{2,3},{3,2},{4,5},{5,4},{6,7},{7,6},{8,9},{9,8},{10,11... | collective-permute-start | bytes 4718600 | tf_op jit(solution)/shard_map/ppermute | solution.py:44
  107.2 72.3 %collective-permute-start.9 = (bf16[2,256,1536]{2,1,0:T(8,128)(2,1)S(1)}, bf16[2,256,1536]{2,1,0:T(8,128)(2,1)}, u32[]{:S(2)}, u32[]{:S(2)}) collective-permute-start(bf16[2,256,1536]{2,1,0:T(8,128)(2,1)S(1)} %multiply_convert_fusion.2.refs_2_.refs_0_), channel_id=1, source_target_pairs={{0,2},{1,3},{2,0},{3,1},{4,6},{5,7},{6,4},{7,5},{8,10},{9,11},{10,... | collective-permute-start | bytes 4718600 | tf_op jit(solution)/shard_map/ppermute | solution.py:44
  242.2 603.9 %reduce-scatter.5.cloned.1.call-start = ((), (), s32[]{:S(2)}) async-start(), calls=%async_computation.6 | async-start | bytes 10616832 | tf_op jit(solution)/shard_map/reduce_scatter | solution.py:638
  249.6 36.6 %collective-permute-start.12 = (bf16[2,256,1536]{2,1,0:T(8,128)(2,1)S(1)}, bf16[2,256,1536]{2,1,0:T(8,128)(2,1)S(1)}, u32[]{:S(2)}, u32[]{:S(2)}) collective-permute-start(bf16[2,256,1536]{2,1,0:T(8,128)(2,1)S(1)} %add_convert_fusion.4), channel_id=1, source_target_pairs={{0,2},{1,3},{2,0},{3,1},{4,6},{5,7},{6,4},{7,5},{8,10},{9,11},{10,... | collective-permute-start | bytes 4718600 | tf_op jit(solution)/shard_map/ppermute | solution.py:44
  251.1 47.0 %collective-permute-start.14 = (bf16[2,256,1536]{2,1,0:T(8,128)(2,1)S(1)}, bf16[2,256,1536]{2,1,0:T(8,128)(2,1)}, u32[]{:S(2)}, u32[]{:S(2)}) collective-permute-start(bf16[2,256,1536]{2,1,0:T(8,128)(2,1)S(1)} %multiply_convert_fusion.2.refs_2_.refs_0_), channel_id=1, source_target_pairs={{0,1},{1,0},{2,3},{3,2},{4,5},{5,4},{6,7},{7,6},{8,9},{9,8},{10,11... | collective-permute-start | bytes 4718600 | tf_op jit(solution)/shard_map/ppermute | solution.py:44
  289.1 36.9 %collective-permute-start.15 = (bf16[2,256,1536]{2,1,0:T(8,128)(2,1)S(1)}, bf16[2,256,1536]{2,1,0:T(8,128)(2,1)}, u32[]{:S(2)}, u32[]{:S(2)}) collective-permute-start(bf16[2,256,1536]{2,1,0:T(8,128)(2,1)S(1)} %add_convert_fusion.3.refs_0_), channel_id=1, source_target_pairs={{0,2},{1,3},{2,0},{3,1},{4,6},{5,7},{6,4},{7,5},{8,10},{9,11},{10,... | collective-permute-start | bytes 4718600 | tf_op jit(solution)/shard_map/ppermute | solution.py:44
  382.2 34.0 %collective-permute-start.20 = (bf16[2,256,1536]{2,1,0:T(8,128)(2,1)S(1)}, bf16[2,256,1536]{2,1,0:T(8,128)(2,1)S(1)}, u32[]{:S(2)}, u32[]{:S(2)}) collective-permute-start(bf16[2,256,1536]{2,1,0:T(8,128)(2,1)S(1)} %get-tuple-element.192), channel_id=1, source_target_pairs={{0,1},{1,0},{2,3},{3,2},{4,5},{5,4},{6,7},{7,6},{8,9},{9,8},{10,11... | collective-permute-start | bytes 4718600 | tf_op jit(solution)/shard_map/ppermute | solution.py:44
  384.4 36.6 %collective-permute-start.22 = (bf16[2,256,1536]{2,1,0:T(8,128)(2,1)}, bf16[2,256,1536]{2,1,0:T(8,128)(2,1)}, u32[]{:S(2)}, u32[]{:S(2)}) collective-permute-start(bf16[2,256,1536]{2,1,0:T(8,128)(2,1)} %add_convert_fusion.2), channel_id=1, source_target_pairs={{0,2},{1,3},{2,0},{3,1},{4,6},{5,7},{6,4},{7,5},{8,10},{9,11},{10,... | collective-permute-start | bytes 4718600 | tf_op jit(solution)/shard_map/ppermute | solution.py:44
  425.7 429.0 %reduce-scatter.3.cloned.1.call-start = ((), (), s32[]{:S(2)}) async-start(), calls=%async_computation.5 | async-start | bytes 10616832 | tf_op jit(solution)/shard_map/reduce_scatter | solution.py:638
  438.0 35.6 %collective-permute-start.23 = (bf16[2,256,1536]{2,1,0:T(8,128)(2,1)S(1)}, bf16[2,256,1536]{2,1,0:T(8,128)(2,1)}, u32[]{:S(2)}, u32[]{:S(2)}) collective-permute-start(bf16[2,256,1536]{2,1,0:T(8,128)(2,1)S(1)} %multiply_convert_fusion.1.refs_0_), channel_id=1, source_target_pairs={{0,2},{1,3},{2,0},{3,1},{4,6},{5,7},{6,4},{7,5},{8,10},{9,11},{10,... | collective-permute-start | bytes 4718600 | tf_op jit(solution)/shard_map/ppermute | solution.py:44
  447.8 50.3 %collective-permute-start.28 = (bf16[2,256,1536]{2,1,0:T(8,128)(2,1)}, bf16[2,256,1536]{2,1,0:T(8,128)(2,1)}, u32[]{:S(2)}, u32[]{:S(2)}) collective-permute-start(bf16[2,256,1536]{2,1,0:T(8,128)(2,1)} %get-tuple-element.217), channel_id=1, source_target_pairs={{0,1},{1,0},{2,3},{3,2},{4,5},{5,4},{6,7},{7,6},{8,9},{9,8},{10,11... | collective-permute-start | bytes 4718600 | tf_op jit(solution)/shard_map/ppermute | solution.py:44
  457.3 56.3 %collective-permute-start.27 = (bf16[2,256,1536]{2,1,0:T(8,128)(2,1)}, bf16[2,256,1536]{2,1,0:T(8,128)(2,1)}, u32[]{:S(2)}, u32[]{:S(2)}) collective-permute-start(bf16[2,256,1536]{2,1,0:T(8,128)(2,1)} %get-tuple-element.221), channel_id=1, source_target_pairs={{0,1},{1,0},{2,3},{3,2},{4,5},{5,4},{6,7},{7,6},{8,9},{9,8},{10,11... | collective-permute-start | bytes 4718600 | tf_op jit(solution)/shard_map/ppermute | solution.py:44
  491.0 37.0 %collective-permute-start.26 = (f32[2,154,1536]{2,0,1:T(2,128)}, f32[2,154,1536]{2,0,1:T(2,128)}, u32[]{:S(2)}, u32[]{:S(2)}) collective-permute-start(f32[2,154,1536]{2,0,1:T(2,128)} %copy.79), channel_id=1, source_target_pairs={{0,1},{1,0},{2,3},{3,2},{4,5},{5,4},{6,7},{7,6},{8,9},{9,8},{10,11... | collective-permute-start | bytes 5677064 | tf_op jit(solution)/shard_map/ppermute | solution.py:44
  491.0 26.3 %collective-permute-start.24 = (bf16[2,256,1536]{2,1,0:T(8,128)(2,1)S(1)}, bf16[2,256,1536]{2,1,0:T(8,128)(2,1)}, u32[]{:S(2)}, u32[]{:S(2)}) collective-permute-start(bf16[2,256,1536]{2,1,0:T(8,128)(2,1)S(1)} %multiply_convert_fusion.1.refs_0_), channel_id=1, source_target_pairs={{0,1},{1,0},{2,3},{3,2},{4,5},{5,4},{6,7},{7,6},{8,9},{9,8},{10,11... | collective-permute-start | bytes 4718600 | tf_op jit(solution)/shard_map/ppermute | solution.py:44
  491.5 25.8 %collective-permute-start.25 = (bf16[2,256,1536]{2,1,0:T(8,128)(2,1)}, bf16[2,256,1536]{2,1,0:T(8,128)(2,1)}, u32[]{:S(2)}, u32[]{:S(2)}) collective-permute-start(bf16[2,256,1536]{2,1,0:T(8,128)(2,1)} %collective-permute-done.23.refs_2_), channel_id=1, source_target_pairs={{0,1},{1,0},{2,3},{3,2},{4,5},{5,4},{6,7},{7,6},{8,9},{9,8},{10,11... | collective-permute-start | bytes 4718600 | tf_op jit(solution)/shard_map/ppermute | solution.py:44
  501.4 78.3 %collective-permute-start.29 = (bf16[2,256,1536]{2,1,0:T(8,128)(2,1)}, bf16[2,256,1536]{2,1,0:T(8,128)(2,1)}, u32[]{:S(2)}, u32[]{:S(2)}) collective-permute-start(bf16[2,256,1536]{2,1,0:T(8,128)(2,1)} %add_convert_fusion.1), channel_id=1, source_target_pairs={{0,2},{1,3},{2,0},{3,1},{4,6},{5,7},{6,4},{7,5},{8,10},{9,11},{10,... | collective-permute-start | bytes 4718600 | tf_op jit(solution)/shard_map/ppermute | solution.py:44
  519.7 62.0 %collective-permute-start.30 = (bf16[192,1536]{1,0:T(8,128)(2,1)}, bf16[192,1536]{1,0:T(8,128)(2,1)}, u32[]{:S(2)}, u32[]{:S(2)}) collective-permute-start(bf16[192,1536]{1,0:T(8,128)(2,1)} %get-tuple-element.385), channel_id=1, source_target_pairs={{0,8},{8,16},{16,24},{24,28},{28,20},{20,12},{12,4},{4,0},{1,9},{9... | collective-permute-start | bytes 1769480 | tf_op jit(solution)/shard_map/ppermute | solution.py:131
  519.7 62.0 %collective-permute-start.31 = (bf16[192,1536]{1,0:T(8,128)(2,1)}, bf16[192,1536]{1,0:T(8,128)(2,1)}, u32[]{:S(2)}, u32[]{:S(2)}) collective-permute-start(bf16[192,1536]{1,0:T(8,128)(2,1)} %get-tuple-element.384), channel_id=1, source_target_pairs={{0,4},{8,0},{16,8},{24,16},{28,24},{20,28},{12,20},{4,12},{1,5},{9... | collective-permute-start | bytes 1769480 | tf_op jit(solution)/shard_map/ppermute | solution.py:131
  531.1 60.3 %collective-permute-start.32 = (bf16[2,154,1536]{2,0,1:T(2,128)(2,1)S(1)}, bf16[2,154,1536]{2,0,1:T(2,128)(2,1)S(1)}, u32[]{:S(2)}, u32[]{:S(2)}) collective-permute-start(bf16[2,154,1536]{2,0,1:T(2,128)(2,1)S(1)} %copy.81), channel_id=1, source_target_pairs={{0,2},{1,3},{2,0},{3,1},{4,6},{5,7},{6,4},{7,5},{8,10},{9,11},{10,... | collective-permute-start | bytes 2838536 | tf_op jit(solution)/shard_map/ppermute | solution.py:44
  585.7 60.0 %collective-permute-start.33 = (bf16[192,3072]{1,0:T(8,128)(2,1)}, bf16[192,3072]{1,0:T(8,128)(2,1)}, u32[]{:S(2)}, u32[]{:S(2)}) collective-permute-start(bf16[192,3072]{1,0:T(8,128)(2,1)} %get-tuple-element.383), channel_id=1, source_target_pairs={{0,8},{8,16},{16,24},{24,28},{28,20},{20,12},{12,4},{4,0},{1,9},{9... | collective-permute-start | bytes 3538952 | tf_op jit(solution)/shard_map/ppermute | solution.py:131
  585.7 59.9 %collective-permute-start.34 = (bf16[192,3072]{1,0:T(8,128)(2,1)}, bf16[192,3072]{1,0:T(8,128)(2,1)}, u32[]{:S(2)}, u32[]{:S(2)}) collective-permute-start(bf16[192,3072]{1,0:T(8,128)(2,1)} %get-tuple-element.382), channel_id=1, source_target_pairs={{0,4},{8,0},{16,8},{24,16},{28,24},{20,28},{12,20},{4,12},{1,5},{9... | collective-permute-start | bytes 3538952 | tf_op jit(solution)/shard_map/ppermute | solution.py:131
  664.4 52.1 %collective-permute-start.42 = (bf16[192,3072]{1,0:T(8,128)(2,1)}, bf16[192,3072]{1,0:T(8,128)(2,1)}, u32[]{:S(2)}, u32[]{:S(2)}) collective-permute-start(bf16[192,3072]{1,0:T(8,128)(2,1)} %get-tuple-element.381), channel_id=1, source_target_pairs={{0,8},{8,16},{16,24},{24,28},{28,20},{20,12},{12,4},{4,0},{1,9},{9... | collective-permute-start | bytes 3538952 | tf_op jit(solution)/shard_map/ppermute | solution.py:131
  664.7 76.5 %collective-permute-start.43 = (bf16[192,3072]{1,0:T(8,128)(2,1)}, bf16[192,3072]{1,0:T(8,128)(2,1)}, u32[]{:S(2)}, u32[]{:S(2)}) collective-permute-start(bf16[192,3072]{1,0:T(8,128)(2,1)} %get-tuple-element.380), channel_id=1, source_target_pairs={{0,4},{8,0},{16,8},{24,16},{28,24},{20,28},{12,20},{4,12},{1,5},{9... | collective-permute-start | bytes 3538952 | tf_op jit(solution)/shard_map/ppermute | solution.py:131
  676.4 86.1 %collective-permute-start.37 = (bf16[2,256,1536]{2,1,0:T(8,128)(2,1)S(1)}, bf16[2,256,1536]{2,1,0:T(8,128)(2,1)S(1)}, u32[]{:S(2)}, u32[]{:S(2)}) collective-permute-start(bf16[2,256,1536]{2,1,0:T(8,128)(2,1)S(1)} %get-tuple-element.278), channel_id=1, source_target_pairs={{0,1},{1,0},{2,3},{3,2},{4,5},{5,4},{6,7},{7,6},{8,9},{9,8},{10,11... | collective-permute-start | bytes 4718600 | tf_op jit(solution)/shard_map/ppermute | solution.py:44
  682.0 80.5 %collective-permute-start.39 = (bf16[2,256,1536]{2,1,0:T(8,128)(2,1)S(1)}, bf16[2,256,1536]{2,1,0:T(8,128)(2,1)S(1)}, u32[]{:S(2)}, u32[]{:S(2)}) collective-permute-start(bf16[2,256,1536]{2,1,0:T(8,128)(2,1)S(1)} %add_convert_fusion), channel_id=1, source_target_pairs={{0,2},{1,3},{2,0},{3,1},{4,6},{5,7},{6,4},{7,5},{8,10},{9,11},{10,... | collective-permute-start | bytes 4718600 | tf_op jit(solution)/shard_map/ppermute | solution.py:44
  702.3 53.0 %collective-permute-start.36 = (bf16[2,154,1536]{2,0,1:T(2,128)(2,1)S(1)}, bf16[2,154,1536]{2,0,1:T(2,128)(2,1)S(1)}, u32[]{:S(2)}, u32[]{:S(2)}) collective-permute-start(bf16[2,154,1536]{2,0,1:T(2,128)(2,1)S(1)} %copy.85), channel_id=1, source_target_pairs={{0,2},{1,3},{2,0},{3,1},{4,6},{5,7},{6,4},{7,5},{8,10},{9,11},{10,... | collective-permute-start | bytes 2838536 | tf_op jit(solution)/shard_map/ppermute | solution.py:44
  744.5 45.7 %collective-permute-start.44 = (bf16[192,3072]{1,0:T(8,128)(2,1)S(1)}, bf16[192,3072]{1,0:T(8,128)(2,1)S(1)}, u32[]{:S(2)}, u32[]{:S(2)}) collective-permute-start(bf16[192,3072]{1,0:T(8,128)(2,1)S(1)} %get-tuple-element.379), channel_id=1, source_target_pairs={{0,8},{8,16},{16,24},{24,28},{28,20},{20,12},{12,4},{4,0},{1,9},{9... | collective-permute-start | bytes 3538952 | tf_op jit(solution)/shard_map/ppermute | solution.py:131
  744.5 45.6 %collective-permute-start.45 = (bf16[192,3072]{1,0:T(8,128)(2,1)S(1)}, bf16[192,3072]{1,0:T(8,128)(2,1)S(1)}, u32[]{:S(2)}, u32[]{:S(2)}) collective-permute-start(bf16[192,3072]{1,0:T(8,128)(2,1)S(1)} %get-tuple-element.378), channel_id=1, source_target_pairs={{0,4},{8,0},{16,8},{24,16},{28,24},{20,28},{12,20},{4,12},{1,5},{9... | collective-permute-start | bytes 3538952 | tf_op jit(solution)/shard_map/ppermute | solution.py:131
  (177 other events, 2690.7 us)
Sparse Core Ops, SparseCore 0:
  11.8 147.2 all-gather.3
  161.8 136.2 all-gather.5
  300.9 136.2 all-gather.7
  440.6 189.2 reduce-scatter.4
  645.8 208.9 reduce-scatter.2

commit v13 on v12

--- a/solution.py
+++ b/solution.py
@@ -709,10 +709,8 @@
     low_have = gather_start(low, size)
     two_products = row_products(after(active, low), down_weight, 1)
     two_kept, two_sent = scatter_start(two_products, size)
-    low_have = after(low_have, two_products)
-    branch_grads = gather_end(low_have, size)
-
-    text_both = after(packed_text, low_have)
+
+    text_both = after(packed_text, low)
     text_up_weight, text_down_weight = (text_both, 0, units), (text_both, units, units)
     text_middle = tokens[1] + spread(mods[1][:, 2]) * text_branch
     text_normed_two, text_inverse_two, text_second = modulated(text_middle, mods[1], 3, 4)
@@ -721,14 +719,16 @@
     )
     (text_product,) = products_of(text_hidden_grad, text_up_weight, 1, [F32])
     text_kept, text_sent = text_start(text_product, size)
+    low_have = after(low_have, two_products, text_product)
+    branch_grads = gather_end(low_have, size)
     text_mlp_grad = weight_grad(
-        after([([down_rows[1]], text_active), ([text_second], text_hidden_grad)], text_product)
+        after([([down_rows[1]], text_active), ([text_second], text_hidden_grad)], low_have)
     )
     (text_two,) = products_of(after(text_active, text_product), text_down_weight, 1, [F32])
 
     upstreams = products_of(branch_grads, weight_out[0], 0, low_kinds)
     upstreams = after(upstreams, text_sent, text_mlp_grad, text_two)
-    text_ring = ring_scatter(after(text_mlp_grad, branch_grads), group_count)
+    text_ring = ring_scatter(after(text_mlp_grad, low_have), group_count)
     text_hop = next(text_ring)
     first_part = attend_back(parts, size, upstreams, sums[:-1])
     branch_two = scatter_end(after(two_kept, first_part), two_sent, size)

time: 872 us -> 866 us (level)
  waiting for transfers between devices: 320 us -> 307 us
    ppermute x48, waiting for transfers between devices: 195 us -> 173 us  [swap(): return lax.ppermute(value, axis, [(i, i ^ bit) for i in range(size)])]
    reduce_scatter x2, waiting for transfers between devices: 4.78 us -> 17.1 us  [scattered(): lax.psum_scatter(grad, 'dp', scatter_dimension=0, tiled=True).astype(F32)]
    unnamed x317 -> x313, local copies, waits for them, and re-layouts: 22.5 us -> 22.3 us
  transfers between devices with their start and end apart: 61 -> 61, of which waited for: 30 -> 29; matrix products, arithmetic and copies ran while one was open for 13% -> 14% of each run, Pallas kernels for 38% -> 38%
where the time goes in v13:
time: 866 us; the launch traced here: 860 us
  Pallas kernels  326 us (38%)
  waiting for transfers between devices  307 us (35%)
  other arithmetic  90.5 us (10%)
  starting transfers between devices  57.4 us (7%)
  local copies, waits for them, and re-layouts  50.5 us (6%)
  between operations  16.7 us (2%)
    ppermute x48, waiting for transfers between devices, swap(): return lax.ppermute(value, axis, [(i, i ^ bit) for i in range(size)])  173 us
    pallas_call x16, Pallas kernels, products_of(): pl.pallas_call(functools.partial(product_kernel, count, weight_dim), grid...  99.6 us
    pallas_call x8, Pallas kernels, weight_grad(): pl.pallas_call(functools.partial(rows_kernel, count), grid=(rows // step,...  68.3 us
    pallas_call x2, Pallas kernels, attend_back(): pl.pallas_call(functools.partial(attend_back_kernel, count, asked, groups...  64 us
    ppermute x8, waiting for transfers between devices, ring_step(): return lax.ppermute(value, 'dp', hops)  59.9 us
    all_gather x3, waiting for transfers between devices, gathered(): return lax.all_gather(joined, 'dp', axis=0, tiled=True)  56.4 us
    pallas_call x1, Pallas kernels, attend(): pl.pallas_call(functools.partial(attend_kernel, count), grid=(slots, grou...  54.8 us
    ppermute x48, starting transfers between devices, swap(): return lax.ppermute(value, axis, [(i, i ^ bit) for i in range(size)])  48.4 us
  transfers between devices with their start and end apart: 61, of which 29 were waited for; matrix products, arithmetic and copies ran while one was open for 14% of the time, Pallas kernels for 38%

profile of v13, /device:TPU:0, one launch (start us, length us, event | category | flops | bytes accessed | tf_op | source)
XLA Modules:
  0.0 859.7 jit_solution(5515283640634600936)
XLA Ops:
  32.7 14.6 %collective-permute-done.3 = f32[4,2,4608]{2,1,0:T(2,128)S(1)} collective-permute-done((f32[4,2,4608]{2,1,0:T(2,128)S(1)}, f32[4,2,4608]{2,1,0:T(2,128)S(1)}, u32[]{:S(2)}, u32[]{:S(2)}) %collective-permute-start.3) | collective-permute-done | bytes 147488 | tf_op jit(solution)/shard_map/ppermute | solution.py:44
  48.2 8.5 collective-permute-done.4
  68.8 35.0 %collective-permute-done.7.refs_2_ = bf16[2,256,1536]{2,1,0:T(8,128)(2,1)S(1)} collective-permute-done((bf16[2,256,1536]{2,1,0:T(8,128)(2,1)S(1)}, bf16[2,256,1536]{2,1,0:T(8,128)(2,1)S(1)}, u32[]{:S(2)}, u32[]{:S(2)}) %collective-permute-start.7) | collective-permute-done | bytes 1572896 | tf_op jit(solution)/shard_map/ppermute | solution.py:44
  110.3 48.8 %all-gather.4.cloned.1.call-done.refs_4_.refs_1_.refs_2_ = bf16[1536,3072]{1,0:T(8,128)(2,1)} async-done(((bf16[192,3072]{1,0:T(8,128)(2,1)}), bf16[1536,3072]{1,0:T(8,128)(2,1)}) %all-gather.4.cloned.1.call-update) | async-done | bytes 9437200 | tf_op jit(solution)/shard_map/all_gather | solution.py:599
  159.1 14.4 %products.16 = (bf16[2,256,1152]{2,1,0:T(8,128)(2,1)S(1)}, bf16[2,256,1152]{2,1,0:T(8,128)(2,1)S(1)}, bf16[2,256,1152]{2,1,0:T(8,128)(2,1)S(1)}, bf16[2,256,1152]{2,1,0:T(8,128)(2,1)S(1)}) custom-call(bf16[2,256,1536]{2,1,0:T(8,128)(2,1)} %copy-done.85, bf16[2,256,1536]{2,1,0:T(8,128)(2,1)} %copy-done.98, bf16[2,256,1536]{2,1,0:T(8,128)(2,1)} %copy-done.97, ...), custom_call_target="tpu_custom_call" | custom-call | bytes 1024 | tf_op jit(solution)/shard_map/products/pallas_call | solution.py:490
  179.5 54.8 %attend.1 = (bf16[2,256,384]{2,1,0:T(8,128)(2,1)S(1)}, bf16[2,256,384]{2,1,0:T(8,128)(2,1)S(1)}, bf16[2,256,384]{2,1,0:T(8,128)(2,1)S(1)}, bf16[2,256,384]{2,1,0...) custom-call(bf16[2,256,1152]{2,1,0:T(8,128)(2,1)S(1)} %get-tuple-ele, ...), custom_call_target="tpu_custom_call" | custom-call | flops 17051860992 | bytes 7237632 | tf_op jit(solution)/shard_map/attend/pallas_call | solution.py:316
  251.2 35.0 %collective-permute-done.12 = bf16[2,256,1536]{2,1,0:T(8,128)(2,1)S(1)} collective-permute-done((bf16[2,256,1536]{2,1,0:T(8,128)(2,1)S(1)}, bf16[2,256,1536]{2,1,0:T(8,128)(2,1)S(1)}, u32[]{:S(2)}, u32[]{:S(2)}) %collective-permute-start.12) | collective-permute-done | bytes 1572896 | tf_op jit(solution)/shard_map/ppermute | solution.py:44
  290.5 7.6 all-gather.6.cloned.1.call-done.refs_4_.refs_5_.refs_2_
  298.1 16.0 %hidden_both.3 = (bf16[2,256,1536]{2,1,0:T(8,128)(2,1)S(1)}, bf16[2,256,1536]{2,1,0:T(8,128)(2,1)S(1)}, bf16[2,256,1536]{2,1,0:T(8,128)(2,1)S(1)}, bf16[2,256,1536]{2,1,0:T(8,128)(2,1)}) custom-call(bf16[2,256,1536]{2,1,0:T(8,128)(2,1)} %copy-done.4, bf16[2,256,1536]{2,1,0:T(8,128)(2,1)} %collective-permute-done.13.refs_1_, bf16[2,256,1536]{2,1,0:T(8,128)(2,1)} %copy-done.2, ...), custom_call_target="tpu_custom_call" | custom-call | bytes 1024 | tf_op jit(solution)/shard_map/hidden_both/pallas_call | solution.py:540
  315.3 10.7 %collective-permute-done.15.refs_0_.refs_2_ = bf16[2,256,1536]{2,1,0:T(8,128)(2,1)} collective-permute-done((bf16[2,256,1536]{2,1,0:T(8,128)(2,1)S(1)}, bf16[2,256,1536]{2,1,0:T(8,128)(2,1)}, u32[]{:S(2)}, u32[]{:S(2)}) %collective-permute-start.15) | collective-permute-done | bytes 1572896 | tf_op jit(solution)/shard_map/ppermute | solution.py:44
  343.3 16.2 %hidden_both.4 = (bf16[2,256,1536]{2,1,0:T(8,128)(2,1)S(1)}, bf16[2,256,1536]{2,1,0:T(8,128)(2,1)S(1)}, bf16[2,256,1536]{2,1,0:T(8,128)(2,1)S(1)}, bf16[2,256,1536]{2,1,0:T(8,128)(2,1)}) custom-call(bf16[2,256,1536]{2,1,0:T(8,128)(2,1)} %collective-permute-done.15.refs_0_.refs_2_, bf16[2,256,1536]{2,1,0:T(8,128)(2,1)} %copy-done.100, ...), custom_call_target="tpu_custom_call" | custom-call | bytes 1024 | tf_op jit(solution)/shard_map/hidden_both/pallas_call | solution.py:540
  366.3 7.9 products.21
  374.3 8.0 products.22
  385.9 15.2 %weight_grad.8.refs_8_ = bf16[1536,3072]{1,0:T(8,128)(2,1)} custom-call(bf16[2,256,1536]{2,1,0:T(8,128)(2,1)S(1)} %copy-done.3, bf16[2,256,1536]{2,1,0:T(8,128)(2,1)} %collective-permute-done.14.refs_3_.refs_1_, bf16[2,256,1536]{2,1,0:T(8,128)(2,1)} %collective-permute-done.9.refs_2_, bf16[2,256,1536]{2,1,0:T(8,128)(2,1)} %copy-done.101, ...), custom_call_target="tpu_custom_call" | custom-call | bytes 1024 | tf_op jit(solution)/shard_map/weight_grad/pallas_call | solution.py:413
  401.1 15.2 %weight_grad.9 = bf16[1536,3072]{1,0:T(8,128)(2,1)} custom-call(bf16[2,256,1536]{2,1,0:T(8,128)(2,1)S(1)} %copy-done.5, bf16[2,256,1536]{2,1,0:T(8,128)(2,1)} %collective-permute-done.13.refs_1_, bf16[2,256,1536]{2,1,0:T(8,128)(2,1)} %collective-permute-done.15.refs_0_.refs_2_, bf16[2,256,1536]{2,1,0:T(8,128)(2,1)} %copy-done.100, ...), custom_call_target="tpu_custom_call", output_to_operand_aliasing={{}: (8, {})} | custom-call | bytes 1024 | tf_op jit(solution)/shard_map/weight_grad/pallas_call | solution.py:413
  439.6 8.2 products.23
  449.2 8.1 products.24
  459.2 7.3 hidden_both.5
  516.9 47.8 %attend_back.2 = (bf16[2,256,384]{2,1,0:T(8,128)(2,1)S(1)}, bf16[2,256,384]{2,1,0:T(8,128)(2,1)S(1)}, bf16[2,256,384]{2,1,0:T(8,128)(2,1)S(1)}, bf16[2,256,384]{...) custom-call(bf16[2,256,1152]{2,1,0:T(8,128)(2,1)S(1)} %copy-done.56, ...), custom_call_target="tpu_custom_call" | custom-call | flops 42629652480 | bytes 12665856 | tf_op jit(solution)/shard_map/attend_back/pallas_call | solution.py:365
  583.0 16.2 %attend_back.3 = (bf16[2,256,1152]{2,1,0:T(8,128)(2,1)S(1)}, bf16[2,256,1152]{2,1,0:T(8,128)(2,1)S(1)}, bf16[2,256,1152]{2,1,0:T(8,128)(2,1)}, bf16[2,256,1152]{2,1,0:T(8,128)(2,1)}, bf16[2,154,1152]{2,1,0:T(8,128)(2,1)S(1)}) custom-call(bf16[2,256,1152]{2,1,0:T(8,128)(2,1)} %copy-done.55, bf16[2,256,1152]{2,1,0:T(8,128)(2,1)} %copy-done.57, ...), custom_call_target="tpu_custom_call" | custom-call | flops 17051860992 | bytes 7237632 | tf_op jit(solution)/shard_map/attend_back/pallas_call | solution.py:365
  602.7 11.6 %weight_grad.12.refs_2_ = bf16[1536,3072]{1,0:T(8,128)(2,1)} custom-call(bf16[2,256,1536]{2,1,0:T(8,128)(2,1)} %copy-done.85, bf16[2,256,1536]{2,1,0:T(8,128)(2,1)} %copy-done.98, bf16[2,256,1536]{2,1,0:T(8,128)(2,1)} %copy-done.97, bf16[2,256,1536]{2,1,0:T(8,128)(2,1)} %copy-done.99, bf16[2,256,1152]{2,1,0:T(8,128)(2,1)S(1)} %get-tuple-element.275.refs_4_.refs_0_, ...), custom_call_target="tpu_custom_call" | custom-call | bytes 1024 | tf_op jit(solution)/shard_map/weight_grad/pallas_call | solution.py:413
  619.3 7.3 weight_grad.14.refs_2_
  631.5 5.8 multiply_reduce_fusion
  643.2 6.7 products.29
  660.2 6.8 products.30
  674.5 18.3 %collective-permute-done.41 = bf16[2,154,1536]{2,0,1:T(2,128)(2,1)S(1)} collective-permute-done((bf16[2,154,1536]{2,0,1:T(2,128)(2,1)S(1)}, bf16[2,154,1536]{2,0,1:T(2,128)(2,1)S(1)}, u32[]{:S(2)}, u32[]{:S(2)}) %collective-permute-start.41) | collective-permute-done | bytes 946208 | tf_op jit(solution)/shard_map/ppermute | solution.py:44
  695.1 12.5 %collective-permute-done.42 = bf16[192,3072]{1,0:T(8,128)(2,1)} collective-permute-done((bf16[192,3072]{1,0:T(8,128)(2,1)}, bf16[192,3072]{1,0:T(8,128)(2,1)}, u32[]{:S(2)}, u32[]{:S(2)}) %collective-permute-start.42) | collective-permute-done | bytes 1179680 | tf_op jit(solution)/shard_map/ppermute | solution.py:131
  707.6 24.9 %collective-permute-done.43 = bf16[192,3072]{1,0:T(8,128)(2,1)} collective-permute-done((bf16[192,3072]{1,0:T(8,128)(2,1)}, bf16[192,3072]{1,0:T(8,128)(2,1)}, u32[]{:S(2)}, u32[]{:S(2)}) %collective-permute-start.43) | collective-permute-done | bytes 1179680 | tf_op jit(solution)/shard_map/ppermute | solution.py:131
  739.2 6.7 collective-permute-done.36
  754.0 20.7 %collective-permute-done.44 = bf16[192,3072]{1,0:T(8,128)(2,1)S(1)} collective-permute-done((bf16[192,3072]{1,0:T(8,128)(2,1)S(1)}, bf16[192,3072]{1,0:T(8,128)(2,1)S(1)}, u32[]{:S(2)}, u32[]{:S(2)}) %collective-permute-start.44) | collective-permute-done | bytes 1179680 | tf_op jit(solution)/shard_map/ppermute | solution.py:131
  817.5 9.1 %collective-permute-done.55 = f32[4,8,2,192]{3,2,1,0:T(2,128)S(1)} collective-permute-done((f32[4,8,2,192]{3,2,1,0:T(2,128)S(1)}, f32[4,8,2,192]{3,2,1,0:T(2,128)S(1)}, u32[]{:S(2)}, u32[]{:S(2)}) %collective-permute-start.55) | collective-permute-done | bytes 49184 | tf_op jit(solution)/shard_map/ppermute | solution.py:44
  831.3 17.1 %reduce-scatter.3.cloned.1.call-done = bf16[192,3072]{1,0:T(8,128)(2,1)} async-done(((bf16[1536,3072]{1,0:T(8,128)(2,1)}), bf16[192,3072]{1,0:T(8,128)(2,1)}) %reduce-scatter.3.cloned.1.call-update) | async-done | bytes 1179664 | tf_op jit(solution)/shard_map/reduce_scatter | solution.py:638
  (567 shorter events, 299.9 us)
Async XLA Ops:
  7.2 151.9 %all-gather.4.cloned.1.call-start = ((), (), s32[]{:S(2)}) async-start(), calls=%async_computation.2 | async-start | bytes 10616832 | tf_op jit(solution)/shard_map/all_gather | solution.py:599
  11.7 286.5 %all-gather.6.cloned.1.call-start = ((), (), s32[]{:S(2)}) async-start(), calls=%async_computation.3 | async-start | bytes 10616832 | tf_op jit(solution)/shard_map/all_gather | solution.py:599
  12.9 446.2 %all-gather.8.cloned.1.call-start = ((), (), s32[]{:S(2)}) async-start(), calls=%async_computation.4 | async-start | bytes 10616832 | tf_op jit(solution)/shard_map/all_gather | solution.py:599
  67.1 36.7 %collective-permute-start.7 = (bf16[2,256,1536]{2,1,0:T(8,128)(2,1)S(1)}, bf16[2,256,1536]{2,1,0:T(8,128)(2,1)S(1)}, u32[]{:S(2)}, u32[]{:S(2)}) collective-permute-start(bf16[2,256,1536]{2,1,0:T(8,128)(2,1)S(1)} %fusion.7.refs_0_), channel_id=1, source_target_pairs={{0,2},{1,3},{2,0},{3,1},{4,6},{5,7},{6,4},{7,5},{8,10},{9,11},{10,... | collective-permute-start | bytes 4718600 | tf_op jit(solution)/shard_map/ppermute | solution.py:44
  68.7 37.7 %collective-permute-start.6 = (bf16[2,256,1536]{2,1,0:T(8,128)(2,1)S(1)}, bf16[2,256,1536]{2,1,0:T(8,128)(2,1)S(1)}, u32[]{:S(2)}, u32[]{:S(2)}) collective-permute-start(bf16[2,256,1536]{2,1,0:T(8,128)(2,1)S(1)} %fusion.7.refs_0_), channel_id=1, source_target_pairs={{0,1},{1,0},{2,3},{3,2},{4,5},{5,4},{6,7},{7,6},{8,9},{9,8},{10,11... | collective-permute-start | bytes 4718600 | tf_op jit(solution)/shard_map/ppermute | solution.py:44
  107.2 72.3 %collective-permute-start.9 = (bf16[2,256,1536]{2,1,0:T(8,128)(2,1)S(1)}, bf16[2,256,1536]{2,1,0:T(8,128)(2,1)}, u32[]{:S(2)}, u32[]{:S(2)}) collective-permute-start(bf16[2,256,1536]{2,1,0:T(8,128)(2,1)S(1)} %multiply_convert_fusion.2.refs_2_.refs_0_), channel_id=1, source_target_pairs={{0,2},{1,3},{2,0},{3,1},{4,6},{5,7},{6,4},{7,5},{8,10},{9,11},{10,... | collective-permute-start | bytes 4718600 | tf_op jit(solution)/shard_map/ppermute | solution.py:44
  242.2 585.2 %reduce-scatter.5.cloned.1.call-start = ((), (), s32[]{:S(2)}) async-start(), calls=%async_computation.6 | async-start | bytes 10616832 | tf_op jit(solution)/shard_map/reduce_scatter | solution.py:638
  249.6 36.6 %collective-permute-start.12 = (bf16[2,256,1536]{2,1,0:T(8,128)(2,1)S(1)}, bf16[2,256,1536]{2,1,0:T(8,128)(2,1)S(1)}, u32[]{:S(2)}, u32[]{:S(2)}) collective-permute-start(bf16[2,256,1536]{2,1,0:T(8,128)(2,1)S(1)} %add_convert_fusion.4), channel_id=1, source_target_pairs={{0,2},{1,3},{2,0},{3,1},{4,6},{5,7},{6,4},{7,5},{8,10},{9,11},{10,... | collective-permute-start | bytes 4718600 | tf_op jit(solution)/shard_map/ppermute | solution.py:44
  251.1 47.0 %collective-permute-start.14 = (bf16[2,256,1536]{2,1,0:T(8,128)(2,1)S(1)}, bf16[2,256,1536]{2,1,0:T(8,128)(2,1)}, u32[]{:S(2)}, u32[]{:S(2)}) collective-permute-start(bf16[2,256,1536]{2,1,0:T(8,128)(2,1)S(1)} %multiply_convert_fusion.2.refs_2_.refs_0_), channel_id=1, source_target_pairs={{0,1},{1,0},{2,3},{3,2},{4,5},{5,4},{6,7},{7,6},{8,9},{9,8},{10,11... | collective-permute-start | bytes 4718600 | tf_op jit(solution)/shard_map/ppermute | solution.py:44
  289.1 36.9 %collective-permute-start.15 = (bf16[2,256,1536]{2,1,0:T(8,128)(2,1)S(1)}, bf16[2,256,1536]{2,1,0:T(8,128)(2,1)}, u32[]{:S(2)}, u32[]{:S(2)}) collective-permute-start(bf16[2,256,1536]{2,1,0:T(8,128)(2,1)S(1)} %add_convert_fusion.3.refs_0_), channel_id=1, source_target_pairs={{0,2},{1,3},{2,0},{3,1},{4,6},{5,7},{6,4},{7,5},{8,10},{9,11},{10,... | collective-permute-start | bytes 4718600 | tf_op jit(solution)/shard_map/ppermute | solution.py:44
  382.3 34.0 %collective-permute-start.20 = (bf16[2,256,1536]{2,1,0:T(8,128)(2,1)S(1)}, bf16[2,256,1536]{2,1,0:T(8,128)(2,1)S(1)}, u32[]{:S(2)}, u32[]{:S(2)}) collective-permute-start(bf16[2,256,1536]{2,1,0:T(8,128)(2,1)S(1)} %get-tuple-element.192), channel_id=1, source_target_pairs={{0,1},{1,0},{2,3},{3,2},{4,5},{5,4},{6,7},{7,6},{8,9},{9,8},{10,11... | collective-permute-start | bytes 4718600 | tf_op jit(solution)/shard_map/ppermute | solution.py:44
  384.4 36.6 %collective-permute-start.22 = (bf16[2,256,1536]{2,1,0:T(8,128)(2,1)}, bf16[2,256,1536]{2,1,0:T(8,128)(2,1)}, u32[]{:S(2)}, u32[]{:S(2)}) collective-permute-start(bf16[2,256,1536]{2,1,0:T(8,128)(2,1)} %add_convert_fusion.2), channel_id=1, source_target_pairs={{0,2},{1,3},{2,0},{3,1},{4,6},{5,7},{6,4},{7,5},{8,10},{9,11},{10,... | collective-permute-start | bytes 4718600 | tf_op jit(solution)/shard_map/ppermute | solution.py:44
  425.8 422.6 %reduce-scatter.3.cloned.1.call-start = ((), (), s32[]{:S(2)}) async-start(), calls=%async_computation.5 | async-start | bytes 10616832 | tf_op jit(solution)/shard_map/reduce_scatter | solution.py:638
  438.1 46.2 %collective-permute-start.23 = (bf16[2,256,1536]{2,1,0:T(8,128)(2,1)S(1)}, bf16[2,256,1536]{2,1,0:T(8,128)(2,1)}, u32[]{:S(2)}, u32[]{:S(2)}) collective-permute-start(bf16[2,256,1536]{2,1,0:T(8,128)(2,1)S(1)} %multiply_convert_fusion.1.refs_0_), channel_id=1, source_target_pairs={{0,2},{1,3},{2,0},{3,1},{4,6},{5,7},{6,4},{7,5},{8,10},{9,11},{10,... | collective-permute-start | bytes 4718600 | tf_op jit(solution)/shard_map/ppermute | solution.py:44
  447.8 50.0 %collective-permute-start.28 = (bf16[2,256,1536]{2,1,0:T(8,128)(2,1)}, bf16[2,256,1536]{2,1,0:T(8,128)(2,1)}, u32[]{:S(2)}, u32[]{:S(2)}) collective-permute-start(bf16[2,256,1536]{2,1,0:T(8,128)(2,1)} %get-tuple-element.217), channel_id=1, source_target_pairs={{0,1},{1,0},{2,3},{3,2},{4,5},{5,4},{6,7},{7,6},{8,9},{9,8},{10,11... | collective-permute-start | bytes 4718600 | tf_op jit(solution)/shard_map/ppermute | solution.py:44
  457.3 44.0 %collective-permute-start.27 = (bf16[2,256,1536]{2,1,0:T(8,128)(2,1)}, bf16[2,256,1536]{2,1,0:T(8,128)(2,1)}, u32[]{:S(2)}, u32[]{:S(2)}) collective-permute-start(bf16[2,256,1536]{2,1,0:T(8,128)(2,1)} %get-tuple-element.221), channel_id=1, source_target_pairs={{0,1},{1,0},{2,3},{3,2},{4,5},{5,4},{6,7},{7,6},{8,9},{9,8},{10,11... | collective-permute-start | bytes 4718600 | tf_op jit(solution)/shard_map/ppermute | solution.py:44
  477.0 28.0 %collective-permute-start.26 = (f32[2,154,1536]{2,0,1:T(2,128)}, f32[2,154,1536]{2,0,1:T(2,128)}, u32[]{:S(2)}, u32[]{:S(2)}) collective-permute-start(f32[2,154,1536]{2,0,1:T(2,128)} %copy.79), channel_id=1, source_target_pairs={{0,1},{1,0},{2,3},{3,2},{4,5},{5,4},{6,7},{7,6},{8,9},{9,8},{10,11... | collective-permute-start | bytes 5677064 | tf_op jit(solution)/shard_map/ppermute | solution.py:44
  484.3 26.3 %collective-permute-start.24 = (bf16[2,256,1536]{2,1,0:T(8,128)(2,1)S(1)}, bf16[2,256,1536]{2,1,0:T(8,128)(2,1)S(1)}, u32[]{:S(2)}, u32[]{:S(2)}) collective-permute-start(bf16[2,256,1536]{2,1,0:T(8,128)(2,1)S(1)} %multiply_convert_fusion.1.refs_0_), channel_id=1, source_target_pairs={{0,1},{1,0},{2,3},{3,2},{4,5},{5,4},{6,7},{7,6},{8,9},{9,8},{10,11... | collective-permute-start | bytes 4718600 | tf_op jit(solution)/shard_map/ppermute | solution.py:44
  484.4 26.8 %collective-permute-start.25 = (bf16[2,256,1536]{2,1,0:T(8,128)(2,1)}, bf16[2,256,1536]{2,1,0:T(8,128)(2,1)}, u32[]{:S(2)}, u32[]{:S(2)}) collective-permute-start(bf16[2,256,1536]{2,1,0:T(8,128)(2,1)} %collective-permute-done.23.refs_2_), channel_id=1, source_target_pairs={{0,1},{1,0},{2,3},{3,2},{4,5},{5,4},{6,7},{7,6},{8,9},{9,8},{10,11... | collective-permute-start | bytes 4718600 | tf_op jit(solution)/shard_map/ppermute | solution.py:44
  497.8 70.6 %collective-permute-start.30 = (bf16[192,1536]{1,0:T(8,128)(2,1)}, bf16[192,1536]{1,0:T(8,128)(2,1)}, u32[]{:S(2)}, u32[]{:S(2)}) collective-permute-start(bf16[192,1536]{1,0:T(8,128)(2,1)} %get-tuple-element.385), channel_id=1, source_target_pairs={{0,8},{8,16},{16,24},{24,28},{28,20},{20,12},{12,4},{4,0},{1,9},{9... | collective-permute-start | bytes 1769480 | tf_op jit(solution)/shard_map/ppermute | solution.py:131
  501.3 67.0 %collective-permute-start.31 = (bf16[192,1536]{1,0:T(8,128)(2,1)}, bf16[192,1536]{1,0:T(8,128)(2,1)}, u32[]{:S(2)}, u32[]{:S(2)}) collective-permute-start(bf16[192,1536]{1,0:T(8,128)(2,1)} %get-tuple-element.384), channel_id=1, source_target_pairs={{0,4},{8,0},{16,8},{24,16},{28,24},{20,28},{12,20},{4,12},{1,5},{9... | collective-permute-start | bytes 1769480 | tf_op jit(solution)/shard_map/ppermute | solution.py:131
  505.1 59.6 %collective-permute-start.29 = (bf16[2,256,1536]{2,1,0:T(8,128)(2,1)}, bf16[2,256,1536]{2,1,0:T(8,128)(2,1)}, u32[]{:S(2)}, u32[]{:S(2)}) collective-permute-start(bf16[2,256,1536]{2,1,0:T(8,128)(2,1)} %add_convert_fusion.1), channel_id=1, source_target_pairs={{0,2},{1,3},{2,0},{3,1},{4,6},{5,7},{6,4},{7,5},{8,10},{9,11},{10,... | collective-permute-start | bytes 4718600 | tf_op jit(solution)/shard_map/ppermute | solution.py:44
  510.6 63.8 %collective-permute-start.32 = (bf16[2,154,1536]{2,0,1:T(2,128)(2,1)}, bf16[2,154,1536]{2,0,1:T(2,128)(2,1)}, u32[]{:S(2)}, u32[]{:S(2)}) collective-permute-start(bf16[2,154,1536]{2,0,1:T(2,128)(2,1)} %copy.81), channel_id=1, source_target_pairs={{0,2},{1,3},{2,0},{3,1},{4,6},{5,7},{6,4},{7,5},{8,10},{9,11},{10,... | collective-permute-start | bytes 2838536 | tf_op jit(solution)/shard_map/ppermute | solution.py:44
  572.4 65.0 %collective-permute-start.33 = (bf16[192,3072]{1,0:T(8,128)(2,1)}, bf16[192,3072]{1,0:T(8,128)(2,1)}, u32[]{:S(2)}, u32[]{:S(2)}) collective-permute-start(bf16[192,3072]{1,0:T(8,128)(2,1)} %get-tuple-element.383), channel_id=1, source_target_pairs={{0,8},{8,16},{16,24},{24,28},{28,20},{20,12},{12,4},{4,0},{1,9},{9... | collective-permute-start | bytes 3538952 | tf_op jit(solution)/shard_map/ppermute | solution.py:131
  572.8 64.6 %collective-permute-start.34 = (bf16[192,3072]{1,0:T(8,128)(2,1)}, bf16[192,3072]{1,0:T(8,128)(2,1)}, u32[]{:S(2)}, u32[]{:S(2)}) collective-permute-start(bf16[192,3072]{1,0:T(8,128)(2,1)} %get-tuple-element.382), channel_id=1, source_target_pairs={{0,4},{8,0},{16,8},{24,16},{28,24},{20,28},{12,20},{4,12},{1,5},{9... | collective-permute-start | bytes 3538952 | tf_op jit(solution)/shard_map/ppermute | solution.py:131
  655.0 52.5 %collective-permute-start.42 = (bf16[192,3072]{1,0:T(8,128)(2,1)}, bf16[192,3072]{1,0:T(8,128)(2,1)}, u32[]{:S(2)}, u32[]{:S(2)}) collective-permute-start(bf16[192,3072]{1,0:T(8,128)(2,1)} %get-tuple-element.381), channel_id=1, source_target_pairs={{0,8},{8,16},{16,24},{24,28},{28,20},{20,12},{12,4},{4,0},{1,9},{9... | collective-permute-start | bytes 3538952 | tf_op jit(solution)/shard_map/ppermute | solution.py:131
  656.0 76.5 %collective-permute-start.43 = (bf16[192,3072]{1,0:T(8,128)(2,1)}, bf16[192,3072]{1,0:T(8,128)(2,1)}, u32[]{:S(2)}, u32[]{:S(2)}) collective-permute-start(bf16[192,3072]{1,0:T(8,128)(2,1)} %get-tuple-element.380), channel_id=1, source_target_pairs={{0,4},{8,0},{16,8},{24,16},{28,24},{20,28},{12,20},{4,12},{1,5},{9... | collective-permute-start | bytes 3538952 | tf_op jit(solution)/shard_map/ppermute | solution.py:131
  667.0 86.1 %collective-permute-start.37 = (bf16[2,256,1536]{2,1,0:T(8,128)(2,1)S(1)}, bf16[2,256,1536]{2,1,0:T(8,128)(2,1)S(1)}, u32[]{:S(2)}, u32[]{:S(2)}) collective-permute-start(bf16[2,256,1536]{2,1,0:T(8,128)(2,1)S(1)} %get-tuple-element.278), channel_id=1, source_target_pairs={{0,1},{1,0},{2,3},{3,2},{4,5},{5,4},{6,7},{7,6},{8,9},{9,8},{10,11... | collective-permute-start | bytes 4718600 | tf_op jit(solution)/shard_map/ppermute | solution.py:44
  672.7 80.4 %collective-permute-start.39 = (bf16[2,256,1536]{2,1,0:T(8,128)(2,1)S(1)}, bf16[2,256,1536]{2,1,0:T(8,128)(2,1)S(1)}, u32[]{:S(2)}, u32[]{:S(2)}) collective-permute-start(bf16[2,256,1536]{2,1,0:T(8,128)(2,1)S(1)} %add_convert_fusion), channel_id=1, source_target_pairs={{0,2},{1,3},{2,0},{3,1},{4,6},{5,7},{6,4},{7,5},{8,10},{9,11},{10,... | collective-permute-start | bytes 4718600 | tf_op jit(solution)/shard_map/ppermute | solution.py:44
  692.8 53.0 %collective-permute-start.36 = (bf16[2,154,1536]{2,0,1:T(2,128)(2,1)S(1)}, bf16[2,154,1536]{2,0,1:T(2,128)(2,1)S(1)}, u32[]{:S(2)}, u32[]{:S(2)}) collective-permute-start(bf16[2,154,1536]{2,0,1:T(2,128)(2,1)S(1)} %copy.85), channel_id=1, source_target_pairs={{0,2},{1,3},{2,0},{3,1},{4,6},{5,7},{6,4},{7,5},{8,10},{9,11},{10,... | collective-permute-start | bytes 2838536 | tf_op jit(solution)/shard_map/ppermute | solution.py:44
  735.8 38.9 %collective-permute-start.44 = (bf16[192,3072]{1,0:T(8,128)(2,1)S(1)}, bf16[192,3072]{1,0:T(8,128)(2,1)S(1)}, u32[]{:S(2)}, u32[]{:S(2)}) collective-permute-start(bf16[192,3072]{1,0:T(8,128)(2,1)S(1)} %get-tuple-element.379), channel_id=1, source_target_pairs={{0,8},{8,16},{16,24},{24,28},{28,20},{20,12},{12,4},{4,0},{1,9},{9... | collective-permute-start | bytes 3538952 | tf_op jit(solution)/shard_map/ppermute | solution.py:131
  735.8 40.6 %collective-permute-start.45 = (bf16[192,3072]{1,0:T(8,128)(2,1)S(1)}, bf16[192,3072]{1,0:T(8,128)(2,1)S(1)}, u32[]{:S(2)}, u32[]{:S(2)}) collective-permute-start(bf16[192,3072]{1,0:T(8,128)(2,1)S(1)} %get-tuple-element.378), channel_id=1, source_target_pairs={{0,4},{8,0},{16,8},{24,16},{28,24},{20,28},{12,20},{4,12},{1,5},{9... | collective-permute-start | bytes 3538952 | tf_op jit(solution)/shard_map/ppermute | solution.py:131
  (175 other events, 2579.8 us)
Sparse Core Ops, SparseCore 0:
  11.7 147.2 all-gather.3
  161.8 136.2 all-gather.5
  300.9 136.2 all-gather.7
  440.6 195.4 reduce-scatter.4
  639.6 208.7 reduce-scatter.2

commit v14 on v13

--- a/solution.py
+++ b/solution.py
@@ -722,7 +722,14 @@
     low_have = after(low_have, two_products, text_product)
     branch_grads = gather_end(low_have, size)
     text_mlp_grad = weight_grad(
-        after([([down_rows[1]], text_active), ([text_second], text_hidden_grad)], low_have)
+        after(
+            [
+                ([down_rows[1]], text_active),
+                ([text_second], text_hidden_grad),
+                (branch_grads, attended_parts[0]),
+            ],
+            low_have,
+        )
     )
     (text_two,) = products_of(after(text_active, text_product), text_down_weight, 1, [F32])
 
@@ -745,7 +752,6 @@
         [
             (first_pieces, packed_grads[:-1]),
             ([text_first], packed_grads[-1:]),
-            (branch_grads, attended_parts[0]),
             ([text_low], attended_parts[1]),
         ]
     )
@@ -847,13 +853,13 @@
         condition_gradient,
         image_ada,
         attention_sum[:, : 3 * width].reshape(share, 3, width),
-        attention_sum[:, 6 * width : 7 * width].T,
+        text_mlp[:, 2 * units :].T,
         image_mlp[:, units:],
         image_mlp[:, :units].T,
         text_ada,
         attention_sum[:, 3 * width : 6 * width].reshape(share, 3, width),
-        attention_sum[:, 7 * width :].T,
-        text_mlp[:, units:],
+        attention_sum[:, 6 * width :].T,
+        text_mlp[:, units : 2 * units],
         text_mlp[:, :units].T,
     )
 

time: 866 us -> 884 us (1.021)
  waiting for transfers between devices: 307 us -> 333 us
  starting transfers between devices: 57.4 us -> 48.4 us
    ppermute x8, waiting for transfers between devices: 59.9 us -> 96.2 us  [ring_step(): return lax.ppermute(value, 'dp', hops)]
    reduce_scatter x2, waiting for transfers between devices: 17.1 us -> 0.01 us  [scattered(): lax.psum_scatter(grad, 'dp', scatter_dimension=0, tiled=True).astype(F32)]
    unnamed x313 -> x301, local copies, waits for them, and re-layouts: 22.3 us -> 21.6 us
  transfers between devices with their start and end apart: 61 -> 61, of which waited for: 29 -> 30; matrix products, arithmetic and copies ran while one was open for 14% -> 14% of each run, Pallas kernels for 38% -> 37%
where the time goes in v14:
time: 884 us; the launch traced here: 878 us
  waiting for transfers between devices  333 us (38%)
  Pallas kernels  327 us (37%)
  other arithmetic  87.9 us (10%)
  local copies, waits for them, and re-layouts  53.5 us (6%)
  starting transfers between devices  48.4 us (5%)
  between operations  16.8 us (2%)
    ppermute x48, waiting for transfers between devices, swap(): return lax.ppermute(value, axis, [(i, i ^ bit) for i in range(size)])  180 us
    pallas_call x16, Pallas kernels, products_of(): pl.pallas_call(functools.partial(product_kernel, count, weight_dim), grid...  100 us
    ppermute x8, waiting for transfers between devices, ring_step(): return lax.ppermute(value, 'dp', hops)  96.2 us
    pallas_call x8, Pallas kernels, weight_grad(): pl.pallas_call(functools.partial(rows_kernel, count), grid=(rows // step,...  68.2 us
    pallas_call x2, Pallas kernels, attend_back(): pl.pallas_call(functools.partial(attend_back_kernel, count, asked, groups...  64.4 us
    all_gather x3, waiting for transfers between devices, gathered(): return lax.all_gather(joined, 'dp', axis=0, tiled=True)  56.3 us
    pallas_call x1, Pallas kernels, attend(): pl.pallas_call(functools.partial(attend_kernel, count), grid=(slots, grou...  54.8 us
    ppermute x48, starting transfers between devices, swap(): return lax.ppermute(value, axis, [(i, i ^ bit) for i in range(size)])  39.9 us
  transfers between devices with their start and end apart: 61, of which 30 were waited for; matrix products, arithmetic and copies ran while one was open for 14% of the time, Pallas kernels for 37%

profile of v14, /device:TPU:0, one launch (start us, length us, event | category | flops | bytes accessed | tf_op | source)
XLA Modules:
  0.0 878.0 jit_solution(15094383705601435079)
XLA Ops:
  32.7 14.6 %collective-permute-done.3 = f32[4,2,4608]{2,1,0:T(2,128)S(1)} collective-permute-done((f32[4,2,4608]{2,1,0:T(2,128)S(1)}, f32[4,2,4608]{2,1,0:T(2,128)S(1)}, u32[]{:S(2)}, u32[]{:S(2)}) %collective-permute-start.3) | collective-permute-done | bytes 147488 | tf_op jit(solution)/shard_map/ppermute | solution.py:44
  48.2 8.5 collective-permute-done.4
  68.8 35.0 %collective-permute-done.7.refs_2_ = bf16[2,256,1536]{2,1,0:T(8,128)(2,1)S(1)} collective-permute-done((bf16[2,256,1536]{2,1,0:T(8,128)(2,1)S(1)}, bf16[2,256,1536]{2,1,0:T(8,128)(2,1)S(1)}, u32[]{:S(2)}, u32[]{:S(2)}) %collective-permute-start.7) | collective-permute-done | bytes 1572896 | tf_op jit(solution)/shard_map/ppermute | solution.py:44
  110.3 48.8 %all-gather.4.cloned.1.call-done.refs_4_.refs_1_.refs_2_ = bf16[1536,3072]{1,0:T(8,128)(2,1)} async-done(((bf16[192,3072]{1,0:T(8,128)(2,1)}), bf16[1536,3072]{1,0:T(8,128)(2,1)}) %all-gather.4.cloned.1.call-update) | async-done | bytes 9437200 | tf_op jit(solution)/shard_map/all_gather | solution.py:599
  159.1 14.1 %products.16 = (bf16[2,256,1152]{2,1,0:T(8,128)(2,1)S(1)}, bf16[2,256,1152]{2,1,0:T(8,128)(2,1)S(1)}, bf16[2,256,1152]{2,1,0:T(8,128)(2,1)S(1)}, bf16[2,256,1152]{2,1,0:T(8,128)(2,1)S(1)}) custom-call(bf16[2,256,1536]{2,1,0:T(8,128)(2,1)} %copy-done.82, bf16[2,256,1536]{2,1,0:T(8,128)(2,1)} %copy-done.96, bf16[2,256,1536]{2,1,0:T(8,128)(2,1)} %copy-done.95, ...), custom_call_target="tpu_custom_call" | custom-call | bytes 1024 | tf_op jit(solution)/shard_map/products/pallas_call | solution.py:490
  179.3 54.8 %attend.1 = (bf16[2,256,384]{2,1,0:T(8,128)(2,1)S(1)}, bf16[2,256,384]{2,1,0:T(8,128)(2,1)S(1)}, bf16[2,256,384]{2,1,0:T(8,128)(2,1)S(1)}, bf16[2,256,384]{2,1,0...) custom-call(bf16[2,256,1152]{2,1,0:T(8,128)(2,1)S(1)} %get-tuple-ele, ...), custom_call_target="tpu_custom_call" | custom-call | flops 17051860992 | bytes 7237632 | tf_op jit(solution)/shard_map/attend/pallas_call | solution.py:316
  251.2 35.0 %collective-permute-done.12 = bf16[2,256,1536]{2,1,0:T(8,128)(2,1)S(1)} collective-permute-done((bf16[2,256,1536]{2,1,0:T(8,128)(2,1)S(1)}, bf16[2,256,1536]{2,1,0:T(8,128)(2,1)S(1)}, u32[]{:S(2)}, u32[]{:S(2)}) %collective-permute-start.12) | collective-permute-done | bytes 1572896 | tf_op jit(solution)/shard_map/ppermute | solution.py:44
  290.6 7.5 all-gather.6.cloned.1.call-done.refs_4_.refs_5_.refs_2_
  298.1 16.0 %hidden_both.3 = (bf16[2,256,1536]{2,1,0:T(8,128)(2,1)S(1)}, bf16[2,256,1536]{2,1,0:T(8,128)(2,1)S(1)}, bf16[2,256,1536]{2,1,0:T(8,128)(2,1)S(1)}, bf16[2,256,1536]{2,1,0:T(8,128)(2,1)}) custom-call(bf16[2,256,1536]{2,1,0:T(8,128)(2,1)} %copy-done.4, bf16[2,256,1536]{2,1,0:T(8,128)(2,1)} %collective-permute-done.13.refs_1_, bf16[2,256,1536]{2,1,0:T(8,128)(2,1)} %copy-done.2, ...), custom_call_target="tpu_custom_call" | custom-call | bytes 1024 | tf_op jit(solution)/shard_map/hidden_both/pallas_call | solution.py:540
  315.3 10.8 %collective-permute-done.15.refs_0_.refs_2_ = bf16[2,256,1536]{2,1,0:T(8,128)(2,1)} collective-permute-done((bf16[2,256,1536]{2,1,0:T(8,128)(2,1)S(1)}, bf16[2,256,1536]{2,1,0:T(8,128)(2,1)}, u32[]{:S(2)}, u32[]{:S(2)}) %collective-permute-start.15) | collective-permute-done | bytes 1572896 | tf_op jit(solution)/shard_map/ppermute | solution.py:44
  343.4 16.1 %hidden_both.4 = (bf16[2,256,1536]{2,1,0:T(8,128)(2,1)S(1)}, bf16[2,256,1536]{2,1,0:T(8,128)(2,1)S(1)}, bf16[2,256,1536]{2,1,0:T(8,128)(2,1)S(1)}, bf16[2,256,1536]{2,1,0:T(8,128)(2,1)}) custom-call(bf16[2,256,1536]{2,1,0:T(8,128)(2,1)} %collective-permute-done.15.refs_0_.refs_2_, bf16[2,256,1536]{2,1,0:T(8,128)(2,1)} %copy-done.98, ...), custom_call_target="tpu_custom_call" | custom-call | bytes 1024 | tf_op jit(solution)/shard_map/hidden_both/pallas_call | solution.py:540
  366.4 7.9 products.21
  374.3 8.0 products.22
  385.9 15.3 %weight_grad.8.refs_8_ = bf16[1536,3072]{1,0:T(8,128)(2,1)} custom-call(bf16[2,256,1536]{2,1,0:T(8,128)(2,1)S(1)} %copy-done.3, bf16[2,256,1536]{2,1,0:T(8,128)(2,1)} %collective-permute-done.14.refs_3_.refs_1_, bf16[2,256,1536]{2,1,0:T(8,128)(2,1)} %collective-permute-done.9.refs_2_, bf16[2,256,1536]{2,1,0:T(8,128)(2,1)} %copy-done.99, ...), custom_call_target="tpu_custom_call" | custom-call | bytes 1024 | tf_op jit(solution)/shard_map/weight_grad/pallas_call | solution.py:413
  401.2 15.1 %weight_grad.9 = bf16[1536,3072]{1,0:T(8,128)(2,1)} custom-call(bf16[2,256,1536]{2,1,0:T(8,128)(2,1)S(1)} %copy-done.5, bf16[2,256,1536]{2,1,0:T(8,128)(2,1)} %collective-permute-done.13.refs_1_, bf16[2,256,1536]{2,1,0:T(8,128)(2,1)} %collective-permute-done.15.refs_0_.refs_2_, bf16[2,256,1536]{2,1,0:T(8,128)(2,1)} %copy-done.98, ...), custom_call_target="tpu_custom_call", output_to_operand_aliasing={{}: (8, {})} | custom-call | bytes 1024 | tf_op jit(solution)/shard_map/weight_grad/pallas_call | solution.py:413
  439.7 8.2 products.23
  449.3 8.1 products.24
  459.3 7.3 hidden_both.5
  507.3 7.2 weight_grad.12
  514.6 5.8 products.26
  520.4 48.1 %attend_back.2 = (bf16[2,256,384]{2,1,0:T(8,128)(2,1)S(1)}, bf16[2,256,384]{2,1,0:T(8,128)(2,1)S(1)}, bf16[2,256,384]{2,1,0:T(8,128)(2,1)S(1)}, bf16[2,256,384]{...) custom-call(bf16[2,256,1152]{2,1,0:T(8,128)(2,1)S(1)} %copy-done.54, ...), custom_call_target="tpu_custom_call" | custom-call | flops 42629652480 | bytes 12665856 | tf_op jit(solution)/shard_map/attend_back/pallas_call | solution.py:365
  585.7 17.3 %collective-permute-done.30 = bf16[192,1664]{1,0:T(8,128)(2,1)} collective-permute-done((bf16[192,1664]{1,0:T(8,128)(2,1)}, bf16[192,1664]{1,0:T(8,128)(2,1)}, u32[]{:S(2)}, u32[]{:S(2)}) %collective-permute-start.30) | collective-permute-done | bytes 639008 | tf_op jit(solution)/shard_map/ppermute | solution.py:131
  603.0 11.3 %collective-permute-done.31 = bf16[192,1792]{1,0:T(8,128)(2,1)} collective-permute-done((bf16[192,1792]{1,0:T(8,128)(2,1)}, bf16[192,1792]{1,0:T(8,128)(2,1)}, u32[]{:S(2)}, u32[]{:S(2)}) %collective-permute-start.31) | collective-permute-done | bytes 688160 | tf_op jit(solution)/shard_map/ppermute | solution.py:131
  620.2 16.4 %attend_back.3 = (bf16[2,256,1152]{2,1,0:T(8,128)(2,1)S(1)}, bf16[2,256,1152]{2,1,0:T(8,128)(2,1)S(1)}, bf16[2,256,1152]{2,1,0:T(8,128)(2,1)}, bf16[2,256,1152]{2,1,0:T(8,128)(2,1)}, bf16[2,154,1152]{2,1,0:T(8,128)(2,1)S(1)}) custom-call(bf16[2,256,1152]{2,1,0:T(8,128)(2,1)} %copy-done.53, bf16[2,256,1152]{2,1,0:T(8,128)(2,1)} %copy-done.55, ...), custom_call_target="tpu_custom_call" | custom-call | flops 17051860992 | bytes 7237632 | tf_op jit(solution)/shard_map/attend_back/pallas_call | solution.py:365
  640.0 11.7 %weight_grad.13.refs_2_ = bf16[1536,2688]{1,0:T(8,128)(2,1)} custom-call(bf16[2,256,1536]{2,1,0:T(8,128)(2,1)} %copy-done.82, bf16[2,256,1536]{2,1,0:T(8,128)(2,1)} %copy-done.96, bf16[2,256,1536]{2,1,0:T(8,128)(2,1)} %copy-done.95, bf16[2,256,1536]{2,1,0:T(8,128)(2,1)} %copy-done.97, bf16[2,256,1152]{2,1,0:T(8,128)(2,1)S(1)} %get-tuple-element.291.refs_4_.refs_0_, ...), custom_call_target="tpu_custom_call" | custom-call | bytes 1024 | tf_op jit(solution)/shard_map/weight_grad/pallas_call | solution.py:413
  672.6 6.7 products.29
  689.2 6.9 products.30
  703.7 18.3 %collective-permute-done.41 = bf16[2,154,1536]{2,0,1:T(2,128)(2,1)S(1)} collective-permute-done((bf16[2,154,1536]{2,0,1:T(2,128)(2,1)S(1)}, bf16[2,154,1536]{2,0,1:T(2,128)(2,1)S(1)}, u32[]{:S(2)}, u32[]{:S(2)}) %collective-permute-start.41) | collective-permute-done | bytes 946208 | tf_op jit(solution)/shard_map/ppermute | solution.py:44
  723.7 20.3 %collective-permute-done.42 = bf16[192,3456]{1,0:T(8,128)(2,1)} collective-permute-done((bf16[192,3456]{1,0:T(8,128)(2,1)}, bf16[192,3456]{1,0:T(8,128)(2,1)}, u32[]{:S(2)}, u32[]{:S(2)}) %collective-permute-start.42) | collective-permute-done | bytes 1327136 | tf_op jit(solution)/shard_map/ppermute | solution.py:131
  744.0 20.0 %collective-permute-done.43 = bf16[192,3456]{1,0:T(8,128)(2,1)} collective-permute-done((bf16[192,3456]{1,0:T(8,128)(2,1)}, bf16[192,3456]{1,0:T(8,128)(2,1)}, u32[]{:S(2)}, u32[]{:S(2)}) %collective-permute-start.43) | collective-permute-done | bytes 1327136 | tf_op jit(solution)/shard_map/ppermute | solution.py:131
  783.0 27.3 %collective-permute-done.44 = bf16[192,3456]{1,0:T(8,128)(2,1)S(1)} collective-permute-done((bf16[192,3456]{1,0:T(8,128)(2,1)S(1)}, bf16[192,3456]{1,0:T(8,128)(2,1)S(1)}, u32[]{:S(2)}, u32[]{:S(2)}) %collective-permute-start.44) | collective-permute-done | bytes 1327136 | tf_op jit(solution)/shard_map/ppermute | solution.py:131
  829.8 11.0 %collective-permute-done.50 = bf16[4,2,2,6,384]{4,1,3,2,0:T(2,128)(2,1)S(1)} collective-permute-done((bf16[4,2,2,6,384]{4,1,3,2,0:T(2,128)(2,1)S(1)}, bf16[4,2,2,6,384]{4,1,3,2,0:T(2,128)(2,1)S(1)}, u32[]{:S(2)}, u32[]{:S(2)}) %collective-permute-start.50) | collective-permute-done | bytes 73760 | tf_op jit(solution)/shard_map/ppermute | solution.py:44
  (557 shorter events, 301.9 us)
Async XLA Ops:
  7.2 151.9 %all-gather.4.cloned.1.call-start = ((), (), s32[]{:S(2)}) async-start(), calls=%async_computation.2 | async-start | bytes 10616832 | tf_op jit(solution)/shard_map/all_gather | solution.py:599
  11.7 286.5 %all-gather.6.cloned.1.call-start = ((), (), s32[]{:S(2)}) async-start(), calls=%async_computation.3 | async-start | bytes 10616832 | tf_op jit(solution)/shard_map/all_gather | solution.py:599
  12.9 446.4 %all-gather.8.cloned.1.call-start = ((), (), s32[]{:S(2)}) async-start(), calls=%async_computation.4 | async-start | bytes 10616832 | tf_op jit(solution)/shard_map/all_gather | solution.py:599
  67.1 36.7 %collective-permute-start.7 = (bf16[2,256,1536]{2,1,0:T(8,128)(2,1)S(1)}, bf16[2,256,1536]{2,1,0:T(8,128)(2,1)S(1)}, u32[]{:S(2)}, u32[]{:S(2)}) collective-permute-start(bf16[2,256,1536]{2,1,0:T(8,128)(2,1)S(1)} %fusion.7.refs_0_), channel_id=1, source_target_pairs={{0,2},{1,3},{2,0},{3,1},{4,6},{5,7},{6,4},{7,5},{8,10},{9,11},{10,... | collective-permute-start | bytes 4718600 | tf_op jit(solution)/shard_map/ppermute | solution.py:44
  68.7 37.6 %collective-permute-start.6 = (bf16[2,256,1536]{2,1,0:T(8,128)(2,1)S(1)}, bf16[2,256,1536]{2,1,0:T(8,128)(2,1)S(1)}, u32[]{:S(2)}, u32[]{:S(2)}) collective-permute-start(bf16[2,256,1536]{2,1,0:T(8,128)(2,1)S(1)} %fusion.7.refs_0_), channel_id=1, source_target_pairs={{0,1},{1,0},{2,3},{3,2},{4,5},{5,4},{6,7},{7,6},{8,9},{9,8},{10,11... | collective-permute-start | bytes 4718600 | tf_op jit(solution)/shard_map/ppermute | solution.py:44
  107.2 72.0 %collective-permute-start.9 = (bf16[2,256,1536]{2,1,0:T(8,128)(2,1)S(1)}, bf16[2,256,1536]{2,1,0:T(8,128)(2,1)}, u32[]{:S(2)}, u32[]{:S(2)}) collective-permute-start(bf16[2,256,1536]{2,1,0:T(8,128)(2,1)S(1)} %multiply_convert_fusion.2.refs_2_.refs_0_), channel_id=1, source_target_pairs={{0,2},{1,3},{2,0},{3,1},{4,6},{5,7},{6,4},{7,5},{8,10},{9,11},{10,... | collective-permute-start | bytes 4718600 | tf_op jit(solution)/shard_map/ppermute | solution.py:44
  241.9 621.4 %reduce-scatter.5.cloned.1.call-start = ((), (), s32[]{:S(2)}) async-start(), calls=%async_computation.6 | async-start | bytes 10616832 | tf_op jit(solution)/shard_map/reduce_scatter | solution.py:638
  249.6 36.6 %collective-permute-start.12 = (bf16[2,256,1536]{2,1,0:T(8,128)(2,1)S(1)}, bf16[2,256,1536]{2,1,0:T(8,128)(2,1)S(1)}, u32[]{:S(2)}, u32[]{:S(2)}) collective-permute-start(bf16[2,256,1536]{2,1,0:T(8,128)(2,1)S(1)} %add_convert_fusion.4), channel_id=1, source_target_pairs={{0,2},{1,3},{2,0},{3,1},{4,6},{5,7},{6,4},{7,5},{8,10},{9,11},{10,... | collective-permute-start | bytes 4718600 | tf_op jit(solution)/shard_map/ppermute | solution.py:44
  251.2 47.0 %collective-permute-start.14 = (bf16[2,256,1536]{2,1,0:T(8,128)(2,1)S(1)}, bf16[2,256,1536]{2,1,0:T(8,128)(2,1)}, u32[]{:S(2)}, u32[]{:S(2)}) collective-permute-start(bf16[2,256,1536]{2,1,0:T(8,128)(2,1)S(1)} %multiply_convert_fusion.2.refs_2_.refs_0_), channel_id=1, source_target_pairs={{0,1},{1,0},{2,3},{3,2},{4,5},{5,4},{6,7},{7,6},{8,9},{9,8},{10,11... | collective-permute-start | bytes 4718600 | tf_op jit(solution)/shard_map/ppermute | solution.py:44
  289.1 36.9 %collective-permute-start.15 = (bf16[2,256,1536]{2,1,0:T(8,128)(2,1)S(1)}, bf16[2,256,1536]{2,1,0:T(8,128)(2,1)}, u32[]{:S(2)}, u32[]{:S(2)}) collective-permute-start(bf16[2,256,1536]{2,1,0:T(8,128)(2,1)S(1)} %add_convert_fusion.3.refs_0_), channel_id=1, source_target_pairs={{0,2},{1,3},{2,0},{3,1},{4,6},{5,7},{6,4},{7,5},{8,10},{9,11},{10,... | collective-permute-start | bytes 4718600 | tf_op jit(solution)/shard_map/ppermute | solution.py:44
  340.7 23.1 %collective-permute-start.19 = (bf16[2,154,1536]{2,0,1:T(2,128)(2,1)S(1)}, bf16[2,154,1536]{2,0,1:T(2,128)(2,1)S(1)}, u32[]{:S(2)}, u32[]{:S(2)}) collective-permute-start(bf16[2,154,1536]{2,0,1:T(2,128)(2,1)S(1)} %copy.76), channel_id=1, source_target_pairs={{0,2},{1,3},{2,0},{3,1},{4,6},{5,7},{6,4},{7,5},{8,10},{9,11},{10,... | collective-permute-start | bytes 2838536 | tf_op jit(solution)/shard_map/ppermute | solution.py:44
  382.3 34.0 %collective-permute-start.20 = (bf16[2,256,1536]{2,1,0:T(8,128)(2,1)S(1)}, bf16[2,256,1536]{2,1,0:T(8,128)(2,1)S(1)}, u32[]{:S(2)}, u32[]{:S(2)}) collective-permute-start(bf16[2,256,1536]{2,1,0:T(8,128)(2,1)S(1)} %get-tuple-element.200), channel_id=1, source_target_pairs={{0,1},{1,0},{2,3},{3,2},{4,5},{5,4},{6,7},{7,6},{8,9},{9,8},{10,11... | collective-permute-start | bytes 4718600 | tf_op jit(solution)/shard_map/ppermute | solution.py:44
  384.4 36.6 %collective-permute-start.22 = (bf16[2,256,1536]{2,1,0:T(8,128)(2,1)}, bf16[2,256,1536]{2,1,0:T(8,128)(2,1)}, u32[]{:S(2)}, u32[]{:S(2)}) collective-permute-start(bf16[2,256,1536]{2,1,0:T(8,128)(2,1)} %add_convert_fusion.2), channel_id=1, source_target_pairs={{0,2},{1,3},{2,0},{3,1},{4,6},{5,7},{6,4},{7,5},{8,10},{9,11},{10,... | collective-permute-start | bytes 4718600 | tf_op jit(solution)/shard_map/ppermute | solution.py:44
  425.8 441.3 %reduce-scatter.3.cloned.1.call-start = ((), (), s32[]{:S(2)}) async-start(), calls=%async_computation.5 | async-start | bytes 9289728 | tf_op jit(solution)/shard_map/reduce_scatter | solution.py:638
  438.2 46.1 %collective-permute-start.23 = (bf16[2,256,1536]{2,1,0:T(8,128)(2,1)S(1)}, bf16[2,256,1536]{2,1,0:T(8,128)(2,1)}, u32[]{:S(2)}, u32[]{:S(2)}) collective-permute-start(bf16[2,256,1536]{2,1,0:T(8,128)(2,1)S(1)} %multiply_convert_fusion.1.refs_0_), channel_id=1, source_target_pairs={{0,2},{1,3},{2,0},{3,1},{4,6},{5,7},{6,4},{7,5},{8,10},{9,11},{10,... | collective-permute-start | bytes 4718600 | tf_op jit(solution)/shard_map/ppermute | solution.py:44
  447.9 37.0 %collective-permute-start.28 = (bf16[2,256,1536]{2,1,0:T(8,128)(2,1)}, bf16[2,256,1536]{2,1,0:T(8,128)(2,1)}, u32[]{:S(2)}, u32[]{:S(2)}) collective-permute-start(bf16[2,256,1536]{2,1,0:T(8,128)(2,1)} %get-tuple-element.225), channel_id=1, source_target_pairs={{0,1},{1,0},{2,3},{3,2},{4,5},{5,4},{6,7},{7,6},{8,9},{9,8},{10,11... | collective-permute-start | bytes 4718600 | tf_op jit(solution)/shard_map/ppermute | solution.py:44
  457.5 32.5 %collective-permute-start.27 = (bf16[2,256,1536]{2,1,0:T(8,128)(2,1)}, bf16[2,256,1536]{2,1,0:T(8,128)(2,1)}, u32[]{:S(2)}, u32[]{:S(2)}) collective-permute-start(bf16[2,256,1536]{2,1,0:T(8,128)(2,1)} %get-tuple-element.229), channel_id=1, source_target_pairs={{0,1},{1,0},{2,3},{3,2},{4,5},{5,4},{6,7},{7,6},{8,9},{9,8},{10,11... | collective-permute-start | bytes 4718600 | tf_op jit(solution)/shard_map/ppermute | solution.py:44
  488.5 93.6 %collective-permute-start.29 = (bf16[2,256,1536]{2,1,0:T(8,128)(2,1)}, bf16[2,256,1536]{2,1,0:T(8,128)(2,1)}, u32[]{:S(2)}, u32[]{:S(2)}) collective-permute-start(bf16[2,256,1536]{2,1,0:T(8,128)(2,1)} %add_convert_fusion.1), channel_id=1, source_target_pairs={{0,2},{1,3},{2,0},{3,1},{4,6},{5,7},{6,4},{7,5},{8,10},{9,11},{10,... | collective-permute-start | bytes 4718600 | tf_op jit(solution)/shard_map/ppermute | solution.py:44
  495.9 78.7 %collective-permute-start.32 = (bf16[2,154,1536]{2,0,1:T(2,128)(2,1)}, bf16[2,154,1536]{2,0,1:T(2,128)(2,1)}, u32[]{:S(2)}, u32[]{:S(2)}) collective-permute-start(bf16[2,154,1536]{2,0,1:T(2,128)(2,1)} %copy.81), channel_id=1, source_target_pairs={{0,2},{1,3},{2,0},{3,1},{4,6},{5,7},{6,4},{7,5},{8,10},{9,11},{10,... | collective-permute-start | bytes 2838536 | tf_op jit(solution)/shard_map/ppermute | solution.py:44
  570.7 43.7 %collective-permute-start.31 = (bf16[192,1792]{1,0:T(8,128)(2,1)}, bf16[192,1792]{1,0:T(8,128)(2,1)}, u32[]{:S(2)}, u32[]{:S(2)}) collective-permute-start(bf16[192,1792]{1,0:T(8,128)(2,1)} %dynamic-slice.1), channel_id=1, source_target_pairs={{0,4},{8,0},{16,8},{24,16},{28,24},{20,28},{12,20},{4,12},{1,5},{9... | collective-permute-start | bytes 2064392 | tf_op jit(solution)/shard_map/ppermute | solution.py:131
  572.6 30.4 %collective-permute-start.30 = (bf16[192,1664]{1,0:T(8,128)(2,1)}, bf16[192,1664]{1,0:T(8,128)(2,1)}, u32[]{:S(2)}, u32[]{:S(2)}) collective-permute-start(bf16[192,1664]{1,0:T(8,128)(2,1)} %constant_dynamic-slice_fusion), channel_id=1, source_target_pairs={{0,8},{8,16},{16,24},{24,28},{28,20},{20,12},{12,4},{4,0},{1,9},{9... | collective-permute-start | bytes 1916936 | tf_op jit(solution)/shard_map/ppermute | solution.py:131
  618.2 48.1 %collective-permute-start.33 = (bf16[192,3456]{1,0:T(8,128)(2,1)}, bf16[192,3456]{1,0:T(8,128)(2,1)}, u32[]{:S(2)}, u32[]{:S(2)}) collective-permute-start(bf16[192,3456]{1,0:T(8,128)(2,1)} %get-tuple-element.399), channel_id=1, source_target_pairs={{0,8},{8,16},{16,24},{24,28},{28,20},{20,12},{12,4},{4,0},{1,9},{9... | collective-permute-start | bytes 3981320 | tf_op jit(solution)/shard_map/ppermute | solution.py:131
  619.9 46.4 %collective-permute-start.34 = (bf16[192,3456]{1,0:T(8,128)(2,1)}, bf16[192,3456]{1,0:T(8,128)(2,1)}, u32[]{:S(2)}, u32[]{:S(2)}) collective-permute-start(bf16[192,3456]{1,0:T(8,128)(2,1)} %get-tuple-element.398), channel_id=1, source_target_pairs={{0,4},{8,0},{16,8},{24,16},{28,24},{20,28},{12,20},{4,12},{1,5},{9... | collective-permute-start | bytes 3981320 | tf_op jit(solution)/shard_map/ppermute | solution.py:131
  672.5 23.7 %collective-permute-start.40 = (f32[2,154,1536]{2,0,1:T(2,128)S(1)}, f32[2,154,1536]{2,0,1:T(2,128)S(1)}, u32[]{:S(2)}, u32[]{:S(2)}) collective-permute-start(f32[2,154,1536]{2,0,1:T(2,128)S(1)} %copy.87), channel_id=1, source_target_pairs={{0,1},{1,0},{2,3},{3,2},{4,5},{5,4},{6,7},{7,6},{8,9},{9,8},{10,11... | collective-permute-start | bytes 5677064 | tf_op jit(solution)/shard_map/ppermute | solution.py:44
  684.5 59.5 %collective-permute-start.42 = (bf16[192,3456]{1,0:T(8,128)(2,1)}, bf16[192,3456]{1,0:T(8,128)(2,1)}, u32[]{:S(2)}, u32[]{:S(2)}) collective-permute-start(bf16[192,3456]{1,0:T(8,128)(2,1)} %get-tuple-element.397), channel_id=1, source_target_pairs={{0,8},{8,16},{16,24},{24,28},{28,20},{20,12},{12,4},{4,0},{1,9},{9... | collective-permute-start | bytes 3981320 | tf_op jit(solution)/shard_map/ppermute | solution.py:131
  686.0 78.0 %collective-permute-start.43 = (bf16[192,3456]{1,0:T(8,128)(2,1)}, bf16[192,3456]{1,0:T(8,128)(2,1)}, u32[]{:S(2)}, u32[]{:S(2)}) collective-permute-start(bf16[192,3456]{1,0:T(8,128)(2,1)} %get-tuple-element.396), channel_id=1, source_target_pairs={{0,4},{8,0},{16,8},{24,16},{28,24},{20,28},{12,20},{4,12},{1,5},{9... | collective-permute-start | bytes 3981320 | tf_op jit(solution)/shard_map/ppermute | solution.py:131
  696.1 86.0 %collective-permute-start.37 = (bf16[2,256,1536]{2,1,0:T(8,128)(2,1)S(1)}, bf16[2,256,1536]{2,1,0:T(8,128)(2,1)S(1)}, u32[]{:S(2)}, u32[]{:S(2)}) collective-permute-start(bf16[2,256,1536]{2,1,0:T(8,128)(2,1)S(1)} %get-tuple-element.294), channel_id=1, source_target_pairs={{0,1},{1,0},{2,3},{3,2},{4,5},{5,4},{6,7},{7,6},{8,9},{9,8},{10,11... | collective-permute-start | bytes 4718600 | tf_op jit(solution)/shard_map/ppermute | solution.py:44
  698.1 23.9 %collective-permute-start.41 = (bf16[2,154,1536]{2,0,1:T(2,128)(2,1)S(1)}, bf16[2,154,1536]{2,0,1:T(2,128)(2,1)S(1)}, u32[]{:S(2)}, u32[]{:S(2)}) collective-permute-start(bf16[2,154,1536]{2,0,1:T(2,128)(2,1)S(1)} %copy.89), channel_id=1, source_target_pairs={{0,2},{1,3},{2,0},{3,1},{4,6},{5,7},{6,4},{7,5},{8,10},{9,11},{10,... | collective-permute-start | bytes 2838536 | tf_op jit(solution)/shard_map/ppermute | solution.py:44
  701.4 80.7 %collective-permute-start.39 = (bf16[2,256,1536]{2,1,0:T(8,128)(2,1)S(1)}, bf16[2,256,1536]{2,1,0:T(8,128)(2,1)S(1)}, u32[]{:S(2)}, u32[]{:S(2)}) collective-permute-start(bf16[2,256,1536]{2,1,0:T(8,128)(2,1)S(1)} %add_convert_fusion), channel_id=1, source_target_pairs={{0,2},{1,3},{2,0},{3,1},{4,6},{5,7},{6,4},{7,5},{8,10},{9,11},{10,... | collective-permute-start | bytes 4718600 | tf_op jit(solution)/shard_map/ppermute | solution.py:44
  722.0 53.0 %collective-permute-start.36 = (bf16[2,154,1536]{2,0,1:T(2,128)(2,1)S(1)}, bf16[2,154,1536]{2,0,1:T(2,128)(2,1)S(1)}, u32[]{:S(2)}, u32[]{:S(2)}) collective-permute-start(bf16[2,154,1536]{2,0,1:T(2,128)(2,1)S(1)} %copy.85), channel_id=1, source_target_pairs={{0,2},{1,3},{2,0},{3,1},{4,6},{5,7},{6,4},{7,5},{8,10},{9,11},{10,... | collective-permute-start | bytes 2838536 | tf_op jit(solution)/shard_map/ppermute | solution.py:44
  767.2 43.1 %collective-permute-start.44 = (bf16[192,3456]{1,0:T(8,128)(2,1)S(1)}, bf16[192,3456]{1,0:T(8,128)(2,1)S(1)}, u32[]{:S(2)}, u32[]{:S(2)}) collective-permute-start(bf16[192,3456]{1,0:T(8,128)(2,1)S(1)} %get-tuple-element.395), channel_id=1, source_target_pairs={{0,8},{8,16},{16,24},{24,28},{28,20},{20,12},{12,4},{4,0},{1,9},{9... | collective-permute-start | bytes 3981320 | tf_op jit(solution)/shard_map/ppermute | solution.py:131
  767.3 43.1 %collective-permute-start.45 = (bf16[192,3456]{1,0:T(8,128)(2,1)S(1)}, bf16[192,3456]{1,0:T(8,128)(2,1)S(1)}, u32[]{:S(2)}, u32[]{:S(2)}) collective-permute-start(bf16[192,3456]{1,0:T(8,128)(2,1)S(1)} %get-tuple-element.394), channel_id=1, source_target_pairs={{0,4},{8,0},{16,8},{24,16},{28,24},{20,28},{12,20},{4,12},{1,5},{9... | collective-permute-start | bytes 3981320 | tf_op jit(solution)/shard_map/ppermute | solution.py:131
  (169 other events, 2516.5 us)
Sparse Core Ops, SparseCore 0:
  11.7 147.2 all-gather.3
  161.8 136.2 all-gather.5
  300.9 136.2 all-gather.7
  440.6 173.4 reduce-scatter.4
  660.3 189.8 reduce-scatter.2
